TPU v7x, 256 devices: a whole 4x4x8 slice. The times are simulated.
256 devices in a mesh: depth: 32 (over y, z), lat: 8 (over x, core).
Axes of the slice: x: 4, y: 4, z: 8, core: 2. Of those that a mesh axis runs over, the one named last changes fastest.
Arguments:
- densities: float32 [8, 1024, 64], P('lat', 'depth'), may hold values from -6 to 6
- source: float32 [8, 1024, 64], P('lat', 'depth'), may hold values from -6 to 6
- jacobian: float32 [8, 1024, 4096], P('lat', 'depth'), may hold values from -0.75 to 0.75
- pattern: int32 [8, 8], replicated, may hold values 0 or 1
- transport: float32 [8, 1024, 64], P('lat', 'depth'), may hold values from 0.2 to 1
- lateral: float32 [8, 1024, 64], P('lat', 'depth'), may hold values from 0.1 to 1
- neighbours: int32 [8, 4], P('lat'), may hold values from 0 to 7, as said below
- factor: float32 [8, 1024, 4096], P('lat', 'depth'), may hold values from -6.1035156e-05 to 0.00012207031
- coupling: float32 [8, 1024, 64], P('lat', 'depth'), may hold values from 8192 to 32768
Outputs:
- correction: float32 [8, 1024, 64], P('lat', 'depth')
Inputs may be any that keep to these rules, and one draw needn't show every extreme that they name: Each line's four neighbours (previous row, next row, previous place, next place) in a periodic arrangement of the lines in rows of 8, under a relabelling of the lines drawn from the seed.
All inputs are finite; a program needn't handle non-finite values.
Results may differ from a plain program's by a relative error of at most 0.0003.
Values sent between devices are 32-bit elements; how exact they have to be, the bound alone decides.
No kernel may reach another device: no remote copies, remote signals or barrier semaphores. Data moves between devices by JAX's collectives and lax.ppermute only.
A program may use at most 128 MiB of HBM per device.

v0:
```python
import jax
import jax.numpy as jnp
from jax import lax
from jax.experimental import pallas as pl
from jax.experimental.pallas import tpu as pltpu
from jax.sharding import PartitionSpec as P

f32 = jnp.float32
bf16 = jnp.bfloat16

CELLS = 32
N = 64
ZS = 8
VLIM = 16 << 20


def lanes(shape):
    return lax.broadcasted_iota(jnp.int32, shape, len(shape) - 1)


def roll(x, shift):
    shift = shift % x.shape[-1]
    return x if shift == 0 else pltpu.roll(x, shift, x.ndim - 1)


def pack(dup):
    hi = dup.astype(bf16).astype(f32)
    return jnp.where(lanes(dup.shape) < N, hi, dup - hi).astype(bf16)


def mm(a, b):
    r = jnp.dot(a, jnp.concatenate([b, b], axis=0), preferred_element_type=f32)
    return r + roll(r, N)


def rhs(x):
    hi = x.astype(bf16).astype(f32)
    y = jnp.where((lanes(x.shape) // CELLS) % 2 == 0, hi, x - hi).astype(bf16)
    return jnp.concatenate([y, y], axis=0)


def fold(r):
    return r + roll(r, CELLS)


def mv(a, x):
    return fold(jnp.dot(a, rhs(x), preferred_element_type=f32))


def stage(mats, x):
    y = rhs(x)
    lane = lanes((N, 128)) % CELLS
    acc = jnp.zeros((N, 128), f32)
    for at, load in mats:
        acc = jnp.where(lane == at, jnp.dot(load(), y, preferred_element_type=f32), acc)
    return fold(acc)


def dup4(x):
    return jnp.concatenate([x, x, x, x], axis=0).T


def eye2():
    return jnp.where(lanes((N, 128)) % N == lax.broadcasted_iota(jnp.int32, (N, 128), 0), 1.0, 0.0)


def put(node, full, j, p, q, w):
    node[j, 0], node[j, 1], node[j, 2] = pack(p), pack(q), pack(w)
    full[j, 0], full[j, 1], full[j, 2] = p, q, w


def tree_leaves(fac_ref, coup_ref, leaf_ref, n1_ref, full_ref, rows):
    c = coup_ref[...]
    c2 = jnp.concatenate([c, c], axis=1)
    low = lanes((CELLS, 128)) < N
    eye = eye2()

    def leaf(k):
        g, s = divmod(k, 8)
        x = fac_ref[pl.ds(g * 256 + s, 32, stride=8), :]
        y = roll(x, N)
        rows[k % 2, pl.ds(0, 32, stride=2), :] = jnp.where(low, x, y)
        rows[k % 2, pl.ds(1, 32, stride=2), :] = jnp.where(low, y, x)
        a = rows[k % 2]
        leaf_ref[k] = pack(a)
        before = max(k - 1, 0)
        return a * c2[before : before + 1] - eye, a * c2[k : k + 1] - eye

    for j in range(CELLS // 2):
        p1, q1 = leaf(2 * j)
        p2, q2 = leaf(2 * j + 1)
        kq1 = pack(q1)
        p = p1 + p2 + mm(pack(p2), pack(p1))
        q = q1 + q2 + mm(kq1, pack(q2))
        w = (eye + eye) + p1 + q1 + p + mm(kq1, pack(p))
        put(n1_ref, full_ref, j, p, q, w)


def tree_upper(n1_ref, full_ref, n2_ref, n3_ref, n4_ref, root_ref, fa, fb):
    node, full = n1_ref, full_ref
    for count, node_to, full_to in ((8, n2_ref, fa), (4, n3_ref, fb), (2, n4_ref, fa), (1, None, None)):
        for j in range(count):
            one, two = 2 * j, 2 * j + 1
            kp1, kq1 = node[one, 0], node[one, 1]
            p = full[one, 0] + full[two, 0] + mm(node[two, 0], kp1)
            t = full[two, 2] + mm(node[two, 2], kp1)
            q = full[one, 1] + full[two, 1] + mm(kq1, node[two, 1])
            w = full[one, 2] + t + mm(kq1, pack(t))
            if node_to is None:
                eye = eye2()
                root_ref[:N] = jnp.where(lanes((N, 128)) < N, p, q) + eye
                root_ref[N:] = w
            else:
                put(node_to, full_to, j, p, q, w)
        node, full = node_to, full_to


def react(jac_ref, dens_ref, src_ref, tran_ref, pat_ref, top_ref, out_ref):
    u = dens_ref[...]
    u2 = jnp.concatenate([u, u], axis=1)
    lane8 = lanes((8, 128))
    pat = pat_ref[...].astype(f32)
    mask_rows = jnp.zeros((8, 128), f32)
    for t in range(8):
        mask_rows = jnp.where((lane8 % N) // 8 == t, pat[:, t : t + 1], mask_rows)
    half = lanes((128, N)) % 2 == lax.broadcasted_iota(jnp.int32, (128, N), 0) // N
    half = jnp.where(half, 1.0, 0.0).astype(bf16)
    lane = lanes((CELLS, N))
    acc = jnp.zeros((CELLS, N), f32)
    for m in range(32):
        y = jac_ref[:, m * 128 : (m + 1) * 128] * (u2 * mask_rows[m // 4 : m // 4 + 1])
        hi = y.astype(bf16)
        lo = (y - hi.astype(f32)).astype(bf16)
        z = jnp.dot(hi, half, preferred_element_type=f32) + jnp.dot(lo, half, preferred_element_type=f32)
        acc = jnp.where(lane // 2 == m, z, acc)
    tran = tran_ref[...]
    flux = tran * u
    row = lax.broadcasted_iota(jnp.int32, (CELLS, N), 0)
    lower = jnp.where(row == 0, 0.0, pltpu.roll(flux, 1, 0))
    upper = jnp.where(row == CELLS - 1, top_ref[0:1], pltpu.roll(u, CELLS - 1, 0))
    out_ref[...] = src_ref[...] - acc + lower + tran * upper


def upsweep(neigh_ref, part_ref, lines_ref, dens_ref, tran_ref, lat_ref, coup_ref, leaf_ref, n1_ref, n2_ref,
            n3_ref, n4_ref, root_ref, pay_ref, vec_ref):
    me = lax.axis_index("lat")
    u = dens_ref[...]
    total = jnp.zeros((CELLS, N), f32)
    for slot, offset in enumerate((0, 1, 2, 3, 6, 7, 4, 5)):
        line = me ^ offset
        count = jnp.int32(0)
        for j in range(4):
            count = count + (neigh_ref[0, j] == line).astype(jnp.int32)
        total = total + count.astype(f32) * lines_ref[slot]
    r_rows = part_ref[...] - lat_ref[...] * (4.0 * u - total)
    r = dup4(r_rows)
    coup = dup4(coup_ref[...])
    lane = lanes((N, 128)) % CELLS
    prev = jnp.where(lane == 0, coup, roll(coup, 1))
    even = [(2 * j, lambda j=j: leaf_ref[2 * j]) for j in range(16)]
    odd = [(2 * j + 1, lambda j=j: leaf_ref[2 * j + 1]) for j in range(16)]
    first = stage(even, r)
    v = stage(odd, r + prev * roll(first, 1))
    w = stage(even, r + coup * roll(v, -1))
    vec_ref[0] = r
    vec_ref[1] = coup
    vec_ref[2] = v
    vec_ref[3] = w
    at = 4
    for h, ref in ((2, n1_ref), (4, n2_ref), (8, n3_ref), (16, n4_ref)):
        count = CELLS // (2 * h)
        v1 = roll(v, 1)
        vs = roll(v, h)
        new_v = v + vs + stage([(2 * h * (j + 1) - 1, lambda j=j, ref=ref: ref[2 * j + 1, 0]) for j in range(count)], vs)
        t = w + stage([(2 * h * j + h, lambda j=j, ref=ref: ref[2 * j + 1, 2]) for j in range(count)], v1)
        ts = roll(t, -h)
        w = w + ts + stage([(2 * h * j, lambda j=j, ref=ref: ref[2 * j, 1]) for j in range(count)], ts)
        v = new_v
        if h < 16:
            vec_ref[at] = v
            vec_ref[at + 1] = w
            at += 2
    last = coup[:, CELLS - 1 : CELLS]
    flux = dup4(tran_ref[...] * u)[:, CELLS - 1 : CELLS]
    low = lanes((N, 128)) < N
    top = root_ref[:N]
    first_c = coup_ref[0:1]
    scale = 1.0 / jnp.concatenate([first_c, first_c], axis=1)
    pay_ref[:N] = jnp.where(low, top * last * scale, top)
    out_v = v[:, CELLS - 1 : CELLS] * last + flux
    tail = jnp.where(lanes((N, 128)) == N, out_v, w[:, 0:1])
    pay_ref[N:] = jnp.where(low, root_ref[N:] * scale, tail)


def unpack(b):
    low = lanes((N, 128)) < N
    b1, b2 = b[:N], b[N:]
    r1, r2 = roll(b1, N), roll(b2, N)
    x = jnp.where(low, b1, r1)
    y = jnp.where(low, r1, b1)
    z = jnp.where(low, b2, r2)
    g = jnp.broadcast_to(b2[:, N : N + 1], (N, 128))
    h = jnp.broadcast_to(b2[:, N + 1 : N + 2], (N, 128))
    return x, y, z, g, h


def repack(ref, x, y, z, g, h):
    lane = lanes((N, 128))
    low = lane < N
    ref[:N] = jnp.where(low, x, y)
    ref[N:] = jnp.where(low, z, jnp.where(lane == N, g, h))


def combine(level, *refs):
    if level == 0:
        own_ref, other_ref, out_ref, fun_out = refs
    else:
        own_ref, other_ref, fun_ref, out_ref, fun_out = refs
    z = lax.axis_index("depth") % ZS
    is_low = ((z // (1, 2, 4)[level]) % 2) == 0
    own, other = own_ref[...], other_ref[...]
    p1, q1, w1, v1, h1 = unpack(jnp.where(is_low, own, other))
    p2, q2, w2, v2, h2 = unpack(jnp.where(is_low, other, own))
    kp1, kq1, kp2, kq2, kw2 = pack(p1), pack(q1), pack(p2), pack(q2), pack(w2)
    t = mm(kw2, kp1)
    th = h2 + mv(kw2, v1)
    p = mm(kp2, kp1)
    v = v2 + mv(kp2, v1)
    q = mm(kq1, kq2)
    kt = pack(t)
    w = w1 + mm(kq1, kt)
    h = h1 + mv(kq1, th)
    repack(out_ref, p, q, w, v, h)
    if level == 0:
        lane = lanes((N, 128))
        eye = jnp.where(lane % N == lax.broadcasted_iota(jnp.int32, (N, 128), 0), 1.0, 0.0)
        repack(
            fun_out,
            jnp.where(is_low, eye, p1),
            jnp.where(is_low, q2, eye),
            jnp.where(is_low, t, 0.0),
            jnp.where(is_low, 0.0, v1),
            jnp.where(is_low, th, 0.0),
        )
    else:
        f, hh, k, g, e = unpack(fun_ref[...])
        kf, kh, kk = pack(f), pack(hh), pack(k)
        x1 = jnp.where(is_low, hh, f)
        kx1 = pack(x1)
        y1 = pack(jnp.where(is_low, q2, p1))
        x2 = pack(jnp.where(is_low, hh, k))
        y2 = pack(jnp.where(is_low, t, p1))
        prod1 = mm(kx1, y1)
        prod2 = mm(x2, y2)
        vec2 = mv(x2, jnp.where(is_low, th, v1))
        vec1 = mv(kf, v1)
        repack(
            fun_out,
            jnp.where(is_low, f, prod1),
            jnp.where(is_low, prod1, hh),
            jnp.where(is_low, k + prod2, prod2),
            jnp.where(is_low, g, g + vec1),
            e + vec2,
        )


def downsweep(own_ref, y1_ref, y3_ref, y2_ref, fun_ref, vec_ref, leaf_ref, n1_ref, n2_ref, n3_ref, n4_ref,
              out_ref, slots):
    yi = lax.axis_index("depth") // ZS
    slots[yi] = own_ref[...]
    slots[yi ^ 1] = y1_ref[...]
    slots[yi ^ 3] = y3_ref[...]
    slots[yi ^ 2] = y2_ref[...]
    f, hh, k, g, e = unpack(fun_ref[...])
    maps = [unpack(slots[i]) for i in range(4)]
    s1 = maps[0][3]
    s2 = mv(pack(maps[1][0]), s1) + maps[1][3]
    s3 = mv(pack(maps[2][0]), s2) + maps[2][3]
    a2 = mv(pack(maps[3][2]), s3) + maps[3][4]
    a1 = mv(pack(maps[2][1]), a2) + mv(pack(maps[2][2]), s2) + maps[2][4]
    a0 = mv(pack(maps[1][1]), a1) + mv(pack(maps[1][2]), s1) + maps[1][4]
    s = jnp.where(yi == 0, 0.0, jnp.where(yi == 1, s1, jnp.where(yi == 2, s2, s3)))
    a = jnp.where(yi == 3, 0.0, jnp.where(yi == 2, a2, jnp.where(yi == 1, a1, a0)))
    s_in = mv(pack(f), s) + g
    a_in = mv(pack(hh), a) + mv(pack(k), s) + e
    lane = lanes((N, 128)) % CELLS
    r, coup = vec_ref[0], vec_ref[1]
    prev = jnp.where(lane == 0, coup, roll(coup, 1))
    ss, aa = s_in / coup[:, 0:1], a_in
    at = 8
    for h, ref in ((16, n4_ref), (8, n3_ref), (4, n2_ref), (2, n1_ref)):
        count = CELLS // (2 * h)
        v, w = vec_ref[at], vec_ref[at + 1]
        at -= 2
        x1 = stage([(2 * h * j, lambda j=j, ref=ref: ref[2 * j, 0]) for j in range(count)], ss)
        x2 = stage([(2 * h * (j + 1) - 1, lambda j=j, ref=ref: ref[2 * j + 1, 1]) for j in range(count)], aa)
        mid = lane % (2 * h) == h
        ss = jnp.where(mid, roll(ss + x1, h) + roll(v, 1), ss)
        x3 = stage([(2 * h * j + h, lambda j=j, ref=ref: ref[2 * j + 1, 2]) for j in range(count)], ss)
        z = roll(aa + x2, -(h - 1)) + x3 + w
        aa = jnp.where(lane % (2 * h) == h - 1, roll(z, -1), aa)
    even = [(2 * j, lambda j=j: leaf_ref[2 * j]) for j in range(16)]
    odd = [(2 * j + 1, lambda j=j: leaf_ref[2 * j + 1]) for j in range(16)]
    base = r + prev * ss
    f1 = stage(even, base)
    x2 = stage(odd, r + prev * roll(f1, 1) + coup * aa)
    x1 = stage(even, base + coup * roll(x2, -1))
    x = jnp.where(lane % 2 == 0, x1, x2)
    out_ref[...] = x.T[:CELLS]


def sds(*shape, dtype=f32):
    return jax.ShapeDtypeStruct(shape, dtype)


def vmem():
    return pl.BlockSpec(memory_space=pltpu.VMEM)


def call(body, outs, n_in, *args, scratch=(), smem=0, flops=0, moved=0, name=None):
    return pl.pallas_call(
        body,
        out_shape=outs,
        in_specs=[pl.BlockSpec(memory_space=pltpu.SMEM)] * smem + [vmem()] * (n_in - smem),
        out_specs=jax.tree.map(lambda _: vmem(), outs),
        scratch_shapes=scratch,
        cost_estimate=pl.CostEstimate(flops=flops, bytes_accessed=moved, transcendentals=0),
        name=name,
        compiler_params=pltpu.CompilerParams(vmem_limit_bytes=VLIM),
    )(*args)


def on_device(densities, source, jacobian, pattern, transport, lateral, neighbours, factor, coupling):
    line_count, cell_count, species = densities.shape
    u = densities.reshape(CELLS, N)
    src = source.reshape(CELLS, N)
    tran = transport.reshape(CELLS, N)
    lat = lateral.reshape(CELLS, N)
    coup = coupling.reshape(CELLS, N)
    jac = jacobian.reshape(CELLS, N * N)
    fac = factor.reshape(4, 8, 32, 128).transpose(0, 2, 1, 3).reshape(1024, 128)

    def xor_lat(value, bits):
        return lax.ppermute(value, "lat", [(i, i ^ bits) for i in range(8)])

    def xor_depth(value, bits):
        return lax.ppermute(value, "depth", [(i, i ^ bits) for i in range(32)])

    top = lax.ppermute(u[0:8], "depth", [(i + 1, i) for i in range(31)])
    lines = u[None]
    lines = jnp.concatenate([lines, xor_lat(lines, 1)], axis=0)
    lines = jnp.concatenate([lines, xor_lat(lines, 2)], axis=0)
    lines = jnp.concatenate([lines, xor_lat(lines, 6)], axis=0)

    leaf, n1, full = call(
        tree_leaves,
        (sds(CELLS, N, 128, dtype=bf16), sds(16, 3, N, 128, dtype=bf16), sds(16, 3, N, 128)),
        2, fac, coup,
        scratch=[pltpu.VMEM((2, N, 128), f32)], flops=2 << 30, moved=1 << 21, name="tree_leaves",
    )
    n2, n3, n4, root = call(
        tree_upper,
        (sds(8, 3, N, 128, dtype=bf16), sds(4, 3, N, 128, dtype=bf16), sds(2, 3, N, 128, dtype=bf16), sds(128, 128)),
        2, n1, full,
        scratch=[pltpu.VMEM((8, 3, N, 128), f32), pltpu.VMEM((4, 3, N, 128), f32)],
        flops=2 << 30, moved=1 << 21, name="tree_upper",
    )
    part = call(react, sds(CELLS, N), 6, jac, u, src, tran, pattern, top, flops=1 << 30, moved=1 << 19, name="react")
    pay, vec = call(
        upsweep, (sds(128, 128), sds(10, N, 128)), 13,
        neighbours, part, lines, u, tran, lat, coup, leaf, n1, n2, n3, n4, root,
        smem=1, flops=1 << 25, moved=1 << 20, name="upsweep",
    )
    fun = None
    for level, bits in enumerate((1, 2, 7)):
        other = xor_depth(pay, bits)
        args = (pay, other) if level == 0 else (pay, other, fun)
        pay, fun = call(
            lambda *refs, level=level: combine(level, *refs), (sds(128, 128), sds(128, 128)), len(args), *args,
            flops=1 << 24, moved=1 << 18, name=f"combine{level}",
        )
    y1, y3, y2 = xor_depth(pay, 8), xor_depth(pay, 24), xor_depth(pay, 16)
    out = call(
        downsweep, sds(CELLS, N), 11, pay, y1, y3, y2, fun, vec, leaf, n1, n2, n3, n4,
        scratch=[pltpu.VMEM((4, 128, 128), f32)], flops=1 << 25, moved=1 << 20, name="downsweep",
    )
    return out.reshape(line_count, cell_count, species)


def solution(mesh):
    return jax.shard_map(
        on_device,
        mesh=mesh,
        in_specs=(
            P("lat", "depth", None),
            P("lat", "depth", None),
            P("lat", "depth", None),
            P(),
            P("lat", "depth", None),
            P("lat", "depth", None),
            P("lat", None),
            P("lat", "depth", None),
            P("lat", "depth", None),
        ),
        out_specs=P("lat", "depth", None),
        check_vma=False,
    )
```

profile of v0, /device:TPU:32, one launch (start us, length us, event | category | flops | bytes accessed | tf_op | source)
XLA Modules:
  0.0 58.4 jit_solution(9592396578233218575)
XLA Ops:
  0.0 0.7 %slice_bitcast_fusion = f32[8,64]{1,0:T(8,128)S(1)} fusion(f32[1,32,64]{2,1,0:T(8,128)} %param.9), kind=kLoop, calls=%fused_computation.3 | loop fusion | bytes 4096 | tf_op jit(solution)/shard_map/slice | solution.py:349
  0.7 3.7 %collective-permute-start = (f32[8,64]{1,0:T(8,128)S(1)}, f32[8,64]{1,0:T(8,128)S(1)}, u32[]{:S(2)}, u32[]{:S(2)}) collective-permute-start(f32[8,64]{1,0:T(8,128)S(1)} %slice_bitcast_fusion), channel_id=1, source_target_pairs={{8,0},{16,8},{24,16},{32,24},{40,32},{48,40},{56,48},{64,56},{72,6... | collective-permute-start | bytes 6152 | tf_op jit(solution)/shard_map/ppermute | solution.py:349
  4.4 0.0 copy-start.3
  4.4 0.7 %copy-done.3 = f32[1,32,64]{2,1,0:T(8,128)S(1)} copy-done((f32[1,32,64]{2,1,0:T(8,128)S(1)}, f32[1,32,64]{2,1,0:T(8,128)}, u32[]{:S(2)}) %copy-start.3) | copy-done | bytes 8216
  5.1 1.0 %copy-done.6 = f32[1,32,4096]{2,1,0:T(8,128)S(1)} copy-done((f32[1,32,4096]{2,1,0:T(8,128)S(1)}, f32[1,32,4096]{2,1,0:T(8,128)}, u32[]{:S(2)}) %copy-start.6) | copy-done | bytes 524312
  6.2 2.6 %tree_leaves.1 = (bf16[32,64,128]{2,1,0:T(8,128)(2,1)S(1)}, bf16[16,3,64,128]{3,2,1,0:T(8,128)(2,1)S(1)}, f32[16,3,64,128]{3,2,1,0:T(8,128)S(1)}) custom-call(f32[1024,128]{1,0:T(8,128)S(1)} %bitcast.21, f32[32,64]{1,0:T(8,128)S(1)} %bitcast.19), custom_call_target="tpu_custom_call" | custom-call | flops 2147483648 | bytes 2097152 | tf_op jit(solution)/shard_map/tree_leaves/pallas_call | solution.py:321
  8.8 0.1 collective-permute-start.2
  8.9 0.0 copy-start.1
  8.9 0.0 copy-start.7
  8.9 0.0 copy-start.9
  8.9 3.9 %tree_upper.1 = (bf16[8,3,64,128]{3,2,1,0:T(8,128)(2,1)S(1)}, bf16[4,3,64,128]{3,2,1,0:T(8,128)(2,1)S(1)}, bf16[2,3,64,128]{3,2,1,0:T(8,128)(2,1)S(1)}, f32[128,128]{1,0:T(8,128)S(1)}) custom-call(bf16[16,3,64,128]{3,2,1,0:T(8,128)(2,1)S(1)} %get-tuple-element.21.n1_ref, f32[16,3,64,128]{3,2,1,0:T(8,128)S(1)} %get-tuple-element.22.full_ref), custom_call_target="tpu_custom_call" | custom-call | flops 2147483648 | bytes 2097152 | tf_op jit(solution)/shard_map/tree_upper/pallas_call | solution.py:321
  12.8 1.9 %collective-permute-start.3 = (f32[4,32,64]{2,1,0:T(8,128)S(1)}, f32[4,32,64]{2,1,0:T(8,128)S(1)}, u32[]{:S(2)}, u32[]{:S(2)}) collective-permute-start(f32[4,32,64]{2,1,0:T(8,128)S(1)} %pad_maximum_fusion.1), channel_id=1, source_target_pairs={{0,6},{1,7},{2,4},{3,5},{4,2},{5,3},{6,0},{7,1},{8,14},{9,15},{10,... | collective-permute-start | bytes 98312 | tf_op jit(solution)/shard_map/ppermute | solution.py:344
  14.8 0.0 copy-start.4
  14.8 0.0 copy-start.5
  14.8 0.7 %react.1.part_ref = f32[32,64]{1,0:T(8,128)S(1)} custom-call(f32[32,4096]{1,0:T(8,128)S(1)} %bitcast.22, f32[32,64]{1,0:T(8,128)S(1)} %bitcast.14, f32[32,64]{1,0:T(8,128)S(1)} %bitcast.23, f32[32,64]{1,0:T(8,128)S(1)} %bitcast.16, s32[8,8]{1,0:T(8,128)S(1)} %copy-done.9, f32[8,64]{1,0:T(8,128)S(1)} %collective-permute-done.top_ref), custom_call_target="tpu_custom_call" | custom-call | flops 1073741824 | bytes 524288 | tf_op jit(solution)/shard_map/react/pallas_call | solution.py:321
  15.6 2.8 %collective-permute-done.3 = f32[4,32,64]{2,1,0:T(8,128)S(1)} collective-permute-done((f32[4,32,64]{2,1,0:T(8,128)S(1)}, f32[4,32,64]{2,1,0:T(8,128)S(1)}, u32[]{:S(2)}, u32[]{:S(2)}) %collective-permute-start.3) | collective-permute-done | bytes 32800 | tf_op jit(solution)/shard_map/ppermute | solution.py:344
  18.4 3.5 %upsweep.1 = (f32[128,128]{1,0:T(8,128)S(1)}, f32[10,64,128]{2,1,0:T(8,128)S(1)}) custom-call(s32[1,4]{1,0:T(1,128)S(1)} %copy-done.5, f32[32,64]{1,0:T(8,128)S(1)} %react.1.part_ref, f32[8,32,64]{2,1,0:T(8,128)S(1)} %pad_maximum_fusion.lines_ref, f32[32,64]{1,0:T(8,128)S(1)} %bitcast.15, f32[32,64]{1,0:T(8,128)S(1)} %bitcast.17, f32[32,64]{1,0:T(8,128)S(1)} %bitcast.18, ...), custom_call_target="tpu_custom_call" | custom-call | flops 33554432 | bytes 1048576 | tf_op jit(solution)/shard_map/upsweep/pallas_call | solution.py:321
  22.0 0.1 collective-permute-start.4
  22.1 4.3 %collective-permute-done.4.refs_1_ = f32[128,128]{1,0:T(8,128)S(1)} collective-permute-done((f32[128,128]{1,0:T(8,128)S(1)}, f32[128,128]{1,0:T(8,128)S(1)}, u32[]{:S(2)}, u32[]{:S(2)}) %collective-permute-start.4) | collective-permute-done | bytes 65568 | tf_op jit(solution)/shard_map/ppermute | solution.py:347
  26.3 0.5 combine0.1
  26.9 3.1 %collective-permute-start.5 = (f32[128,128]{1,0:T(8,128)S(1)}, f32[128,128]{1,0:T(8,128)S(1)}, u32[]{:S(2)}, u32[]{:S(2)}) collective-permute-start(f32[128,128]{1,0:T(8,128)S(1)} %get-tuple-element.28.refs_0_), channel_id=1, source_target_pairs={{0,16},{8,24},{16,0},{24,8},{32,48},{40,56},{48,32},{56,40},{64,80... | collective-permute-start | bytes 196616 | tf_op jit(solution)/shard_map/ppermute | solution.py:347
  30.0 2.2 %collective-permute-done.5.refs_1_ = f32[128,128]{1,0:T(8,128)S(1)} collective-permute-done((f32[128,128]{1,0:T(8,128)S(1)}, f32[128,128]{1,0:T(8,128)S(1)}, u32[]{:S(2)}, u32[]{:S(2)}) %collective-permute-start.5) | collective-permute-done | bytes 65568 | tf_op jit(solution)/shard_map/ppermute | solution.py:347
  32.2 0.6 combine1.1
  32.8 6.6 %collective-permute-start.6 = (f32[128,128]{1,0:T(8,128)S(1)}, f32[128,128]{1,0:T(8,128)S(1)}, u32[]{:S(2)}, u32[]{:S(2)}) collective-permute-start(f32[128,128]{1,0:T(8,128)S(1)} %get-tuple-element.30.refs_0_), channel_id=1, source_target_pairs={{0,56},{8,48},{16,40},{24,32},{32,24},{40,16},{48,8},{56,0},{64,12... | collective-permute-start | bytes 196616 | tf_op jit(solution)/shard_map/ppermute | solution.py:347
  39.4 2.3 %collective-permute-done.6.refs_1_ = f32[128,128]{1,0:T(8,128)S(1)} collective-permute-done((f32[128,128]{1,0:T(8,128)S(1)}, f32[128,128]{1,0:T(8,128)S(1)}, u32[]{:S(2)}, u32[]{:S(2)}) %collective-permute-start.6) | collective-permute-done | bytes 65568 | tf_op jit(solution)/shard_map/ppermute | solution.py:347
  41.7 0.6 combine2.1
  42.3 3.6 %collective-permute-start.7 = (f32[128,128]{1,0:T(8,128)S(1)}, f32[128,128]{1,0:T(8,128)S(1)}, u32[]{:S(2)}, u32[]{:S(2)}) collective-permute-start(f32[128,128]{1,0:T(8,128)S(1)} %get-tuple-element.32.own_ref), channel_id=1, source_target_pairs={{0,64},{8,72},{16,80},{24,88},{32,96},{40,104},{48,112},{56,120},{... | collective-permute-start | bytes 196616 | tf_op jit(solution)/shard_map/ppermute | solution.py:347
  45.9 2.2 %collective-permute-start.8 = (f32[128,128]{1,0:T(8,128)S(1)}, f32[128,128]{1,0:T(8,128)S(1)}, u32[]{:S(2)}, u32[]{:S(2)}) collective-permute-start(f32[128,128]{1,0:T(8,128)S(1)} %get-tuple-element.32.own_ref), channel_id=1, source_target_pairs={{0,192},{8,200},{16,208},{24,216},{32,224},{40,232},{48,240},{56,2... | collective-permute-start | bytes 196616 | tf_op jit(solution)/shard_map/ppermute | solution.py:347
  48.0 1.0 %collective-permute-start.9 = (f32[128,128]{1,0:T(8,128)S(1)}, f32[128,128]{1,0:T(8,128)S(1)}, u32[]{:S(2)}, u32[]{:S(2)}) collective-permute-start(f32[128,128]{1,0:T(8,128)S(1)} %get-tuple-element.32.own_ref), channel_id=1, source_target_pairs={{0,128},{8,136},{16,144},{24,152},{32,160},{40,168},{48,176},{56,1... | collective-permute-start | bytes 196616 | tf_op jit(solution)/shard_map/ppermute | solution.py:347
  49.1 2.3 %collective-permute-done.8.y3_ref = f32[128,128]{1,0:T(8,128)S(1)} collective-permute-done((f32[128,128]{1,0:T(8,128)S(1)}, f32[128,128]{1,0:T(8,128)S(1)}, u32[]{:S(2)}, u32[]{:S(2)}) %collective-permute-start.8) | collective-permute-done | bytes 65568 | tf_op jit(solution)/shard_map/ppermute | solution.py:347
  51.3 2.5 %collective-permute-done.9.y2_ref = f32[128,128]{1,0:T(8,128)S(1)} collective-permute-done((f32[128,128]{1,0:T(8,128)S(1)}, f32[128,128]{1,0:T(8,128)S(1)}, u32[]{:S(2)}, u32[]{:S(2)}) %collective-permute-start.9) | collective-permute-done | bytes 65568 | tf_op jit(solution)/shard_map/ppermute | solution.py:347
  53.8 4.5 %downsweep.1 = f32[32,64]{1,0:T(8,128)} custom-call(f32[128,128]{1,0:T(8,128)S(1)} %get-tuple-element.32.own_ref, f32[128,128]{1,0:T(8,128)S(1)} %collective-permute-done.7.y1_ref, f32[128,128]{1,0:T(8,128)S(1)} %collective-permute-done.8.y3_ref, f32[128,128]{1,0:T(8,128)S(1)} %collective-permute-done.9.y2_ref, f32[128,128]{1,0:T(8,128)S(1)} %get-tuple-element.33.fun_ref, ...), custom_call_target="tpu_custom_call" | custom-call | flops 33554432 | bytes 1048576 | tf_op jit(solution)/shard_map/downsweep/pallas_call | solution.py:321
  (20 shorter events, 0.1 us)
Async XLA Ops:
  0.0 8.7 %collective-permute-start.1 = (f32[1,32,64]{2,1,0:T(8,128)}, f32[1,32,64]{2,1,0:T(8,128)S(1)}, u32[]{:S(2)}, u32[]{:S(2)}) collective-permute-start(f32[1,32,64]{2,1,0:T(8,128)} %param.9), channel_id=1, source_target_pairs={{0,1},{1,0},{2,3},{3,2},{4,5},{5,4},{6,7},{7,6},{8,9},{9,8},{10,11... | collective-permute-start | bytes 24584 | tf_op jit(solution)/shard_map/ppermute | solution.py:344
  0.7 14.1 %collective-permute-start = (f32[8,64]{1,0:T(8,128)S(1)}, f32[8,64]{1,0:T(8,128)S(1)}, u32[]{:S(2)}, u32[]{:S(2)}) collective-permute-start(f32[8,64]{1,0:T(8,128)S(1)} %slice_bitcast_fusion), channel_id=1, source_target_pairs={{8,0},{16,8},{24,16},{32,24},{40,32},{48,40},{56,48},{64,56},{72,6... | collective-permute-start | bytes 6152 | tf_op jit(solution)/shard_map/ppermute | solution.py:349
  4.4 0.7 %copy-start.3 = (f32[1,32,64]{2,1,0:T(8,128)S(1)}, f32[1,32,64]{2,1,0:T(8,128)}, u32[]{:S(2)}) copy-start(f32[1,32,64]{2,1,0:T(8,128)} %param.17) | copy-start | bytes 24580
  5.1 1.0 %copy-start.6 = (f32[1,32,4096]{2,1,0:T(8,128)S(1)}, f32[1,32,4096]{2,1,0:T(8,128)}, u32[]{:S(2)}) copy-start(f32[1,32,4096]{2,1,0:T(8,128)} %param.16) | copy-start | bytes 1572868
  6.2 2.6 %copy-start = (f32[1,32,64]{2,1,0:T(8,128)S(1)}, f32[1,32,64]{2,1,0:T(8,128)}, u32[]{:S(2)}) copy-start(f32[1,32,64]{2,1,0:T(8,128)} %param.9) | copy-start | bytes 24580
  8.8 4.0 %collective-permute-start.2 = (f32[2,32,64]{2,1,0:T(8,128)S(1)}, f32[2,32,64]{2,1,0:T(8,128)S(1)}, u32[]{:S(2)}, u32[]{:S(2)}) collective-permute-start(f32[2,32,64]{2,1,0:T(8,128)S(1)} %pad_maximum_fusion.2), channel_id=1, source_target_pairs={{0,2},{1,3},{2,0},{3,1},{4,6},{5,7},{6,4},{7,5},{8,10},{9,11},{10,... | collective-permute-start | bytes 49160 | tf_op jit(solution)/shard_map/ppermute | solution.py:344
  8.9 5.9 %copy-start.1 = (f32[1,32,64]{2,1,0:T(8,128)S(1)}, f32[1,32,64]{2,1,0:T(8,128)}, u32[]{:S(2)}) copy-start(f32[1,32,64]{2,1,0:T(8,128)} %param.13) | copy-start | bytes 24580
  8.9 5.9 %copy-start.7 = (f32[1,32,4096]{2,1,0:T(8,128)S(1)}, f32[1,32,4096]{2,1,0:T(8,128)}, u32[]{:S(2)}) copy-start(f32[1,32,4096]{2,1,0:T(8,128)} %param.11) | copy-start | bytes 1572868
  8.9 5.9 %copy-start.8 = (f32[1,32,64]{2,1,0:T(8,128)S(1)}, f32[1,32,64]{2,1,0:T(8,128)}, u32[]{:S(2)}) copy-start(f32[1,32,64]{2,1,0:T(8,128)} %param.10) | copy-start | bytes 24580
  8.9 5.9 %copy-start.9 = (s32[8,8]{1,0:T(8,128)S(1)}, s32[8,8]{1,0:T(8,128)}, u32[]{:S(2)}) copy-start(s32[8,8]{1,0:T(8,128)} %pat_ref.1) | copy-start | bytes 772
  12.8 5.6 %collective-permute-start.3 = (f32[4,32,64]{2,1,0:T(8,128)S(1)}, f32[4,32,64]{2,1,0:T(8,128)S(1)}, u32[]{:S(2)}, u32[]{:S(2)}) collective-permute-start(f32[4,32,64]{2,1,0:T(8,128)S(1)} %pad_maximum_fusion.1), channel_id=1, source_target_pairs={{0,6},{1,7},{2,4},{3,5},{4,2},{5,3},{6,0},{7,1},{8,14},{9,15},{10,... | collective-permute-start | bytes 98312 | tf_op jit(solution)/shard_map/ppermute | solution.py:344
  14.8 3.6 %copy-start.2 = (f32[1,32,64]{2,1,0:T(8,128)S(1)}, f32[1,32,64]{2,1,0:T(8,128)}, u32[]{:S(2)}) copy-start(f32[1,32,64]{2,1,0:T(8,128)} %param.14) | copy-start | bytes 24580
  14.8 3.6 %copy-start.4 = (f32[1,32,64]{2,1,0:T(8,128)S(1)}, f32[1,32,64]{2,1,0:T(8,128)}, u32[]{:S(2)}) copy-start(f32[1,32,64]{2,1,0:T(8,128)} %param.17) | copy-start | bytes 24580
  14.8 3.6 %copy-start.5 = (s32[1,4]{1,0:T(1,128)S(1)}, s32[1,4]{1,0:T(1,128)}, u32[]{:S(2)}) copy-start(s32[1,4]{1,0:T(1,128)} %neigh_ref.1) | copy-start | bytes 52
  22.0 4.4 %collective-permute-start.4 = (f32[128,128]{1,0:T(8,128)S(1)}, f32[128,128]{1,0:T(8,128)S(1)}, u32[]{:S(2)}, u32[]{:S(2)}) collective-permute-start(f32[128,128]{1,0:T(8,128)S(1)} %get-tuple-element.27.refs_0_), channel_id=1, source_target_pairs={{0,8},{8,0},{16,24},{24,16},{32,40},{40,32},{48,56},{56,48},{64,72... | collective-permute-start | bytes 196616 | tf_op jit(solution)/shard_map/ppermute | solution.py:347
  26.9 5.3 %collective-permute-start.5 = (f32[128,128]{1,0:T(8,128)S(1)}, f32[128,128]{1,0:T(8,128)S(1)}, u32[]{:S(2)}, u32[]{:S(2)}) collective-permute-start(f32[128,128]{1,0:T(8,128)S(1)} %get-tuple-element.28.refs_0_), channel_id=1, source_target_pairs={{0,16},{8,24},{16,0},{24,8},{32,48},{40,56},{48,32},{56,40},{64,80... | collective-permute-start | bytes 196616 | tf_op jit(solution)/shard_map/ppermute | solution.py:347
  32.8 8.9 %collective-permute-start.6 = (f32[128,128]{1,0:T(8,128)S(1)}, f32[128,128]{1,0:T(8,128)S(1)}, u32[]{:S(2)}, u32[]{:S(2)}) collective-permute-start(f32[128,128]{1,0:T(8,128)S(1)} %get-tuple-element.30.refs_0_), channel_id=1, source_target_pairs={{0,56},{8,48},{16,40},{24,32},{32,24},{40,16},{48,8},{56,0},{64,12... | collective-permute-start | bytes 196616 | tf_op jit(solution)/shard_map/ppermute | solution.py:347
  42.3 6.8 %collective-permute-start.7 = (f32[128,128]{1,0:T(8,128)S(1)}, f32[128,128]{1,0:T(8,128)S(1)}, u32[]{:S(2)}, u32[]{:S(2)}) collective-permute-start(f32[128,128]{1,0:T(8,128)S(1)} %get-tuple-element.32.own_ref), channel_id=1, source_target_pairs={{0,64},{8,72},{16,80},{24,88},{32,96},{40,104},{48,112},{56,120},{... | collective-permute-start | bytes 196616 | tf_op jit(solution)/shard_map/ppermute | solution.py:347
  45.9 5.5 %collective-permute-start.8 = (f32[128,128]{1,0:T(8,128)S(1)}, f32[128,128]{1,0:T(8,128)S(1)}, u32[]{:S(2)}, u32[]{:S(2)}) collective-permute-start(f32[128,128]{1,0:T(8,128)S(1)} %get-tuple-element.32.own_ref), channel_id=1, source_target_pairs={{0,192},{8,200},{16,208},{24,216},{32,224},{40,232},{48,240},{56,2... | collective-permute-start | bytes 196616 | tf_op jit(solution)/shard_map/ppermute | solution.py:347
  48.0 5.8 %collective-permute-start.9 = (f32[128,128]{1,0:T(8,128)S(1)}, f32[128,128]{1,0:T(8,128)S(1)}, u32[]{:S(2)}, u32[]{:S(2)}) collective-permute-start(f32[128,128]{1,0:T(8,128)S(1)} %get-tuple-element.32.own_ref), channel_id=1, source_target_pairs={{0,128},{8,136},{16,144},{24,152},{32,160},{40,168},{48,176},{56,1... | collective-permute-start | bytes 196616 | tf_op jit(solution)/shard_map/ppermute | solution.py:347
where the time goes:
time: 58.9 us; the launch traced here: 58.4 us
  starting transfers between devices  22.3 us (38%)
  Pallas kernels  16.9 us (29%)
  waiting for transfers between devices  16.4 us (28%)
  local copies, waits for them, and re-layouts  2.49 us (4%)
    pallas_call x8, Pallas kernels, call(): pl.pallas_call(body, out_shape=outs, in_specs=[pl.BlockSpec(memory_space=...  16.9 us
    ppermute x6, starting transfers between devices, xor_depth(): return lax.ppermute(value, 'depth', [(i, i ^ bits) for i in range(32)])  16.6 us
    ppermute x6, waiting for transfers between devices, xor_depth(): return lax.ppermute(value, 'depth', [(i, i ^ bits) for i in range(32)])  13.6 us
    ppermute x1, starting transfers between devices, on_device(): top = lax.ppermute(u[0:8], 'depth', [(i + 1, i) for i in range(31)])  3.71 us
    ppermute x3, waiting for transfers between devices, xor_lat(): return lax.ppermute(value, 'lat', [(i, i ^ bits) for i in range(8)])  2.85 us
    ppermute x3, starting transfers between devices, xor_lat(): return lax.ppermute(value, 'lat', [(i, i ^ bits) for i in range(8)])  2.01 us
    unnamed x20, local copies, waits for them, and re-layouts  1.8 us
  transfers between devices with their start and end apart: 10, of which 6 were waited for; matrix products, arithmetic and copies ran while one was open for 1% of the time, Pallas kernels for 12%

commit v1 on v0

v1 whole, which is shorter than its diff:
```python
import jax
import jax.numpy as jnp
from jax import lax
from jax.experimental import pallas as pl
from jax.experimental.pallas import tpu as pltpu
from jax.sharding import PartitionSpec as P

f32 = jnp.float32
bf16 = jnp.bfloat16

CELLS = 32
N = 64
ZS = 8
VLIM = 16 << 20


def lanes(shape):
    return lax.broadcasted_iota(jnp.int32, shape, len(shape) - 1)


def roll(x, shift):
    shift = shift % x.shape[-1]
    return x if shift == 0 else pltpu.roll(x, shift, x.ndim - 1)


def pack(dup):
    hi = dup.astype(bf16).astype(f32)
    return jnp.where(lanes(dup.shape) < N, hi, dup - hi).astype(bf16)


def mm(a, b):
    r = jnp.dot(a, jnp.concatenate([b, b], axis=0), preferred_element_type=f32)
    return r + roll(r, N)


def rhs(x):
    hi = x.astype(bf16).astype(f32)
    y = jnp.where((lanes(x.shape) // CELLS) % 2 == 0, hi, x - hi).astype(bf16)
    return jnp.concatenate([y, y], axis=0)


def fold(r):
    return r + roll(r, CELLS)


def mv(a, x):
    return fold(jnp.dot(a, rhs(x), preferred_element_type=f32))


def stage(mats, x):
    y = rhs(x)
    lane = lanes((N, 128)) % CELLS
    acc = jnp.zeros((N, 128), f32)
    for at, load in mats:
        acc = jnp.where(lane == at, jnp.dot(load(), y, preferred_element_type=f32), acc)
    return fold(acc)


def dup4(x):
    return jnp.concatenate([x, x, x, x], axis=0).T


def eye2():
    return jnp.where(lanes((N, 128)) % N == lax.broadcasted_iota(jnp.int32, (N, 128), 0), 1.0, 0.0)


def put(node, full, j, p, q, w, u):
    node[j, 0], node[j, 1], node[j, 2], node[j, 3] = pack(p), pack(q), pack(w), pack(u)
    full[j, 0], full[j, 1], full[j, 2] = p, q, w


def tree_leaves(fac_ref, coup_ref, after_ref, leaf_ref, n1_ref, full_ref, rows):
    del after_ref
    c = coup_ref[...]
    c2 = jnp.concatenate([c, c], axis=1)
    low = lanes((CELLS, 128)) < N
    eye = eye2()

    def leaf(k):
        g, s = divmod(k, 8)
        x = fac_ref[pl.ds(g * 256 + s, 32, stride=8), :]
        y = roll(x, N)
        rows[k % 2, pl.ds(0, 32, stride=2), :] = jnp.where(low, x, y)
        rows[k % 2, pl.ds(1, 32, stride=2), :] = jnp.where(low, y, x)
        a = rows[k % 2]
        before = max(k - 1, 0)
        return a * c2[before : before + 1] - eye, a * c2[k : k + 1] - eye

    for j in range(CELLS // 2):
        p1, q1 = leaf(2 * j)
        p2, q2 = leaf(2 * j + 1)
        kp1, kq1, kp2, kq2 = pack(p1), pack(q1), pack(p2), pack(q2)
        leaf_ref[j, 0], leaf_ref[j, 1] = kp2, kq2
        p = p1 + p2 + mm(kp2, kp1)
        q = q1 + q2 + mm(kq1, kq2)
        u = eye + q1 + p2 + mm(kq1, kp2)
        w = (eye + eye) + p1 + q1 + p + mm(kq1, pack(p))
        put(n1_ref, full_ref, j, p, q, w, u)


def tree_upper(n1_ref, full_ref, n2_ref, n3_ref, n4_ref, n5_ref, root_ref, fa, fb):
    node, full = n1_ref, full_ref
    for count, node_to, full_to in ((8, n2_ref, fa), (4, n3_ref, fb), (2, n4_ref, fa), (1, None, None)):
        for j in range(count):
            one, two = 2 * j, 2 * j + 1
            kp1, kq1 = node[one, 0], node[one, 1]
            u = full[two, 2] + mm(kq1, node[two, 2])
            p = full[one, 0] + full[two, 0] + mm(node[two, 0], kp1)
            q = full[one, 1] + full[two, 1] + mm(kq1, node[two, 1])
            ku = pack(u)
            w = full[one, 2] + u + mm(ku, kp1)
            if node_to is None:
                eye = eye2()
                n5_ref[0] = ku
                root_ref[:N] = jnp.where(lanes((N, 128)) < N, p, q) + eye
                root_ref[N:] = w
            else:
                put(node_to, full_to, j, p, q, w, u)
        node, full = node_to, full_to


def react(jac_hbm, dens_hbm, src_hbm, tran_hbm, pat_hbm, out_ref, jac_ref, dens_ref, src_ref, tran_ref, pat_ref,
          sems):
    pairs = ((dens_hbm, dens_ref), (pat_hbm, pat_ref), (jac_hbm, jac_ref), (src_hbm, src_ref), (tran_hbm, tran_ref))
    copies = [pltpu.make_async_copy(a, b, sems.at[i]) for i, (a, b) in enumerate(pairs)]
    for copy in copies:
        copy.start()
    half = lanes((128, N)) % 2 == lax.broadcasted_iota(jnp.int32, (128, N), 0) // N
    half = jnp.where(half, 1.0, 0.0).astype(bf16)
    for copy in copies:
        copy.wait()
    u = dens_ref[...]
    u2 = jnp.concatenate([u, u], axis=1)
    lane8 = lanes((8, 128))
    pat = pat_ref[...].astype(f32)
    mask_rows = jnp.zeros((8, 128), f32)
    for t in range(8):
        mask_rows = jnp.where((lane8 % N) // 8 == t, pat[:, t : t + 1], mask_rows)
    lane = lanes((CELLS, N))
    acc = jnp.zeros((CELLS, N), f32)
    for m in range(32):
        y = jac_ref[:, m * 128 : (m + 1) * 128] * (u2 * mask_rows[m // 4 : m // 4 + 1])
        hi = y.astype(bf16)
        lo = (y - hi.astype(f32)).astype(bf16)
        z = jnp.dot(hi, half, preferred_element_type=f32) + jnp.dot(lo, half, preferred_element_type=f32)
        acc = jnp.where(lane // 2 == m, z, acc)
    tran = tran_ref[...]
    flux = tran * u
    row = lax.broadcasted_iota(jnp.int32, (CELLS, N), 0)
    lower = jnp.where(row == 0, 0.0, pltpu.roll(flux, 1, 0))
    upper = jnp.where(row == CELLS - 1, 0.0, pltpu.roll(u, CELLS - 1, 0))
    out_ref[...] = src_ref[...] - acc + lower + tran * upper


LEVELS = (2, 4, 8, 16)


def upsweep(neigh_ref, part_ref, a_ref, b_ref, c_ref, top_ref, dens_ref, tran_ref, lat_ref, coup_ref, leaf_ref,
            n1_ref, n2_ref, n3_ref, n4_ref, n5_ref, root_ref, pay_ref, vec_ref):
    me = lax.axis_index("lat")
    u = dens_ref[...]
    total = jnp.zeros((CELLS, N), f32)
    lines = [(0, u), (1, a_ref[0])] + [(2 + i, b_ref[i]) for i in range(2)]
    lines += [((6, 7, 4, 5)[i], c_ref[i]) for i in range(4)]
    for offset, value in lines:
        line = me ^ offset
        count = jnp.int32(0)
        for j in range(4):
            count = count + (neigh_ref[0, j] == line).astype(jnp.int32)
        total = total + count.astype(f32) * value
    tran = tran_ref[...]
    row = lax.broadcasted_iota(jnp.int32, (CELLS, N), 0)
    r = part_ref[...] - lat_ref[...] * (4.0 * u - total) + jnp.where(row == CELLS - 1, tran * top_ref[0, 0:1], 0.0)
    c = coup_ref[...]
    g = dup4(r / jnp.where(row == 0, c, pltpu.roll(c, 1, 0)))
    lane = lanes((N, 128)) % CELLS
    x = g + stage([(k, (lambda k=k: leaf_ref[k // 2, 0]) if k % 2 else (lambda k=k: n1_ref[k // 2, 0]))
                   for k in range(CELLS)], g)
    v = x + roll(x, 1)
    y = stage([(k, lambda k=k: n1_ref[k // 2, 3 if k % 2 else 2]) for k in range(CELLS)], g)
    w = y + roll(y, -1)
    vec_ref[0], vec_ref[1] = v, w
    refs = (n1_ref, n2_ref, n3_ref, n4_ref, n5_ref)
    for i, h in enumerate(LEVELS):
        count = CELLS // (2 * h)
        ref, above = refs[i], refs[i + 1]
        start = lane % (2 * h) == 0
        x = jnp.where(start, roll(w, -h), roll(v, h))
        x = x + stage([(2 * h * (j + 1) - 1, lambda j=j, ref=ref: ref[2 * j + 1, 0]) for j in range(count)]
                      + [(2 * h * j, lambda j=j, ref=ref: ref[2 * j, 1]) for j in range(count)], x)
        if h < 16:
            y = stage([(2 * h * j, lambda j=j, above=above: above[j, 3]) for j in range(count)], roll(v, -(h - 1)))
        else:
            y = stage([(0, lambda above=above: above[0])], roll(v, -(h - 1)))
        v, w = v + x, w + x + y
        if h < 16:
            vec_ref[2 * i + 2], vec_ref[2 * i + 3] = v, w
    last = dup4(c)[:, CELLS - 1 : CELLS]
    flux = dup4(tran * u)[:, CELLS - 1 : CELLS]
    low = lanes((N, 128)) < N
    first_c = c[0:1]
    scale = 1.0 / jnp.concatenate([first_c, first_c], axis=1)
    pay_ref[:N] = jnp.where(low, root_ref[:N] * last * scale, root_ref[:N])
    out_v = v[:, CELLS - 1 : CELLS] * last + flux
    tail = jnp.where(lanes((N, 128)) == N, out_v, w[:, 0:1])
    pay_ref[N:] = jnp.where(low, root_ref[N:] * scale, tail)


def prepare(vec_ref, n1_ref, n2_ref, n3_ref, n4_ref, t_ref, t0_ref):
    refs = (n1_ref, n2_ref, n3_ref, n4_ref)
    at = 0
    for i, h in enumerate(LEVELS):
        ref = refs[i]
        for j in range(CELLS // (2 * h)):
            kw = ref[2 * j + 1, 2]
            wide = kw.astype(f32)
            t_ref[at] = pack(wide + roll(wide, N) + mm(kw, ref[2 * j, 0]))
            at += 1
        v, w = vec_ref[2 * i], vec_ref[2 * i + 1]
        t0_ref[i] = w + stage([(2 * h * j + h, lambda j=j, ref=ref: ref[2 * j + 1, 2])
                               for j in range(CELLS // (2 * h))], roll(v, 1))


def unpack(b):
    low = lanes((N, 128)) < N
    b1, b2 = b[:N], b[N:]
    r1, r2 = roll(b1, N), roll(b2, N)
    x = jnp.where(low, b1, r1)
    y = jnp.where(low, r1, b1)
    z = jnp.where(low, b2, r2)
    g = jnp.broadcast_to(b2[:, N : N + 1], (N, 128))
    h = jnp.broadcast_to(b2[:, N + 1 : N + 2], (N, 128))
    return x, y, z, g, h


def repack(ref, x, y, z, g, h):
    lane = lanes((N, 128))
    low = lane < N
    ref[:N] = jnp.where(low, x, y)
    ref[N:] = jnp.where(low, z, jnp.where(lane == N, g, h))


def combine(level, *refs):
    if level == 0:
        own_ref, other_ref, out_ref, fun_out = refs
    else:
        own_ref, other_ref, fun_ref, out_ref, fun_out = refs
    at = lax.axis_index("depth")
    is_low = ((at // (1, 2, 4, 8)[level]) % 2) == 0
    own, other = own_ref[...], other_ref[...]
    p1, q1, w1, v1, h1 = unpack(jnp.where(is_low, own, other))
    p2, q2, w2, v2, h2 = unpack(jnp.where(is_low, other, own))
    kp1, kq1, kp2, kw2 = pack(p1), pack(q1), pack(p2), pack(w2)
    t = mm(kw2, kp1)
    th = h2 + mv(kw2, v1)
    v = v2 + mv(kp2, v1)
    w = w1 + mm(kq1, pack(t))
    h = h1 + mv(kq1, th)
    lane = lanes((N, 128))
    low = lane < N
    tail = jnp.where(low, w, jnp.where(lane == N, v, h))
    if level == 3:
        out_ref[...] = tail
    else:
        out_ref[:N] = jnp.where(low, mm(kp2, kp1), mm(kq1, pack(q2)))
        out_ref[N:] = tail
    if level == 0:
        eye = eye2()
        repack(
            fun_out,
            jnp.where(is_low, eye, p1),
            jnp.where(is_low, q2, eye),
            jnp.where(is_low, t, 0.0),
            jnp.where(is_low, 0.0, v1),
            jnp.where(is_low, th, 0.0),
        )
    else:
        f, hh, k, g, e = unpack(fun_ref[...])
        x1 = pack(jnp.where(is_low, hh, f))
        y1 = pack(jnp.where(is_low, q2, p1))
        x2 = pack(jnp.where(is_low, hh, k))
        y2 = pack(jnp.where(is_low, t, p1))
        prod1 = mm(x1, y1)
        prod2 = mm(x2, y2)
        vec1 = mv(x1, v1)
        vec2 = mv(x2, jnp.where(is_low, th, v1))
        repack(
            fun_out,
            jnp.where(is_low, f, prod1),
            jnp.where(is_low, prod1, hh),
            jnp.where(is_low, k + prod2, prod2),
            jnp.where(is_low, g, g + vec1),
            e + vec2,
        )


def downsweep(own_ref, other_ref, fun_ref, vec_ref, t0_ref, coup_ref, leaf_ref, n1_ref, n2_ref, n3_ref, n4_ref, t_ref,
              out_ref):
    is_low = lax.axis_index("depth") < 2 * ZS
    f, hh, k, g, e = unpack(fun_ref[...])
    own, other = own_ref[...], other_ref[...]
    other_w = jnp.where(lanes((N, 128)) < N, other, roll(other, N))
    v_own = jnp.broadcast_to(own[:, N : N + 1], (N, 128))
    v_other = jnp.broadcast_to(other[:, N : N + 1], (N, 128))
    w_other = jnp.broadcast_to(other[:, N + 1 : N + 2], (N, 128))
    up = g + mv(pack(f), v_other)
    t = w_other + mv(pack(other_w), v_own)
    a_in = e + mv(pack(jnp.where(is_low, hh, k)), jnp.where(is_low, t, v_other))
    s_in = jnp.where(is_low, g, up)
    lane = lanes((N, 128)) % CELLS
    ss, aa = s_in / dup4(coup_ref[...])[:, 0:1], a_in
    first = (14, 12, 8, 0)
    for i, h, ref in ((3, 16, n4_ref), (2, 8, n3_ref), (1, 4, n2_ref), (0, 2, n1_ref)):
        count = CELLS // (2 * h)
        base = first[3 - i]
        v = vec_ref[2 * i]
        x = jnp.where(lane % (2 * h) == 0, ss, aa)
        y = x + stage([(2 * h * j, lambda j=j, ref=ref: ref[2 * j, 0]) for j in range(count)]
                      + [(2 * h * (j + 1) - 1, lambda j=j, ref=ref: ref[2 * j + 1, 1]) for j in range(count)], x)
        z = stage([(2 * h * j, lambda j=j, base=base: t_ref[base + j]) for j in range(count)], ss)
        ss = jnp.where(lane % (2 * h) == h, roll(y, h) + roll(v, 1), ss)
        aa = jnp.where(lane % (2 * h) == h - 1, roll(y, -h) + roll(z, h - 1) + roll(t0_ref[i], -1), aa)
    even = lane % 2 == 0
    x = jnp.where(even, ss, aa)
    y = stage([(k, lambda k=k: n1_ref[k // 2, 1 if k % 2 else 2]) for k in range(CELLS)], x)
    z = x + stage([(k, (lambda k=k: leaf_ref[k // 2, 1]) if k % 2 else (lambda k=k: n1_ref[k // 2, 0]))
                   for k in range(CELLS)], x)
    x1 = y + roll(aa + y, -1) + vec_ref[1]
    x2 = z + roll(z, 1) + vec_ref[0]
    out_ref[...] = jnp.where(even, x1, x2).T[:CELLS]


def sds(*shape, dtype=f32):
    return jax.ShapeDtypeStruct(shape, dtype)


def call(body, outs, *args, scratch=(), smem=0, hbm=0, flops=0, name=None):
    args = [pltpu.with_memory_space_constraint(x, pltpu.HBM) if smem <= i < smem + hbm else x for i, x in enumerate(args)]
    spaces = [pltpu.SMEM] * smem + [pltpu.HBM] * hbm + [pltpu.VMEM] * (len(args) - smem - hbm)
    return pl.pallas_call(
        body,
        out_shape=outs,
        in_specs=[pl.BlockSpec(memory_space=space) for space in spaces],
        out_specs=jax.tree.map(lambda _: pl.BlockSpec(memory_space=pltpu.VMEM), outs),
        scratch_shapes=scratch,
        cost_estimate=pl.CostEstimate(flops=flops, bytes_accessed=1 << 16, transcendentals=0),
        name=name,
        compiler_params=pltpu.CompilerParams(vmem_limit_bytes=VLIM),
    )(*args)


def node(count):
    return sds(count, 4, N, 128, dtype=bf16)


def on_device(densities, source, jacobian, pattern, transport, lateral, neighbours, factor, coupling):
    line_count, cell_count, species = densities.shape
    u = densities.reshape(CELLS, N)
    src = source.reshape(CELLS, N)
    tran = transport.reshape(CELLS, N)
    lat = lateral.reshape(CELLS, N)
    coup = coupling.reshape(CELLS, N)
    jac = jacobian.reshape(CELLS, N * N)
    fac = factor.reshape(4, 8, 32, 128).transpose(0, 2, 1, 3).reshape(1024, 128)

    def xor_lat(value, bits):
        return lax.ppermute(value, "lat", [(i, i ^ bits) for i in range(8)])

    def xor_depth(value, bits):
        return lax.ppermute(value, "depth", [(i, i ^ bits) for i in range(32)])

    line_a = xor_lat(densities, 1)
    part = call(
        react, sds(CELLS, N), jac, u, src, tran, pattern, hbm=5, flops=1 << 30, name="react",
        scratch=[pltpu.VMEM((CELLS, N * N), f32)] + [pltpu.VMEM((CELLS, N), f32)] * 3
        + [pltpu.VMEM((8, 8), jnp.int32), pltpu.SemaphoreType.DMA((5,))],
    )
    line_b = xor_lat(jnp.concatenate([densities, line_a], axis=0), 2)
    leaf, n1, full = call(
        tree_leaves,
        (sds(16, 2, N, 128, dtype=bf16), node(16), sds(16, 3, N, 128)),
        fac, coup, part, scratch=[pltpu.VMEM((2, N, 128), f32)], flops=2 << 30, name="tree_leaves",
    )
    top = lax.ppermute(densities, "depth", [(i + 1, i) for i in range(31)])
    line_c = xor_lat(jnp.concatenate([densities, line_a, line_b], axis=0), 6)
    n2, n3, n4, n5, root = call(
        tree_upper,
        (node(8), node(4), node(2), sds(1, N, 128, dtype=bf16), sds(128, 128)),
        n1, full, scratch=[pltpu.VMEM((8, 3, N, 128), f32), pltpu.VMEM((4, 3, N, 128), f32)],
        flops=2 << 30, name="tree_upper",
    )
    pay, vec = call(
        upsweep, (sds(128, 128), sds(8, N, 128)),
        neighbours, part, line_a, line_b, line_c, top, u, tran, lat, coup, leaf, n1, n2, n3, n4, n5, root,
        smem=1, flops=1 << 25, name="upsweep",
    )
    fun = None
    for level, bits in enumerate((1, 2, 7, 8)):
        other = xor_depth(pay, bits)
        if level == 0:
            tees, t0 = call(
                prepare, (sds(15, N, 128, dtype=bf16), sds(4, N, 128)), vec, n1, n2, n3, n4,
                flops=1 << 30, name="prepare",
            )
        args = (pay, other) if level == 0 else (pay, other, fun)
        pay, fun = call(
            lambda *refs, level=level: combine(level, *refs),
            (sds(N if level == 3 else 128, 128), sds(128, 128)), *args, flops=1 << 24, name=f"combine{level}",
        )
    other = xor_depth(pay, 24)
    out = call(
        downsweep, sds(CELLS, N), pay, other, fun, vec, t0, coup, leaf, n1, n2, n3, n4, tees, flops=1 << 25,
        name="downsweep",
    )
    return out.reshape(line_count, cell_count, species)


def solution(mesh):
    return jax.shard_map(
        on_device,
        mesh=mesh,
        in_specs=(
            P("lat", "depth", None),
            P("lat", "depth", None),
            P("lat", "depth", None),
            P(),
            P("lat", "depth", None),
            P("lat", "depth", None),
            P("lat", None),
            P("lat", "depth", None),
            P("lat", "depth", None),
        ),
        out_specs=P("lat", "depth", None),
        check_vma=False,
    )
```

time: 58.9 us -> 54.2 us (0.920)
  the two profiles are of different devices: /device:TPU:32 before, /device:TPU:30 now
where the time goes in v1:
time: 54.2 us; the launch traced here: 54.1 us
  waiting for transfers between devices  27.6 us (51%)
  Pallas kernels  14.6 us (27%)
  starting transfers between devices  11.7 us (22%)
    ppermute x5, waiting for transfers between devices, xor_depth(): return lax.ppermute(value, 'depth', [(i, i ^ bits) for i in range(32)])  22.8 us
    pallas_call x10, Pallas kernels, call(): pl.pallas_call(body, out_shape=outs, in_specs=[pl.BlockSpec(memory_space=...  14.6 us
    ppermute x1, starting transfers between devices, on_device(): top = lax.ppermute(densities, 'depth', [(i + 1, i) for i in range(31)])  7.93 us
    ppermute x3, waiting for transfers between devices, xor_lat(): return lax.ppermute(value, 'lat', [(i, i ^ bits) for i in range(8)])  4.8 us
    ppermute x5, starting transfers between devices, xor_depth(): return lax.ppermute(value, 'depth', [(i, i ^ bits) for i in range(32)])  2.31 us
    ppermute x3, starting transfers between devices, xor_lat(): return lax.ppermute(value, 'lat', [(i, i ^ bits) for i in range(8)])  1.48 us
  transfers between devices with their start and end apart: 9, of which 7 were waited for; matrix products, arithmetic and copies ran while one was open for 0% of the time, Pallas kernels for 10%

profile of v1, /device:TPU:30, one launch (start us, length us, event | category | flops | bytes accessed | tf_op | source)
XLA Modules:
  0.0 54.1 jit_solution(17210820451555548301)
XLA Ops:
  0.0 0.0 collective-permute-start
  0.0 7.9 %collective-permute-start.3 = (f32[1,32,64]{2,1,0:T(8,128)}, f32[1,32,64]{2,1,0:T(8,128)S(1)}, u32[]{:S(2)}, u32[]{:S(2)}) collective-permute-start(f32[1,32,64]{2,1,0:T(8,128)} %param.9), channel_id=1, source_target_pairs={{8,0},{16,8},{24,16},{32,24},{40,32},{48,40},{56,48},{64,56},{72,6... | collective-permute-start | bytes 24584 | tf_op jit(solution)/shard_map/ppermute | solution.py:384
  7.9 0.0 copy-start
  8.0 0.0 copy-start.1
  8.0 0.0 copy-start.5
  8.0 1.9 %react.1.after_ref.part_ref = f32[32,64]{1,0:T(8,128)S(1)} custom-call(f32[32,4096]{1,0:T(8,128)} %bitcast.21, f32[32,64]{1,0:T(8,128)} %bitcast.12, f32[32,64]{1,0:T(8,128)} %bitcast.22, f32[32,64]{1,0:T(8,128)} %bitcast.17, s32[8,8]{1,0:T(8,128)} %pat_hbm.1), custom_call_target="tpu_custom_call" | custom-call | flops 1073741824 | bytes 65536 | tf_op jit(solution)/shard_map/react/pallas_call | solution.py:340
  9.9 0.0 collective-permute-done.a_ref
  9.9 0.9 %collective-permute-start.1 = (f32[2,32,64]{2,1,0:T(8,128)S(1)}, f32[2,32,64]{2,1,0:T(8,128)S(1)}, u32[]{:S(2)}, u32[]{:S(2)}) collective-permute-start(f32[2,32,64]{2,1,0:T(8,128)S(1)} %pad_maximum_fusion.1), channel_id=1, source_target_pairs={{0,2},{1,3},{2,0},{3,1},{4,6},{5,7},{6,4},{7,5},{8,10},{9,11},{10,... | collective-permute-start | bytes 49160 | tf_op jit(solution)/shard_map/ppermute | solution.py:367
  10.9 0.0 copy-done.1
  10.9 1.3 %tree_leaves.1 = (bf16[16,2,64,128]{3,2,1,0:T(8,128)(2,1)S(1)}, bf16[16,4,64,128]{3,2,1,0:T(8,128)(2,1)S(1)}, f32[16,3,64,128]{3,2,1,0:T(8,128)S(1)}) custom-call(f32[1024,128]{1,0:T(8,128)S(1)} %bitcast.20, f32[32,64]{1,0:T(8,128)S(1)} %bitcast.14, f32[32,64]{1,0:T(8,128)S(1)} %react.1.after_ref.part_ref), custom_call_target="tpu_custom_call" | custom-call | flops 2147483648 | bytes 65536 | tf_op jit(solution)/shard_map/tree_leaves/pallas_call | solution.py:340
  12.2 1.7 %collective-permute-done.1.b_ref = f32[2,32,64]{2,1,0:T(8,128)S(1)} collective-permute-done((f32[2,32,64]{2,1,0:T(8,128)S(1)}, f32[2,32,64]{2,1,0:T(8,128)S(1)}, u32[]{:S(2)}, u32[]{:S(2)}) %collective-permute-start.1) | collective-permute-done | bytes 16416 | tf_op jit(solution)/shard_map/ppermute | solution.py:367
  14.0 0.6 %collective-permute-start.2 = (f32[4,32,64]{2,1,0:T(8,128)S(1)}, f32[4,32,64]{2,1,0:T(8,128)S(1)}, u32[]{:S(2)}, u32[]{:S(2)}) collective-permute-start(f32[4,32,64]{2,1,0:T(8,128)S(1)} %pad_maximum_fusion), channel_id=1, source_target_pairs={{0,6},{1,7},{2,4},{3,5},{4,2},{5,3},{6,0},{7,1},{8,14},{9,15},{10,... | collective-permute-start | bytes 98312 | tf_op jit(solution)/shard_map/ppermute | solution.py:367
  14.5 1.9 %tree_upper.1 = (bf16[8,4,64,128]{3,2,1,0:T(8,128)(2,1)S(1)}, bf16[4,4,64,128]{3,2,1,0:T(8,128)(2,1)S(1)}, bf16[2,4,64,128]{3,2,1,0:T(8,128)(2,1)S(1)}, bf16[1,64,128]{2,1,0:T(8,128)(2,1)S(1)}, f32[128,128]{1,0:T(8,128)S(1)}) custom-call(bf16[16,4,64,128]{3,2,1,0:T(8,128)(2,1)S(1)} %get-tuple-element.26.n1_ref, f32[16,3,64,128]{3,2,1,0:T(8,128)S(1)} %get-tuple-element.27.full_ref), custom_call_target="tpu_custom_call" | custom-call | flops 2147483648 | bytes 65536 | tf_op jit(solution)/shard_map/tree_upper/pallas_call | solution.py:340
  16.4 0.0 collective-permute-done.3.top_ref
  16.4 3.1 %collective-permute-done.2.c_ref = f32[4,32,64]{2,1,0:T(8,128)S(1)} collective-permute-done((f32[4,32,64]{2,1,0:T(8,128)S(1)}, f32[4,32,64]{2,1,0:T(8,128)S(1)}, u32[]{:S(2)}, u32[]{:S(2)}) %collective-permute-start.2) | collective-permute-done | bytes 32800 | tf_op jit(solution)/shard_map/ppermute | solution.py:367
  19.5 3.1 %upsweep.1 = (f32[128,128]{1,0:T(8,128)S(1)}, f32[8,64,128]{2,1,0:T(8,128)S(1)}) custom-call(s32[1,4]{1,0:T(1,128)S(1)} %copy-done.4, f32[32,64]{1,0:T(8,128)S(1)} %react.1.after_ref.part_ref, f32[1,32,64]{2,1,0:T(8,128)S(1)} %collective-permute-done.a_ref, f32[2,32,64]{2,1,0:T(8,128)S(1)} %collective-permute-done.1.b_ref, ...), custom_call_target="tpu_custom_call" | custom-call | flops 33554432 | bytes 65536 | tf_op jit(solution)/shard_map/upsweep/pallas_call | solution.py:340
  22.7 0.1 collective-permute-start.4
  22.8 4.3 %collective-permute-done.4.refs_1_ = f32[128,128]{1,0:T(8,128)S(1)} collective-permute-done((f32[128,128]{1,0:T(8,128)S(1)}, f32[128,128]{1,0:T(8,128)S(1)}, u32[]{:S(2)}, u32[]{:S(2)}) %collective-permute-start.4) | collective-permute-done | bytes 65568 | tf_op jit(solution)/shard_map/ppermute | solution.py:370
  27.0 0.6 %combine0.1 = (f32[128,128]{1,0:T(8,128)S(1)}, f32[128,128]{1,0:T(8,128)S(1)}) custom-call(f32[128,128]{1,0:T(8,128)S(1)} %get-tuple-element.33.refs_0_, f32[128,128]{1,0:T(8,128)S(1)} %collective-permute-done.4.refs_1_), custom_call_target="tpu_custom_call" | custom-call | flops 16777216 | bytes 65536 | tf_op jit(solution)/shard_map/combine0/pallas_call | solution.py:340
  27.6 0.1 collective-permute-start.5
  27.7 5.3 %collective-permute-done.5.refs_1_ = f32[128,128]{1,0:T(8,128)S(1)} collective-permute-done((f32[128,128]{1,0:T(8,128)S(1)}, f32[128,128]{1,0:T(8,128)S(1)}, u32[]{:S(2)}, u32[]{:S(2)}) %collective-permute-start.5) | collective-permute-done | bytes 65568 | tf_op jit(solution)/shard_map/ppermute | solution.py:370
  33.0 0.6 %combine1.1 = (f32[128,128]{1,0:T(8,128)S(1)}, f32[128,128]{1,0:T(8,128)S(1)}) custom-call(f32[128,128]{1,0:T(8,128)S(1)} %get-tuple-element.34.refs_0_, f32[128,128]{1,0:T(8,128)S(1)} %collective-permute-done.5.refs_1_, f32[128,128]{1,0:T(8,128)S(1)} %get-tuple-element.35.refs_2_), custom_call_target="tpu_custom_call" | custom-call | flops 16777216 | bytes 65536 | tf_op jit(solution)/shard_map/combine1/pallas_call | solution.py:340
  33.6 1.5 %collective-permute-start.6 = (f32[128,128]{1,0:T(8,128)S(1)}, f32[128,128]{1,0:T(8,128)S(1)}, u32[]{:S(2)}, u32[]{:S(2)}) collective-permute-start(f32[128,128]{1,0:T(8,128)S(1)} %get-tuple-element.36.refs_0_), channel_id=1, source_target_pairs={{0,56},{8,48},{16,40},{24,32},{32,24},{40,16},{48,8},{56,0},{64,12... | collective-permute-start | bytes 196616 | tf_op jit(solution)/shard_map/ppermute | solution.py:370
  35.1 4.7 %collective-permute-done.6.refs_1_ = f32[128,128]{1,0:T(8,128)S(1)} collective-permute-done((f32[128,128]{1,0:T(8,128)S(1)}, f32[128,128]{1,0:T(8,128)S(1)}, u32[]{:S(2)}, u32[]{:S(2)}) %collective-permute-start.6) | collective-permute-done | bytes 65568 | tf_op jit(solution)/shard_map/ppermute | solution.py:370
  39.9 0.6 %combine2.1 = (f32[128,128]{1,0:T(8,128)S(1)}, f32[128,128]{1,0:T(8,128)S(1)}) custom-call(f32[128,128]{1,0:T(8,128)S(1)} %get-tuple-element.36.refs_0_, f32[128,128]{1,0:T(8,128)S(1)} %collective-permute-done.6.refs_1_, f32[128,128]{1,0:T(8,128)S(1)} %get-tuple-element.37.refs_2_), custom_call_target="tpu_custom_call" | custom-call | flops 16777216 | bytes 65536 | tf_op jit(solution)/shard_map/combine2/pallas_call | solution.py:340
  40.5 0.5 collective-permute-start.7
  41.0 3.8 %collective-permute-done.7.refs_1_ = f32[128,128]{1,0:T(8,128)S(1)} collective-permute-done((f32[128,128]{1,0:T(8,128)S(1)}, f32[128,128]{1,0:T(8,128)S(1)}, u32[]{:S(2)}, u32[]{:S(2)}) %collective-permute-start.7) | collective-permute-done | bytes 65568 | tf_op jit(solution)/shard_map/ppermute | solution.py:370
  44.8 0.6 %combine3.1 = (f32[64,128]{1,0:T(8,128)S(1)}, f32[128,128]{1,0:T(8,128)S(1)}) custom-call(f32[128,128]{1,0:T(8,128)S(1)} %get-tuple-element.38.refs_0_, f32[128,128]{1,0:T(8,128)S(1)} %collective-permute-done.7.refs_1_, f32[128,128]{1,0:T(8,128)S(1)} %get-tuple-element.39.refs_2_), custom_call_target="tpu_custom_call" | custom-call | flops 16777216 | bytes 65536 | tf_op jit(solution)/shard_map/combine3/pallas_call | solution.py:340
  45.4 0.1 collective-permute-start.8
  45.5 0.5 prepare.1
  46.0 4.6 %collective-permute-done.8.other_ref = f32[64,128]{1,0:T(8,128)S(1)} collective-permute-done((f32[64,128]{1,0:T(8,128)S(1)}, f32[64,128]{1,0:T(8,128)S(1)}, u32[]{:S(2)}, u32[]{:S(2)}) %collective-permute-start.8) | collective-permute-done | bytes 32800 | tf_op jit(solution)/shard_map/ppermute | solution.py:370
  50.6 3.5 %downsweep.1 = f32[32,64]{1,0:T(8,128)} custom-call(f32[64,128]{1,0:T(8,128)S(1)} %get-tuple-element.40.own_ref, f32[64,128]{1,0:T(8,128)S(1)} %collective-permute-done.8.other_ref, f32[128,128]{1,0:T(8,128)S(1)} %get-tuple-element.41.fun_ref, f32[8,64,128]{2,1,0:T(8,128)S(1)} %get-tuple-element.42.vec_ref, f32[4,64,128]{2,1,0:T(8,128)S(1)} %get-tuple-element.43.t0_ref, ...), custom_call_target="tpu_custom_call" | custom-call | flops 33554432 | bytes 65536 | tf_op jit(solution)/shard_map/downsweep/pallas_call | solution.py:340
  (10 shorter events, 0.0 us)
Async XLA Ops:
  0.0 9.9 %collective-permute-start = (f32[1,32,64]{2,1,0:T(8,128)}, f32[1,32,64]{2,1,0:T(8,128)S(1)}, u32[]{:S(2)}, u32[]{:S(2)}) collective-permute-start(f32[1,32,64]{2,1,0:T(8,128)} %param.9), channel_id=1, source_target_pairs={{0,1},{1,0},{2,3},{3,2},{4,5},{5,4},{6,7},{7,6},{8,9},{9,8},{10,11... | collective-permute-start | bytes 24584 | tf_op jit(solution)/shard_map/ppermute | solution.py:367
  0.0 16.4 %collective-permute-start.3 = (f32[1,32,64]{2,1,0:T(8,128)}, f32[1,32,64]{2,1,0:T(8,128)S(1)}, u32[]{:S(2)}, u32[]{:S(2)}) collective-permute-start(f32[1,32,64]{2,1,0:T(8,128)} %param.9), channel_id=1, source_target_pairs={{8,0},{16,8},{24,16},{32,24},{40,32},{48,40},{56,48},{64,56},{72,6... | collective-permute-start | bytes 24584 | tf_op jit(solution)/shard_map/ppermute | solution.py:384
  7.9 2.0 %copy-start = (f32[1,32,64]{2,1,0:T(8,128)S(1)}, f32[1,32,64]{2,1,0:T(8,128)}, u32[]{:S(2)}) copy-start(f32[1,32,64]{2,1,0:T(8,128)} %param.9) | copy-start | bytes 24580
  8.0 2.9 %copy-start.1 = (f32[1,32,64]{2,1,0:T(8,128)S(1)}, f32[1,32,64]{2,1,0:T(8,128)}, u32[]{:S(2)}) copy-start(f32[1,32,64]{2,1,0:T(8,128)} %param.17) | copy-start | bytes 24580
  8.0 2.9 %copy-start.5 = (f32[1,32,4096]{2,1,0:T(8,128)S(1)}, f32[1,32,4096]{2,1,0:T(8,128)}, u32[]{:S(2)}) copy-start(f32[1,32,4096]{2,1,0:T(8,128)} %param.16) | copy-start | bytes 1572868
  9.9 4.0 %collective-permute-start.1 = (f32[2,32,64]{2,1,0:T(8,128)S(1)}, f32[2,32,64]{2,1,0:T(8,128)S(1)}, u32[]{:S(2)}, u32[]{:S(2)}) collective-permute-start(f32[2,32,64]{2,1,0:T(8,128)S(1)} %pad_maximum_fusion.1), channel_id=1, source_target_pairs={{0,2},{1,3},{2,0},{3,1},{4,6},{5,7},{6,4},{7,5},{8,10},{9,11},{10,... | collective-permute-start | bytes 49160 | tf_op jit(solution)/shard_map/ppermute | solution.py:367
  14.0 5.6 %collective-permute-start.2 = (f32[4,32,64]{2,1,0:T(8,128)S(1)}, f32[4,32,64]{2,1,0:T(8,128)S(1)}, u32[]{:S(2)}, u32[]{:S(2)}) collective-permute-start(f32[4,32,64]{2,1,0:T(8,128)S(1)} %pad_maximum_fusion), channel_id=1, source_target_pairs={{0,6},{1,7},{2,4},{3,5},{4,2},{5,3},{6,0},{7,1},{8,14},{9,15},{10,... | collective-permute-start | bytes 98312 | tf_op jit(solution)/shard_map/ppermute | solution.py:367
  14.5 5.0 %copy-start.2 = (f32[1,32,64]{2,1,0:T(8,128)S(1)}, f32[1,32,64]{2,1,0:T(8,128)}, u32[]{:S(2)}) copy-start(f32[1,32,64]{2,1,0:T(8,128)} %param.13) | copy-start | bytes 24580
  14.5 5.0 %copy-start.3 = (f32[1,32,64]{2,1,0:T(8,128)S(1)}, f32[1,32,64]{2,1,0:T(8,128)}, u32[]{:S(2)}) copy-start(f32[1,32,64]{2,1,0:T(8,128)} %param.14) | copy-start | bytes 24580
  14.5 5.0 %copy-start.4 = (s32[1,4]{1,0:T(1,128)S(1)}, s32[1,4]{1,0:T(1,128)}, u32[]{:S(2)}) copy-start(s32[1,4]{1,0:T(1,128)} %neigh_ref.1) | copy-start | bytes 52
  22.7 4.4 %collective-permute-start.4 = (f32[128,128]{1,0:T(8,128)S(1)}, f32[128,128]{1,0:T(8,128)S(1)}, u32[]{:S(2)}, u32[]{:S(2)}) collective-permute-start(f32[128,128]{1,0:T(8,128)S(1)} %get-tuple-element.33.refs_0_), channel_id=1, source_target_pairs={{0,8},{8,0},{16,24},{24,16},{32,40},{40,32},{48,56},{56,48},{64,72... | collective-permute-start | bytes 196616 | tf_op jit(solution)/shard_map/ppermute | solution.py:370
  27.6 5.4 %collective-permute-start.5 = (f32[128,128]{1,0:T(8,128)S(1)}, f32[128,128]{1,0:T(8,128)S(1)}, u32[]{:S(2)}, u32[]{:S(2)}) collective-permute-start(f32[128,128]{1,0:T(8,128)S(1)} %get-tuple-element.34.refs_0_), channel_id=1, source_target_pairs={{0,16},{8,24},{16,0},{24,8},{32,48},{40,56},{48,32},{56,40},{64,80... | collective-permute-start | bytes 196616 | tf_op jit(solution)/shard_map/ppermute | solution.py:370
  33.6 6.3 %collective-permute-start.6 = (f32[128,128]{1,0:T(8,128)S(1)}, f32[128,128]{1,0:T(8,128)S(1)}, u32[]{:S(2)}, u32[]{:S(2)}) collective-permute-start(f32[128,128]{1,0:T(8,128)S(1)} %get-tuple-element.36.refs_0_), channel_id=1, source_target_pairs={{0,56},{8,48},{16,40},{24,32},{32,24},{40,16},{48,8},{56,0},{64,12... | collective-permute-start | bytes 196616 | tf_op jit(solution)/shard_map/ppermute | solution.py:370
  40.5 4.4 %collective-permute-start.7 = (f32[128,128]{1,0:T(8,128)S(1)}, f32[128,128]{1,0:T(8,128)S(1)}, u32[]{:S(2)}, u32[]{:S(2)}) collective-permute-start(f32[128,128]{1,0:T(8,128)S(1)} %get-tuple-element.38.refs_0_), channel_id=1, source_target_pairs={{0,64},{8,72},{16,80},{24,88},{32,96},{40,104},{48,112},{56,120},{... | collective-permute-start | bytes 196616 | tf_op jit(solution)/shard_map/ppermute | solution.py:370
  45.4 5.2 %collective-permute-start.8 = (f32[64,128]{1,0:T(8,128)S(1)}, f32[64,128]{1,0:T(8,128)S(1)}, u32[]{:S(2)}, u32[]{:S(2)}) collective-permute-start(f32[64,128]{1,0:T(8,128)S(1)} %get-tuple-element.40.own_ref), channel_id=1, source_target_pairs={{0,192},{8,200},{16,208},{24,216},{32,224},{40,232},{48,240},{56,2... | collective-permute-start | bytes 98312 | tf_op jit(solution)/shard_map/ppermute | solution.py:370

commit v2 on v1

v2 whole, which is shorter than its diff:
```python
import jax
import jax.numpy as jnp
from jax import lax
from jax.experimental import pallas as pl
from jax.experimental.pallas import tpu as pltpu
from jax.sharding import PartitionSpec as P

f32 = jnp.float32
bf16 = jnp.bfloat16

CELLS = 32
N = 64
ZS = 8
VLIM = 16 << 20


def lanes(shape):
    return lax.broadcasted_iota(jnp.int32, shape, len(shape) - 1)


def roll(x, shift):
    shift = shift % x.shape[-1]
    return x if shift == 0 else pltpu.roll(x, shift, x.ndim - 1)


def pack(dup):
    hi = dup.astype(bf16).astype(f32)
    return jnp.where(lanes(dup.shape) < N, hi, dup - hi).astype(bf16)


def mm(a, b):
    r = jnp.dot(a, jnp.concatenate([b, b], axis=0), preferred_element_type=f32)
    return r + roll(r, N)


def rhs(x):
    hi = x.astype(bf16)
    lo = (x - hi.astype(f32)).astype(bf16)
    return jnp.concatenate([hi, hi, lo, lo], axis=0)


def dot(a, y):
    return jnp.dot(jnp.concatenate([a, a], axis=1), y, preferred_element_type=f32)


def column(row):
    return jnp.broadcast_to(row, (128, N)).T


def eye2():
    return jnp.where(lanes((N, 128)) % N == lax.broadcasted_iota(jnp.int32, (N, 128), 0), 1.0, 0.0)


def put(node, full, j, p, q, w, u):
    node[j, 0], node[j, 1], node[j, 2], node[j, 3] = pack(p), pack(q), pack(w), pack(u)
    full[j, 0], full[j, 1], full[j, 2] = p, q, w


def tree_leaves(fac_ref, coup_ref, after_ref, leaf_ref, n1_ref, full_ref, cols_ref, rows):
    del after_ref
    c = coup_ref[...]
    cols_ref[0] = column(c[CELLS - 1 : CELLS])
    cols_ref[1] = column(1.0 / c[0:1])
    c2 = jnp.concatenate([c, c], axis=1)
    low = lanes((CELLS, 128)) < N
    eye = eye2()

    def leaf(k):
        g, s = divmod(k, 8)
        x = fac_ref[pl.ds(g * 256 + s, 32, stride=8), :]
        y = roll(x, N)
        rows[k % 2, pl.ds(0, 32, stride=2), :] = jnp.where(low, x, y)
        rows[k % 2, pl.ds(1, 32, stride=2), :] = jnp.where(low, y, x)
        a = rows[k % 2]
        before = max(k - 1, 0)
        return a * c2[before : before + 1] - eye, a * c2[k : k + 1] - eye

    for j in range(CELLS // 2):
        p1, q1 = leaf(2 * j)
        p2, q2 = leaf(2 * j + 1)
        kp1, kq1, kp2, kq2 = pack(p1), pack(q1), pack(p2), pack(q2)
        leaf_ref[j, 0], leaf_ref[j, 1] = kp2, kq2
        p = p1 + p2 + mm(kp2, kp1)
        q = q1 + q2 + mm(kq1, kq2)
        u = eye + q1 + p2 + mm(kq1, kp2)
        w = (eye + eye) + p1 + q1 + p + mm(kq1, pack(p))
        put(n1_ref, full_ref, j, p, q, w, u)


def tree_upper(n1_ref, full_ref, coup_ref, cols_ref, n2_ref, n3_ref, n4_ref, n5_ref, root_ref, fa, fb):
    node, full = n1_ref, full_ref
    for count, node_to, full_to in ((8, n2_ref, fa), (4, n3_ref, fb), (2, n4_ref, fa), (1, None, None)):
        for j in range(count):
            one, two = 2 * j, 2 * j + 1
            kp1, kq1 = node[one, 0], node[one, 1]
            u = full[two, 2] + mm(kq1, node[two, 2])
            p = full[one, 0] + full[two, 0] + mm(node[two, 0], kp1)
            q = full[one, 1] + full[two, 1] + mm(kq1, node[two, 1])
            ku = pack(u)
            w = full[one, 2] + u + mm(ku, kp1)
            if node_to is None:
                eye = eye2()
                n5_ref[0] = ku
                first = coup_ref[0:1]
                scale = 1.0 / jnp.concatenate([first, first], axis=1)
                root_ref[:N] = jnp.where(lanes((N, 128)) < N, (p + eye) * cols_ref[0] * scale, q + eye)
                root_ref[N:] = w * scale
            else:
                put(node_to, full_to, j, p, q, w, u)
        node, full = node_to, full_to


def react(jac_hbm, dens_hbm, src_hbm, tran_hbm, pat_hbm, out_ref, flux_ref, jac_ref, dens_ref, src_ref, tran_ref,
          pat_ref, sems):
    pairs = ((dens_hbm, dens_ref), (pat_hbm, pat_ref), (jac_hbm, jac_ref), (src_hbm, src_ref), (tran_hbm, tran_ref))
    copies = [pltpu.make_async_copy(a, b, sems.at[i]) for i, (a, b) in enumerate(pairs)]
    for copy in copies:
        copy.start()
    half = lanes((128, N)) % 2 == lax.broadcasted_iota(jnp.int32, (128, N), 0) // N
    half = jnp.where(half, 1.0, 0.0).astype(bf16)
    for copy in copies:
        copy.wait()
    u = dens_ref[...]
    u2 = jnp.concatenate([u, u], axis=1)
    lane8 = lanes((8, 128))
    pat = pat_ref[...].astype(f32)
    mask_rows = jnp.zeros((8, 128), f32)
    for t in range(8):
        mask_rows = jnp.where((lane8 % N) // 8 == t, pat[:, t : t + 1], mask_rows)
    lane = lanes((CELLS, N))
    acc = jnp.zeros((CELLS, N), f32)
    for m in range(32):
        y = jac_ref[:, m * 128 : (m + 1) * 128] * (u2 * mask_rows[m // 4 : m // 4 + 1])
        hi = y.astype(bf16)
        lo = (y - hi.astype(f32)).astype(bf16)
        z = jnp.dot(hi, half, preferred_element_type=f32) + jnp.dot(lo, half, preferred_element_type=f32)
        acc = jnp.where(lane // 2 == m, z, acc)
    tran = tran_ref[...]
    flux = tran * u
    flux_ref[...] = column(flux[CELLS - 1 : CELLS])
    row = lax.broadcasted_iota(jnp.int32, (CELLS, N), 0)
    lower = jnp.where(row == 0, 0.0, pltpu.roll(flux, 1, 0))
    upper = jnp.where(row == CELLS - 1, 0.0, pltpu.roll(u, CELLS - 1, 0))
    out_ref[...] = src_ref[...] - acc + lower + tran * upper


def upsweep(neigh_ref, part_ref, a_ref, b_ref, c_ref, top_ref, flux_ref, dens_ref, tran_ref, lat_ref, coup_ref, cols_ref,
            leaf_ref, n1_ref, n2_ref, n3_ref, n4_ref, n5_ref, root_ref, pay_ref, pair_ref, v_ref, w_ref):
    me = lax.axis_index("lat")
    u = dens_ref[...]
    total = jnp.zeros((CELLS, N), f32)
    lines = [(0, u), (1, a_ref[0])] + [(2 + i, b_ref[i]) for i in range(2)]
    lines += [((6, 7, 4, 5)[i], c_ref[i]) for i in range(4)]
    for offset, value in lines:
        line = me ^ offset
        count = jnp.int32(0)
        for j in range(4):
            count = count + (neigh_ref[0, j] == line).astype(jnp.int32)
        total = total + count.astype(f32) * value
    row = lax.broadcasted_iota(jnp.int32, (CELLS, N), 0)
    r = part_ref[...] - lat_ref[...] * (4.0 * u - total)
    r = r + jnp.where(row == CELLS - 1, tran_ref[...] * top_ref[0, 0:1], 0.0)
    c = coup_ref[...]
    g = r / jnp.where(row == 0, c, pltpu.roll(c, 1, 0))
    x = [(g if i == 0 else pltpu.roll(g, CELLS - i, 0)).T for i in range(4)]
    y = [rhs(t) for t in x]
    lane = lanes((N, CELLS))
    pair_v, pair_w = [], []
    for half in range(2):
        y0, y1 = y[2 * half], y[2 * half + 1]
        v = jnp.zeros((N, CELLS), f32)
        w = jnp.zeros((N, CELLS), f32)
        for j in range(8):
            at = 2 * j + half
            here = lane == 4 * j
            v = jnp.where(here, dot(n1_ref[at, 0], y0) + dot(leaf_ref[at, 0], y1), v)
            w = jnp.where(here, dot(n1_ref[at, 2], y0) + dot(n1_ref[at, 3], y1), w)
        pair_v.append(v + x[2 * half] + x[2 * half + 1])
        pair_w.append(w)
        pair_ref[half, :, 0:CELLS] = pair_v[half]
        pair_ref[2 + half, :, 0:CELLS] = w
    yv, yw = rhs(pair_v[0]), rhs(pair_w[1])
    v, w = pair_v[0] + pair_v[1], pair_w[0] + pair_w[1]
    dv = jnp.zeros((N, CELLS), f32)
    dw = jnp.zeros((N, CELLS), f32)
    for j in range(8):
        here = lane == 4 * j
        dv = jnp.where(here, dot(n1_ref[2 * j + 1, 0], yv), dv)
        dw = jnp.where(here, dot(n1_ref[2 * j, 1], yw) + dot(n2_ref[j, 3], yv), dw)
    v, w = v + dv, w + dw
    vs = [jnp.broadcast_to(v[:, 4 * j : 4 * j + 1], (N, 128)) for j in range(8)]
    ws = [jnp.broadcast_to(w[:, 4 * j : 4 * j + 1], (N, 128)) for j in range(8)]
    at = 0
    for count, ref, above in ((4, n2_ref, n3_ref), (2, n3_ref, n4_ref), (1, n4_ref, n5_ref)):
        next_v, next_w = [], []
        for j in range(count):
            v1, v2, w1, w2 = vs[2 * j], vs[2 * j + 1], ws[2 * j], ws[2 * j + 1]
            v_ref[at], w_ref[at] = v1, w2
            at += 1
            yv, yw = rhs(v1), rhs(w2)
            u_map = above[j, 3] if count > 1 else above[0]
            next_v.append(v1 + v2 + dot(ref[2 * j + 1, 0], yv))
            next_w.append(w1 + w2 + dot(ref[2 * j, 1], yw) + dot(u_map, yv))
        vs, ws = next_v, next_w
    lane = lanes((N, 128))
    pay_ref[:N] = root_ref[:N]
    tail = jnp.where(lane == N, vs[0] * cols_ref[0] + flux_ref[...], ws[0])
    pay_ref[N:] = jnp.where(lane < N, root_ref[N:], tail)


def prepare(pair_ref, v_ref, w_ref, n1_ref, n2_ref, n3_ref, n4_ref, t_ref, add_v, add_a, add_x):
    lane = lanes((N, 128))
    at, vec = 0, 0
    for level, size, ref in ((1, 8, n2_ref), (2, 16, n3_ref), (3, 32, n4_ref)):
        acc_v = jnp.zeros((N, 128), f32)
        acc_a = jnp.zeros((N, 128), f32)
        for j in range(CELLS // size):
            kw = ref[2 * j + 1, 2]
            wide = kw.astype(f32)
            t_ref[at] = pack(wide + roll(wide, N) + mm(kw, ref[2 * j, 0]))
            at += 1
            here = lane // size == j
            acc_v = jnp.where(here, v_ref[vec], acc_v)
            acc_a = jnp.where(here, w_ref[vec] + dot(kw, rhs(v_ref[vec])), acc_a)
            vec += 1
        add_v[level], add_a[level] = acc_v, acc_a
    first = lane % 4 == 0
    v0, v1, w0, w1 = [jnp.where(first, pair_ref[i], 0.0) for i in range(4)]
    y = rhs(v0)
    acc_a = jnp.zeros((N, 128), f32)
    for j in range(8):
        kw = n1_ref[2 * j + 1, 2]
        wide = kw.astype(f32)
        t_ref[at] = pack(wide + roll(wide, N) + mm(kw, n1_ref[2 * j, 0]))
        at += 1
        acc_a = jnp.where(lane == 4 * j, dot(kw, y), acc_a)
    acc_a = acc_a + w1
    spread_v = v0 + roll(v0, 1)
    spread_a = acc_a + roll(acc_a, 1)
    add_v[0] = spread_v + roll(spread_v, 2)
    add_a[0] = spread_a + roll(spread_a, 2)
    add_x[...] = w0 + roll(w1, 2) + roll(v0, 1) + roll(v1, 3)


def unpack(b):
    low = lanes((N, 128)) < N
    b1, b2 = b[:N], b[N:]
    r1, r2 = roll(b1, N), roll(b2, N)
    x = jnp.where(low, b1, r1)
    y = jnp.where(low, r1, b1)
    z = jnp.where(low, b2, r2)
    g = jnp.broadcast_to(b2[:, N : N + 1], (N, 128))
    h = jnp.broadcast_to(b2[:, N + 1 : N + 2], (N, 128))
    return x, y, z, g, h


def repack(ref, x, y, z, g, h):
    lane = lanes((N, 128))
    low = lane < N
    ref[:N] = jnp.where(low, x, y)
    ref[N:] = jnp.where(low, z, jnp.where(lane == N, g, h))


def combine(level, *refs):
    if level == 0:
        own_ref, other_ref, out_ref, fun_out = refs
    else:
        own_ref, other_ref, fun_ref, out_ref, fun_out = refs
    at = lax.axis_index("depth")
    is_low = ((at // (1, 2, 4, 8)[level]) % 2) == 0
    own, other = own_ref[...], other_ref[...]
    p1, q1, w1, v1, h1 = unpack(jnp.where(is_low, own, other))
    p2, q2, w2, v2, h2 = unpack(jnp.where(is_low, other, own))
    kq1, kp2, kw2 = pack(q1), pack(p2), pack(w2)
    yp1, yv1 = rhs(p1), rhs(v1)
    t = dot(kw2, yp1)
    th = h2 + dot(kw2, yv1)
    v = v2 + dot(kp2, yv1)
    yt, yth = rhs(t), rhs(th)
    w = w1 + dot(kq1, yt)
    h = h1 + dot(kq1, yth)
    lane = lanes((N, 128))
    low = lane < N
    tail = jnp.where(low, w, jnp.where(lane == N, v, h))
    if level == 3:
        out_ref[...] = tail
    else:
        out_ref[:N] = jnp.where(low, dot(kp2, yp1), dot(kq1, rhs(q2)))
        out_ref[N:] = tail
    if level == 0:
        eye = eye2()
        repack(
            fun_out,
            jnp.where(is_low, eye, p1),
            jnp.where(is_low, q2, eye),
            jnp.where(is_low, t, 0.0),
            jnp.where(is_low, 0.0, v1),
            jnp.where(is_low, th, 0.0),
        )
    else:
        f, hh, k, g, e = unpack(fun_ref[...])
        x1 = pack(jnp.where(is_low, hh, f))
        x2 = pack(jnp.where(is_low, hh, k))
        prod1 = dot(x1, rhs(jnp.where(is_low, q2, p1)))
        prod2 = dot(x2, jnp.where(is_low, yt, yp1))
        vec1 = dot(x1, yv1)
        vec2 = dot(x2, jnp.where(is_low, yth, yv1))
        repack(
            fun_out,
            jnp.where(is_low, f, prod1),
            jnp.where(is_low, prod1, hh),
            jnp.where(is_low, k + prod2, prod2),
            jnp.where(is_low, g, g + vec1),
            e + vec2,
        )


def downsweep(own_ref, other_ref, fun_ref, cols_ref, add_v, add_a, add_x, leaf_ref, n1_ref, n2_ref, n3_ref, n4_ref, t_ref,
              out_ref):
    is_low = lax.axis_index("depth") < 2 * ZS
    f, hh, k, g, e = unpack(fun_ref[...])
    own, other = own_ref[...], other_ref[...]
    other_w = jnp.where(lanes((N, 128)) < N, other, roll(other, N))
    v_own = jnp.broadcast_to(own[:, N : N + 1], (N, 128))
    v_other = jnp.broadcast_to(other[:, N : N + 1], (N, 128))
    w_other = jnp.broadcast_to(other[:, N + 1 : N + 2], (N, 128))
    y_other = rhs(v_other)
    t = w_other + dot(pack(other_w), rhs(v_own))
    up = g + dot(pack(f), y_other)
    aa = e + dot(pack(jnp.where(is_low, hh, k)), rhs(jnp.where(is_low, t, v_other)))
    ss = jnp.where(is_low, g, up) * cols_ref[1]
    lane = lanes((N, 128))
    for level, size, ref, base in ((3, 32, n4_ref, 6), (2, 16, n3_ref, 4), (1, 8, n2_ref, 0), (0, 4, n1_ref, 7)):
        ys, ya = rhs(ss), rhs(aa)
        ds = jnp.zeros((N, 128), f32)
        da = jnp.zeros((N, 128), f32)
        for j in range(CELLS // size):
            here = lane // size == j
            ds = jnp.where(here, dot(ref[2 * j, 0], ys), ds)
            da = jnp.where(here, dot(ref[2 * j + 1, 1], ya) + dot(t_ref[base + j], ys), da)
        upper = lane % size >= size // 2
        new_s = ss + add_v[level] + ds
        new_a = aa + add_a[level] + da
        ss = jnp.where(upper, new_s, ss)
        aa = jnp.where(upper, aa, new_a)
    ys, ya = rhs(ss), rhs(aa)
    x = jnp.zeros((N, 128), f32)
    for j in range(CELLS // 2):
        x = jnp.where(lane == 2 * j, dot(n1_ref[j, 2], ys) + dot(n1_ref[j, 1], ya), x)
        x = jnp.where(lane == 2 * j + 1, dot(n1_ref[j, 0], ys) + dot(leaf_ref[j, 1], ya), x)
    x = x + aa + add_x[...] + jnp.where(lane % 2 == 1, ss, 0.0)
    out_ref[...] = x.T[:CELLS]


def sds(*shape, dtype=f32):
    return jax.ShapeDtypeStruct(shape, dtype)


def call(body, outs, *args, scratch=(), smem=0, hbm=0, flops=0, name=None):
    args = [pltpu.with_memory_space_constraint(x, pltpu.HBM) if smem <= i < smem + hbm else x for i, x in enumerate(args)]
    spaces = [pltpu.SMEM] * smem + [pltpu.HBM] * hbm + [pltpu.VMEM] * (len(args) - smem - hbm)
    return pl.pallas_call(
        body,
        out_shape=outs,
        in_specs=[pl.BlockSpec(memory_space=space) for space in spaces],
        out_specs=jax.tree.map(lambda _: pl.BlockSpec(memory_space=pltpu.VMEM), outs),
        scratch_shapes=scratch,
        cost_estimate=pl.CostEstimate(flops=flops, bytes_accessed=1 << 16, transcendentals=0),
        name=name,
        compiler_params=pltpu.CompilerParams(vmem_limit_bytes=VLIM),
    )(*args)


def node(count):
    return sds(count, 4, N, 128, dtype=bf16)


def on_device(densities, source, jacobian, pattern, transport, lateral, neighbours, factor, coupling):
    line_count, cell_count, species = densities.shape
    u = densities.reshape(CELLS, N)
    src = source.reshape(CELLS, N)
    tran = transport.reshape(CELLS, N)
    lat = lateral.reshape(CELLS, N)
    coup = coupling.reshape(CELLS, N)
    jac = jacobian.reshape(CELLS, N * N)
    fac = factor.reshape(4, 8, 32, 128).transpose(0, 2, 1, 3).reshape(1024, 128)

    def xor_lat(value, bits):
        return lax.ppermute(value, "lat", [(i, i ^ bits) for i in range(8)])

    def xor_depth(value, bits):
        return lax.ppermute(value, "depth", [(i, i ^ bits) for i in range(32)])

    line_a = xor_lat(densities, 1)
    part, flux = call(
        react, (sds(CELLS, N), sds(N, 128)), jac, u, src, tran, pattern, hbm=5, flops=1 << 30, name="react",
        scratch=[pltpu.VMEM((CELLS, N * N), f32)] + [pltpu.VMEM((CELLS, N), f32)] * 3
        + [pltpu.VMEM((8, 8), jnp.int32), pltpu.SemaphoreType.DMA((5,))],
    )
    line_b = xor_lat(jnp.concatenate([densities, line_a], axis=0), 2)
    leaf, n1, full, cols = call(
        tree_leaves,
        (sds(16, 2, N, 128, dtype=bf16), node(16), sds(16, 3, N, 128), sds(2, N, 128)),
        fac, coup, part, scratch=[pltpu.VMEM((2, N, 128), f32)], flops=2 << 30, name="tree_leaves",
    )
    top = lax.ppermute(lax.optimization_barrier((densities, part))[0], "depth", [(i + 1, i) for i in range(31)])
    line_c = xor_lat(jnp.concatenate([densities, line_a, line_b], axis=0), 6)
    n2, n3, n4, n5, root = call(
        tree_upper,
        (node(8), node(4), node(2), sds(1, N, 128, dtype=bf16), sds(128, 128)),
        n1, full, coup, cols, scratch=[pltpu.VMEM((8, 3, N, 128), f32), pltpu.VMEM((4, 3, N, 128), f32)],
        flops=2 << 30, name="tree_upper",
    )
    pay, pair, vs, ws = call(
        upsweep, (sds(128, 128), sds(4, N, 128), sds(7, N, 128), sds(7, N, 128)),
        neighbours, part, line_a, line_b, line_c, top, flux, u, tran, lat, coup, cols, leaf, n1, n2, n3, n4, n5, root,
        smem=1, flops=1 << 25, name="upsweep",
    )
    fun = None
    for level, bits in enumerate((1, 2, 7, 8)):
        other = xor_depth(pay, bits)
        if level == 0:
            tees, add_v, add_a, add_x = call(
                prepare, (sds(15, N, 128, dtype=bf16), sds(4, N, 128), sds(4, N, 128), sds(N, 128)),
                pair, vs, ws, n1, n2, n3, n4, flops=1 << 30, name="prepare",
            )
        args = (pay, other) if level == 0 else (pay, other, fun)
        pay, fun = call(
            lambda *refs, level=level: combine(level, *refs),
            (sds(N if level == 3 else 128, 128), sds(128, 128)), *args, flops=1 << 24, name=f"combine{level}",
        )
    other = xor_depth(pay, 24)
    out = call(
        downsweep, sds(CELLS, N), pay, other, fun, cols, add_v, add_a, add_x, leaf, n1, n2, n3, n4, tees,
        flops=1 << 25, name="downsweep",
    )
    return out.reshape(line_count, cell_count, species)


def solution(mesh):
    return jax.shard_map(
        on_device,
        mesh=mesh,
        in_specs=(
            P("lat", "depth", None),
            P("lat", "depth", None),
            P("lat", "depth", None),
            P(),
            P("lat", "depth", None),
            P("lat", "depth", None),
            P("lat", None),
            P("lat", "depth", None),
            P("lat", "depth", None),
        ),
        out_specs=P("lat", "depth", None),
        check_vma=False,
    )
```

time: 54.2 us -> 52.1 us (0.961)
  Pallas kernels: 14.6 us -> 12.5 us
    pallas_call x10, Pallas kernels: 14.6 us -> 12.5 us  [call(): pl.pallas_call(body, out_shape=outs, in_specs=[pl.BlockSpec(memory_space=...]
  transfers between devices with their start and end apart: 9 -> 9, of which waited for: 7 -> 7; matrix products, arithmetic and copies ran while one was open for 0% -> 0% of each run, Pallas kernels for 10% -> 11%
where the time goes in v2:
time: 52.1 us; the launch traced here: 52 us
  waiting for transfers between devices  27.6 us (53%)
  Pallas kernels  12.5 us (24%)
  starting transfers between devices  11.7 us (22%)
    ppermute x5, waiting for transfers between devices, xor_depth(): return lax.ppermute(value, 'depth', [(i, i ^ bits) for i in range(32)])  22.8 us
    pallas_call x10, Pallas kernels, call(): pl.pallas_call(body, out_shape=outs, in_specs=[pl.BlockSpec(memory_space=...  12.5 us
    ppermute x1, starting transfers between devices, on_device(): lax.ppermute(lax.optimization_barrier((densities, part))[0], 'depth', [(i...  7.94 us
    ppermute x3, waiting for transfers between devices, xor_lat(): return lax.ppermute(value, 'lat', [(i, i ^ bits) for i in range(8)])  4.79 us
    ppermute x5, starting transfers between devices, xor_depth(): return lax.ppermute(value, 'depth', [(i, i ^ bits) for i in range(32)])  2.29 us
    ppermute x3, starting transfers between devices, xor_lat(): return lax.ppermute(value, 'lat', [(i, i ^ bits) for i in range(8)])  1.48 us
  transfers between devices with their start and end apart: 9, of which 7 were waited for; matrix products, arithmetic and copies ran while one was open for 0% of the time, Pallas kernels for 11%

profile of v2, /device:TPU:30, one launch (start us, length us, event | category | flops | bytes accessed | tf_op | source)
XLA Modules:
  0.0 52.0 jit_solution(9947601192221420289)
XLA Ops:
  0.0 0.0 collective-permute-start
  0.0 0.0 copy-start.5
  0.0 1.9 %react.1 = (f32[32,64]{1,0:T(8,128)S(1)}, f32[64,128]{1,0:T(8,128)S(1)}) custom-call(f32[32,4096]{1,0:T(8,128)} %bitcast.21, f32[32,64]{1,0:T(8,128)} %bitcast.12, f32[32,64]{1,0:T(8,128)} %bitcast.22, f32[32,64]{1,0:T(8,128)} %bitcast.14, s32[8,8]{1,0:T(8,128)} %pat_hbm.1), custom_call_target="tpu_custom_call" | custom-call | flops 1073741824 | bytes 65536 | tf_op jit(solution)/shard_map/react/pallas_call | solution.py:362
  1.9 0.0 copy-done
  2.0 7.9 %collective-permute-start.3 = (f32[1,32,64]{2,1,0:T(8,128)S(1)}, f32[1,32,64]{2,1,0:T(8,128)S(1)}, u32[]{:S(2)}, u32[]{:S(2)}) collective-permute-start(f32[1,32,64]{2,1,0:T(8,128)S(1)} %copy-done), channel_id=1, source_target_pairs={{8,0},{16,8},{24,16},{32,24},{40,32},{48,40},{56,48},{64,56},{72,6... | collective-permute-start | bytes 24584 | tf_op jit(solution)/shard_map/ppermute | solution.py:406
  9.9 0.0 collective-permute-done.a_ref
  9.9 0.9 %collective-permute-start.1 = (f32[2,32,64]{2,1,0:T(8,128)S(1)}, f32[2,32,64]{2,1,0:T(8,128)S(1)}, u32[]{:S(2)}, u32[]{:S(2)}) collective-permute-start(f32[2,32,64]{2,1,0:T(8,128)S(1)} %pad_maximum_fusion.1), channel_id=1, source_target_pairs={{0,2},{1,3},{2,0},{3,1},{4,6},{5,7},{6,4},{7,5},{8,10},{9,11},{10,... | collective-permute-start | bytes 49160 | tf_op jit(solution)/shard_map/ppermute | solution.py:389
  10.9 0.0 copy-done.5
  10.9 1.4 %tree_leaves.1 = (bf16[16,2,64,128]{3,2,1,0:T(8,128)(2,1)S(1)}, bf16[16,4,64,128]{3,2,1,0:T(8,128)(2,1)S(1)}, f32[16,3,64,128]{3,2,1,0:T(8,128)S(1)}, f32[2,64,128]{2,1,0:T(8,128)S(1)}) custom-call(f32[1024,128]{1,0:T(8,128)S(1)} %bitcast.20, f32[32,64]{1,0:T(8,128)S(1)} %bitcast.17, f32[32,64]{1,0:T(8,128)S(1)} %get-tuple-element.33.after_ref.part_ref), custom_call_target="tpu_custom_call" | custom-call | flops 2147483648 | bytes 65536 | tf_op jit(solution)/shard_map/tree_leaves/pallas_call | solution.py:362
  12.2 1.7 %collective-permute-done.1.b_ref = f32[2,32,64]{2,1,0:T(8,128)S(1)} collective-permute-done((f32[2,32,64]{2,1,0:T(8,128)S(1)}, f32[2,32,64]{2,1,0:T(8,128)S(1)}, u32[]{:S(2)}, u32[]{:S(2)}) %collective-permute-start.1) | collective-permute-done | bytes 16416 | tf_op jit(solution)/shard_map/ppermute | solution.py:389
  13.9 0.6 %collective-permute-start.2 = (f32[4,32,64]{2,1,0:T(8,128)S(1)}, f32[4,32,64]{2,1,0:T(8,128)S(1)}, u32[]{:S(2)}, u32[]{:S(2)}) collective-permute-start(f32[4,32,64]{2,1,0:T(8,128)S(1)} %pad_maximum_fusion), channel_id=1, source_target_pairs={{0,6},{1,7},{2,4},{3,5},{4,2},{5,3},{6,0},{7,1},{8,14},{9,15},{10,... | collective-permute-start | bytes 98312 | tf_op jit(solution)/shard_map/ppermute | solution.py:389
  14.5 1.9 %tree_upper.1 = (bf16[8,4,64,128]{3,2,1,0:T(8,128)(2,1)S(1)}, bf16[4,4,64,128]{3,2,1,0:T(8,128)(2,1)S(1)}, bf16[2,4,64,128]{3,2,1,0:T(8,128)(2,1)S(1)}, bf16[1,64,128]{2,1,0:T(8,128)(2,1)S(1)}, f32[128,128]{1,0:T(8,128)S(1)}) custom-call(bf16[16,4,64,128]{3,2,1,0:T(8,128)(2,1)S(1)} %get-tuple-element.38.n1_ref, ...), custom_call_target="tpu_custom_call" | custom-call | flops 2147483648 | bytes 65536 | tf_op jit(solution)/shard_map/tree_upper/pallas_call | solution.py:362
  16.4 0.0 collective-permute-done.3.top_ref
  16.4 3.1 %collective-permute-done.2.c_ref = f32[4,32,64]{2,1,0:T(8,128)S(1)} collective-permute-done((f32[4,32,64]{2,1,0:T(8,128)S(1)}, f32[4,32,64]{2,1,0:T(8,128)S(1)}, u32[]{:S(2)}, u32[]{:S(2)}) %collective-permute-start.2) | collective-permute-done | bytes 32800 | tf_op jit(solution)/shard_map/ppermute | solution.py:389
  19.5 0.0 copy-done.1
  19.5 2.3 %upsweep.1 = (f32[128,128]{1,0:T(8,128)S(1)}, f32[4,64,128]{2,1,0:T(8,128)S(1)}, f32[7,64,128]{2,1,0:T(8,128)S(1)}, f32[7,64,128]{2,1,0:T(8,128)S(1)}) custom-call(s32[1,4]{1,0:T(1,128)S(1)} %copy-done.4, f32[32,64]{1,0:T(8,128)S(1)} %get-tuple-element.33.after_ref.part_ref, f32[1,32,64]{2,1,0:T(8,128)S(1)} %collective-permute-done.a_ref, ...), custom_call_target="tpu_custom_call" | custom-call | flops 33554432 | bytes 65536 | tf_op jit(solution)/shard_map/upsweep/pallas_call | solution.py:362
  21.9 0.1 collective-permute-start.4
  22.0 4.3 %collective-permute-done.4.refs_1_ = f32[128,128]{1,0:T(8,128)S(1)} collective-permute-done((f32[128,128]{1,0:T(8,128)S(1)}, f32[128,128]{1,0:T(8,128)S(1)}, u32[]{:S(2)}, u32[]{:S(2)}) %collective-permute-start.4) | collective-permute-done | bytes 65568 | tf_op jit(solution)/shard_map/ppermute | solution.py:392
  26.2 0.4 combine0.1
  26.6 0.1 collective-permute-start.5
  26.7 5.4 %collective-permute-done.5.refs_1_ = f32[128,128]{1,0:T(8,128)S(1)} collective-permute-done((f32[128,128]{1,0:T(8,128)S(1)}, f32[128,128]{1,0:T(8,128)S(1)}, u32[]{:S(2)}, u32[]{:S(2)}) %collective-permute-start.5) | collective-permute-done | bytes 65568 | tf_op jit(solution)/shard_map/ppermute | solution.py:392
  32.1 0.5 combine1.1
  32.6 1.5 %collective-permute-start.6 = (f32[128,128]{1,0:T(8,128)S(1)}, f32[128,128]{1,0:T(8,128)S(1)}, u32[]{:S(2)}, u32[]{:S(2)}) collective-permute-start(f32[128,128]{1,0:T(8,128)S(1)} %get-tuple-element.48.refs_0_), channel_id=1, source_target_pairs={{0,56},{8,48},{16,40},{24,32},{32,24},{40,16},{48,8},{56,0},{64,12... | collective-permute-start | bytes 196616 | tf_op jit(solution)/shard_map/ppermute | solution.py:392
  34.1 4.8 %collective-permute-done.6.refs_1_ = f32[128,128]{1,0:T(8,128)S(1)} collective-permute-done((f32[128,128]{1,0:T(8,128)S(1)}, f32[128,128]{1,0:T(8,128)S(1)}, u32[]{:S(2)}, u32[]{:S(2)}) %collective-permute-start.6) | collective-permute-done | bytes 65568 | tf_op jit(solution)/shard_map/ppermute | solution.py:392
  38.8 0.5 combine2.1
  39.3 0.5 collective-permute-start.7
  39.8 3.8 %collective-permute-done.7.refs_1_ = f32[128,128]{1,0:T(8,128)S(1)} collective-permute-done((f32[128,128]{1,0:T(8,128)S(1)}, f32[128,128]{1,0:T(8,128)S(1)}, u32[]{:S(2)}, u32[]{:S(2)}) %collective-permute-start.7) | collective-permute-done | bytes 65568 | tf_op jit(solution)/shard_map/ppermute | solution.py:392
  43.6 0.4 combine3.1
  44.1 0.1 collective-permute-start.8
  44.2 0.5 %prepare.1 = (bf16[15,64,128]{2,1,0:T(8,128)(2,1)S(1)}, f32[4,64,128]{2,1,0:T(8,128)S(1)}, f32[4,64,128]{2,1,0:T(8,128)S(1)}, f32[64,128]{1,0:T(8,128)S(1)}) custom-call(f32[4,64,128]{2,1,0:T(8,128)S(1)} %get-tuple-element.54.pair_ref, f32[7,64,128]{2,1,0:T(8,128)S(1)} %get-tuple-element.55.v_ref, f32[7,64,128]{2,1,0:T(8,128)S(1)} %get-tuple-element.56.w_ref, ...), custom_call_target="tpu_custom_call" | custom-call | flops 1073741824 | bytes 65536 | tf_op jit(solution)/shard_map/prepare/pallas_call | solution.py:362
  44.7 4.6 %collective-permute-done.8.other_ref = f32[64,128]{1,0:T(8,128)S(1)} collective-permute-done((f32[64,128]{1,0:T(8,128)S(1)}, f32[64,128]{1,0:T(8,128)S(1)}, u32[]{:S(2)}, u32[]{:S(2)}) %collective-permute-start.8) | collective-permute-done | bytes 32800 | tf_op jit(solution)/shard_map/ppermute | solution.py:392
  49.3 2.6 %downsweep.1 = f32[32,64]{1,0:T(8,128)} custom-call(f32[64,128]{1,0:T(8,128)S(1)} %get-tuple-element.52.own_ref, f32[64,128]{1,0:T(8,128)S(1)} %collective-permute-done.8.other_ref, f32[128,128]{1,0:T(8,128)S(1)} %get-tuple-element.53.fun_ref, f32[2,64,128]{2,1,0:T(8,128)S(1)} %get-tuple-element.36.cols_ref, f32[4,64,128]{2,1,0:T(8,128)S(1)} %get-tuple-element.57.add_v, ...), custom_call_target="tpu_custom_call" | custom-call | flops 33554432 | bytes 65536 | tf_op jit(solution)/shard_map/downsweep/pallas_call | solution.py:362
  (10 shorter events, 0.0 us)
Async XLA Ops:
  0.0 9.9 %collective-permute-start = (f32[1,32,64]{2,1,0:T(8,128)}, f32[1,32,64]{2,1,0:T(8,128)S(1)}, u32[]{:S(2)}, u32[]{:S(2)}) collective-permute-start(f32[1,32,64]{2,1,0:T(8,128)} %param.9), channel_id=1, source_target_pairs={{0,1},{1,0},{2,3},{3,2},{4,5},{5,4},{6,7},{7,6},{8,9},{9,8},{10,11... | collective-permute-start | bytes 24584 | tf_op jit(solution)/shard_map/ppermute | solution.py:389
  0.0 1.9 %copy-start = (f32[1,32,64]{2,1,0:T(8,128)S(1)}, f32[1,32,64]{2,1,0:T(8,128)}, u32[]{:S(2)}) copy-start(f32[1,32,64]{2,1,0:T(8,128)} %param.9) | copy-start | bytes 24580
  0.0 10.8 %copy-start.3 = (f32[1,32,64]{2,1,0:T(8,128)S(1)}, f32[1,32,64]{2,1,0:T(8,128)}, u32[]{:S(2)}) copy-start(f32[1,32,64]{2,1,0:T(8,128)} %param.17) | copy-start | bytes 24580
  0.0 10.8 %copy-start.5 = (f32[1,32,4096]{2,1,0:T(8,128)S(1)}, f32[1,32,4096]{2,1,0:T(8,128)}, u32[]{:S(2)}) copy-start(f32[1,32,4096]{2,1,0:T(8,128)} %param.16) | copy-start | bytes 1572868
  2.0 14.5 %collective-permute-start.3 = (f32[1,32,64]{2,1,0:T(8,128)S(1)}, f32[1,32,64]{2,1,0:T(8,128)S(1)}, u32[]{:S(2)}, u32[]{:S(2)}) collective-permute-start(f32[1,32,64]{2,1,0:T(8,128)S(1)} %copy-done), channel_id=1, source_target_pairs={{8,0},{16,8},{24,16},{32,24},{40,32},{48,40},{56,48},{64,56},{72,6... | collective-permute-start | bytes 24584 | tf_op jit(solution)/shard_map/ppermute | solution.py:406
  9.9 4.0 %collective-permute-start.1 = (f32[2,32,64]{2,1,0:T(8,128)S(1)}, f32[2,32,64]{2,1,0:T(8,128)S(1)}, u32[]{:S(2)}, u32[]{:S(2)}) collective-permute-start(f32[2,32,64]{2,1,0:T(8,128)S(1)} %pad_maximum_fusion.1), channel_id=1, source_target_pairs={{0,2},{1,3},{2,0},{3,1},{4,6},{5,7},{6,4},{7,5},{8,10},{9,11},{10,... | collective-permute-start | bytes 49160 | tf_op jit(solution)/shard_map/ppermute | solution.py:389
  13.9 5.6 %collective-permute-start.2 = (f32[4,32,64]{2,1,0:T(8,128)S(1)}, f32[4,32,64]{2,1,0:T(8,128)S(1)}, u32[]{:S(2)}, u32[]{:S(2)}) collective-permute-start(f32[4,32,64]{2,1,0:T(8,128)S(1)} %pad_maximum_fusion), channel_id=1, source_target_pairs={{0,6},{1,7},{2,4},{3,5},{4,2},{5,3},{6,0},{7,1},{8,14},{9,15},{10,... | collective-permute-start | bytes 98312 | tf_op jit(solution)/shard_map/ppermute | solution.py:389
  14.5 5.0 %copy-start.1 = (f32[1,32,64]{2,1,0:T(8,128)S(1)}, f32[1,32,64]{2,1,0:T(8,128)}, u32[]{:S(2)}) copy-start(f32[1,32,64]{2,1,0:T(8,128)} %param.13) | copy-start | bytes 24580
  14.5 5.0 %copy-start.2 = (f32[1,32,64]{2,1,0:T(8,128)S(1)}, f32[1,32,64]{2,1,0:T(8,128)}, u32[]{:S(2)}) copy-start(f32[1,32,64]{2,1,0:T(8,128)} %param.14) | copy-start | bytes 24580
  14.5 5.0 %copy-start.4 = (s32[1,4]{1,0:T(1,128)S(1)}, s32[1,4]{1,0:T(1,128)}, u32[]{:S(2)}) copy-start(s32[1,4]{1,0:T(1,128)} %neigh_ref.1) | copy-start | bytes 52
  21.9 4.4 %collective-permute-start.4 = (f32[128,128]{1,0:T(8,128)S(1)}, f32[128,128]{1,0:T(8,128)S(1)}, u32[]{:S(2)}, u32[]{:S(2)}) collective-permute-start(f32[128,128]{1,0:T(8,128)S(1)} %get-tuple-element.45.refs_0_), channel_id=1, source_target_pairs={{0,8},{8,0},{16,24},{24,16},{32,40},{40,32},{48,56},{56,48},{64,72... | collective-permute-start | bytes 196616 | tf_op jit(solution)/shard_map/ppermute | solution.py:392
  26.6 5.5 %collective-permute-start.5 = (f32[128,128]{1,0:T(8,128)S(1)}, f32[128,128]{1,0:T(8,128)S(1)}, u32[]{:S(2)}, u32[]{:S(2)}) collective-permute-start(f32[128,128]{1,0:T(8,128)S(1)} %get-tuple-element.46.refs_0_), channel_id=1, source_target_pairs={{0,16},{8,24},{16,0},{24,8},{32,48},{40,56},{48,32},{56,40},{64,80... | collective-permute-start | bytes 196616 | tf_op jit(solution)/shard_map/ppermute | solution.py:392
  32.6 6.3 %collective-permute-start.6 = (f32[128,128]{1,0:T(8,128)S(1)}, f32[128,128]{1,0:T(8,128)S(1)}, u32[]{:S(2)}, u32[]{:S(2)}) collective-permute-start(f32[128,128]{1,0:T(8,128)S(1)} %get-tuple-element.48.refs_0_), channel_id=1, source_target_pairs={{0,56},{8,48},{16,40},{24,32},{32,24},{40,16},{48,8},{56,0},{64,12... | collective-permute-start | bytes 196616 | tf_op jit(solution)/shard_map/ppermute | solution.py:392
  39.3 4.4 %collective-permute-start.7 = (f32[128,128]{1,0:T(8,128)S(1)}, f32[128,128]{1,0:T(8,128)S(1)}, u32[]{:S(2)}, u32[]{:S(2)}) collective-permute-start(f32[128,128]{1,0:T(8,128)S(1)} %get-tuple-element.50.refs_0_), channel_id=1, source_target_pairs={{0,64},{8,72},{16,80},{24,88},{32,96},{40,104},{48,112},{56,120},{... | collective-permute-start | bytes 196616 | tf_op jit(solution)/shard_map/ppermute | solution.py:392
  44.1 5.2 %collective-permute-start.8 = (f32[64,128]{1,0:T(8,128)S(1)}, f32[64,128]{1,0:T(8,128)S(1)}, u32[]{:S(2)}, u32[]{:S(2)}) collective-permute-start(f32[64,128]{1,0:T(8,128)S(1)} %get-tuple-element.52.own_ref), channel_id=1, source_target_pairs={{0,192},{8,200},{16,208},{24,216},{32,224},{40,232},{48,240},{56,2... | collective-permute-start | bytes 98312 | tf_op jit(solution)/shard_map/ppermute | solution.py:392

commit v3 on v2

--- a/solution.py
+++ b/solution.py
@@ -87,7 +87,8 @@
         put(n1_ref, full_ref, j, p, q, w, u)
 
 
-def tree_upper(n1_ref, full_ref, coup_ref, cols_ref, n2_ref, n3_ref, n4_ref, n5_ref, root_ref, fa, fb):
+def tree_upper(n1_ref, full_ref, coup_ref, cols_ref, after_ref, n2_ref, n3_ref, n4_ref, n5_ref, root_ref, fa, fb):
+    del after_ref
     node, full = n1_ref, full_ref
     for count, node_to, full_to in ((8, n2_ref, fa), (4, n3_ref, fb), (2, n4_ref, fa), (1, None, None)):
         for j in range(count):
@@ -112,14 +113,16 @@
 
 def react(jac_hbm, dens_hbm, src_hbm, tran_hbm, pat_hbm, out_ref, flux_ref, jac_ref, dens_ref, src_ref, tran_ref,
           pat_ref, sems):
-    pairs = ((dens_hbm, dens_ref), (pat_hbm, pat_ref), (jac_hbm, jac_ref), (src_hbm, src_ref), (tran_hbm, tran_ref))
+    parts = [(slice(None), pl.ds(i * 1024, 1024)) for i in range(4)]
+    pairs = [(dens_hbm, dens_ref), (pat_hbm, pat_ref)] + [(jac_hbm.at[part], jac_ref.at[part]) for part in parts]
+    pairs += [(src_hbm, src_ref), (tran_hbm, tran_ref)]
     copies = [pltpu.make_async_copy(a, b, sems.at[i]) for i, (a, b) in enumerate(pairs)]
     for copy in copies:
         copy.start()
     half = lanes((128, N)) % 2 == lax.broadcasted_iota(jnp.int32, (128, N), 0) // N
     half = jnp.where(half, 1.0, 0.0).astype(bf16)
-    for copy in copies:
-        copy.wait()
+    copies[0].wait()
+    copies[1].wait()
     u = dens_ref[...]
     u2 = jnp.concatenate([u, u], axis=1)
     lane8 = lanes((8, 128))
@@ -130,11 +133,15 @@
     lane = lanes((CELLS, N))
     acc = jnp.zeros((CELLS, N), f32)
     for m in range(32):
+        if m % 8 == 0:
+            copies[2 + m // 8].wait()
         y = jac_ref[:, m * 128 : (m + 1) * 128] * (u2 * mask_rows[m // 4 : m // 4 + 1])
         hi = y.astype(bf16)
         lo = (y - hi.astype(f32)).astype(bf16)
         z = jnp.dot(hi, half, preferred_element_type=f32) + jnp.dot(lo, half, preferred_element_type=f32)
         acc = jnp.where(lane // 2 == m, z, acc)
+    copies[6].wait()
+    copies[7].wait()
     tran = tran_ref[...]
     flux = tran * u
     flux_ref[...] = column(flux[CELLS - 1 : CELLS])
@@ -254,23 +261,9 @@
     return x, y, z, g, h
 
 
-def repack(ref, x, y, z, g, h):
-    lane = lanes((N, 128))
-    low = lane < N
-    ref[:N] = jnp.where(low, x, y)
-    ref[N:] = jnp.where(low, z, jnp.where(lane == N, g, h))
-
-
-def combine(level, *refs):
-    if level == 0:
-        own_ref, other_ref, out_ref, fun_out = refs
-    else:
-        own_ref, other_ref, fun_ref, out_ref, fun_out = refs
-    at = lax.axis_index("depth")
-    is_low = ((at // (1, 2, 4, 8)[level]) % 2) == 0
-    own, other = own_ref[...], other_ref[...]
-    p1, q1, w1, v1, h1 = unpack(jnp.where(is_low, own, other))
-    p2, q2, w2, v2, h2 = unpack(jnp.where(is_low, other, own))
+def join(one, two, last=False):
+    p1, q1, w1, v1, h1 = one
+    p2, q2, w2, v2, h2 = two
     kq1, kp2, kw2 = pack(q1), pack(p2), pack(w2)
     yp1, yv1 = rhs(p1), rhs(v1)
     t = dot(kw2, yp1)
@@ -279,40 +272,82 @@
     yt, yth = rhs(t), rhs(th)
     w = w1 + dot(kq1, yt)
     h = h1 + dot(kq1, yth)
+    yq2 = rhs(q2)
+    p, q = (None, None) if last else (dot(kp2, yp1), dot(kq1, yq2))
+    return (p, q, w, v, h), (t, th, yp1, yv1, yq2, yt, yth)
+
+
+def track_first(is_low, one, two, extra):
+    eye = eye2()
+    t, th = extra[:2]
+    return (
+        jnp.where(is_low, eye, one[0]),
+        jnp.where(is_low, two[1], eye),
+        jnp.where(is_low, t, 0.0),
+        jnp.where(is_low, 0.0, one[3]),
+        jnp.where(is_low, th, 0.0),
+    )
+
+
+def track(is_low, fun, extra):
+    f, hh, k, g, e = fun
+    t, th, yp1, yv1, yq2, yt, yth = extra
+    x1 = pack(jnp.where(is_low, hh, f))
+    x2 = pack(jnp.where(is_low, hh, k))
+    prod1 = dot(x1, jnp.where(is_low, yq2, yp1))
+    prod2 = dot(x2, jnp.where(is_low, yt, yp1))
+    vec1 = dot(x1, yv1)
+    vec2 = dot(x2, jnp.where(is_low, yth, yv1))
+    return (
+        jnp.where(is_low, f, prod1),
+        jnp.where(is_low, prod1, hh),
+        jnp.where(is_low, k + prod2, prod2),
+        jnp.where(is_low, g, g + vec1),
+        e + vec2,
+    )
+
+
+def put_map(ref, p, q, w, v, h, last=False):
     lane = lanes((N, 128))
     low = lane < N
     tail = jnp.where(low, w, jnp.where(lane == N, v, h))
-    if level == 3:
-        out_ref[...] = tail
+    if last:
+        ref[...] = tail
     else:
-        out_ref[:N] = jnp.where(low, dot(kp2, yp1), dot(kq1, rhs(q2)))
-        out_ref[N:] = tail
-    if level == 0:
-        eye = eye2()
-        repack(
-            fun_out,
-            jnp.where(is_low, eye, p1),
-            jnp.where(is_low, q2, eye),
-            jnp.where(is_low, t, 0.0),
-            jnp.where(is_low, 0.0, v1),
-            jnp.where(is_low, th, 0.0),
-        )
-    else:
-        f, hh, k, g, e = unpack(fun_ref[...])
-        x1 = pack(jnp.where(is_low, hh, f))
-        x2 = pack(jnp.where(is_low, hh, k))
-        prod1 = dot(x1, rhs(jnp.where(is_low, q2, p1)))
-        prod2 = dot(x2, jnp.where(is_low, yt, yp1))
-        vec1 = dot(x1, yv1)
-        vec2 = dot(x2, jnp.where(is_low, yth, yv1))
-        repack(
-            fun_out,
-            jnp.where(is_low, f, prod1),
-            jnp.where(is_low, prod1, hh),
-            jnp.where(is_low, k + prod2, prod2),
-            jnp.where(is_low, g, g + vec1),
-            e + vec2,
-        )
+        ref[:N] = jnp.where(low, p, q)
+        ref[N:] = tail
+
+
+def combine_two(level, own_ref, other_ref, fun_ref, out_ref, fun_out):
+    is_low = ((lax.axis_index("depth") // (1, 2, 4, 8)[level]) % 2) == 0
+    own, other = own_ref[...], other_ref[...]
+    one = unpack(jnp.where(is_low, own, other))
+    two = unpack(jnp.where(is_low, other, own))
+    total, extra = join(one, two, last=level == 3)
+    put_map(out_ref, *total, last=level == 3)
+    put_map(fun_out, *track(is_low, unpack(fun_ref[...]), extra))
+
+
+def combine_four(own_ref, x1_ref, x2_ref, x3_ref, out_ref, fun_out, slots):
+    at = lax.axis_index("depth") % 4
+    slots[at] = own_ref[...]
+    slots[at ^ 1] = x1_ref[...]
+    slots[at ^ 2] = x2_ref[...]
+    slots[at ^ 3] = x3_ref[...]
+    maps = [unpack(slots[i]) for i in range(4)]
+    lower, extra_lower = join(maps[0], maps[1])
+    upper, extra_upper = join(maps[2], maps[3])
+    in_lower = at < 2
+    mine = lambda a, b: jnp.where(in_lower, a, b)
+    fun = track_first(
+        at % 2 == 0,
+        [mine(a, b) for a, b in zip(maps[0], maps[2])],
+        [mine(a, b) for a, b in zip(maps[1], maps[3])],
+        [mine(a, b) for a, b in zip(extra_lower[:2], extra_upper[:2])],
+    )
+    total, extra = join(lower, upper)
+    put_map(out_ref, *total)
+    put_map(fun_out, *track(in_lower, fun, extra))
 
 
 def downsweep(own_ref, other_ref, fun_ref, cols_ref, add_v, add_a, add_x, leaf_ref, n1_ref, n2_ref, n3_ref, n4_ref, t_ref,
@@ -395,7 +430,7 @@
     part, flux = call(
         react, (sds(CELLS, N), sds(N, 128)), jac, u, src, tran, pattern, hbm=5, flops=1 << 30, name="react",
         scratch=[pltpu.VMEM((CELLS, N * N), f32)] + [pltpu.VMEM((CELLS, N), f32)] * 3
-        + [pltpu.VMEM((8, 8), jnp.int32), pltpu.SemaphoreType.DMA((5,))],
+        + [pltpu.VMEM((8, 8), jnp.int32), pltpu.SemaphoreType.DMA((8,))],
     )
     line_b = xor_lat(jnp.concatenate([densities, line_a], axis=0), 2)
     leaf, n1, full, cols = call(
@@ -403,12 +438,12 @@
         (sds(16, 2, N, 128, dtype=bf16), node(16), sds(16, 3, N, 128), sds(2, N, 128)),
         fac, coup, part, scratch=[pltpu.VMEM((2, N, 128), f32)], flops=2 << 30, name="tree_leaves",
     )
-    top = lax.ppermute(lax.optimization_barrier((densities, part))[0], "depth", [(i + 1, i) for i in range(31)])
+    top = lax.ppermute(lax.optimization_barrier((densities, cols))[0], "depth", [(i + 1, i) for i in range(31)])
     line_c = xor_lat(jnp.concatenate([densities, line_a, line_b], axis=0), 6)
     n2, n3, n4, n5, root = call(
         tree_upper,
         (node(8), node(4), node(2), sds(1, N, 128, dtype=bf16), sds(128, 128)),
-        n1, full, coup, cols, scratch=[pltpu.VMEM((8, 3, N, 128), f32), pltpu.VMEM((4, 3, N, 128), f32)],
+        n1, full, coup, cols, part, scratch=[pltpu.VMEM((8, 3, N, 128), f32), pltpu.VMEM((4, 3, N, 128), f32)],
         flops=2 << 30, name="tree_upper",
     )
     pay, pair, vs, ws = call(
@@ -416,18 +451,21 @@
         neighbours, part, line_a, line_b, line_c, top, flux, u, tran, lat, coup, cols, leaf, n1, n2, n3, n4, n5, root,
         smem=1, flops=1 << 25, name="upsweep",
     )
-    fun = None
-    for level, bits in enumerate((1, 2, 7, 8)):
+    others = [xor_depth(pay, bits) for bits in (1, 2, 3)]
+    tees, add_v, add_a, add_x = call(
+        prepare, (sds(15, N, 128, dtype=bf16), sds(4, N, 128), sds(4, N, 128), sds(N, 128)),
+        pair, vs, ws, n1, n2, n3, n4, flops=1 << 30, name="prepare",
+    )
+    pay, fun = call(
+        combine_four, (sds(128, 128), sds(128, 128)), pay, *others, scratch=[pltpu.VMEM((4, 128, 128), f32)],
+        flops=1 << 24, name="combine_four",
+    )
+    for level, bits in ((2, 7), (3, 8)):
         other = xor_depth(pay, bits)
-        if level == 0:
-            tees, add_v, add_a, add_x = call(
-                prepare, (sds(15, N, 128, dtype=bf16), sds(4, N, 128), sds(4, N, 128), sds(N, 128)),
-                pair, vs, ws, n1, n2, n3, n4, flops=1 << 30, name="prepare",
-            )
-        args = (pay, other) if level == 0 else (pay, other, fun)
         pay, fun = call(
-            lambda *refs, level=level: combine(level, *refs),
-            (sds(N if level == 3 else 128, 128), sds(128, 128)), *args, flops=1 << 24, name=f"combine{level}",
+            lambda *refs, level=level: combine_two(level, *refs),
+            (sds(N if level == 3 else 128, 128), sds(128, 128)), pay, other, fun, flops=1 << 24,
+            name=f"combine{level}",
         )
     other = xor_depth(pay, 24)
     out = call(

time: 52.1 us -> 49.3 us (0.946)
  the two profiles are of different devices: /device:TPU:30 before, /device:TPU:32 now
where the time goes in v3:
time: 49.3 us; the launch traced here: 49 us
  starting transfers between devices  23.8 us (48%)
  Pallas kernels  12.8 us (26%)
  waiting for transfers between devices  12.3 us (25%)
    ppermute x6, starting transfers between devices, xor_depth(): return lax.ppermute(value, 'depth', [(i, i ^ bits) for i in range(32)])  18 us
    pallas_call x9, Pallas kernels, call(): pl.pallas_call(body, out_shape=outs, in_specs=[pl.BlockSpec(memory_space=...  12.8 us
    ppermute x6, waiting for transfers between devices, xor_depth(): return lax.ppermute(value, 'depth', [(i, i ^ bits) for i in range(32)])  10.6 us
    ppermute x3, starting transfers between devices, xor_lat(): return lax.ppermute(value, 'lat', [(i, i ^ bits) for i in range(8)])  3.53 us
    ppermute x1, starting transfers between devices, on_device(): lax.ppermute(lax.optimization_barrier((densities, cols))[0], 'depth', [(i...  2.25 us
    ppermute x3, waiting for transfers between devices, xor_lat(): return lax.ppermute(value, 'lat', [(i, i ^ bits) for i in range(8)])  1.69 us
  transfers between devices with their start and end apart: 10, of which 7 were waited for; matrix products, arithmetic and copies ran while one was open for 0% of the time, Pallas kernels for 12%

profile of v3, /device:TPU:32, one launch (start us, length us, event | category | flops | bytes accessed | tf_op | source)
XLA Modules:
  0.0 49.0 jit_solution(14040234002980723280)
XLA Ops:
  0.0 0.0 collective-permute-start
  0.0 0.0 copy-start.5
  0.0 2.2 %react.1 = (f32[32,64]{1,0:T(8,128)S(1)}, f32[64,128]{1,0:T(8,128)S(1)}) custom-call(f32[32,4096]{1,0:T(8,128)} %bitcast.21, f32[32,64]{1,0:T(8,128)} %bitcast.12, f32[32,64]{1,0:T(8,128)} %bitcast.22, f32[32,64]{1,0:T(8,128)} %bitcast.14, s32[8,8]{1,0:T(8,128)} %pat_hbm.1), custom_call_target="tpu_custom_call" | custom-call | flops 1073741824 | bytes 65536 | tf_op jit(solution)/shard_map/react/pallas_call | solution.py:397
  2.2 0.0 collective-permute-done.a_ref
  2.2 0.0 copy-done
  2.2 1.6 %collective-permute-start.1 = (f32[2,32,64]{2,1,0:T(8,128)S(1)}, f32[2,32,64]{2,1,0:T(8,128)S(1)}, u32[]{:S(2)}, u32[]{:S(2)}) collective-permute-start(f32[2,32,64]{2,1,0:T(8,128)S(1)} %pad_maximum_fusion.1), channel_id=1, source_target_pairs={{0,2},{1,3},{2,0},{3,1},{4,6},{5,7},{6,4},{7,5},{8,10},{9,11},{10,... | collective-permute-start | bytes 49160 | tf_op jit(solution)/shard_map/ppermute | solution.py:424
  3.8 1.4 %tree_leaves.1 = (bf16[16,2,64,128]{3,2,1,0:T(8,128)(2,1)S(1)}, bf16[16,4,64,128]{3,2,1,0:T(8,128)(2,1)S(1)}, f32[16,3,64,128]{3,2,1,0:T(8,128)S(1)}, f32[2,64,128]{2,1,0:T(8,128)S(1)}) custom-call(f32[1024,128]{1,0:T(8,128)S(1)} %bitcast.20, f32[32,64]{1,0:T(8,128)S(1)} %bitcast.17, f32[32,64]{1,0:T(8,128)S(1)} %get-tuple-element.31.after_ref.part_ref), custom_call_target="tpu_custom_call" | custom-call | flops 2147483648 | bytes 65536 | tf_op jit(solution)/shard_map/tree_leaves/pallas_call | solution.py:397
  5.2 2.3 %collective-permute-start.3 = (f32[1,32,64]{2,1,0:T(8,128)S(1)}, f32[1,32,64]{2,1,0:T(8,128)S(1)}, u32[]{:S(2)}, u32[]{:S(2)}) collective-permute-start(f32[1,32,64]{2,1,0:T(8,128)S(1)} %copy-done), channel_id=1, source_target_pairs={{8,0},{16,8},{24,16},{32,24},{40,32},{48,40},{56,48},{64,56},{72,6... | collective-permute-start | bytes 24584 | tf_op jit(solution)/shard_map/ppermute | solution.py:441
  7.4 0.0 collective-permute-done.1.b_ref
  7.5 1.9 %collective-permute-start.2 = (f32[4,32,64]{2,1,0:T(8,128)S(1)}, f32[4,32,64]{2,1,0:T(8,128)S(1)}, u32[]{:S(2)}, u32[]{:S(2)}) collective-permute-start(f32[4,32,64]{2,1,0:T(8,128)S(1)} %pad_maximum_fusion), channel_id=1, source_target_pairs={{0,6},{1,7},{2,4},{3,5},{4,2},{5,3},{6,0},{7,1},{8,14},{9,15},{10,... | collective-permute-start | bytes 98312 | tf_op jit(solution)/shard_map/ppermute | solution.py:424
  9.4 1.9 %tree_upper.1 = (bf16[8,4,64,128]{3,2,1,0:T(8,128)(2,1)S(1)}, bf16[4,4,64,128]{3,2,1,0:T(8,128)(2,1)S(1)}, bf16[2,4,64,128]{3,2,1,0:T(8,128)(2,1)S(1)}, bf16[1,64,128]{2,1,0:T(8,128)(2,1)S(1)}, f32[128,128]{1,0:T(8,128)S(1)}) custom-call(bf16[16,4,64,128]{3,2,1,0:T(8,128)(2,1)S(1)} %get-tuple-element.36.n1_ref, ...), custom_call_target="tpu_custom_call" | custom-call | flops 2147483648 | bytes 65536 | tf_op jit(solution)/shard_map/tree_upper/pallas_call | solution.py:397
  11.3 0.0 collective-permute-done.3.top_ref
  11.3 1.7 %collective-permute-done.2.c_ref = f32[4,32,64]{2,1,0:T(8,128)S(1)} collective-permute-done((f32[4,32,64]{2,1,0:T(8,128)S(1)}, f32[4,32,64]{2,1,0:T(8,128)S(1)}, u32[]{:S(2)}, u32[]{:S(2)}) %collective-permute-start.2) | collective-permute-done | bytes 32800 | tf_op jit(solution)/shard_map/ppermute | solution.py:424
  13.0 0.0 copy-done.1
  13.0 2.3 %upsweep.1 = (f32[128,128]{1,0:T(8,128)S(1)}, f32[4,64,128]{2,1,0:T(8,128)S(1)}, f32[7,64,128]{2,1,0:T(8,128)S(1)}, f32[7,64,128]{2,1,0:T(8,128)S(1)}) custom-call(s32[1,4]{1,0:T(1,128)S(1)} %copy-done.4, f32[32,64]{1,0:T(8,128)S(1)} %get-tuple-element.31.after_ref.part_ref, f32[1,32,64]{2,1,0:T(8,128)S(1)} %collective-permute-done.a_ref, ...), custom_call_target="tpu_custom_call" | custom-call | flops 33554432 | bytes 65536 | tf_op jit(solution)/shard_map/upsweep/pallas_call | solution.py:397
  15.4 0.7 %collective-permute-start.4 = (f32[128,128]{1,0:T(8,128)S(1)}, f32[128,128]{1,0:T(8,128)S(1)}, u32[]{:S(2)}, u32[]{:S(2)}) collective-permute-start(f32[128,128]{1,0:T(8,128)S(1)} %get-tuple-element.43.own_ref), channel_id=1, source_target_pairs={{0,8},{8,0},{16,24},{24,16},{32,40},{40,32},{48,56},{56,48},{64,72... | collective-permute-start | bytes 196616 | tf_op jit(solution)/shard_map/ppermute | solution.py:427
  16.1 2.6 %collective-permute-start.5 = (f32[128,128]{1,0:T(8,128)S(1)}, f32[128,128]{1,0:T(8,128)S(1)}, u32[]{:S(2)}, u32[]{:S(2)}) collective-permute-start(f32[128,128]{1,0:T(8,128)S(1)} %get-tuple-element.43.own_ref), channel_id=1, source_target_pairs={{0,16},{8,24},{16,0},{24,8},{32,48},{40,56},{48,32},{56,40},{64,80... | collective-permute-start | bytes 196616 | tf_op jit(solution)/shard_map/ppermute | solution.py:427
  18.6 0.4 collective-permute-start.6
  19.1 0.7 %collective-permute-done.4.x1_ref = f32[128,128]{1,0:T(8,128)S(1)} collective-permute-done((f32[128,128]{1,0:T(8,128)S(1)}, f32[128,128]{1,0:T(8,128)S(1)}, u32[]{:S(2)}, u32[]{:S(2)}) %collective-permute-start.4) | collective-permute-done | bytes 65568 | tf_op jit(solution)/shard_map/ppermute | solution.py:427
  19.7 3.2 %collective-permute-done.5.x2_ref = f32[128,128]{1,0:T(8,128)S(1)} collective-permute-done((f32[128,128]{1,0:T(8,128)S(1)}, f32[128,128]{1,0:T(8,128)S(1)}, u32[]{:S(2)}, u32[]{:S(2)}) %collective-permute-start.5) | collective-permute-done | bytes 65568 | tf_op jit(solution)/shard_map/ppermute | solution.py:427
  22.9 0.9 %collective-permute-done.6.x3_ref = f32[128,128]{1,0:T(8,128)S(1)} collective-permute-done((f32[128,128]{1,0:T(8,128)S(1)}, f32[128,128]{1,0:T(8,128)S(1)}, u32[]{:S(2)}, u32[]{:S(2)}) %collective-permute-start.6) | collective-permute-done | bytes 65568 | tf_op jit(solution)/shard_map/ppermute | solution.py:427
  23.8 1.0 %combine_four.1 = (f32[128,128]{1,0:T(8,128)S(1)}, f32[128,128]{1,0:T(8,128)S(1)}) custom-call(f32[128,128]{1,0:T(8,128)S(1)} %get-tuple-element.43.own_ref, f32[128,128]{1,0:T(8,128)S(1)} %collective-permute-done.4.x1_ref, f32[128,128]{1,0:T(8,128)S(1)} %collective-permute-done.5.x2_ref, f32[128,128]{1,0:T(8,128)S(1)} %collective-permute-done.6.x3_ref), custom_call_target="tpu_custom_call" | custom-call | flops 16777216 | bytes 65536 | tf_op jit(solution)/shard_map/combine_four/pallas_call | solution.py:397
  24.8 6.5 %collective-permute-start.7 = (f32[128,128]{1,0:T(8,128)S(1)}, f32[128,128]{1,0:T(8,128)S(1)}, u32[]{:S(2)}, u32[]{:S(2)}) collective-permute-start(f32[128,128]{1,0:T(8,128)S(1)} %get-tuple-element.44.refs_0_), channel_id=1, source_target_pairs={{0,56},{8,48},{16,40},{24,32},{32,24},{40,16},{48,8},{56,0},{64,12... | collective-permute-start | bytes 196616 | tf_op jit(solution)/shard_map/ppermute | solution.py:427
  31.2 2.3 %collective-permute-done.7.refs_1_ = f32[128,128]{1,0:T(8,128)S(1)} collective-permute-done((f32[128,128]{1,0:T(8,128)S(1)}, f32[128,128]{1,0:T(8,128)S(1)}, u32[]{:S(2)}, u32[]{:S(2)}) %collective-permute-start.7) | collective-permute-done | bytes 65568 | tf_op jit(solution)/shard_map/ppermute | solution.py:427
  33.5 0.5 combine2.1
  33.9 4.0 %collective-permute-start.8 = (f32[128,128]{1,0:T(8,128)S(1)}, f32[128,128]{1,0:T(8,128)S(1)}, u32[]{:S(2)}, u32[]{:S(2)}) collective-permute-start(f32[128,128]{1,0:T(8,128)S(1)} %get-tuple-element.46.refs_0_), channel_id=1, source_target_pairs={{0,64},{8,72},{16,80},{24,88},{32,96},{40,104},{48,112},{56,120},{... | collective-permute-start | bytes 196616 | tf_op jit(solution)/shard_map/ppermute | solution.py:427
  37.9 2.2 %collective-permute-done.8.refs_1_ = f32[128,128]{1,0:T(8,128)S(1)} collective-permute-done((f32[128,128]{1,0:T(8,128)S(1)}, f32[128,128]{1,0:T(8,128)S(1)}, u32[]{:S(2)}, u32[]{:S(2)}) %collective-permute-start.8) | collective-permute-done | bytes 65568 | tf_op jit(solution)/shard_map/ppermute | solution.py:427
  40.2 0.4 combine3.1
  40.6 3.8 %collective-permute-start.9 = (f32[64,128]{1,0:T(8,128)S(1)}, f32[64,128]{1,0:T(8,128)S(1)}, u32[]{:S(2)}, u32[]{:S(2)}) collective-permute-start(f32[64,128]{1,0:T(8,128)S(1)} %get-tuple-element.48.own_ref), channel_id=1, source_target_pairs={{0,192},{8,200},{16,208},{24,216},{32,224},{40,232},{48,240},{56,2... | collective-permute-start | bytes 98312 | tf_op jit(solution)/shard_map/ppermute | solution.py:427
  44.5 0.5 %prepare.1 = (bf16[15,64,128]{2,1,0:T(8,128)(2,1)S(1)}, f32[4,64,128]{2,1,0:T(8,128)S(1)}, f32[4,64,128]{2,1,0:T(8,128)S(1)}, f32[64,128]{1,0:T(8,128)S(1)}) custom-call(f32[4,64,128]{2,1,0:T(8,128)S(1)} %get-tuple-element.50.pair_ref, f32[7,64,128]{2,1,0:T(8,128)S(1)} %get-tuple-element.51.v_ref, f32[7,64,128]{2,1,0:T(8,128)S(1)} %get-tuple-element.52.w_ref, ...), custom_call_target="tpu_custom_call" | custom-call | flops 1073741824 | bytes 65536 | tf_op jit(solution)/shard_map/prepare/pallas_call | solution.py:397
  45.0 1.4 %collective-permute-done.9.other_ref = f32[64,128]{1,0:T(8,128)S(1)} collective-permute-done((f32[64,128]{1,0:T(8,128)S(1)}, f32[64,128]{1,0:T(8,128)S(1)}, u32[]{:S(2)}, u32[]{:S(2)}) %collective-permute-start.9) | collective-permute-done | bytes 32800 | tf_op jit(solution)/shard_map/ppermute | solution.py:427
  46.4 2.6 %downsweep.1 = f32[32,64]{1,0:T(8,128)} custom-call(f32[64,128]{1,0:T(8,128)S(1)} %get-tuple-element.48.own_ref, f32[64,128]{1,0:T(8,128)S(1)} %collective-permute-done.9.other_ref, f32[128,128]{1,0:T(8,128)S(1)} %get-tuple-element.49.fun_ref, f32[2,64,128]{2,1,0:T(8,128)S(1)} %get-tuple-element.32.cols_ref, f32[4,64,128]{2,1,0:T(8,128)S(1)} %get-tuple-element.53.add_v, ...), custom_call_target="tpu_custom_call" | custom-call | flops 33554432 | bytes 65536 | tf_op jit(solution)/shard_map/downsweep/pallas_call | solution.py:397
  (11 shorter events, 0.0 us)
Async XLA Ops:
  0.0 2.2 %collective-permute-start = (f32[1,32,64]{2,1,0:T(8,128)}, f32[1,32,64]{2,1,0:T(8,128)S(1)}, u32[]{:S(2)}, u32[]{:S(2)}) collective-permute-start(f32[1,32,64]{2,1,0:T(8,128)} %param.9), channel_id=1, source_target_pairs={{0,1},{1,0},{2,3},{3,2},{4,5},{5,4},{6,7},{7,6},{8,9},{9,8},{10,11... | collective-permute-start | bytes 24584 | tf_op jit(solution)/shard_map/ppermute | solution.py:424
  0.0 2.2 %copy-start = (f32[1,32,64]{2,1,0:T(8,128)S(1)}, f32[1,32,64]{2,1,0:T(8,128)}, u32[]{:S(2)}) copy-start(f32[1,32,64]{2,1,0:T(8,128)} %param.9) | copy-start | bytes 24580
  0.0 3.8 %copy-start.3 = (f32[1,32,64]{2,1,0:T(8,128)S(1)}, f32[1,32,64]{2,1,0:T(8,128)}, u32[]{:S(2)}) copy-start(f32[1,32,64]{2,1,0:T(8,128)} %param.17) | copy-start | bytes 24580
  0.0 3.8 %copy-start.5 = (f32[1,32,4096]{2,1,0:T(8,128)S(1)}, f32[1,32,4096]{2,1,0:T(8,128)}, u32[]{:S(2)}) copy-start(f32[1,32,4096]{2,1,0:T(8,128)} %param.16) | copy-start | bytes 1572868
  2.2 5.2 %collective-permute-start.1 = (f32[2,32,64]{2,1,0:T(8,128)S(1)}, f32[2,32,64]{2,1,0:T(8,128)S(1)}, u32[]{:S(2)}, u32[]{:S(2)}) collective-permute-start(f32[2,32,64]{2,1,0:T(8,128)S(1)} %pad_maximum_fusion.1), channel_id=1, source_target_pairs={{0,2},{1,3},{2,0},{3,1},{4,6},{5,7},{6,4},{7,5},{8,10},{9,11},{10,... | collective-permute-start | bytes 49160 | tf_op jit(solution)/shard_map/ppermute | solution.py:424
  5.2 6.2 %collective-permute-start.3 = (f32[1,32,64]{2,1,0:T(8,128)S(1)}, f32[1,32,64]{2,1,0:T(8,128)S(1)}, u32[]{:S(2)}, u32[]{:S(2)}) collective-permute-start(f32[1,32,64]{2,1,0:T(8,128)S(1)} %copy-done), channel_id=1, source_target_pairs={{8,0},{16,8},{24,16},{32,24},{40,32},{48,40},{56,48},{64,56},{72,6... | collective-permute-start | bytes 24584 | tf_op jit(solution)/shard_map/ppermute | solution.py:441
  7.5 5.6 %collective-permute-start.2 = (f32[4,32,64]{2,1,0:T(8,128)S(1)}, f32[4,32,64]{2,1,0:T(8,128)S(1)}, u32[]{:S(2)}, u32[]{:S(2)}) collective-permute-start(f32[4,32,64]{2,1,0:T(8,128)S(1)} %pad_maximum_fusion), channel_id=1, source_target_pairs={{0,6},{1,7},{2,4},{3,5},{4,2},{5,3},{6,0},{7,1},{8,14},{9,15},{10,... | collective-permute-start | bytes 98312 | tf_op jit(solution)/shard_map/ppermute | solution.py:424
  9.4 3.6 %copy-start.1 = (f32[1,32,64]{2,1,0:T(8,128)S(1)}, f32[1,32,64]{2,1,0:T(8,128)}, u32[]{:S(2)}) copy-start(f32[1,32,64]{2,1,0:T(8,128)} %param.13) | copy-start | bytes 24580
  9.4 3.6 %copy-start.2 = (f32[1,32,64]{2,1,0:T(8,128)S(1)}, f32[1,32,64]{2,1,0:T(8,128)}, u32[]{:S(2)}) copy-start(f32[1,32,64]{2,1,0:T(8,128)} %param.14) | copy-start | bytes 24580
  9.4 3.6 %copy-start.4 = (s32[1,4]{1,0:T(1,128)S(1)}, s32[1,4]{1,0:T(1,128)}, u32[]{:S(2)}) copy-start(s32[1,4]{1,0:T(1,128)} %neigh_ref.1) | copy-start | bytes 52
  15.4 4.4 %collective-permute-start.4 = (f32[128,128]{1,0:T(8,128)S(1)}, f32[128,128]{1,0:T(8,128)S(1)}, u32[]{:S(2)}, u32[]{:S(2)}) collective-permute-start(f32[128,128]{1,0:T(8,128)S(1)} %get-tuple-element.43.own_ref), channel_id=1, source_target_pairs={{0,8},{8,0},{16,24},{24,16},{32,40},{40,32},{48,56},{56,48},{64,72... | collective-permute-start | bytes 196616 | tf_op jit(solution)/shard_map/ppermute | solution.py:427
  16.1 6.9 %collective-permute-start.5 = (f32[128,128]{1,0:T(8,128)S(1)}, f32[128,128]{1,0:T(8,128)S(1)}, u32[]{:S(2)}, u32[]{:S(2)}) collective-permute-start(f32[128,128]{1,0:T(8,128)S(1)} %get-tuple-element.43.own_ref), channel_id=1, source_target_pairs={{0,16},{8,24},{16,0},{24,8},{32,48},{40,56},{48,32},{56,40},{64,80... | collective-permute-start | bytes 196616 | tf_op jit(solution)/shard_map/ppermute | solution.py:427
  18.6 5.2 %collective-permute-start.6 = (f32[128,128]{1,0:T(8,128)S(1)}, f32[128,128]{1,0:T(8,128)S(1)}, u32[]{:S(2)}, u32[]{:S(2)}) collective-permute-start(f32[128,128]{1,0:T(8,128)S(1)} %get-tuple-element.43.own_ref), channel_id=1, source_target_pairs={{0,24},{8,16},{16,8},{24,0},{32,56},{40,48},{48,40},{56,32},{64,88... | collective-permute-start | bytes 196616 | tf_op jit(solution)/shard_map/ppermute | solution.py:427
  24.8 8.7 %collective-permute-start.7 = (f32[128,128]{1,0:T(8,128)S(1)}, f32[128,128]{1,0:T(8,128)S(1)}, u32[]{:S(2)}, u32[]{:S(2)}) collective-permute-start(f32[128,128]{1,0:T(8,128)S(1)} %get-tuple-element.44.refs_0_), channel_id=1, source_target_pairs={{0,56},{8,48},{16,40},{24,32},{32,24},{40,16},{48,8},{56,0},{64,12... | collective-permute-start | bytes 196616 | tf_op jit(solution)/shard_map/ppermute | solution.py:427
  33.9 6.3 %collective-permute-start.8 = (f32[128,128]{1,0:T(8,128)S(1)}, f32[128,128]{1,0:T(8,128)S(1)}, u32[]{:S(2)}, u32[]{:S(2)}) collective-permute-start(f32[128,128]{1,0:T(8,128)S(1)} %get-tuple-element.46.refs_0_), channel_id=1, source_target_pairs={{0,64},{8,72},{16,80},{24,88},{32,96},{40,104},{48,112},{56,120},{... | collective-permute-start | bytes 196616 | tf_op jit(solution)/shard_map/ppermute | solution.py:427
  40.6 5.7 %collective-permute-start.9 = (f32[64,128]{1,0:T(8,128)S(1)}, f32[64,128]{1,0:T(8,128)S(1)}, u32[]{:S(2)}, u32[]{:S(2)}) collective-permute-start(f32[64,128]{1,0:T(8,128)S(1)} %get-tuple-element.48.own_ref), channel_id=1, source_target_pairs={{0,192},{8,200},{16,208},{24,216},{32,224},{40,232},{48,240},{56,2... | collective-permute-start | bytes 98312 | tf_op jit(solution)/shard_map/ppermute | solution.py:427

commit v4 on v3

--- a/solution.py
+++ b/solution.py
@@ -5,6 +5,7 @@
 from jax.experimental.pallas import tpu as pltpu
 from jax.sharding import PartitionSpec as P
 
+
 f32 = jnp.float32
 bf16 = jnp.bfloat16
 
@@ -47,16 +48,35 @@
     return jnp.broadcast_to(row, (128, N)).T
 
 
+def pair(a, b):
+    low = lanes(a.shape) < N
+    a_hi, b_hi = a.astype(bf16).astype(f32), b.astype(bf16).astype(f32)
+    hi = jnp.where(low, a_hi, b_hi).astype(bf16)
+    lo = jnp.where(low, a - a_hi, b - b_hi).astype(bf16)
+    return jnp.concatenate([hi, lo], axis=1)
+
+
+def pair_rhs(x, y):
+    def split(z):
+        hi = z.astype(bf16).astype(f32)
+        return jnp.where(lanes(z.shape) % 64 < CELLS, hi, z - hi).astype(bf16)
+
+    a, b = split(x), split(y)
+    return jnp.concatenate([a, b, a, b], axis=0)
+
+
 def eye2():
     return jnp.where(lanes((N, 128)) % N == lax.broadcasted_iota(jnp.int32, (N, 128), 0), 1.0, 0.0)
 
 
-def put(node, full, j, p, q, w, u):
-    node[j, 0], node[j, 1], node[j, 2], node[j, 3] = pack(p), pack(q), pack(w), pack(u)
+def put(node, full, j, p, q, w, u=None):
+    node[j, 0], node[j, 1], node[j, 2] = pack(p), pack(q), pack(w)
     full[j, 0], full[j, 1], full[j, 2] = p, q, w
-
-
-def tree_leaves(fac_ref, coup_ref, after_ref, leaf_ref, n1_ref, full_ref, cols_ref, rows):
+    if u is not None:
+        node[j, 3] = pack(u)
+
+
+def tree_leaves(fac_ref, coup_ref, after_ref, quad_ref, n1_ref, full_ref, cols_ref, rows):
     del after_ref
     c = coup_ref[...]
     cols_ref[0] = column(c[CELLS - 1 : CELLS])
@@ -78,13 +98,16 @@
     for j in range(CELLS // 2):
         p1, q1 = leaf(2 * j)
         p2, q2 = leaf(2 * j + 1)
-        kp1, kq1, kp2, kq2 = pack(p1), pack(q1), pack(p2), pack(q2)
-        leaf_ref[j, 0], leaf_ref[j, 1] = kp2, kq2
-        p = p1 + p2 + mm(kp2, kp1)
-        q = q1 + q2 + mm(kq1, kq2)
-        u = eye + q1 + p2 + mm(kq1, kp2)
-        w = (eye + eye) + p1 + q1 + p + mm(kq1, pack(p))
-        put(n1_ref, full_ref, j, p, q, w, u)
+        kq1 = pack(q1)
+        p = p1 + p2 + dot(pack(p2), rhs(p1))
+        q = q1 + q2 + dot(kq1, rhs(q2))
+        u = eye + q1 + p2 + dot(kq1, rhs(p2))
+        w = (eye + eye) + p1 + q1 + p + dot(kq1, rhs(p))
+        put(n1_ref, full_ref, j, p, q, w)
+        quad_ref[j, 0] = pair(p, p2)
+        quad_ref[j, 1] = pair(w, u)
+        quad_ref[j, 2] = pair(w, q)
+        quad_ref[j, 3] = pair(p, q2)
 
 
 def tree_upper(n1_ref, full_ref, coup_ref, cols_ref, after_ref, n2_ref, n3_ref, n4_ref, n5_ref, root_ref, fa, fb):
@@ -93,12 +116,12 @@
     for count, node_to, full_to in ((8, n2_ref, fa), (4, n3_ref, fb), (2, n4_ref, fa), (1, None, None)):
         for j in range(count):
             one, two = 2 * j, 2 * j + 1
-            kp1, kq1 = node[one, 0], node[one, 1]
-            u = full[two, 2] + mm(kq1, node[two, 2])
-            p = full[one, 0] + full[two, 0] + mm(node[two, 0], kp1)
-            q = full[one, 1] + full[two, 1] + mm(kq1, node[two, 1])
+            kq1, yp1 = node[one, 1], rhs(full[one, 0])
+            u = full[two, 2] + dot(kq1, rhs(full[two, 2]))
+            p = full[one, 0] + full[two, 0] + dot(node[two, 0], yp1)
+            q = full[one, 1] + full[two, 1] + dot(kq1, rhs(full[two, 1]))
             ku = pack(u)
-            w = full[one, 2] + u + mm(ku, kp1)
+            w = full[one, 2] + u + dot(ku, yp1)
             if node_to is None:
                 eye = eye2()
                 n5_ref[0] = ku
@@ -152,7 +175,7 @@
 
 
 def upsweep(neigh_ref, part_ref, a_ref, b_ref, c_ref, top_ref, flux_ref, dens_ref, tran_ref, lat_ref, coup_ref, cols_ref,
-            leaf_ref, n1_ref, n2_ref, n3_ref, n4_ref, n5_ref, root_ref, pay_ref, pair_ref, v_ref, w_ref):
+            quad_ref, n1_ref, n2_ref, n3_ref, n4_ref, n5_ref, root_ref, pay_ref, pair_ref, v_ref, w_ref):
     me = lax.axis_index("lat")
     u = dens_ref[...]
     total = jnp.zeros((CELLS, N), f32)
@@ -169,20 +192,26 @@
     r = r + jnp.where(row == CELLS - 1, tran_ref[...] * top_ref[0, 0:1], 0.0)
     c = coup_ref[...]
     g = r / jnp.where(row == 0, c, pltpu.roll(c, 1, 0))
-    x = [(g if i == 0 else pltpu.roll(g, CELLS - i, 0)).T for i in range(4)]
-    y = [rhs(t) for t in x]
+    x = []
+    for i in range(4):
+        rolled = g if i == 0 else pltpu.roll(g, CELLS - i, 0)
+        x.append(jnp.concatenate([rolled, rolled], axis=0).T)
+    lane2 = lanes((N, N)) % CELLS
     lane = lanes((N, CELLS))
     pair_v, pair_w = [], []
     for half in range(2):
-        y0, y1 = y[2 * half], y[2 * half + 1]
-        v = jnp.zeros((N, CELLS), f32)
-        w = jnp.zeros((N, CELLS), f32)
+        x0, x1 = x[2 * half], x[2 * half + 1]
+        y = pair_rhs(x0, x1)
+        v = jnp.zeros((N, N), f32)
+        w = jnp.zeros((N, N), f32)
         for j in range(8):
             at = 2 * j + half
-            here = lane == 4 * j
-            v = jnp.where(here, dot(n1_ref[at, 0], y0) + dot(leaf_ref[at, 0], y1), v)
-            w = jnp.where(here, dot(n1_ref[at, 2], y0) + dot(n1_ref[at, 3], y1), w)
-        pair_v.append(v + x[2 * half] + x[2 * half + 1])
+            here = lane2 == 4 * j
+            v = jnp.where(here, jnp.dot(quad_ref[at, 0], y, preferred_element_type=f32), v)
+            w = jnp.where(here, jnp.dot(quad_ref[at, 1], y, preferred_element_type=f32), w)
+        v = v[:, :CELLS] + v[:, CELLS:] + x0[:, :CELLS] + x1[:, :CELLS]
+        w = w[:, :CELLS] + w[:, CELLS:]
+        pair_v.append(v)
         pair_w.append(w)
         pair_ref[half, :, 0:CELLS] = pair_v[half]
         pair_ref[2 + half, :, 0:CELLS] = w
@@ -217,6 +246,7 @@
 
 def prepare(pair_ref, v_ref, w_ref, n1_ref, n2_ref, n3_ref, n4_ref, t_ref, add_v, add_a, add_x):
     lane = lanes((N, 128))
+    part = lane % CELLS
     at, vec = 0, 0
     for level, size, ref in ((1, 8, n2_ref), (2, 16, n3_ref), (3, 32, n4_ref)):
         acc_v = jnp.zeros((N, 128), f32)
@@ -226,12 +256,17 @@
             wide = kw.astype(f32)
             t_ref[at] = pack(wide + roll(wide, N) + mm(kw, ref[2 * j, 0]))
             at += 1
-            here = lane // size == j
+            here = part // size == j
             acc_v = jnp.where(here, v_ref[vec], acc_v)
             acc_a = jnp.where(here, w_ref[vec] + dot(kw, rhs(v_ref[vec])), acc_a)
             vec += 1
         add_v[level], add_a[level] = acc_v, acc_a
-    first = lane % 4 == 0
+
+    def repeat(x):
+        x = x + roll(x, CELLS)
+        return x + roll(x, 2 * CELLS)
+
+    first = jnp.logical_and(lane % 4 == 0, lane < CELLS)
     v0, v1, w0, w1 = [jnp.where(first, pair_ref[i], 0.0) for i in range(4)]
     y = rhs(v0)
     acc_a = jnp.zeros((N, 128), f32)
@@ -244,9 +279,22 @@
     acc_a = acc_a + w1
     spread_v = v0 + roll(v0, 1)
     spread_a = acc_a + roll(acc_a, 1)
-    add_v[0] = spread_v + roll(spread_v, 2)
-    add_a[0] = spread_a + roll(spread_a, 2)
-    add_x[...] = w0 + roll(w1, 2) + roll(v0, 1) + roll(v1, 3)
+    add_v[0] = repeat(spread_v + roll(spread_v, 2))
+    add_a[0] = repeat(spread_a + roll(spread_a, 2))
+    add_x[...] = repeat(w0 + roll(w1, 2) + roll(v0, 1) + roll(v1, 3))
+
+
+def prepare_last(own_ref, fun_ref, maps_ref, vecs_ref, own_rhs):
+    is_low = lax.axis_index("depth") < 2 * ZS
+    f, hh, k, g, e = unpack(fun_ref[...])
+    maps_ref[0], maps_ref[1] = pack(f), pack(jnp.where(is_low, hh, k))
+    vecs_ref[0], vecs_ref[1] = g, e
+    v = jnp.broadcast_to(own_ref[:, N : N + 1], (N, 128))
+    hi = v.astype(bf16)
+    lo = (v - hi.astype(f32)).astype(bf16)
+    zero = jnp.zeros((N, 128), bf16)
+    own_rhs[0] = jnp.concatenate([hi, zero, hi, zero], axis=0)
+    own_rhs[1] = jnp.concatenate([lo, zero, lo, zero], axis=0)
 
 
 def unpack(b):
@@ -291,7 +339,7 @@
 
 def track(is_low, fun, extra):
     f, hh, k, g, e = fun
-    t, th, yp1, yv1, yq2, yt, yth = extra
+    _, _, yp1, yv1, yq2, yt, yth = extra
     x1 = pack(jnp.where(is_low, hh, f))
     x2 = pack(jnp.where(is_low, hh, k))
     prod1 = dot(x1, jnp.where(is_low, yq2, yp1))
@@ -350,21 +398,21 @@
     put_map(fun_out, *track(in_lower, fun, extra))
 
 
-def downsweep(own_ref, other_ref, fun_ref, cols_ref, add_v, add_a, add_x, leaf_ref, n1_ref, n2_ref, n3_ref, n4_ref, t_ref,
-              out_ref):
+def downsweep(other_ref, maps_ref, vecs_ref, own_rhs, cols_ref, add_v, add_a, add_x, quad_ref, n1_ref, n2_ref, n3_ref,
+              n4_ref, t_ref, out_ref):
     is_low = lax.axis_index("depth") < 2 * ZS
-    f, hh, k, g, e = unpack(fun_ref[...])
-    own, other = own_ref[...], other_ref[...]
-    other_w = jnp.where(lanes((N, 128)) < N, other, roll(other, N))
-    v_own = jnp.broadcast_to(own[:, N : N + 1], (N, 128))
+    g, e = vecs_ref[0], vecs_ref[1]
+    other = other_ref[...]
+    hi = other.astype(bf16)
+    wide = jnp.concatenate([hi, (other - hi.astype(f32)).astype(bf16)], axis=1)
     v_other = jnp.broadcast_to(other[:, N : N + 1], (N, 128))
     w_other = jnp.broadcast_to(other[:, N + 1 : N + 2], (N, 128))
-    y_other = rhs(v_other)
-    t = w_other + dot(pack(other_w), rhs(v_own))
-    up = g + dot(pack(f), y_other)
-    aa = e + dot(pack(jnp.where(is_low, hh, k)), rhs(jnp.where(is_low, t, v_other)))
+    t = w_other + jnp.dot(wide, own_rhs[0], preferred_element_type=f32)
+    t = t + jnp.dot(wide, own_rhs[1], preferred_element_type=f32)
+    up = g + dot(maps_ref[0], rhs(v_other))
+    aa = e + dot(maps_ref[1], rhs(jnp.where(is_low, t, v_other)))
     ss = jnp.where(is_low, g, up) * cols_ref[1]
-    lane = lanes((N, 128))
+    lane = lanes((N, 128)) % CELLS
     for level, size, ref, base in ((3, 32, n4_ref, 6), (2, 16, n3_ref, 4), (1, 8, n2_ref, 0), (0, 4, n1_ref, 7)):
         ys, ya = rhs(ss), rhs(aa)
         ds = jnp.zeros((N, 128), f32)
@@ -378,12 +426,12 @@
         new_a = aa + add_a[level] + da
         ss = jnp.where(upper, new_s, ss)
         aa = jnp.where(upper, aa, new_a)
-    ys, ya = rhs(ss), rhs(aa)
+    y = pair_rhs(ss, aa)
     x = jnp.zeros((N, 128), f32)
     for j in range(CELLS // 2):
-        x = jnp.where(lane == 2 * j, dot(n1_ref[j, 2], ys) + dot(n1_ref[j, 1], ya), x)
-        x = jnp.where(lane == 2 * j + 1, dot(n1_ref[j, 0], ys) + dot(leaf_ref[j, 1], ya), x)
-    x = x + aa + add_x[...] + jnp.where(lane % 2 == 1, ss, 0.0)
+        x = jnp.where(lane == 2 * j, jnp.dot(quad_ref[j, 2], y, preferred_element_type=f32), x)
+        x = jnp.where(lane == 2 * j + 1, jnp.dot(quad_ref[j, 3], y, preferred_element_type=f32), x)
+    x = x + roll(x, CELLS) + (aa + add_x[...] + jnp.where(lane % 2 == 1, ss, 0.0))
     out_ref[...] = x.T[:CELLS]
 
 
@@ -391,7 +439,7 @@
     return jax.ShapeDtypeStruct(shape, dtype)
 
 
-def call(body, outs, *args, scratch=(), smem=0, hbm=0, flops=0, name=None):
+def call(body, outs, *args, scratch=(), smem=0, hbm=0, flops=0):
     args = [pltpu.with_memory_space_constraint(x, pltpu.HBM) if smem <= i < smem + hbm else x for i, x in enumerate(args)]
     spaces = [pltpu.SMEM] * smem + [pltpu.HBM] * hbm + [pltpu.VMEM] * (len(args) - smem - hbm)
     return pl.pallas_call(
@@ -401,7 +449,6 @@
         out_specs=jax.tree.map(lambda _: pl.BlockSpec(memory_space=pltpu.VMEM), outs),
         scratch_shapes=scratch,
         cost_estimate=pl.CostEstimate(flops=flops, bytes_accessed=1 << 16, transcendentals=0),
-        name=name,
         compiler_params=pltpu.CompilerParams(vmem_limit_bytes=VLIM),
     )(*args)
 
@@ -426,51 +473,55 @@
     def xor_depth(value, bits):
         return lax.ppermute(value, "depth", [(i, i ^ bits) for i in range(32)])
 
+    top = lax.ppermute(densities, "depth", [(i + 1, i) for i in range(31)])
     line_a = xor_lat(densities, 1)
     part, flux = call(
-        react, (sds(CELLS, N), sds(N, 128)), jac, u, src, tran, pattern, hbm=5, flops=1 << 30, name="react",
+        react, (sds(CELLS, N), sds(N, 128)), jac, u, src, tran, pattern, hbm=5, flops=1 << 30,
         scratch=[pltpu.VMEM((CELLS, N * N), f32)] + [pltpu.VMEM((CELLS, N), f32)] * 3
         + [pltpu.VMEM((8, 8), jnp.int32), pltpu.SemaphoreType.DMA((8,))],
     )
     line_b = xor_lat(jnp.concatenate([densities, line_a], axis=0), 2)
-    leaf, n1, full, cols = call(
+    quad, n1, full, cols = call(
         tree_leaves,
-        (sds(16, 2, N, 128, dtype=bf16), node(16), sds(16, 3, N, 128), sds(2, N, 128)),
-        fac, coup, part, scratch=[pltpu.VMEM((2, N, 128), f32)], flops=2 << 30, name="tree_leaves",
-    )
-    top = lax.ppermute(lax.optimization_barrier((densities, cols))[0], "depth", [(i + 1, i) for i in range(31)])
+        (sds(16, 4, N, 256, dtype=bf16), sds(16, 3, N, 128, dtype=bf16), sds(16, 3, N, 128), sds(2, N, 128)),
+        fac, coup, part, scratch=[pltpu.VMEM((2, N, 128), f32)], flops=2 << 30,
+    )
     line_c = xor_lat(jnp.concatenate([densities, line_a, line_b], axis=0), 6)
     n2, n3, n4, n5, root = call(
         tree_upper,
         (node(8), node(4), node(2), sds(1, N, 128, dtype=bf16), sds(128, 128)),
         n1, full, coup, cols, part, scratch=[pltpu.VMEM((8, 3, N, 128), f32), pltpu.VMEM((4, 3, N, 128), f32)],
-        flops=2 << 30, name="tree_upper",
+        flops=2 << 30,
     )
     pay, pair, vs, ws = call(
         upsweep, (sds(128, 128), sds(4, N, 128), sds(7, N, 128), sds(7, N, 128)),
-        neighbours, part, line_a, line_b, line_c, top, flux, u, tran, lat, coup, cols, leaf, n1, n2, n3, n4, n5, root,
-        smem=1, flops=1 << 25, name="upsweep",
+        neighbours, part, line_a, line_b, line_c, top, flux, u, tran, lat, coup, cols, quad, n1, n2, n3, n4, n5, root,
+        smem=1, flops=1 << 25,
     )
     others = [xor_depth(pay, bits) for bits in (1, 2, 3)]
     tees, add_v, add_a, add_x = call(
         prepare, (sds(15, N, 128, dtype=bf16), sds(4, N, 128), sds(4, N, 128), sds(N, 128)),
-        pair, vs, ws, n1, n2, n3, n4, flops=1 << 30, name="prepare",
+        pair, vs, ws, n1, n2, n3, n4, flops=1 << 30,
     )
     pay, fun = call(
         combine_four, (sds(128, 128), sds(128, 128)), pay, *others, scratch=[pltpu.VMEM((4, 128, 128), f32)],
-        flops=1 << 24, name="combine_four",
+        flops=1 << 24,
     )
     for level, bits in ((2, 7), (3, 8)):
         other = xor_depth(pay, bits)
         pay, fun = call(
             lambda *refs, level=level: combine_two(level, *refs),
             (sds(N if level == 3 else 128, 128), sds(128, 128)), pay, other, fun, flops=1 << 24,
-            name=f"combine{level}",
         )
     other = xor_depth(pay, 24)
+    maps, vecs, own_rhs = call(
+        prepare_last,
+        (sds(2, N, 128, dtype=bf16), sds(2, N, 128), sds(2, 256, 128, dtype=bf16)),
+        pay, fun, flops=1 << 30,
+    )
     out = call(
-        downsweep, sds(CELLS, N), pay, other, fun, cols, add_v, add_a, add_x, leaf, n1, n2, n3, n4, tees,
-        flops=1 << 25, name="downsweep",
+        downsweep, sds(CELLS, N), other, maps, vecs, own_rhs, cols, add_v, add_a, add_x, quad, n1, n2, n3, n4, tees,
+        flops=1 << 25,
     )
     return out.reshape(line_count, cell_count, species)
 

time: 49.3 us -> 49.8 us (1.010)
  the two profiles are of different devices: /device:TPU:32 before, /device:TPU:30 now
where the time goes in v4:
time: 49.8 us; the launch traced here: 49.6 us
  waiting for transfers between devices  21.3 us (43%)
  starting transfers between devices  15.9 us (32%)
  Pallas kernels  12.3 us (25%)
    ppermute x6, waiting for transfers between devices, xor_depth(): return lax.ppermute(value, 'depth', [(i, i ^ bits) for i in range(32)])  16.2 us
    pallas_call x10, Pallas kernels, call(): pl.pallas_call(body, out_shape=outs, in_specs=[pl.BlockSpec(memory_space=...  12.3 us
    ppermute x1, starting transfers between devices, on_device(): top = lax.ppermute(densities, 'depth', [(i + 1, i) for i in range(31)])  8.08 us
    ppermute x6, starting transfers between devices, xor_depth(): return lax.ppermute(value, 'depth', [(i, i ^ bits) for i in range(32)])  6.24 us
    ppermute x3, waiting for transfers between devices, xor_lat(): return lax.ppermute(value, 'lat', [(i, i ^ bits) for i in range(8)])  5.05 us
    ppermute x3, starting transfers between devices, xor_lat(): return lax.ppermute(value, 'lat', [(i, i ^ bits) for i in range(8)])  1.57 us
  transfers between devices with their start and end apart: 10, of which 8 were waited for; matrix products, arithmetic and copies ran while one was open for 0% of the time, Pallas kernels for 12%

profile of v4, /device:TPU:30, one launch (start us, length us, event | category | flops | bytes accessed | tf_op | source)
XLA Modules:
  0.0 49.6 jit_solution(14816543981189828911)
XLA Ops:
  0.0 0.1 collective-permute-start
  0.1 8.1 %collective-permute-start.3 = (f32[1,32,64]{2,1,0:T(8,128)}, f32[1,32,64]{2,1,0:T(8,128)S(1)}, u32[]{:S(2)}, u32[]{:S(2)}) collective-permute-start(f32[1,32,64]{2,1,0:T(8,128)} %param.9), channel_id=1, source_target_pairs={{8,0},{16,8},{24,16},{32,24},{40,32},{48,40},{56,48},{64,56},{72,6... | collective-permute-start | bytes 24584 | tf_op jit(solution)/shard_map/ppermute | solution.py:476
  8.2 2.1 %shard_map.91 = (f32[32,64]{1,0:T(8,128)S(1)}, f32[64,128]{1,0:T(8,128)S(1)}) custom-call(f32[32,4096]{1,0:T(8,128)} %bitcast.21, f32[32,64]{1,0:T(8,128)} %bitcast.12, f32[32,64]{1,0:T(8,128)} %bitcast.22, f32[32,64]{1,0:T(8,128)} %bitcast.14, s32[8,8]{1,0:T(8,128)} %pat_hbm.1), custom_call_target="tpu_custom_call" | custom-call | flops 1073741824 | bytes 65536 | tf_op jit(solution)/shard_map/pallas_call | solution.py:445
  10.3 0.0 collective-permute-done.a_ref
  10.3 0.0 copy-done
  10.3 0.9 %collective-permute-start.1 = (f32[2,32,64]{2,1,0:T(8,128)S(1)}, f32[2,32,64]{2,1,0:T(8,128)S(1)}, u32[]{:S(2)}, u32[]{:S(2)}) collective-permute-start(f32[2,32,64]{2,1,0:T(8,128)S(1)} %pad_maximum_fusion.1), channel_id=1, source_target_pairs={{0,2},{1,3},{2,0},{3,1},{4,6},{5,7},{6,4},{7,5},{8,10},{9,11},{10,... | collective-permute-start | bytes 49160 | tf_op jit(solution)/shard_map/ppermute | solution.py:471
  11.3 1.6 %shard_map.92 = (bf16[16,4,64,256]{3,2,1,0:T(8,128)(2,1)S(1)}, bf16[16,3,64,128]{3,2,1,0:T(8,128)(2,1)S(1)}, f32[16,3,64,128]{3,2,1,0:T(8,128)S(1)}, f32[2,64,128]{2,1,0:T(8,128)S(1)}) custom-call(f32[1024,128]{1,0:T(8,128)S(1)} %bitcast.20, f32[32,64]{1,0:T(8,128)S(1)} %bitcast.17, f32[32,64]{1,0:T(8,128)S(1)} %get-tuple-element.33.after_ref.part_ref), custom_call_target="tpu_custom_call" | custom-call | flops 2147483648 | bytes 65536 | tf_op jit(solution)/shard_map/pallas_call | solution.py:445
  12.9 1.4 %collective-permute-done.1.b_ref = f32[2,32,64]{2,1,0:T(8,128)S(1)} collective-permute-done((f32[2,32,64]{2,1,0:T(8,128)S(1)}, f32[2,32,64]{2,1,0:T(8,128)S(1)}, u32[]{:S(2)}, u32[]{:S(2)}) %collective-permute-start.1) | collective-permute-done | bytes 16416 | tf_op jit(solution)/shard_map/ppermute | solution.py:471
  14.3 0.6 %collective-permute-start.2 = (f32[4,32,64]{2,1,0:T(8,128)S(1)}, f32[4,32,64]{2,1,0:T(8,128)S(1)}, u32[]{:S(2)}, u32[]{:S(2)}) collective-permute-start(f32[4,32,64]{2,1,0:T(8,128)S(1)} %pad_maximum_fusion), channel_id=1, source_target_pairs={{0,6},{1,7},{2,4},{3,5},{4,2},{5,3},{6,0},{7,1},{8,14},{9,15},{10,... | collective-permute-start | bytes 98312 | tf_op jit(solution)/shard_map/ppermute | solution.py:471
  14.9 1.4 %shard_map.93 = (bf16[8,4,64,128]{3,2,1,0:T(8,128)(2,1)S(1)}, bf16[4,4,64,128]{3,2,1,0:T(8,128)(2,1)S(1)}, bf16[2,4,64,128]{3,2,1,0:T(8,128)(2,1)S(1)}, bf16[1,64,128]{2,1,0:T(8,128)(2,1)S(1)}, f32[128,128]{1,0:T(8,128)S(1)}) custom-call(bf16[16,3,64,128]{3,2,1,0:T(8,128)(2,1)S(1)} %get-tuple-element.37.n1_ref, ...), custom_call_target="tpu_custom_call" | custom-call | flops 2147483648 | bytes 65536 | tf_op jit(solution)/shard_map/pallas_call | solution.py:445
  16.3 0.0 collective-permute-done.3.top_ref
  16.3 3.6 %collective-permute-done.2.c_ref = f32[4,32,64]{2,1,0:T(8,128)S(1)} collective-permute-done((f32[4,32,64]{2,1,0:T(8,128)S(1)}, f32[4,32,64]{2,1,0:T(8,128)S(1)}, u32[]{:S(2)}, u32[]{:S(2)}) %collective-permute-start.2) | collective-permute-done | bytes 32800 | tf_op jit(solution)/shard_map/ppermute | solution.py:471
  19.9 0.0 copy-done.4
  19.9 2.2 %shard_map.94 = (f32[128,128]{1,0:T(8,128)S(1)}, f32[4,64,128]{2,1,0:T(8,128)S(1)}, f32[7,64,128]{2,1,0:T(8,128)S(1)}, f32[7,64,128]{2,1,0:T(8,128)S(1)}) custom-call(s32[1,4]{1,0:T(1,128)S(1)} %copy-done.4, f32[32,64]{1,0:T(8,128)S(1)} %get-tuple-element.33.after_ref.part_ref, f32[1,32,64]{2,1,0:T(8,128)S(1)} %collective-permute-done.a_ref, ...), custom_call_target="tpu_custom_call" | custom-call | flops 33554432 | bytes 65536 | tf_op jit(solution)/shard_map/pallas_call | solution.py:445
  22.1 0.1 collective-permute-start.4
  22.2 0.1 collective-permute-start.5
  22.3 4.3 %collective-permute-start.6 = (f32[128,128]{1,0:T(8,128)S(1)}, f32[128,128]{1,0:T(8,128)S(1)}, u32[]{:S(2)}, u32[]{:S(2)}) collective-permute-start(f32[128,128]{1,0:T(8,128)S(1)} %get-tuple-element.44.own_ref), channel_id=1, source_target_pairs={{0,24},{8,16},{16,8},{24,0},{32,56},{40,48},{48,40},{56,32},{64,88... | collective-permute-start | bytes 196616 | tf_op jit(solution)/shard_map/ppermute | solution.py:474
  26.6 0.3 collective-permute-done.4.x1_ref
  26.9 0.7 %collective-permute-done.5.x2_ref = f32[128,128]{1,0:T(8,128)S(1)} collective-permute-done((f32[128,128]{1,0:T(8,128)S(1)}, f32[128,128]{1,0:T(8,128)S(1)}, u32[]{:S(2)}, u32[]{:S(2)}) %collective-permute-start.5) | collective-permute-done | bytes 65568 | tf_op jit(solution)/shard_map/ppermute | solution.py:474
  27.5 2.0 %collective-permute-done.6.x3_ref = f32[128,128]{1,0:T(8,128)S(1)} collective-permute-done((f32[128,128]{1,0:T(8,128)S(1)}, f32[128,128]{1,0:T(8,128)S(1)}, u32[]{:S(2)}, u32[]{:S(2)}) %collective-permute-start.6) | collective-permute-done | bytes 65568 | tf_op jit(solution)/shard_map/ppermute | solution.py:474
  29.6 1.0 %shard_map.95 = (f32[128,128]{1,0:T(8,128)S(1)}, f32[128,128]{1,0:T(8,128)S(1)}) custom-call(f32[128,128]{1,0:T(8,128)S(1)} %get-tuple-element.44.own_ref, f32[128,128]{1,0:T(8,128)S(1)} %collective-permute-done.4.x1_ref, f32[128,128]{1,0:T(8,128)S(1)} %collective-permute-done.5.x2_ref, f32[128,128]{1,0:T(8,128)S(1)} %collective-permute-done.6.x3_ref), custom_call_target="tpu_custom_call" | custom-call | flops 16777216 | bytes 65536 | tf_op jit(solution)/shard_map/pallas_call | solution.py:445
  30.5 1.2 %collective-permute-start.7 = (f32[128,128]{1,0:T(8,128)S(1)}, f32[128,128]{1,0:T(8,128)S(1)}, u32[]{:S(2)}, u32[]{:S(2)}) collective-permute-start(f32[128,128]{1,0:T(8,128)S(1)} %get-tuple-element.45.refs_0_), channel_id=1, source_target_pairs={{0,56},{8,48},{16,40},{24,32},{32,24},{40,16},{48,8},{56,0},{64,12... | collective-permute-start | bytes 196616 | tf_op jit(solution)/shard_map/ppermute | solution.py:474
  31.7 5.1 %collective-permute-done.7.refs_1_ = f32[128,128]{1,0:T(8,128)S(1)} collective-permute-done((f32[128,128]{1,0:T(8,128)S(1)}, f32[128,128]{1,0:T(8,128)S(1)}, u32[]{:S(2)}, u32[]{:S(2)}) %collective-permute-start.7) | collective-permute-done | bytes 65568 | tf_op jit(solution)/shard_map/ppermute | solution.py:474
  36.8 0.5 shard_map.96
  37.3 0.5 %collective-permute-start.8 = (f32[128,128]{1,0:T(8,128)S(1)}, f32[128,128]{1,0:T(8,128)S(1)}, u32[]{:S(2)}, u32[]{:S(2)}) collective-permute-start(f32[128,128]{1,0:T(8,128)S(1)} %get-tuple-element.47.refs_0_), channel_id=1, source_target_pairs={{0,64},{8,72},{16,80},{24,88},{32,96},{40,104},{48,112},{56,120},{... | collective-permute-start | bytes 196616 | tf_op jit(solution)/shard_map/ppermute | solution.py:474
  37.8 0.7 %shard_map.99 = (bf16[15,64,128]{2,1,0:T(8,128)(2,1)S(1)}, f32[4,64,128]{2,1,0:T(8,128)S(1)}, f32[4,64,128]{2,1,0:T(8,128)S(1)}, f32[64,128]{1,0:T(8,128)S(1)}) custom-call(f32[4,64,128]{2,1,0:T(8,128)S(1)} %get-tuple-element.54.pair_ref, f32[7,64,128]{2,1,0:T(8,128)S(1)} %get-tuple-element.55.v_ref, f32[7,64,128]{2,1,0:T(8,128)S(1)} %get-tuple-element.56.w_ref, ...), custom_call_target="tpu_custom_call" | custom-call | flops 1073741824 | bytes 65536 | tf_op jit(solution)/shard_map/pallas_call | solution.py:445
  38.5 3.1 %collective-permute-done.8.refs_1_ = f32[128,128]{1,0:T(8,128)S(1)} collective-permute-done((f32[128,128]{1,0:T(8,128)S(1)}, f32[128,128]{1,0:T(8,128)S(1)}, u32[]{:S(2)}, u32[]{:S(2)}) %collective-permute-start.8) | collective-permute-done | bytes 65568 | tf_op jit(solution)/shard_map/ppermute | solution.py:474
  41.6 0.4 shard_map.97
  42.1 0.1 collective-permute-start.9
  42.2 0.1 shard_map.98
  42.3 5.0 %collective-permute-done.9.other_ref = f32[64,128]{1,0:T(8,128)S(1)} collective-permute-done((f32[64,128]{1,0:T(8,128)S(1)}, f32[64,128]{1,0:T(8,128)S(1)}, u32[]{:S(2)}, u32[]{:S(2)}) %collective-permute-start.9) | collective-permute-done | bytes 32800 | tf_op jit(solution)/shard_map/ppermute | solution.py:474
  47.3 2.4 %shard_map.100 = f32[32,64]{1,0:T(8,128)} custom-call(f32[64,128]{1,0:T(8,128)S(1)} %collective-permute-done.9.other_ref, bf16[2,64,128]{2,1,0:T(8,128)(2,1)S(1)} %get-tuple-element.51.maps_ref, f32[2,64,128]{2,1,0:T(8,128)S(1)} %get-tuple-element.52.vecs_ref, bf16[2,256,128]{2,1,0:T(8,128)(2,1)S(1)} %get-tuple-element.53.own_rhs, ...), custom_call_target="tpu_custom_call" | custom-call | flops 33554432 | bytes 65536 | tf_op jit(solution)/shard_map/pallas_call | solution.py:445
  (12 shorter events, 0.0 us)
Async XLA Ops:
  0.0 10.3 %copy-start = (f32[1,32,64]{2,1,0:T(8,128)S(1)}, f32[1,32,64]{2,1,0:T(8,128)}, u32[]{:S(2)}) copy-start(f32[1,32,64]{2,1,0:T(8,128)} %param.9) | copy-start | bytes 24580
  0.0 11.3 %copy-start.3 = (f32[1,32,64]{2,1,0:T(8,128)S(1)}, f32[1,32,64]{2,1,0:T(8,128)}, u32[]{:S(2)}) copy-start(f32[1,32,64]{2,1,0:T(8,128)} %param.17) | copy-start | bytes 24580
  0.0 11.3 %copy-start.5 = (f32[1,32,4096]{2,1,0:T(8,128)S(1)}, f32[1,32,4096]{2,1,0:T(8,128)}, u32[]{:S(2)}) copy-start(f32[1,32,4096]{2,1,0:T(8,128)} %param.16) | copy-start | bytes 1572868
  0.0 10.3 %collective-permute-start = (f32[1,32,64]{2,1,0:T(8,128)}, f32[1,32,64]{2,1,0:T(8,128)S(1)}, u32[]{:S(2)}, u32[]{:S(2)}) collective-permute-start(f32[1,32,64]{2,1,0:T(8,128)} %param.9), channel_id=1, source_target_pairs={{0,1},{1,0},{2,3},{3,2},{4,5},{5,4},{6,7},{7,6},{8,9},{9,8},{10,11... | collective-permute-start | bytes 24584 | tf_op jit(solution)/shard_map/ppermute | solution.py:471
  0.1 16.2 %collective-permute-start.3 = (f32[1,32,64]{2,1,0:T(8,128)}, f32[1,32,64]{2,1,0:T(8,128)S(1)}, u32[]{:S(2)}, u32[]{:S(2)}) collective-permute-start(f32[1,32,64]{2,1,0:T(8,128)} %param.9), channel_id=1, source_target_pairs={{8,0},{16,8},{24,16},{32,24},{40,32},{48,40},{56,48},{64,56},{72,6... | collective-permute-start | bytes 24584 | tf_op jit(solution)/shard_map/ppermute | solution.py:476
  10.3 4.0 %collective-permute-start.1 = (f32[2,32,64]{2,1,0:T(8,128)S(1)}, f32[2,32,64]{2,1,0:T(8,128)S(1)}, u32[]{:S(2)}, u32[]{:S(2)}) collective-permute-start(f32[2,32,64]{2,1,0:T(8,128)S(1)} %pad_maximum_fusion.1), channel_id=1, source_target_pairs={{0,2},{1,3},{2,0},{3,1},{4,6},{5,7},{6,4},{7,5},{8,10},{9,11},{10,... | collective-permute-start | bytes 49160 | tf_op jit(solution)/shard_map/ppermute | solution.py:471
  14.3 5.6 %collective-permute-start.2 = (f32[4,32,64]{2,1,0:T(8,128)S(1)}, f32[4,32,64]{2,1,0:T(8,128)S(1)}, u32[]{:S(2)}, u32[]{:S(2)}) collective-permute-start(f32[4,32,64]{2,1,0:T(8,128)S(1)} %pad_maximum_fusion), channel_id=1, source_target_pairs={{0,6},{1,7},{2,4},{3,5},{4,2},{5,3},{6,0},{7,1},{8,14},{9,15},{10,... | collective-permute-start | bytes 98312 | tf_op jit(solution)/shard_map/ppermute | solution.py:471
  14.9 5.0 %copy-start.1 = (f32[1,32,64]{2,1,0:T(8,128)S(1)}, f32[1,32,64]{2,1,0:T(8,128)}, u32[]{:S(2)}) copy-start(f32[1,32,64]{2,1,0:T(8,128)} %param.13) | copy-start | bytes 24580
  14.9 5.0 %copy-start.2 = (f32[1,32,64]{2,1,0:T(8,128)S(1)}, f32[1,32,64]{2,1,0:T(8,128)}, u32[]{:S(2)}) copy-start(f32[1,32,64]{2,1,0:T(8,128)} %param.14) | copy-start | bytes 24580
  14.9 5.0 %copy-start.4 = (s32[1,4]{1,0:T(1,128)S(1)}, s32[1,4]{1,0:T(1,128)}, u32[]{:S(2)}) copy-start(s32[1,4]{1,0:T(1,128)} %neigh_ref.1) | copy-start | bytes 52
  22.1 4.8 %collective-permute-start.4 = (f32[128,128]{1,0:T(8,128)S(1)}, f32[128,128]{1,0:T(8,128)S(1)}, u32[]{:S(2)}, u32[]{:S(2)}) collective-permute-start(f32[128,128]{1,0:T(8,128)S(1)} %get-tuple-element.44.own_ref), channel_id=1, source_target_pairs={{0,8},{8,0},{16,24},{24,16},{32,40},{40,32},{48,56},{56,48},{64,72... | collective-permute-start | bytes 196616 | tf_op jit(solution)/shard_map/ppermute | solution.py:474
  22.2 5.3 %collective-permute-start.5 = (f32[128,128]{1,0:T(8,128)S(1)}, f32[128,128]{1,0:T(8,128)S(1)}, u32[]{:S(2)}, u32[]{:S(2)}) collective-permute-start(f32[128,128]{1,0:T(8,128)S(1)} %get-tuple-element.44.own_ref), channel_id=1, source_target_pairs={{0,16},{8,24},{16,0},{24,8},{32,48},{40,56},{48,32},{56,40},{64,80... | collective-permute-start | bytes 196616 | tf_op jit(solution)/shard_map/ppermute | solution.py:474
  22.3 7.3 %collective-permute-start.6 = (f32[128,128]{1,0:T(8,128)S(1)}, f32[128,128]{1,0:T(8,128)S(1)}, u32[]{:S(2)}, u32[]{:S(2)}) collective-permute-start(f32[128,128]{1,0:T(8,128)S(1)} %get-tuple-element.44.own_ref), channel_id=1, source_target_pairs={{0,24},{8,16},{16,8},{24,0},{32,56},{40,48},{48,40},{56,32},{64,88... | collective-permute-start | bytes 196616 | tf_op jit(solution)/shard_map/ppermute | solution.py:474
  30.5 6.3 %collective-permute-start.7 = (f32[128,128]{1,0:T(8,128)S(1)}, f32[128,128]{1,0:T(8,128)S(1)}, u32[]{:S(2)}, u32[]{:S(2)}) collective-permute-start(f32[128,128]{1,0:T(8,128)S(1)} %get-tuple-element.45.refs_0_), channel_id=1, source_target_pairs={{0,56},{8,48},{16,40},{24,32},{32,24},{40,16},{48,8},{56,0},{64,12... | collective-permute-start | bytes 196616 | tf_op jit(solution)/shard_map/ppermute | solution.py:474
  37.3 4.4 %collective-permute-start.8 = (f32[128,128]{1,0:T(8,128)S(1)}, f32[128,128]{1,0:T(8,128)S(1)}, u32[]{:S(2)}, u32[]{:S(2)}) collective-permute-start(f32[128,128]{1,0:T(8,128)S(1)} %get-tuple-element.47.refs_0_), channel_id=1, source_target_pairs={{0,64},{8,72},{16,80},{24,88},{32,96},{40,104},{48,112},{56,120},{... | collective-permute-start | bytes 196616 | tf_op jit(solution)/shard_map/ppermute | solution.py:474
  42.1 5.2 %collective-permute-start.9 = (f32[64,128]{1,0:T(8,128)S(1)}, f32[64,128]{1,0:T(8,128)S(1)}, u32[]{:S(2)}, u32[]{:S(2)}) collective-permute-start(f32[64,128]{1,0:T(8,128)S(1)} %get-tuple-element.49.own_ref), channel_id=1, source_target_pairs={{0,192},{8,200},{16,208},{24,216},{32,224},{40,232},{48,240},{56,2... | collective-permute-start | bytes 98312 | tf_op jit(solution)/shard_map/ppermute | solution.py:474

commit v5 on v4

--- a/solution.py
+++ b/solution.py
@@ -4,7 +4,6 @@
 from jax.experimental import pallas as pl
 from jax.experimental.pallas import tpu as pltpu
 from jax.sharding import PartitionSpec as P
-
 
 f32 = jnp.float32
 bf16 = jnp.bfloat16
@@ -174,7 +173,7 @@
     out_ref[...] = src_ref[...] - acc + lower + tran * upper
 
 
-def upsweep(neigh_ref, part_ref, a_ref, b_ref, c_ref, top_ref, flux_ref, dens_ref, tran_ref, lat_ref, coup_ref, cols_ref,
+def upsweep(neigh_ref, part_ref, a_ref, b_ref, c_ref, even_ref, odd_ref, flux_ref, dens_ref, tran_ref, lat_ref, coup_ref, cols_ref,
             quad_ref, n1_ref, n2_ref, n3_ref, n4_ref, n5_ref, root_ref, pay_ref, pair_ref, v_ref, w_ref):
     me = lax.axis_index("lat")
     u = dens_ref[...]
@@ -189,7 +188,10 @@
         total = total + count.astype(f32) * value
     row = lax.broadcasted_iota(jnp.int32, (CELLS, N), 0)
     r = part_ref[...] - lat_ref[...] * (4.0 * u - total)
-    r = r + jnp.where(row == CELLS - 1, tran_ref[...] * top_ref[0, 0:1], 0.0)
+    depth = lax.axis_index("depth")
+    above = jnp.where(depth % 2 == 0, even_ref[0, 0:1], odd_ref[0, 0:1])
+    above = jnp.where(depth == lax.axis_size("depth") - 1, 0.0, above)
+    r = r + jnp.where(row == CELLS - 1, tran_ref[...] * above, 0.0)
     c = coup_ref[...]
     g = r / jnp.where(row == 0, c, pltpu.roll(c, 1, 0))
     x = []
@@ -339,7 +341,7 @@
 
 def track(is_low, fun, extra):
     f, hh, k, g, e = fun
-    _, _, yp1, yv1, yq2, yt, yth = extra
+    t, th, yp1, yv1, yq2, yt, yth = extra
     x1 = pack(jnp.where(is_low, hh, f))
     x2 = pack(jnp.where(is_low, hh, k))
     prod1 = dot(x1, jnp.where(is_low, yq2, yp1))
@@ -366,18 +368,13 @@
         ref[N:] = tail
 
 
-def combine_two(level, own_ref, other_ref, fun_ref, out_ref, fun_out):
-    is_low = ((lax.axis_index("depth") // (1, 2, 4, 8)[level]) % 2) == 0
-    own, other = own_ref[...], other_ref[...]
-    one = unpack(jnp.where(is_low, own, other))
-    two = unpack(jnp.where(is_low, other, own))
-    total, extra = join(one, two, last=level == 3)
-    put_map(out_ref, *total, last=level == 3)
-    put_map(fun_out, *track(is_low, unpack(fun_ref[...]), extra))
-
-
-def combine_four(own_ref, x1_ref, x2_ref, x3_ref, out_ref, fun_out, slots):
-    at = lax.axis_index("depth") % 4
+def combine_four(last, *refs):
+    if last:
+        own_ref, x1_ref, x2_ref, x3_ref, fun_ref, out_ref, fun_out, slots = refs
+    else:
+        own_ref, x1_ref, x2_ref, x3_ref, out_ref, fun_out, slots = refs
+    depth = lax.axis_index("depth")
+    at = ((depth // ZS) % 2) * 2 + (depth % ZS) // 4 if last else depth % 4
     slots[at] = own_ref[...]
     slots[at ^ 1] = x1_ref[...]
     slots[at ^ 2] = x2_ref[...]
@@ -386,15 +383,15 @@
     lower, extra_lower = join(maps[0], maps[1])
     upper, extra_upper = join(maps[2], maps[3])
     in_lower = at < 2
-    mine = lambda a, b: jnp.where(in_lower, a, b)
-    fun = track_first(
-        at % 2 == 0,
-        [mine(a, b) for a, b in zip(maps[0], maps[2])],
-        [mine(a, b) for a, b in zip(maps[1], maps[3])],
-        [mine(a, b) for a, b in zip(extra_lower[:2], extra_upper[:2])],
-    )
-    total, extra = join(lower, upper)
-    put_map(out_ref, *total)
+    mine = lambda x, y: [jnp.where(in_lower, a, b) for a, b in zip(x, y)]
+    if last:
+        fun = track(at % 2 == 0, unpack(fun_ref[...]), mine(extra_lower, extra_upper))
+    else:
+        fun = track_first(
+            at % 2 == 0, mine(maps[0], maps[2]), mine(maps[1], maps[3]), mine(extra_lower[:2], extra_upper[:2])
+        )
+    total, extra = join(lower, upper, last)
+    put_map(out_ref, *total, last=last)
     put_map(fun_out, *track(in_lower, fun, extra))
 
 
@@ -439,7 +436,7 @@
     return jax.ShapeDtypeStruct(shape, dtype)
 
 
-def call(body, outs, *args, scratch=(), smem=0, hbm=0, flops=0):
+def call(body, outs, *args, scratch=(), smem=0, hbm=0, flops=0, name=None):
     args = [pltpu.with_memory_space_constraint(x, pltpu.HBM) if smem <= i < smem + hbm else x for i, x in enumerate(args)]
     spaces = [pltpu.SMEM] * smem + [pltpu.HBM] * hbm + [pltpu.VMEM] * (len(args) - smem - hbm)
     return pl.pallas_call(
@@ -449,6 +446,7 @@
         out_specs=jax.tree.map(lambda _: pl.BlockSpec(memory_space=pltpu.VMEM), outs),
         scratch_shapes=scratch,
         cost_estimate=pl.CostEstimate(flops=flops, bytes_accessed=1 << 16, transcendentals=0),
+        name=name,
         compiler_params=pltpu.CompilerParams(vmem_limit_bytes=VLIM),
     )(*args)
 
@@ -473,10 +471,9 @@
     def xor_depth(value, bits):
         return lax.ppermute(value, "depth", [(i, i ^ bits) for i in range(32)])
 
-    top = lax.ppermute(densities, "depth", [(i + 1, i) for i in range(31)])
     line_a = xor_lat(densities, 1)
     part, flux = call(
-        react, (sds(CELLS, N), sds(N, 128)), jac, u, src, tran, pattern, hbm=5, flops=1 << 30,
+        react, (sds(CELLS, N), sds(N, 128)), jac, u, src, tran, pattern, hbm=5, flops=1 << 30, name="react",
         scratch=[pltpu.VMEM((CELLS, N * N), f32)] + [pltpu.VMEM((CELLS, N), f32)] * 3
         + [pltpu.VMEM((8, 8), jnp.int32), pltpu.SemaphoreType.DMA((8,))],
     )
@@ -484,44 +481,49 @@
     quad, n1, full, cols = call(
         tree_leaves,
         (sds(16, 4, N, 256, dtype=bf16), sds(16, 3, N, 128, dtype=bf16), sds(16, 3, N, 128), sds(2, N, 128)),
-        fac, coup, part, scratch=[pltpu.VMEM((2, N, 128), f32)], flops=2 << 30,
+        fac, coup, part, scratch=[pltpu.VMEM((2, N, 128), f32)], flops=2 << 30, name="tree_leaves",
+    )
+    top_even = xor_depth(lax.optimization_barrier((densities, cols))[0], 1)
+    top_odd = lax.ppermute(
+        lax.optimization_barrier((densities, line_b))[0], "depth",
+        [(i, (i + 1) % 32 if i % 2 else (i - 1) % 32) for i in range(32)],
     )
     line_c = xor_lat(jnp.concatenate([densities, line_a, line_b], axis=0), 6)
     n2, n3, n4, n5, root = call(
         tree_upper,
         (node(8), node(4), node(2), sds(1, N, 128, dtype=bf16), sds(128, 128)),
         n1, full, coup, cols, part, scratch=[pltpu.VMEM((8, 3, N, 128), f32), pltpu.VMEM((4, 3, N, 128), f32)],
-        flops=2 << 30,
+        flops=2 << 30, name="tree_upper",
     )
     pay, pair, vs, ws = call(
         upsweep, (sds(128, 128), sds(4, N, 128), sds(7, N, 128), sds(7, N, 128)),
-        neighbours, part, line_a, line_b, line_c, top, flux, u, tran, lat, coup, cols, quad, n1, n2, n3, n4, n5, root,
-        smem=1, flops=1 << 25,
+        neighbours, part, line_a, line_b, line_c, top_even, top_odd, flux, u, tran, lat, coup, cols, quad, n1, n2, n3, n4, n5, root,
+        smem=1, flops=1 << 25, name="upsweep",
     )
     others = [xor_depth(pay, bits) for bits in (1, 2, 3)]
     tees, add_v, add_a, add_x = call(
         prepare, (sds(15, N, 128, dtype=bf16), sds(4, N, 128), sds(4, N, 128), sds(N, 128)),
-        pair, vs, ws, n1, n2, n3, n4, flops=1 << 30,
-    )
+        pair, vs, ws, n1, n2, n3, n4, flops=1 << 30, name="prepare",
+    )
+    slots = [pltpu.VMEM((4, 128, 128), f32)]
     pay, fun = call(
-        combine_four, (sds(128, 128), sds(128, 128)), pay, *others, scratch=[pltpu.VMEM((4, 128, 128), f32)],
-        flops=1 << 24,
-    )
-    for level, bits in ((2, 7), (3, 8)):
-        other = xor_depth(pay, bits)
-        pay, fun = call(
-            lambda *refs, level=level: combine_two(level, *refs),
-            (sds(N if level == 3 else 128, 128), sds(128, 128)), pay, other, fun, flops=1 << 24,
-        )
+        lambda *refs: combine_four(False, *refs), (sds(128, 128), sds(128, 128)), pay, *others, scratch=slots,
+        flops=1 << 24, name="combine_low",
+    )
+    others = [xor_depth(pay, bits) for bits in (7, 8, 15)]
+    pay, fun = call(
+        lambda *refs: combine_four(True, *refs), (sds(N, 128), sds(128, 128)), pay, *others, fun, scratch=slots,
+        flops=1 << 24, name="combine_high",
+    )
     other = xor_depth(pay, 24)
     maps, vecs, own_rhs = call(
         prepare_last,
         (sds(2, N, 128, dtype=bf16), sds(2, N, 128), sds(2, 256, 128, dtype=bf16)),
-        pay, fun, flops=1 << 30,
+        pay, fun, flops=1 << 30, name="prepare_last",
     )
     out = call(
         downsweep, sds(CELLS, N), other, maps, vecs, own_rhs, cols, add_v, add_a, add_x, quad, n1, n2, n3, n4, tees,
-        flops=1 << 25,
+        flops=1 << 25, name="downsweep",
     )
     return out.reshape(line_count, cell_count, species)
 

time: 49.8 us -> 47.5 us (0.954)
  the two profiles are of different devices: /device:TPU:30 before, /device:TPU:32 now
where the time goes in v5:
time: 47.5 us; the launch traced here: 47.4 us
  starting transfers between devices  23.8 us (50%)
  Pallas kernels  12.4 us (26%)
  waiting for transfers between devices  11.1 us (23%)
    ppermute x8, starting transfers between devices, xor_depth(): return lax.ppermute(value, 'depth', [(i, i ^ bits) for i in range(32)])  16.8 us
    pallas_call x9, Pallas kernels, call(): pl.pallas_call(body, out_shape=outs, in_specs=[pl.BlockSpec(memory_space=...  12.4 us
    ppermute x8, waiting for transfers between devices, xor_depth(): return lax.ppermute(value, 'depth', [(i, i ^ bits) for i in range(32)])  10.3 us
    ppermute x3, starting transfers between devices, xor_lat(): return lax.ppermute(value, 'lat', [(i, i ^ bits) for i in range(8)])  4.52 us
    ppermute x1, starting transfers between devices, on_device(): lax.ppermute(lax.optimization_barrier((densities, line_b))[0], 'depth', [...  2.48 us
  transfers between devices with their start and end apart: 12, of which 8 were waited for; matrix products, arithmetic and copies ran while one was open for 0% of the time, Pallas kernels for 13%

profile of v5, /device:TPU:32, one launch (start us, length us, event | category | flops | bytes accessed | tf_op | source)
XLA Modules:
  0.0 47.4 jit_solution(6111011272975466239)
XLA Ops:
  0.0 0.1 collective-permute-start
  0.1 2.2 %react.1 = (f32[32,64]{1,0:T(8,128)S(1)}, f32[64,128]{1,0:T(8,128)S(1)}) custom-call(f32[32,4096]{1,0:T(8,128)} %bitcast.21, f32[32,64]{1,0:T(8,128)} %bitcast.12, f32[32,64]{1,0:T(8,128)} %bitcast.22, f32[32,64]{1,0:T(8,128)} %bitcast.14, s32[8,8]{1,0:T(8,128)} %pat_hbm.1), custom_call_target="tpu_custom_call" | custom-call | flops 1073741824 | bytes 65536 | tf_op jit(solution)/shard_map/react/pallas_call | solution.py:442
  2.3 0.0 collective-permute-done.a_ref
  2.3 1.6 %collective-permute-start.1 = (f32[2,32,64]{2,1,0:T(8,128)S(1)}, f32[2,32,64]{2,1,0:T(8,128)S(1)}, u32[]{:S(2)}, u32[]{:S(2)}) collective-permute-start(f32[2,32,64]{2,1,0:T(8,128)S(1)} %pad_maximum_fusion.1), channel_id=1, source_target_pairs={{0,2},{1,3},{2,0},{3,1},{4,6},{5,7},{6,4},{7,5},{8,10},{9,11},{10,... | collective-permute-start | bytes 49160 | tf_op jit(solution)/shard_map/ppermute | solution.py:469
  3.9 1.6 %tree_leaves.1 = (bf16[16,4,64,256]{3,2,1,0:T(8,128)(2,1)S(1)}, bf16[16,3,64,128]{3,2,1,0:T(8,128)(2,1)S(1)}, f32[16,3,64,128]{3,2,1,0:T(8,128)S(1)}, f32[2,64,128]{2,1,0:T(8,128)S(1)}) custom-call(f32[1024,128]{1,0:T(8,128)S(1)} %bitcast.20, f32[32,64]{1,0:T(8,128)S(1)} %bitcast.17, f32[32,64]{1,0:T(8,128)S(1)} %get-tuple-element.33.after_ref.part_ref), custom_call_target="tpu_custom_call" | custom-call | flops 2147483648 | bytes 65536 | tf_op jit(solution)/shard_map/tree_leaves/pallas_call | solution.py:442
  5.5 0.3 collective-permute-start.3
  5.9 0.5 collective-permute-done.1.b_ref
  6.3 2.8 %collective-permute-start.2 = (f32[4,32,64]{2,1,0:T(8,128)S(1)}, f32[4,32,64]{2,1,0:T(8,128)S(1)}, u32[]{:S(2)}, u32[]{:S(2)}) collective-permute-start(f32[4,32,64]{2,1,0:T(8,128)S(1)} %pad_maximum_fusion), channel_id=1, source_target_pairs={{0,6},{1,7},{2,4},{3,5},{4,2},{5,3},{6,0},{7,1},{8,14},{9,15},{10,... | collective-permute-start | bytes 98312 | tf_op jit(solution)/shard_map/ppermute | solution.py:469
  9.2 2.5 %collective-permute-start.4 = (f32[1,32,64]{2,1,0:T(8,128)S(1)}, f32[1,32,64]{2,1,0:T(8,128)S(1)}, u32[]{:S(2)}, u32[]{:S(2)}) collective-permute-start(f32[1,32,64]{2,1,0:T(8,128)S(1)} %copy-done), channel_id=1, source_target_pairs={{0,248},{8,16},{16,8},{24,32},{32,24},{40,48},{48,40},{56,64},{64,... | collective-permute-start | bytes 24584 | tf_op jit(solution)/shard_map/ppermute | solution.py:487
  11.7 1.4 %tree_upper.1 = (bf16[8,4,64,128]{3,2,1,0:T(8,128)(2,1)S(1)}, bf16[4,4,64,128]{3,2,1,0:T(8,128)(2,1)S(1)}, bf16[2,4,64,128]{3,2,1,0:T(8,128)(2,1)S(1)}, bf16[1,64,128]{2,1,0:T(8,128)(2,1)S(1)}, f32[128,128]{1,0:T(8,128)S(1)}) custom-call(bf16[16,3,64,128]{3,2,1,0:T(8,128)(2,1)S(1)} %get-tuple-element.39.n1_ref, ...), custom_call_target="tpu_custom_call" | custom-call | flops 2147483648 | bytes 65536 | tf_op jit(solution)/shard_map/tree_upper/pallas_call | solution.py:442
  13.1 0.0 collective-permute-done.3.even_ref
  13.1 0.3 collective-permute-done.4.odd_ref
  13.4 0.0 collective-permute-done.2.c_ref
  13.4 2.2 %upsweep.1 = (f32[128,128]{1,0:T(8,128)S(1)}, f32[4,64,128]{2,1,0:T(8,128)S(1)}, f32[7,64,128]{2,1,0:T(8,128)S(1)}, f32[7,64,128]{2,1,0:T(8,128)S(1)}) custom-call(s32[1,4]{1,0:T(1,128)S(1)} %copy-done.4, f32[32,64]{1,0:T(8,128)S(1)} %get-tuple-element.33.after_ref.part_ref, f32[1,32,64]{2,1,0:T(8,128)S(1)} %collective-permute-done.a_ref, ...), custom_call_target="tpu_custom_call" | custom-call | flops 33554432 | bytes 65536 | tf_op jit(solution)/shard_map/upsweep/pallas_call | solution.py:442
  15.6 6.0 %collective-permute-start.5 = (f32[128,128]{1,0:T(8,128)S(1)}, f32[128,128]{1,0:T(8,128)S(1)}, u32[]{:S(2)}, u32[]{:S(2)}) collective-permute-start(f32[128,128]{1,0:T(8,128)S(1)} %get-tuple-element.46.refs_0_), channel_id=1, source_target_pairs={{0,8},{8,0},{16,24},{24,16},{32,40},{40,32},{48,56},{56,48},{64,72... | collective-permute-start | bytes 196616 | tf_op jit(solution)/shard_map/ppermute | solution.py:472
  21.6 1.6 %collective-permute-start.7 = (f32[128,128]{1,0:T(8,128)S(1)}, f32[128,128]{1,0:T(8,128)S(1)}, u32[]{:S(2)}, u32[]{:S(2)}) collective-permute-start(f32[128,128]{1,0:T(8,128)S(1)} %get-tuple-element.46.refs_0_), channel_id=1, source_target_pairs={{0,24},{8,16},{16,8},{24,0},{32,56},{40,48},{48,40},{56,32},{64,88... | collective-permute-start | bytes 196616 | tf_op jit(solution)/shard_map/ppermute | solution.py:472
  23.2 0.7 %collective-permute-done.5.refs_1_ = f32[128,128]{1,0:T(8,128)S(1)} collective-permute-done((f32[128,128]{1,0:T(8,128)S(1)}, f32[128,128]{1,0:T(8,128)S(1)}, u32[]{:S(2)}, u32[]{:S(2)}) %collective-permute-start.5) | collective-permute-done | bytes 65568 | tf_op jit(solution)/shard_map/ppermute | solution.py:472
  23.9 3.0 %collective-permute-done.6.refs_2_ = f32[128,128]{1,0:T(8,128)S(1)} collective-permute-done((f32[128,128]{1,0:T(8,128)S(1)}, f32[128,128]{1,0:T(8,128)S(1)}, u32[]{:S(2)}, u32[]{:S(2)}) %collective-permute-start.6) | collective-permute-done | bytes 65568 | tf_op jit(solution)/shard_map/ppermute | solution.py:472
  26.9 1.1 %collective-permute-done.7.refs_3_ = f32[128,128]{1,0:T(8,128)S(1)} collective-permute-done((f32[128,128]{1,0:T(8,128)S(1)}, f32[128,128]{1,0:T(8,128)S(1)}, u32[]{:S(2)}, u32[]{:S(2)}) %collective-permute-start.7) | collective-permute-done | bytes 65568 | tf_op jit(solution)/shard_map/ppermute | solution.py:472
  28.0 1.0 %combine_low.1 = (f32[128,128]{1,0:T(8,128)S(1)}, f32[128,128]{1,0:T(8,128)S(1)}) custom-call(f32[128,128]{1,0:T(8,128)S(1)} %get-tuple-element.46.refs_0_, f32[128,128]{1,0:T(8,128)S(1)} %collective-permute-done.5.refs_1_, f32[128,128]{1,0:T(8,128)S(1)} %collective-permute-done.6.refs_2_, f32[128,128]{1,0:T(8,128)S(1)} %collective-permute-done.7.refs_3_), custom_call_target="tpu_custom_call" | custom-call | flops 16777216 | bytes 65536 | tf_op jit(solution)/shard_map/combine_low/pallas_call | solution.py:442
  29.0 2.6 %collective-permute-start.10 = (f32[128,128]{1,0:T(8,128)S(1)}, f32[128,128]{1,0:T(8,128)S(1)}, u32[]{:S(2)}, u32[]{:S(2)}) collective-permute-start(f32[128,128]{1,0:T(8,128)S(1)} %get-tuple-element.47.refs_0_), channel_id=1, source_target_pairs={{0,120},{8,112},{16,104},{24,96},{32,88},{40,80},{48,72},{56,64},{... | collective-permute-start | bytes 196616 | tf_op jit(solution)/shard_map/ppermute | solution.py:472
  31.6 0.5 collective-permute-start.8
  32.1 3.5 %collective-permute-start.9 = (f32[128,128]{1,0:T(8,128)S(1)}, f32[128,128]{1,0:T(8,128)S(1)}, u32[]{:S(2)}, u32[]{:S(2)}) collective-permute-start(f32[128,128]{1,0:T(8,128)S(1)} %get-tuple-element.47.refs_0_), channel_id=1, source_target_pairs={{0,64},{8,72},{16,80},{24,88},{32,96},{40,104},{48,112},{56,120},{... | collective-permute-start | bytes 196616 | tf_op jit(solution)/shard_map/ppermute | solution.py:472
  35.6 0.7 %prepare.1 = (bf16[15,64,128]{2,1,0:T(8,128)(2,1)S(1)}, f32[4,64,128]{2,1,0:T(8,128)S(1)}, f32[4,64,128]{2,1,0:T(8,128)S(1)}, f32[64,128]{1,0:T(8,128)S(1)}) custom-call(f32[4,64,128]{2,1,0:T(8,128)S(1)} %get-tuple-element.54.pair_ref, f32[7,64,128]{2,1,0:T(8,128)S(1)} %get-tuple-element.55.v_ref, f32[7,64,128]{2,1,0:T(8,128)S(1)} %get-tuple-element.56.w_ref, ...), custom_call_target="tpu_custom_call" | custom-call | flops 1073741824 | bytes 65536 | tf_op jit(solution)/shard_map/prepare/pallas_call | solution.py:442
  36.3 1.0 %collective-permute-done.10.refs_3_ = f32[128,128]{1,0:T(8,128)S(1)} collective-permute-done((f32[128,128]{1,0:T(8,128)S(1)}, f32[128,128]{1,0:T(8,128)S(1)}, u32[]{:S(2)}, u32[]{:S(2)}) %collective-permute-start.10) | collective-permute-done | bytes 65568 | tf_op jit(solution)/shard_map/ppermute | solution.py:472
  37.3 1.6 %collective-permute-done.8.refs_1_ = f32[128,128]{1,0:T(8,128)S(1)} collective-permute-done((f32[128,128]{1,0:T(8,128)S(1)}, f32[128,128]{1,0:T(8,128)S(1)}, u32[]{:S(2)}, u32[]{:S(2)}) %collective-permute-start.8) | collective-permute-done | bytes 65568 | tf_op jit(solution)/shard_map/ppermute | solution.py:472
  38.9 0.0 collective-permute-done.9.refs_2_
  38.9 0.9 %combine_high.1 = (f32[64,128]{1,0:T(8,128)S(1)}, f32[128,128]{1,0:T(8,128)S(1)}) custom-call(f32[128,128]{1,0:T(8,128)S(1)} %get-tuple-element.47.refs_0_, f32[128,128]{1,0:T(8,128)S(1)} %collective-permute-done.8.refs_1_, f32[128,128]{1,0:T(8,128)S(1)} %collective-permute-done.9.refs_2_, f32[128,128]{1,0:T(8,128)S(1)} %collective-permute-done.10.refs_3_, ...), custom_call_target="tpu_custom_call" | custom-call | flops 16777216 | bytes 65536 | tf_op jit(solution)/shard_map/combine_high/pallas_call | solution.py:442
  39.8 2.3 %collective-permute-start.11 = (f32[64,128]{1,0:T(8,128)S(1)}, f32[64,128]{1,0:T(8,128)S(1)}, u32[]{:S(2)}, u32[]{:S(2)}) collective-permute-start(f32[64,128]{1,0:T(8,128)S(1)} %get-tuple-element.49.own_ref), channel_id=1, source_target_pairs={{0,192},{8,200},{16,208},{24,216},{32,224},{40,232},{48,240},{56,2... | collective-permute-start | bytes 98312 | tf_op jit(solution)/shard_map/ppermute | solution.py:472
  42.1 0.1 prepare_last.1
  42.2 2.8 %collective-permute-done.11.other_ref = f32[64,128]{1,0:T(8,128)S(1)} collective-permute-done((f32[64,128]{1,0:T(8,128)S(1)}, f32[64,128]{1,0:T(8,128)S(1)}, u32[]{:S(2)}, u32[]{:S(2)}) %collective-permute-start.11) | collective-permute-done | bytes 32800 | tf_op jit(solution)/shard_map/ppermute | solution.py:472
  45.0 2.4 %downsweep.1 = f32[32,64]{1,0:T(8,128)} custom-call(f32[64,128]{1,0:T(8,128)S(1)} %collective-permute-done.11.other_ref, bf16[2,64,128]{2,1,0:T(8,128)(2,1)S(1)} %get-tuple-element.51.maps_ref, f32[2,64,128]{2,1,0:T(8,128)S(1)} %get-tuple-element.52.vecs_ref, bf16[2,256,128]{2,1,0:T(8,128)(2,1)S(1)} %get-tuple-element.53.own_rhs, ...), custom_call_target="tpu_custom_call" | custom-call | flops 33554432 | bytes 65536 | tf_op jit(solution)/shard_map/downsweep/pallas_call | solution.py:442
  (15 shorter events, 0.0 us)
Async XLA Ops:
  0.0 2.3 %copy-start = (f32[1,32,64]{2,1,0:T(8,128)S(1)}, f32[1,32,64]{2,1,0:T(8,128)}, u32[]{:S(2)}) copy-start(f32[1,32,64]{2,1,0:T(8,128)} %param.9) | copy-start | bytes 24580
  0.0 3.9 %copy-start.3 = (f32[1,32,64]{2,1,0:T(8,128)S(1)}, f32[1,32,64]{2,1,0:T(8,128)}, u32[]{:S(2)}) copy-start(f32[1,32,64]{2,1,0:T(8,128)} %param.17) | copy-start | bytes 24580
  0.0 3.9 %copy-start.5 = (f32[1,32,4096]{2,1,0:T(8,128)S(1)}, f32[1,32,4096]{2,1,0:T(8,128)}, u32[]{:S(2)}) copy-start(f32[1,32,4096]{2,1,0:T(8,128)} %param.16) | copy-start | bytes 1572868
  0.0 2.3 %collective-permute-start = (f32[1,32,64]{2,1,0:T(8,128)}, f32[1,32,64]{2,1,0:T(8,128)S(1)}, u32[]{:S(2)}, u32[]{:S(2)}) collective-permute-start(f32[1,32,64]{2,1,0:T(8,128)} %param.9), channel_id=1, source_target_pairs={{0,1},{1,0},{2,3},{3,2},{4,5},{5,4},{6,7},{7,6},{8,9},{9,8},{10,11... | collective-permute-start | bytes 24584 | tf_op jit(solution)/shard_map/ppermute | solution.py:469
  2.3 4.0 %collective-permute-start.1 = (f32[2,32,64]{2,1,0:T(8,128)S(1)}, f32[2,32,64]{2,1,0:T(8,128)S(1)}, u32[]{:S(2)}, u32[]{:S(2)}) collective-permute-start(f32[2,32,64]{2,1,0:T(8,128)S(1)} %pad_maximum_fusion.1), channel_id=1, source_target_pairs={{0,2},{1,3},{2,0},{3,1},{4,6},{5,7},{6,4},{7,5},{8,10},{9,11},{10,... | collective-permute-start | bytes 49160 | tf_op jit(solution)/shard_map/ppermute | solution.py:469
  5.5 7.5 %collective-permute-start.3 = (f32[1,32,64]{2,1,0:T(8,128)S(1)}, f32[1,32,64]{2,1,0:T(8,128)S(1)}, u32[]{:S(2)}, u32[]{:S(2)}) collective-permute-start(f32[1,32,64]{2,1,0:T(8,128)S(1)} %copy-done), channel_id=1, source_target_pairs={{0,8},{8,0},{16,24},{24,16},{32,40},{40,32},{48,56},{56,48},{64,72... | collective-permute-start | bytes 24584 | tf_op jit(solution)/shard_map/ppermute | solution.py:472
  6.3 7.0 %collective-permute-start.2 = (f32[4,32,64]{2,1,0:T(8,128)S(1)}, f32[4,32,64]{2,1,0:T(8,128)S(1)}, u32[]{:S(2)}, u32[]{:S(2)}) collective-permute-start(f32[4,32,64]{2,1,0:T(8,128)S(1)} %pad_maximum_fusion), channel_id=1, source_target_pairs={{0,6},{1,7},{2,4},{3,5},{4,2},{5,3},{6,0},{7,1},{8,14},{9,15},{10,... | collective-permute-start | bytes 98312 | tf_op jit(solution)/shard_map/ppermute | solution.py:469
  9.2 4.2 %collective-permute-start.4 = (f32[1,32,64]{2,1,0:T(8,128)S(1)}, f32[1,32,64]{2,1,0:T(8,128)S(1)}, u32[]{:S(2)}, u32[]{:S(2)}) collective-permute-start(f32[1,32,64]{2,1,0:T(8,128)S(1)} %copy-done), channel_id=1, source_target_pairs={{0,248},{8,16},{16,8},{24,32},{32,24},{40,48},{48,40},{56,64},{64,... | collective-permute-start | bytes 24584 | tf_op jit(solution)/shard_map/ppermute | solution.py:487
  11.7 1.7 %copy-start.1 = (f32[1,32,64]{2,1,0:T(8,128)S(1)}, f32[1,32,64]{2,1,0:T(8,128)}, u32[]{:S(2)}) copy-start(f32[1,32,64]{2,1,0:T(8,128)} %param.13) | copy-start | bytes 24580
  11.7 1.7 %copy-start.2 = (f32[1,32,64]{2,1,0:T(8,128)S(1)}, f32[1,32,64]{2,1,0:T(8,128)}, u32[]{:S(2)}) copy-start(f32[1,32,64]{2,1,0:T(8,128)} %param.14) | copy-start | bytes 24580
  11.7 1.7 %copy-start.4 = (s32[1,4]{1,0:T(1,128)S(1)}, s32[1,4]{1,0:T(1,128)}, u32[]{:S(2)}) copy-start(s32[1,4]{1,0:T(1,128)} %neigh_ref.1) | copy-start | bytes 52
  15.6 8.3 %collective-permute-start.5 = (f32[128,128]{1,0:T(8,128)S(1)}, f32[128,128]{1,0:T(8,128)S(1)}, u32[]{:S(2)}, u32[]{:S(2)}) collective-permute-start(f32[128,128]{1,0:T(8,128)S(1)} %get-tuple-element.46.refs_0_), channel_id=1, source_target_pairs={{0,8},{8,0},{16,24},{24,16},{32,40},{40,32},{48,56},{56,48},{64,72... | collective-permute-start | bytes 196616 | tf_op jit(solution)/shard_map/ppermute | solution.py:472
  21.6 5.3 %collective-permute-start.6 = (f32[128,128]{1,0:T(8,128)S(1)}, f32[128,128]{1,0:T(8,128)S(1)}, u32[]{:S(2)}, u32[]{:S(2)}) collective-permute-start(f32[128,128]{1,0:T(8,128)S(1)} %get-tuple-element.46.refs_0_), channel_id=1, source_target_pairs={{0,16},{8,24},{16,0},{24,8},{32,48},{40,56},{48,32},{56,40},{64,80... | collective-permute-start | bytes 196616 | tf_op jit(solution)/shard_map/ppermute | solution.py:472
  21.6 6.4 %collective-permute-start.7 = (f32[128,128]{1,0:T(8,128)S(1)}, f32[128,128]{1,0:T(8,128)S(1)}, u32[]{:S(2)}, u32[]{:S(2)}) collective-permute-start(f32[128,128]{1,0:T(8,128)S(1)} %get-tuple-element.46.refs_0_), channel_id=1, source_target_pairs={{0,24},{8,16},{16,8},{24,0},{32,56},{40,48},{48,40},{56,32},{64,88... | collective-permute-start | bytes 196616 | tf_op jit(solution)/shard_map/ppermute | solution.py:472
  29.0 8.3 %collective-permute-start.10 = (f32[128,128]{1,0:T(8,128)S(1)}, f32[128,128]{1,0:T(8,128)S(1)}, u32[]{:S(2)}, u32[]{:S(2)}) collective-permute-start(f32[128,128]{1,0:T(8,128)S(1)} %get-tuple-element.47.refs_0_), channel_id=1, source_target_pairs={{0,120},{8,112},{16,104},{24,96},{32,88},{40,80},{48,72},{56,64},{... | collective-permute-start | bytes 196616 | tf_op jit(solution)/shard_map/ppermute | solution.py:472
  31.6 7.3 %collective-permute-start.8 = (f32[128,128]{1,0:T(8,128)S(1)}, f32[128,128]{1,0:T(8,128)S(1)}, u32[]{:S(2)}, u32[]{:S(2)}) collective-permute-start(f32[128,128]{1,0:T(8,128)S(1)} %get-tuple-element.47.refs_0_), channel_id=1, source_target_pairs={{0,56},{8,48},{16,40},{24,32},{32,24},{40,16},{48,8},{56,0},{64,12... | collective-permute-start | bytes 196616 | tf_op jit(solution)/shard_map/ppermute | solution.py:472
  32.1 6.8 %collective-permute-start.9 = (f32[128,128]{1,0:T(8,128)S(1)}, f32[128,128]{1,0:T(8,128)S(1)}, u32[]{:S(2)}, u32[]{:S(2)}) collective-permute-start(f32[128,128]{1,0:T(8,128)S(1)} %get-tuple-element.47.refs_0_), channel_id=1, source_target_pairs={{0,64},{8,72},{16,80},{24,88},{32,96},{40,104},{48,112},{56,120},{... | collective-permute-start | bytes 196616 | tf_op jit(solution)/shard_map/ppermute | solution.py:472
  39.8 5.2 %collective-permute-start.11 = (f32[64,128]{1,0:T(8,128)S(1)}, f32[64,128]{1,0:T(8,128)S(1)}, u32[]{:S(2)}, u32[]{:S(2)}) collective-permute-start(f32[64,128]{1,0:T(8,128)S(1)} %get-tuple-element.49.own_ref), channel_id=1, source_target_pairs={{0,192},{8,200},{16,208},{24,216},{32,224},{40,232},{48,240},{56,2... | collective-permute-start | bytes 98312 | tf_op jit(solution)/shard_map/ppermute | solution.py:472

commit v6 on v4

--- a/solution.py
+++ b/solution.py
@@ -4,7 +4,6 @@
 from jax.experimental import pallas as pl
 from jax.experimental.pallas import tpu as pltpu
 from jax.sharding import PartitionSpec as P
-
 
 f32 = jnp.float32
 bf16 = jnp.bfloat16
@@ -174,7 +173,7 @@
     out_ref[...] = src_ref[...] - acc + lower + tran * upper
 
 
-def upsweep(neigh_ref, part_ref, a_ref, b_ref, c_ref, top_ref, flux_ref, dens_ref, tran_ref, lat_ref, coup_ref, cols_ref,
+def upsweep(neigh_ref, part_ref, a_ref, b_ref, c_ref, even_ref, odd_ref, flux_ref, dens_ref, tran_ref, lat_ref, coup_ref, cols_ref,
             quad_ref, n1_ref, n2_ref, n3_ref, n4_ref, n5_ref, root_ref, pay_ref, pair_ref, v_ref, w_ref):
     me = lax.axis_index("lat")
     u = dens_ref[...]
@@ -189,7 +188,10 @@
         total = total + count.astype(f32) * value
     row = lax.broadcasted_iota(jnp.int32, (CELLS, N), 0)
     r = part_ref[...] - lat_ref[...] * (4.0 * u - total)
-    r = r + jnp.where(row == CELLS - 1, tran_ref[...] * top_ref[0, 0:1], 0.0)
+    depth = lax.axis_index("depth")
+    above = jnp.where(depth % 2 == 0, even_ref[0, 0:1], odd_ref[0, 0:1])
+    above = jnp.where(depth == lax.axis_size("depth") - 1, 0.0, above)
+    r = r + jnp.where(row == CELLS - 1, tran_ref[...] * above, 0.0)
     c = coup_ref[...]
     g = r / jnp.where(row == 0, c, pltpu.roll(c, 1, 0))
     x = []
@@ -339,7 +341,7 @@
 
 def track(is_low, fun, extra):
     f, hh, k, g, e = fun
-    _, _, yp1, yv1, yq2, yt, yth = extra
+    t, th, yp1, yv1, yq2, yt, yth = extra
     x1 = pack(jnp.where(is_low, hh, f))
     x2 = pack(jnp.where(is_low, hh, k))
     prod1 = dot(x1, jnp.where(is_low, yq2, yp1))
@@ -439,7 +441,7 @@
     return jax.ShapeDtypeStruct(shape, dtype)
 
 
-def call(body, outs, *args, scratch=(), smem=0, hbm=0, flops=0):
+def call(body, outs, *args, scratch=(), smem=0, hbm=0, flops=0, name=None):
     args = [pltpu.with_memory_space_constraint(x, pltpu.HBM) if smem <= i < smem + hbm else x for i, x in enumerate(args)]
     spaces = [pltpu.SMEM] * smem + [pltpu.HBM] * hbm + [pltpu.VMEM] * (len(args) - smem - hbm)
     return pl.pallas_call(
@@ -449,6 +451,7 @@
         out_specs=jax.tree.map(lambda _: pl.BlockSpec(memory_space=pltpu.VMEM), outs),
         scratch_shapes=scratch,
         cost_estimate=pl.CostEstimate(flops=flops, bytes_accessed=1 << 16, transcendentals=0),
+        name=name,
         compiler_params=pltpu.CompilerParams(vmem_limit_bytes=VLIM),
     )(*args)
 
@@ -473,10 +476,9 @@
     def xor_depth(value, bits):
         return lax.ppermute(value, "depth", [(i, i ^ bits) for i in range(32)])
 
-    top = lax.ppermute(densities, "depth", [(i + 1, i) for i in range(31)])
     line_a = xor_lat(densities, 1)
     part, flux = call(
-        react, (sds(CELLS, N), sds(N, 128)), jac, u, src, tran, pattern, hbm=5, flops=1 << 30,
+        react, (sds(CELLS, N), sds(N, 128)), jac, u, src, tran, pattern, hbm=5, flops=1 << 30, name="react",
         scratch=[pltpu.VMEM((CELLS, N * N), f32)] + [pltpu.VMEM((CELLS, N), f32)] * 3
         + [pltpu.VMEM((8, 8), jnp.int32), pltpu.SemaphoreType.DMA((8,))],
     )
@@ -484,44 +486,50 @@
     quad, n1, full, cols = call(
         tree_leaves,
         (sds(16, 4, N, 256, dtype=bf16), sds(16, 3, N, 128, dtype=bf16), sds(16, 3, N, 128), sds(2, N, 128)),
-        fac, coup, part, scratch=[pltpu.VMEM((2, N, 128), f32)], flops=2 << 30,
+        fac, coup, part, scratch=[pltpu.VMEM((2, N, 128), f32)], flops=2 << 30, name="tree_leaves",
+    )
+    top_even = xor_depth(lax.optimization_barrier((densities, cols))[0], 1)
+    top_odd = lax.ppermute(
+        lax.optimization_barrier((densities, line_b))[0], "depth",
+        [(i, (i + 1) % 32 if i % 2 else (i - 1) % 32) for i in range(32)],
     )
     line_c = xor_lat(jnp.concatenate([densities, line_a, line_b], axis=0), 6)
     n2, n3, n4, n5, root = call(
         tree_upper,
         (node(8), node(4), node(2), sds(1, N, 128, dtype=bf16), sds(128, 128)),
         n1, full, coup, cols, part, scratch=[pltpu.VMEM((8, 3, N, 128), f32), pltpu.VMEM((4, 3, N, 128), f32)],
-        flops=2 << 30,
+        flops=2 << 30, name="tree_upper",
     )
     pay, pair, vs, ws = call(
         upsweep, (sds(128, 128), sds(4, N, 128), sds(7, N, 128), sds(7, N, 128)),
-        neighbours, part, line_a, line_b, line_c, top, flux, u, tran, lat, coup, cols, quad, n1, n2, n3, n4, n5, root,
-        smem=1, flops=1 << 25,
+        neighbours, part, line_a, line_b, line_c, top_even, top_odd, flux, u, tran, lat, coup, cols, quad, n1, n2, n3, n4, n5, root,
+        smem=1, flops=1 << 25, name="upsweep",
     )
     others = [xor_depth(pay, bits) for bits in (1, 2, 3)]
     tees, add_v, add_a, add_x = call(
         prepare, (sds(15, N, 128, dtype=bf16), sds(4, N, 128), sds(4, N, 128), sds(N, 128)),
-        pair, vs, ws, n1, n2, n3, n4, flops=1 << 30,
+        pair, vs, ws, n1, n2, n3, n4, flops=1 << 30, name="prepare",
     )
     pay, fun = call(
         combine_four, (sds(128, 128), sds(128, 128)), pay, *others, scratch=[pltpu.VMEM((4, 128, 128), f32)],
-        flops=1 << 24,
+        flops=1 << 24, name="combine_four",
     )
     for level, bits in ((2, 7), (3, 8)):
         other = xor_depth(pay, bits)
         pay, fun = call(
             lambda *refs, level=level: combine_two(level, *refs),
             (sds(N if level == 3 else 128, 128), sds(128, 128)), pay, other, fun, flops=1 << 24,
+            name=f"combine{level}",
         )
     other = xor_depth(pay, 24)
     maps, vecs, own_rhs = call(
         prepare_last,
         (sds(2, N, 128, dtype=bf16), sds(2, N, 128), sds(2, 256, 128, dtype=bf16)),
-        pay, fun, flops=1 << 30,
+        pay, fun, flops=1 << 30, name="prepare_last",
     )
     out = call(
         downsweep, sds(CELLS, N), other, maps, vecs, own_rhs, cols, add_v, add_a, add_x, quad, n1, n2, n3, n4, tees,
-        flops=1 << 25,
+        flops=1 << 25, name="downsweep",
     )
     return out.reshape(line_count, cell_count, species)
 

time: 49.8 us -> 49.3 us (0.990)
  the two profiles are of different devices: /device:TPU:30 before, /device:TPU:32 now
where the time goes in v6:
time: 49.3 us; the launch traced here: 49.2 us
  waiting for transfers between devices  19.4 us (39%)
  starting transfers between devices  17.2 us (35%)
  Pallas kernels  12.4 us (25%)
    ppermute x7, waiting for transfers between devices, xor_depth(): return lax.ppermute(value, 'depth', [(i, i ^ bits) for i in range(32)])  18.6 us
    pallas_call x10, Pallas kernels, call(): pl.pallas_call(body, out_shape=outs, in_specs=[pl.BlockSpec(memory_space=...  12.4 us
    ppermute x7, starting transfers between devices, xor_depth(): return lax.ppermute(value, 'depth', [(i, i ^ bits) for i in range(32)])  10.2 us
    ppermute x3, starting transfers between devices, xor_lat(): return lax.ppermute(value, 'lat', [(i, i ^ bits) for i in range(8)])  4.52 us
    ppermute x1, starting transfers between devices, on_device(): lax.ppermute(lax.optimization_barrier((densities, line_b))[0], 'depth', [...  2.48 us
  transfers between devices with their start and end apart: 11, of which 8 were waited for; matrix products, arithmetic and copies ran while one was open for 0% of the time, Pallas kernels for 12%

profile of v6, /device:TPU:32, one launch (start us, length us, event | category | flops | bytes accessed | tf_op | source)
XLA Modules:
  0.0 49.2 jit_solution(14546409811856029276)
XLA Ops:
  0.0 0.1 collective-permute-start
  0.1 2.2 %react.1 = (f32[32,64]{1,0:T(8,128)S(1)}, f32[64,128]{1,0:T(8,128)S(1)}) custom-call(f32[32,4096]{1,0:T(8,128)} %bitcast.21, f32[32,64]{1,0:T(8,128)} %bitcast.12, f32[32,64]{1,0:T(8,128)} %bitcast.22, f32[32,64]{1,0:T(8,128)} %bitcast.14, s32[8,8]{1,0:T(8,128)} %pat_hbm.1), custom_call_target="tpu_custom_call" | custom-call | flops 1073741824 | bytes 65536 | tf_op jit(solution)/shard_map/react/pallas_call | solution.py:447
  2.3 0.0 collective-permute-done.a_ref
  2.3 1.6 %collective-permute-start.1 = (f32[2,32,64]{2,1,0:T(8,128)S(1)}, f32[2,32,64]{2,1,0:T(8,128)S(1)}, u32[]{:S(2)}, u32[]{:S(2)}) collective-permute-start(f32[2,32,64]{2,1,0:T(8,128)S(1)} %pad_maximum_fusion.1), channel_id=1, source_target_pairs={{0,2},{1,3},{2,0},{3,1},{4,6},{5,7},{6,4},{7,5},{8,10},{9,11},{10,... | collective-permute-start | bytes 49160 | tf_op jit(solution)/shard_map/ppermute | solution.py:474
  3.9 1.6 %tree_leaves.1 = (bf16[16,4,64,256]{3,2,1,0:T(8,128)(2,1)S(1)}, bf16[16,3,64,128]{3,2,1,0:T(8,128)(2,1)S(1)}, f32[16,3,64,128]{3,2,1,0:T(8,128)S(1)}, f32[2,64,128]{2,1,0:T(8,128)S(1)}) custom-call(f32[1024,128]{1,0:T(8,128)S(1)} %bitcast.20, f32[32,64]{1,0:T(8,128)S(1)} %bitcast.17, f32[32,64]{1,0:T(8,128)S(1)} %get-tuple-element.35.after_ref.part_ref), custom_call_target="tpu_custom_call" | custom-call | flops 2147483648 | bytes 65536 | tf_op jit(solution)/shard_map/tree_leaves/pallas_call | solution.py:447
  5.6 0.3 collective-permute-start.3
  5.9 0.5 collective-permute-done.1.b_ref
  6.3 2.8 %collective-permute-start.2 = (f32[4,32,64]{2,1,0:T(8,128)S(1)}, f32[4,32,64]{2,1,0:T(8,128)S(1)}, u32[]{:S(2)}, u32[]{:S(2)}) collective-permute-start(f32[4,32,64]{2,1,0:T(8,128)S(1)} %pad_maximum_fusion), channel_id=1, source_target_pairs={{0,6},{1,7},{2,4},{3,5},{4,2},{5,3},{6,0},{7,1},{8,14},{9,15},{10,... | collective-permute-start | bytes 98312 | tf_op jit(solution)/shard_map/ppermute | solution.py:474
  9.2 2.5 %collective-permute-start.4 = (f32[1,32,64]{2,1,0:T(8,128)S(1)}, f32[1,32,64]{2,1,0:T(8,128)S(1)}, u32[]{:S(2)}, u32[]{:S(2)}) collective-permute-start(f32[1,32,64]{2,1,0:T(8,128)S(1)} %copy-done), channel_id=1, source_target_pairs={{0,248},{8,16},{16,8},{24,32},{32,24},{40,48},{48,40},{56,64},{64,... | collective-permute-start | bytes 24584 | tf_op jit(solution)/shard_map/ppermute | solution.py:492
  11.7 1.4 %tree_upper.1 = (bf16[8,4,64,128]{3,2,1,0:T(8,128)(2,1)S(1)}, bf16[4,4,64,128]{3,2,1,0:T(8,128)(2,1)S(1)}, bf16[2,4,64,128]{3,2,1,0:T(8,128)(2,1)S(1)}, bf16[1,64,128]{2,1,0:T(8,128)(2,1)S(1)}, f32[128,128]{1,0:T(8,128)S(1)}) custom-call(bf16[16,3,64,128]{3,2,1,0:T(8,128)(2,1)S(1)} %get-tuple-element.41.n1_ref, ...), custom_call_target="tpu_custom_call" | custom-call | flops 2147483648 | bytes 65536 | tf_op jit(solution)/shard_map/tree_upper/pallas_call | solution.py:447
  13.1 0.0 collective-permute-done.3.even_ref
  13.1 0.3 collective-permute-done.4.odd_ref
  13.4 0.0 collective-permute-done.2.c_ref
  13.4 2.2 %upsweep.1 = (f32[128,128]{1,0:T(8,128)S(1)}, f32[4,64,128]{2,1,0:T(8,128)S(1)}, f32[7,64,128]{2,1,0:T(8,128)S(1)}, f32[7,64,128]{2,1,0:T(8,128)S(1)}) custom-call(s32[1,4]{1,0:T(1,128)S(1)} %copy-done.4, f32[32,64]{1,0:T(8,128)S(1)} %get-tuple-element.35.after_ref.part_ref, f32[1,32,64]{2,1,0:T(8,128)S(1)} %collective-permute-done.a_ref, ...), custom_call_target="tpu_custom_call" | custom-call | flops 33554432 | bytes 65536 | tf_op jit(solution)/shard_map/upsweep/pallas_call | solution.py:447
  15.6 6.0 %collective-permute-start.5 = (f32[128,128]{1,0:T(8,128)S(1)}, f32[128,128]{1,0:T(8,128)S(1)}, u32[]{:S(2)}, u32[]{:S(2)}) collective-permute-start(f32[128,128]{1,0:T(8,128)S(1)} %get-tuple-element.48.own_ref), channel_id=1, source_target_pairs={{0,8},{8,0},{16,24},{24,16},{32,40},{40,32},{48,56},{56,48},{64,72... | collective-permute-start | bytes 196616 | tf_op jit(solution)/shard_map/ppermute | solution.py:477
  21.6 0.0 collective-permute-start.6
  21.6 1.6 %collective-permute-start.7 = (f32[128,128]{1,0:T(8,128)S(1)}, f32[128,128]{1,0:T(8,128)S(1)}, u32[]{:S(2)}, u32[]{:S(2)}) collective-permute-start(f32[128,128]{1,0:T(8,128)S(1)} %get-tuple-element.48.own_ref), channel_id=1, source_target_pairs={{0,24},{8,16},{16,8},{24,0},{32,56},{40,48},{48,40},{56,32},{64,88... | collective-permute-start | bytes 196616 | tf_op jit(solution)/shard_map/ppermute | solution.py:477
  23.2 0.7 %collective-permute-done.5.x1_ref = f32[128,128]{1,0:T(8,128)S(1)} collective-permute-done((f32[128,128]{1,0:T(8,128)S(1)}, f32[128,128]{1,0:T(8,128)S(1)}, u32[]{:S(2)}, u32[]{:S(2)}) %collective-permute-start.5) | collective-permute-done | bytes 65568 | tf_op jit(solution)/shard_map/ppermute | solution.py:477
  23.8 3.0 %collective-permute-done.6.x2_ref = f32[128,128]{1,0:T(8,128)S(1)} collective-permute-done((f32[128,128]{1,0:T(8,128)S(1)}, f32[128,128]{1,0:T(8,128)S(1)}, u32[]{:S(2)}, u32[]{:S(2)}) %collective-permute-start.6) | collective-permute-done | bytes 65568 | tf_op jit(solution)/shard_map/ppermute | solution.py:477
  26.9 1.2 %collective-permute-done.7.x3_ref = f32[128,128]{1,0:T(8,128)S(1)} collective-permute-done((f32[128,128]{1,0:T(8,128)S(1)}, f32[128,128]{1,0:T(8,128)S(1)}, u32[]{:S(2)}, u32[]{:S(2)}) %collective-permute-start.7) | collective-permute-done | bytes 65568 | tf_op jit(solution)/shard_map/ppermute | solution.py:477
  28.0 1.0 %combine_four.1 = (f32[128,128]{1,0:T(8,128)S(1)}, f32[128,128]{1,0:T(8,128)S(1)}) custom-call(f32[128,128]{1,0:T(8,128)S(1)} %get-tuple-element.48.own_ref, f32[128,128]{1,0:T(8,128)S(1)} %collective-permute-done.5.x1_ref, f32[128,128]{1,0:T(8,128)S(1)} %collective-permute-done.6.x2_ref, f32[128,128]{1,0:T(8,128)S(1)} %collective-permute-done.7.x3_ref), custom_call_target="tpu_custom_call" | custom-call | flops 16777216 | bytes 65536 | tf_op jit(solution)/shard_map/combine_four/pallas_call | solution.py:447
  29.0 1.6 %collective-permute-start.8 = (f32[128,128]{1,0:T(8,128)S(1)}, f32[128,128]{1,0:T(8,128)S(1)}, u32[]{:S(2)}, u32[]{:S(2)}) collective-permute-start(f32[128,128]{1,0:T(8,128)S(1)} %get-tuple-element.49.refs_0_), channel_id=1, source_target_pairs={{0,56},{8,48},{16,40},{24,32},{32,24},{40,16},{48,8},{56,0},{64,12... | collective-permute-start | bytes 196616 | tf_op jit(solution)/shard_map/ppermute | solution.py:477
  30.6 5.8 %collective-permute-done.8.refs_1_ = f32[128,128]{1,0:T(8,128)S(1)} collective-permute-done((f32[128,128]{1,0:T(8,128)S(1)}, f32[128,128]{1,0:T(8,128)S(1)}, u32[]{:S(2)}, u32[]{:S(2)}) %collective-permute-start.8) | collective-permute-done | bytes 65568 | tf_op jit(solution)/shard_map/ppermute | solution.py:477
  36.3 0.5 combine2.1
  36.8 0.1 collective-permute-start.9
  36.9 0.7 %prepare.1 = (bf16[15,64,128]{2,1,0:T(8,128)(2,1)S(1)}, f32[4,64,128]{2,1,0:T(8,128)S(1)}, f32[4,64,128]{2,1,0:T(8,128)S(1)}, f32[64,128]{1,0:T(8,128)S(1)}) custom-call(f32[4,64,128]{2,1,0:T(8,128)S(1)} %get-tuple-element.58.pair_ref, f32[7,64,128]{2,1,0:T(8,128)S(1)} %get-tuple-element.59.v_ref, f32[7,64,128]{2,1,0:T(8,128)S(1)} %get-tuple-element.60.w_ref, ...), custom_call_target="tpu_custom_call" | custom-call | flops 1073741824 | bytes 65536 | tf_op jit(solution)/shard_map/prepare/pallas_call | solution.py:447
  37.6 3.6 %collective-permute-done.9.refs_1_ = f32[128,128]{1,0:T(8,128)S(1)} collective-permute-done((f32[128,128]{1,0:T(8,128)S(1)}, f32[128,128]{1,0:T(8,128)S(1)}, u32[]{:S(2)}, u32[]{:S(2)}) %collective-permute-start.9) | collective-permute-done | bytes 65568 | tf_op jit(solution)/shard_map/ppermute | solution.py:477
  41.2 0.4 combine3.1
  41.6 0.7 %collective-permute-start.10 = (f32[64,128]{1,0:T(8,128)S(1)}, f32[64,128]{1,0:T(8,128)S(1)}, u32[]{:S(2)}, u32[]{:S(2)}) collective-permute-start(f32[64,128]{1,0:T(8,128)S(1)} %get-tuple-element.53.own_ref), channel_id=1, source_target_pairs={{0,192},{8,200},{16,208},{24,216},{32,224},{40,232},{48,240},{56,2... | collective-permute-start | bytes 98312 | tf_op jit(solution)/shard_map/ppermute | solution.py:477
  42.3 0.1 prepare_last.1
  42.4 4.5 %collective-permute-done.10.other_ref = f32[64,128]{1,0:T(8,128)S(1)} collective-permute-done((f32[64,128]{1,0:T(8,128)S(1)}, f32[64,128]{1,0:T(8,128)S(1)}, u32[]{:S(2)}, u32[]{:S(2)}) %collective-permute-start.10) | collective-permute-done | bytes 32800 | tf_op jit(solution)/shard_map/ppermute | solution.py:477
  46.8 2.4 %downsweep.1 = f32[32,64]{1,0:T(8,128)} custom-call(f32[64,128]{1,0:T(8,128)S(1)} %collective-permute-done.10.other_ref, bf16[2,64,128]{2,1,0:T(8,128)(2,1)S(1)} %get-tuple-element.55.maps_ref, f32[2,64,128]{2,1,0:T(8,128)S(1)} %get-tuple-element.56.vecs_ref, bf16[2,256,128]{2,1,0:T(8,128)(2,1)S(1)} %get-tuple-element.57.own_rhs, ...), custom_call_target="tpu_custom_call" | custom-call | flops 33554432 | bytes 65536 | tf_op jit(solution)/shard_map/downsweep/pallas_call | solution.py:447
  (14 shorter events, 0.0 us)
Async XLA Ops:
  0.0 2.3 %copy-start = (f32[1,32,64]{2,1,0:T(8,128)S(1)}, f32[1,32,64]{2,1,0:T(8,128)}, u32[]{:S(2)}) copy-start(f32[1,32,64]{2,1,0:T(8,128)} %param.9) | copy-start | bytes 24580
  0.0 3.9 %copy-start.3 = (f32[1,32,64]{2,1,0:T(8,128)S(1)}, f32[1,32,64]{2,1,0:T(8,128)}, u32[]{:S(2)}) copy-start(f32[1,32,64]{2,1,0:T(8,128)} %param.17) | copy-start | bytes 24580
  0.0 3.9 %copy-start.5 = (f32[1,32,4096]{2,1,0:T(8,128)S(1)}, f32[1,32,4096]{2,1,0:T(8,128)}, u32[]{:S(2)}) copy-start(f32[1,32,4096]{2,1,0:T(8,128)} %param.16) | copy-start | bytes 1572868
  0.0 2.3 %collective-permute-start = (f32[1,32,64]{2,1,0:T(8,128)}, f32[1,32,64]{2,1,0:T(8,128)S(1)}, u32[]{:S(2)}, u32[]{:S(2)}) collective-permute-start(f32[1,32,64]{2,1,0:T(8,128)} %param.9), channel_id=1, source_target_pairs={{0,1},{1,0},{2,3},{3,2},{4,5},{5,4},{6,7},{7,6},{8,9},{9,8},{10,11... | collective-permute-start | bytes 24584 | tf_op jit(solution)/shard_map/ppermute | solution.py:474
  2.3 4.0 %collective-permute-start.1 = (f32[2,32,64]{2,1,0:T(8,128)S(1)}, f32[2,32,64]{2,1,0:T(8,128)S(1)}, u32[]{:S(2)}, u32[]{:S(2)}) collective-permute-start(f32[2,32,64]{2,1,0:T(8,128)S(1)} %pad_maximum_fusion.1), channel_id=1, source_target_pairs={{0,2},{1,3},{2,0},{3,1},{4,6},{5,7},{6,4},{7,5},{8,10},{9,11},{10,... | collective-permute-start | bytes 49160 | tf_op jit(solution)/shard_map/ppermute | solution.py:474
  5.6 7.5 %collective-permute-start.3 = (f32[1,32,64]{2,1,0:T(8,128)S(1)}, f32[1,32,64]{2,1,0:T(8,128)S(1)}, u32[]{:S(2)}, u32[]{:S(2)}) collective-permute-start(f32[1,32,64]{2,1,0:T(8,128)S(1)} %copy-done), channel_id=1, source_target_pairs={{0,8},{8,0},{16,24},{24,16},{32,40},{40,32},{48,56},{56,48},{64,72... | collective-permute-start | bytes 24584 | tf_op jit(solution)/shard_map/ppermute | solution.py:477
  6.3 7.0 %collective-permute-start.2 = (f32[4,32,64]{2,1,0:T(8,128)S(1)}, f32[4,32,64]{2,1,0:T(8,128)S(1)}, u32[]{:S(2)}, u32[]{:S(2)}) collective-permute-start(f32[4,32,64]{2,1,0:T(8,128)S(1)} %pad_maximum_fusion), channel_id=1, source_target_pairs={{0,6},{1,7},{2,4},{3,5},{4,2},{5,3},{6,0},{7,1},{8,14},{9,15},{10,... | collective-permute-start | bytes 98312 | tf_op jit(solution)/shard_map/ppermute | solution.py:474
  9.2 4.2 %collective-permute-start.4 = (f32[1,32,64]{2,1,0:T(8,128)S(1)}, f32[1,32,64]{2,1,0:T(8,128)S(1)}, u32[]{:S(2)}, u32[]{:S(2)}) collective-permute-start(f32[1,32,64]{2,1,0:T(8,128)S(1)} %copy-done), channel_id=1, source_target_pairs={{0,248},{8,16},{16,8},{24,32},{32,24},{40,48},{48,40},{56,64},{64,... | collective-permute-start | bytes 24584 | tf_op jit(solution)/shard_map/ppermute | solution.py:492
  11.7 1.7 %copy-start.1 = (f32[1,32,64]{2,1,0:T(8,128)S(1)}, f32[1,32,64]{2,1,0:T(8,128)}, u32[]{:S(2)}) copy-start(f32[1,32,64]{2,1,0:T(8,128)} %param.13) | copy-start | bytes 24580
  11.7 1.7 %copy-start.2 = (f32[1,32,64]{2,1,0:T(8,128)S(1)}, f32[1,32,64]{2,1,0:T(8,128)}, u32[]{:S(2)}) copy-start(f32[1,32,64]{2,1,0:T(8,128)} %param.14) | copy-start | bytes 24580
  11.7 1.7 %copy-start.4 = (s32[1,4]{1,0:T(1,128)S(1)}, s32[1,4]{1,0:T(1,128)}, u32[]{:S(2)}) copy-start(s32[1,4]{1,0:T(1,128)} %neigh_ref.1) | copy-start | bytes 52
  15.6 8.3 %collective-permute-start.5 = (f32[128,128]{1,0:T(8,128)S(1)}, f32[128,128]{1,0:T(8,128)S(1)}, u32[]{:S(2)}, u32[]{:S(2)}) collective-permute-start(f32[128,128]{1,0:T(8,128)S(1)} %get-tuple-element.48.own_ref), channel_id=1, source_target_pairs={{0,8},{8,0},{16,24},{24,16},{32,40},{40,32},{48,56},{56,48},{64,72... | collective-permute-start | bytes 196616 | tf_op jit(solution)/shard_map/ppermute | solution.py:477
  21.6 5.3 %collective-permute-start.6 = (f32[128,128]{1,0:T(8,128)S(1)}, f32[128,128]{1,0:T(8,128)S(1)}, u32[]{:S(2)}, u32[]{:S(2)}) collective-permute-start(f32[128,128]{1,0:T(8,128)S(1)} %get-tuple-element.48.own_ref), channel_id=1, source_target_pairs={{0,16},{8,24},{16,0},{24,8},{32,48},{40,56},{48,32},{56,40},{64,80... | collective-permute-start | bytes 196616 | tf_op jit(solution)/shard_map/ppermute | solution.py:477
  21.6 6.4 %collective-permute-start.7 = (f32[128,128]{1,0:T(8,128)S(1)}, f32[128,128]{1,0:T(8,128)S(1)}, u32[]{:S(2)}, u32[]{:S(2)}) collective-permute-start(f32[128,128]{1,0:T(8,128)S(1)} %get-tuple-element.48.own_ref), channel_id=1, source_target_pairs={{0,24},{8,16},{16,8},{24,0},{32,56},{40,48},{48,40},{56,32},{64,88... | collective-permute-start | bytes 196616 | tf_op jit(solution)/shard_map/ppermute | solution.py:477
  29.0 7.4 %collective-permute-start.8 = (f32[128,128]{1,0:T(8,128)S(1)}, f32[128,128]{1,0:T(8,128)S(1)}, u32[]{:S(2)}, u32[]{:S(2)}) collective-permute-start(f32[128,128]{1,0:T(8,128)S(1)} %get-tuple-element.49.refs_0_), channel_id=1, source_target_pairs={{0,56},{8,48},{16,40},{24,32},{32,24},{40,16},{48,8},{56,0},{64,12... | collective-permute-start | bytes 196616 | tf_op jit(solution)/shard_map/ppermute | solution.py:477
  36.8 4.4 %collective-permute-start.9 = (f32[128,128]{1,0:T(8,128)S(1)}, f32[128,128]{1,0:T(8,128)S(1)}, u32[]{:S(2)}, u32[]{:S(2)}) collective-permute-start(f32[128,128]{1,0:T(8,128)S(1)} %get-tuple-element.51.refs_0_), channel_id=1, source_target_pairs={{0,64},{8,72},{16,80},{24,88},{32,96},{40,104},{48,112},{56,120},{... | collective-permute-start | bytes 196616 | tf_op jit(solution)/shard_map/ppermute | solution.py:477
  41.6 5.2 %collective-permute-start.10 = (f32[64,128]{1,0:T(8,128)S(1)}, f32[64,128]{1,0:T(8,128)S(1)}, u32[]{:S(2)}, u32[]{:S(2)}) collective-permute-start(f32[64,128]{1,0:T(8,128)S(1)} %get-tuple-element.53.own_ref), channel_id=1, source_target_pairs={{0,192},{8,200},{16,208},{24,216},{32,224},{40,232},{48,240},{56,2... | collective-permute-start | bytes 98312 | tf_op jit(solution)/shard_map/ppermute | solution.py:477

commit v7 on v5

--- a/solution.py
+++ b/solution.py
@@ -486,7 +486,7 @@
     top_even = xor_depth(lax.optimization_barrier((densities, cols))[0], 1)
     top_odd = lax.ppermute(
         lax.optimization_barrier((densities, line_b))[0], "depth",
-        [(i, (i + 1) % 32 if i % 2 else (i - 1) % 32) for i in range(32)],
+        [(i, i + 1 if i % 2 else i - 1) for i in range(1, 31)],
     )
     line_c = xor_lat(jnp.concatenate([densities, line_a, line_b], axis=0), 6)
     n2, n3, n4, n5, root = call(

time: 47.5 us -> 49.4 us (1.040)
  waiting for transfers between devices: 11.1 us -> 13.8 us
  starting transfers between devices: 23.8 us -> 22.8 us
    ppermute x8, starting transfers between devices: 16.8 us -> 13.9 us  [xor_depth(): return lax.ppermute(value, 'depth', [(i, i ^ bits) for i in range(32)])]
    ppermute x8, waiting for transfers between devices: 10.3 us -> 13.1 us  [xor_depth(): return lax.ppermute(value, 'depth', [(i, i ^ bits) for i in range(32)])]
    ppermute x1, starting transfers between devices: 2.48 us -> 4.38 us  [on_device(): lax.ppermute(lax.optimization_barrier((densities, line_b))[0], 'depth', [...]
  transfers between devices with their start and end apart: 12 -> 12, of which waited for: 8 -> 7; matrix products, arithmetic and copies ran while one was open for 0% -> 0% of each run, Pallas kernels for 13% -> 12%
where the time goes in v7:
time: 49.4 us; the launch traced here: 49.3 us
  starting transfers between devices  22.8 us (46%)
  waiting for transfers between devices  13.8 us (28%)
  Pallas kernels  12.4 us (25%)
    ppermute x8, starting transfers between devices, xor_depth(): return lax.ppermute(value, 'depth', [(i, i ^ bits) for i in range(32)])  13.9 us
    ppermute x8, waiting for transfers between devices, xor_depth(): return lax.ppermute(value, 'depth', [(i, i ^ bits) for i in range(32)])  13.1 us
    pallas_call x9, Pallas kernels, call(): pl.pallas_call(body, out_shape=outs, in_specs=[pl.BlockSpec(memory_space=...  12.4 us
    ppermute x3, starting transfers between devices, xor_lat(): return lax.ppermute(value, 'lat', [(i, i ^ bits) for i in range(8)])  4.52 us
    ppermute x1, starting transfers between devices, on_device(): lax.ppermute(lax.optimization_barrier((densities, line_b))[0], 'depth', [...  4.38 us
  transfers between devices with their start and end apart: 12, of which 7 were waited for; matrix products, arithmetic and copies ran while one was open for 0% of the time, Pallas kernels for 12%

profile of v7, /device:TPU:32, one launch (start us, length us, event | category | flops | bytes accessed | tf_op | source)
XLA Modules:
  0.0 49.3 jit_solution(10423298764807672657)
XLA Ops:
  0.0 0.1 collective-permute-start
  0.1 2.2 %react.1 = (f32[32,64]{1,0:T(8,128)S(1)}, f32[64,128]{1,0:T(8,128)S(1)}) custom-call(f32[32,4096]{1,0:T(8,128)} %bitcast.21, f32[32,64]{1,0:T(8,128)} %bitcast.12, f32[32,64]{1,0:T(8,128)} %bitcast.22, f32[32,64]{1,0:T(8,128)} %bitcast.14, s32[8,8]{1,0:T(8,128)} %pat_hbm.1), custom_call_target="tpu_custom_call" | custom-call | flops 1073741824 | bytes 65536 | tf_op jit(solution)/shard_map/react/pallas_call | solution.py:442
  2.3 0.0 collective-permute-done.a_ref
  2.3 1.6 %collective-permute-start.1 = (f32[2,32,64]{2,1,0:T(8,128)S(1)}, f32[2,32,64]{2,1,0:T(8,128)S(1)}, u32[]{:S(2)}, u32[]{:S(2)}) collective-permute-start(f32[2,32,64]{2,1,0:T(8,128)S(1)} %pad_maximum_fusion.1), channel_id=1, source_target_pairs={{0,2},{1,3},{2,0},{3,1},{4,6},{5,7},{6,4},{7,5},{8,10},{9,11},{10,... | collective-permute-start | bytes 49160 | tf_op jit(solution)/shard_map/ppermute | solution.py:469
  3.9 1.6 %tree_leaves.1 = (bf16[16,4,64,256]{3,2,1,0:T(8,128)(2,1)S(1)}, bf16[16,3,64,128]{3,2,1,0:T(8,128)(2,1)S(1)}, f32[16,3,64,128]{3,2,1,0:T(8,128)S(1)}, f32[2,64,128]{2,1,0:T(8,128)S(1)}) custom-call(f32[1024,128]{1,0:T(8,128)S(1)} %bitcast.20, f32[32,64]{1,0:T(8,128)S(1)} %bitcast.17, f32[32,64]{1,0:T(8,128)S(1)} %get-tuple-element.33.after_ref.part_ref), custom_call_target="tpu_custom_call" | custom-call | flops 2147483648 | bytes 65536 | tf_op jit(solution)/shard_map/tree_leaves/pallas_call | solution.py:442
  5.6 0.3 collective-permute-start.3
  5.9 0.5 collective-permute-done.1.b_ref
  6.3 2.8 %collective-permute-start.2 = (f32[4,32,64]{2,1,0:T(8,128)S(1)}, f32[4,32,64]{2,1,0:T(8,128)S(1)}, u32[]{:S(2)}, u32[]{:S(2)}) collective-permute-start(f32[4,32,64]{2,1,0:T(8,128)S(1)} %pad_maximum_fusion), channel_id=1, source_target_pairs={{0,6},{1,7},{2,4},{3,5},{4,2},{5,3},{6,0},{7,1},{8,14},{9,15},{10,... | collective-permute-start | bytes 98312 | tf_op jit(solution)/shard_map/ppermute | solution.py:469
  9.2 4.4 %collective-permute-start.4 = (f32[1,32,64]{2,1,0:T(8,128)S(1)}, f32[1,32,64]{2,1,0:T(8,128)S(1)}, u32[]{:S(2)}, u32[]{:S(2)}) collective-permute-start(f32[1,32,64]{2,1,0:T(8,128)S(1)} %copy-done), channel_id=1, source_target_pairs={{8,16},{16,8},{24,32},{32,24},{40,48},{48,40},{56,64},{64,56},{72,... | collective-permute-start | bytes 24584 | tf_op jit(solution)/shard_map/ppermute | solution.py:487
  13.6 0.0 copy-start.1
  13.6 0.0 copy-start.2
  13.6 0.0 copy-start.4
  13.6 1.4 %tree_upper.1 = (bf16[8,4,64,128]{3,2,1,0:T(8,128)(2,1)S(1)}, bf16[4,4,64,128]{3,2,1,0:T(8,128)(2,1)S(1)}, bf16[2,4,64,128]{3,2,1,0:T(8,128)(2,1)S(1)}, bf16[1,64,128]{2,1,0:T(8,128)(2,1)S(1)}, f32[128,128]{1,0:T(8,128)S(1)}) custom-call(bf16[16,3,64,128]{3,2,1,0:T(8,128)(2,1)S(1)} %get-tuple-element.39.n1_ref, ...), custom_call_target="tpu_custom_call" | custom-call | flops 2147483648 | bytes 65536 | tf_op jit(solution)/shard_map/tree_upper/pallas_call | solution.py:442
  15.0 0.3 collective-permute-done.4.odd_ref
  15.3 2.2 %upsweep.1 = (f32[128,128]{1,0:T(8,128)S(1)}, f32[4,64,128]{2,1,0:T(8,128)S(1)}, f32[7,64,128]{2,1,0:T(8,128)S(1)}, f32[7,64,128]{2,1,0:T(8,128)S(1)}) custom-call(s32[1,4]{1,0:T(1,128)S(1)} %copy-done.4, f32[32,64]{1,0:T(8,128)S(1)} %get-tuple-element.33.after_ref.part_ref, f32[1,32,64]{2,1,0:T(8,128)S(1)} %collective-permute-done.a_ref, ...), custom_call_target="tpu_custom_call" | custom-call | flops 33554432 | bytes 65536 | tf_op jit(solution)/shard_map/upsweep/pallas_call | solution.py:442
  17.5 0.1 collective-permute-start.5
  17.6 4.1 %collective-permute-start.6 = (f32[128,128]{1,0:T(8,128)S(1)}, f32[128,128]{1,0:T(8,128)S(1)}, u32[]{:S(2)}, u32[]{:S(2)}) collective-permute-start(f32[128,128]{1,0:T(8,128)S(1)} %get-tuple-element.46.refs_0_), channel_id=1, source_target_pairs={{0,16},{8,24},{16,0},{24,8},{32,48},{40,56},{48,32},{56,40},{64,80... | collective-permute-start | bytes 196616 | tf_op jit(solution)/shard_map/ppermute | solution.py:472
  21.7 0.5 collective-permute-start.7
  22.1 2.5 %collective-permute-done.6.refs_2_ = f32[128,128]{1,0:T(8,128)S(1)} collective-permute-done((f32[128,128]{1,0:T(8,128)S(1)}, f32[128,128]{1,0:T(8,128)S(1)}, u32[]{:S(2)}, u32[]{:S(2)}) %collective-permute-start.6) | collective-permute-done | bytes 65568 | tf_op jit(solution)/shard_map/ppermute | solution.py:472
  24.6 1.9 %collective-permute-done.7.refs_3_ = f32[128,128]{1,0:T(8,128)S(1)} collective-permute-done((f32[128,128]{1,0:T(8,128)S(1)}, f32[128,128]{1,0:T(8,128)S(1)}, u32[]{:S(2)}, u32[]{:S(2)}) %collective-permute-start.7) | collective-permute-done | bytes 65568 | tf_op jit(solution)/shard_map/ppermute | solution.py:472
  26.5 1.0 %combine_low.1 = (f32[128,128]{1,0:T(8,128)S(1)}, f32[128,128]{1,0:T(8,128)S(1)}) custom-call(f32[128,128]{1,0:T(8,128)S(1)} %get-tuple-element.46.refs_0_, f32[128,128]{1,0:T(8,128)S(1)} %collective-permute-done.5.refs_1_, f32[128,128]{1,0:T(8,128)S(1)} %collective-permute-done.6.refs_2_, f32[128,128]{1,0:T(8,128)S(1)} %collective-permute-done.7.refs_3_), custom_call_target="tpu_custom_call" | custom-call | flops 16777216 | bytes 65536 | tf_op jit(solution)/shard_map/combine_low/pallas_call | solution.py:442
  27.4 6.0 %collective-permute-start.10 = (f32[128,128]{1,0:T(8,128)S(1)}, f32[128,128]{1,0:T(8,128)S(1)}, u32[]{:S(2)}, u32[]{:S(2)}) collective-permute-start(f32[128,128]{1,0:T(8,128)S(1)} %get-tuple-element.47.refs_0_), channel_id=1, source_target_pairs={{0,120},{8,112},{16,104},{24,96},{32,88},{40,80},{48,72},{56,64},{... | collective-permute-start | bytes 196616 | tf_op jit(solution)/shard_map/ppermute | solution.py:472
  33.5 0.5 collective-permute-start.8
  33.9 0.2 collective-permute-start.9
  34.1 0.7 %prepare.1 = (bf16[15,64,128]{2,1,0:T(8,128)(2,1)S(1)}, f32[4,64,128]{2,1,0:T(8,128)S(1)}, f32[4,64,128]{2,1,0:T(8,128)S(1)}, f32[64,128]{1,0:T(8,128)S(1)}) custom-call(f32[4,64,128]{2,1,0:T(8,128)S(1)} %get-tuple-element.54.pair_ref, f32[7,64,128]{2,1,0:T(8,128)S(1)} %get-tuple-element.55.v_ref, f32[7,64,128]{2,1,0:T(8,128)S(1)} %get-tuple-element.56.w_ref, ...), custom_call_target="tpu_custom_call" | custom-call | flops 1073741824 | bytes 65536 | tf_op jit(solution)/shard_map/prepare/pallas_call | solution.py:442
  34.8 1.0 %collective-permute-done.10.refs_3_ = f32[128,128]{1,0:T(8,128)S(1)} collective-permute-done((f32[128,128]{1,0:T(8,128)S(1)}, f32[128,128]{1,0:T(8,128)S(1)}, u32[]{:S(2)}, u32[]{:S(2)}) %collective-permute-start.10) | collective-permute-done | bytes 65568 | tf_op jit(solution)/shard_map/ppermute | solution.py:472
  35.9 4.9 %collective-permute-done.8.refs_1_ = f32[128,128]{1,0:T(8,128)S(1)} collective-permute-done((f32[128,128]{1,0:T(8,128)S(1)}, f32[128,128]{1,0:T(8,128)S(1)}, u32[]{:S(2)}, u32[]{:S(2)}) %collective-permute-start.8) | collective-permute-done | bytes 65568 | tf_op jit(solution)/shard_map/ppermute | solution.py:472
  40.8 0.9 %combine_high.1 = (f32[64,128]{1,0:T(8,128)S(1)}, f32[128,128]{1,0:T(8,128)S(1)}) custom-call(f32[128,128]{1,0:T(8,128)S(1)} %get-tuple-element.47.refs_0_, f32[128,128]{1,0:T(8,128)S(1)} %collective-permute-done.8.refs_1_, f32[128,128]{1,0:T(8,128)S(1)} %collective-permute-done.9.refs_2_, f32[128,128]{1,0:T(8,128)S(1)} %collective-permute-done.10.refs_3_, ...), custom_call_target="tpu_custom_call" | custom-call | flops 16777216 | bytes 65536 | tf_op jit(solution)/shard_map/combine_high/pallas_call | solution.py:442
  41.7 2.3 %collective-permute-start.11 = (f32[64,128]{1,0:T(8,128)S(1)}, f32[64,128]{1,0:T(8,128)S(1)}, u32[]{:S(2)}, u32[]{:S(2)}) collective-permute-start(f32[64,128]{1,0:T(8,128)S(1)} %get-tuple-element.49.own_ref), channel_id=1, source_target_pairs={{0,192},{8,200},{16,208},{24,216},{32,224},{40,232},{48,240},{56,2... | collective-permute-start | bytes 98312 | tf_op jit(solution)/shard_map/ppermute | solution.py:472
  44.0 0.1 prepare_last.1
  44.1 2.8 %collective-permute-done.11.other_ref = f32[64,128]{1,0:T(8,128)S(1)} collective-permute-done((f32[64,128]{1,0:T(8,128)S(1)}, f32[64,128]{1,0:T(8,128)S(1)}, u32[]{:S(2)}, u32[]{:S(2)}) %collective-permute-start.11) | collective-permute-done | bytes 32800 | tf_op jit(solution)/shard_map/ppermute | solution.py:472
  46.9 2.4 %downsweep.1 = f32[32,64]{1,0:T(8,128)} custom-call(f32[64,128]{1,0:T(8,128)S(1)} %collective-permute-done.11.other_ref, bf16[2,64,128]{2,1,0:T(8,128)(2,1)S(1)} %get-tuple-element.51.maps_ref, f32[2,64,128]{2,1,0:T(8,128)S(1)} %get-tuple-element.52.vecs_ref, bf16[2,256,128]{2,1,0:T(8,128)(2,1)S(1)} %get-tuple-element.53.own_rhs, ...), custom_call_target="tpu_custom_call" | custom-call | flops 33554432 | bytes 65536 | tf_op jit(solution)/shard_map/downsweep/pallas_call | solution.py:442
  (15 shorter events, 0.0 us)
Async XLA Ops:
  0.0 2.3 %copy-start = (f32[1,32,64]{2,1,0:T(8,128)S(1)}, f32[1,32,64]{2,1,0:T(8,128)}, u32[]{:S(2)}) copy-start(f32[1,32,64]{2,1,0:T(8,128)} %param.9) | copy-start | bytes 24580
  0.0 3.9 %copy-start.3 = (f32[1,32,64]{2,1,0:T(8,128)S(1)}, f32[1,32,64]{2,1,0:T(8,128)}, u32[]{:S(2)}) copy-start(f32[1,32,64]{2,1,0:T(8,128)} %param.17) | copy-start | bytes 24580
  0.0 3.9 %copy-start.5 = (f32[1,32,4096]{2,1,0:T(8,128)S(1)}, f32[1,32,4096]{2,1,0:T(8,128)}, u32[]{:S(2)}) copy-start(f32[1,32,4096]{2,1,0:T(8,128)} %param.16) | copy-start | bytes 1572868
  0.0 2.3 %collective-permute-start = (f32[1,32,64]{2,1,0:T(8,128)}, f32[1,32,64]{2,1,0:T(8,128)S(1)}, u32[]{:S(2)}, u32[]{:S(2)}) collective-permute-start(f32[1,32,64]{2,1,0:T(8,128)} %param.9), channel_id=1, source_target_pairs={{0,1},{1,0},{2,3},{3,2},{4,5},{5,4},{6,7},{7,6},{8,9},{9,8},{10,11... | collective-permute-start | bytes 24584 | tf_op jit(solution)/shard_map/ppermute | solution.py:469
  2.3 4.0 %collective-permute-start.1 = (f32[2,32,64]{2,1,0:T(8,128)S(1)}, f32[2,32,64]{2,1,0:T(8,128)S(1)}, u32[]{:S(2)}, u32[]{:S(2)}) collective-permute-start(f32[2,32,64]{2,1,0:T(8,128)S(1)} %pad_maximum_fusion.1), channel_id=1, source_target_pairs={{0,2},{1,3},{2,0},{3,1},{4,6},{5,7},{6,4},{7,5},{8,10},{9,11},{10,... | collective-permute-start | bytes 49160 | tf_op jit(solution)/shard_map/ppermute | solution.py:469
  5.6 9.4 %collective-permute-start.3 = (f32[1,32,64]{2,1,0:T(8,128)S(1)}, f32[1,32,64]{2,1,0:T(8,128)S(1)}, u32[]{:S(2)}, u32[]{:S(2)}) collective-permute-start(f32[1,32,64]{2,1,0:T(8,128)S(1)} %copy-done), channel_id=1, source_target_pairs={{0,8},{8,0},{16,24},{24,16},{32,40},{40,32},{48,56},{56,48},{64,72... | collective-permute-start | bytes 24584 | tf_op jit(solution)/shard_map/ppermute | solution.py:472
  6.3 8.9 %collective-permute-start.2 = (f32[4,32,64]{2,1,0:T(8,128)S(1)}, f32[4,32,64]{2,1,0:T(8,128)S(1)}, u32[]{:S(2)}, u32[]{:S(2)}) collective-permute-start(f32[4,32,64]{2,1,0:T(8,128)S(1)} %pad_maximum_fusion), channel_id=1, source_target_pairs={{0,6},{1,7},{2,4},{3,5},{4,2},{5,3},{6,0},{7,1},{8,14},{9,15},{10,... | collective-permute-start | bytes 98312 | tf_op jit(solution)/shard_map/ppermute | solution.py:469
  9.2 6.1 %collective-permute-start.4 = (f32[1,32,64]{2,1,0:T(8,128)S(1)}, f32[1,32,64]{2,1,0:T(8,128)S(1)}, u32[]{:S(2)}, u32[]{:S(2)}) collective-permute-start(f32[1,32,64]{2,1,0:T(8,128)S(1)} %copy-done), channel_id=1, source_target_pairs={{8,16},{16,8},{24,32},{32,24},{40,48},{48,40},{56,64},{64,56},{72,... | collective-permute-start | bytes 24584 | tf_op jit(solution)/shard_map/ppermute | solution.py:487
  13.6 1.7 %copy-start.1 = (f32[1,32,64]{2,1,0:T(8,128)S(1)}, f32[1,32,64]{2,1,0:T(8,128)}, u32[]{:S(2)}) copy-start(f32[1,32,64]{2,1,0:T(8,128)} %param.13) | copy-start | bytes 24580
  13.6 1.7 %copy-start.2 = (f32[1,32,64]{2,1,0:T(8,128)S(1)}, f32[1,32,64]{2,1,0:T(8,128)}, u32[]{:S(2)}) copy-start(f32[1,32,64]{2,1,0:T(8,128)} %param.14) | copy-start | bytes 24580
  13.6 1.7 %copy-start.4 = (s32[1,4]{1,0:T(1,128)S(1)}, s32[1,4]{1,0:T(1,128)}, u32[]{:S(2)}) copy-start(s32[1,4]{1,0:T(1,128)} %neigh_ref.1) | copy-start | bytes 52
  17.5 4.7 %collective-permute-start.5 = (f32[128,128]{1,0:T(8,128)S(1)}, f32[128,128]{1,0:T(8,128)S(1)}, u32[]{:S(2)}, u32[]{:S(2)}) collective-permute-start(f32[128,128]{1,0:T(8,128)S(1)} %get-tuple-element.46.refs_0_), channel_id=1, source_target_pairs={{0,8},{8,0},{16,24},{24,16},{32,40},{40,32},{48,56},{56,48},{64,72... | collective-permute-start | bytes 196616 | tf_op jit(solution)/shard_map/ppermute | solution.py:472
  17.6 7.0 %collective-permute-start.6 = (f32[128,128]{1,0:T(8,128)S(1)}, f32[128,128]{1,0:T(8,128)S(1)}, u32[]{:S(2)}, u32[]{:S(2)}) collective-permute-start(f32[128,128]{1,0:T(8,128)S(1)} %get-tuple-element.46.refs_0_), channel_id=1, source_target_pairs={{0,16},{8,24},{16,0},{24,8},{32,48},{40,56},{48,32},{56,40},{64,80... | collective-permute-start | bytes 196616 | tf_op jit(solution)/shard_map/ppermute | solution.py:472
  21.7 4.8 %collective-permute-start.7 = (f32[128,128]{1,0:T(8,128)S(1)}, f32[128,128]{1,0:T(8,128)S(1)}, u32[]{:S(2)}, u32[]{:S(2)}) collective-permute-start(f32[128,128]{1,0:T(8,128)S(1)} %get-tuple-element.46.refs_0_), channel_id=1, source_target_pairs={{0,24},{8,16},{16,8},{24,0},{32,56},{40,48},{48,40},{56,32},{64,88... | collective-permute-start | bytes 196616 | tf_op jit(solution)/shard_map/ppermute | solution.py:472
  27.4 8.4 %collective-permute-start.10 = (f32[128,128]{1,0:T(8,128)S(1)}, f32[128,128]{1,0:T(8,128)S(1)}, u32[]{:S(2)}, u32[]{:S(2)}) collective-permute-start(f32[128,128]{1,0:T(8,128)S(1)} %get-tuple-element.47.refs_0_), channel_id=1, source_target_pairs={{0,120},{8,112},{16,104},{24,96},{32,88},{40,80},{48,72},{56,64},{... | collective-permute-start | bytes 196616 | tf_op jit(solution)/shard_map/ppermute | solution.py:472
  33.5 7.3 %collective-permute-start.8 = (f32[128,128]{1,0:T(8,128)S(1)}, f32[128,128]{1,0:T(8,128)S(1)}, u32[]{:S(2)}, u32[]{:S(2)}) collective-permute-start(f32[128,128]{1,0:T(8,128)S(1)} %get-tuple-element.47.refs_0_), channel_id=1, source_target_pairs={{0,56},{8,48},{16,40},{24,32},{32,24},{40,16},{48,8},{56,0},{64,12... | collective-permute-start | bytes 196616 | tf_op jit(solution)/shard_map/ppermute | solution.py:472
  33.9 6.8 %collective-permute-start.9 = (f32[128,128]{1,0:T(8,128)S(1)}, f32[128,128]{1,0:T(8,128)S(1)}, u32[]{:S(2)}, u32[]{:S(2)}) collective-permute-start(f32[128,128]{1,0:T(8,128)S(1)} %get-tuple-element.47.refs_0_), channel_id=1, source_target_pairs={{0,64},{8,72},{16,80},{24,88},{32,96},{40,104},{48,112},{56,120},{... | collective-permute-start | bytes 196616 | tf_op jit(solution)/shard_map/ppermute | solution.py:472
  41.7 5.2 %collective-permute-start.11 = (f32[64,128]{1,0:T(8,128)S(1)}, f32[64,128]{1,0:T(8,128)S(1)}, u32[]{:S(2)}, u32[]{:S(2)}) collective-permute-start(f32[64,128]{1,0:T(8,128)S(1)} %get-tuple-element.49.own_ref), channel_id=1, source_target_pairs={{0,192},{8,200},{16,208},{24,216},{32,224},{40,232},{48,240},{56,2... | collective-permute-start | bytes 98312 | tf_op jit(solution)/shard_map/ppermute | solution.py:472

commit v8 on v7

--- a/solution.py
+++ b/solution.py
@@ -486,7 +486,7 @@
     top_even = xor_depth(lax.optimization_barrier((densities, cols))[0], 1)
     top_odd = lax.ppermute(
         lax.optimization_barrier((densities, line_b))[0], "depth",
-        [(i, i + 1 if i % 2 else i - 1) for i in range(1, 31)],
+        [(i, i if i in (0, 31) else i + 1 if i % 2 else i - 1) for i in range(32)],
     )
     line_c = xor_lat(jnp.concatenate([densities, line_a, line_b], axis=0), 6)
     n2, n3, n4, n5, root = call(

time: 49.4 us -> 49.4 us (level)
  no operation moved by 1% of the time
where the time goes in v8:
time: 49.4 us; the launch traced here: 49.3 us
  starting transfers between devices  22.8 us (46%)
  waiting for transfers between devices  13.8 us (28%)
  Pallas kernels  12.4 us (25%)
    ppermute x8, starting transfers between devices, xor_depth(): return lax.ppermute(value, 'depth', [(i, i ^ bits) for i in range(32)])  13.9 us
    ppermute x8, waiting for transfers between devices, xor_depth(): return lax.ppermute(value, 'depth', [(i, i ^ bits) for i in range(32)])  13.1 us
    pallas_call x9, Pallas kernels, call(): pl.pallas_call(body, out_shape=outs, in_specs=[pl.BlockSpec(memory_space=...  12.4 us
    ppermute x3, starting transfers between devices, xor_lat(): return lax.ppermute(value, 'lat', [(i, i ^ bits) for i in range(8)])  4.52 us
    ppermute x1, starting transfers between devices, on_device(): lax.ppermute(lax.optimization_barrier((densities, line_b))[0], 'depth', [...  4.38 us
  transfers between devices with their start and end apart: 12, of which 7 were waited for; matrix products, arithmetic and copies ran while one was open for 0% of the time, Pallas kernels for 12%

profile of v8, /device:TPU:32, one launch (start us, length us, event | category | flops | bytes accessed | tf_op | source)
XLA Modules:
  0.0 49.3 jit_solution(15443785067214320604)
XLA Ops:
  0.0 0.1 collective-permute-start
  0.1 2.2 %react.1 = (f32[32,64]{1,0:T(8,128)S(1)}, f32[64,128]{1,0:T(8,128)S(1)}) custom-call(f32[32,4096]{1,0:T(8,128)} %bitcast.21, f32[32,64]{1,0:T(8,128)} %bitcast.12, f32[32,64]{1,0:T(8,128)} %bitcast.22, f32[32,64]{1,0:T(8,128)} %bitcast.14, s32[8,8]{1,0:T(8,128)} %pat_hbm.1), custom_call_target="tpu_custom_call" | custom-call | flops 1073741824 | bytes 65536 | tf_op jit(solution)/shard_map/react/pallas_call | solution.py:442
  2.3 0.0 collective-permute-done.a_ref
  2.3 1.6 %collective-permute-start.1 = (f32[2,32,64]{2,1,0:T(8,128)S(1)}, f32[2,32,64]{2,1,0:T(8,128)S(1)}, u32[]{:S(2)}, u32[]{:S(2)}) collective-permute-start(f32[2,32,64]{2,1,0:T(8,128)S(1)} %pad_maximum_fusion.1), channel_id=1, source_target_pairs={{0,2},{1,3},{2,0},{3,1},{4,6},{5,7},{6,4},{7,5},{8,10},{9,11},{10,... | collective-permute-start | bytes 49160 | tf_op jit(solution)/shard_map/ppermute | solution.py:469
  3.9 1.6 %tree_leaves.1 = (bf16[16,4,64,256]{3,2,1,0:T(8,128)(2,1)S(1)}, bf16[16,3,64,128]{3,2,1,0:T(8,128)(2,1)S(1)}, f32[16,3,64,128]{3,2,1,0:T(8,128)S(1)}, f32[2,64,128]{2,1,0:T(8,128)S(1)}) custom-call(f32[1024,128]{1,0:T(8,128)S(1)} %bitcast.20, f32[32,64]{1,0:T(8,128)S(1)} %bitcast.17, f32[32,64]{1,0:T(8,128)S(1)} %get-tuple-element.33.after_ref.part_ref), custom_call_target="tpu_custom_call" | custom-call | flops 2147483648 | bytes 65536 | tf_op jit(solution)/shard_map/tree_leaves/pallas_call | solution.py:442
  5.6 0.3 collective-permute-start.3
  5.9 0.5 collective-permute-done.1.b_ref
  6.3 2.8 %collective-permute-start.2 = (f32[4,32,64]{2,1,0:T(8,128)S(1)}, f32[4,32,64]{2,1,0:T(8,128)S(1)}, u32[]{:S(2)}, u32[]{:S(2)}) collective-permute-start(f32[4,32,64]{2,1,0:T(8,128)S(1)} %pad_maximum_fusion), channel_id=1, source_target_pairs={{0,6},{1,7},{2,4},{3,5},{4,2},{5,3},{6,0},{7,1},{8,14},{9,15},{10,... | collective-permute-start | bytes 98312 | tf_op jit(solution)/shard_map/ppermute | solution.py:469
  9.2 4.4 %collective-permute-start.4 = (f32[1,32,64]{2,1,0:T(8,128)S(1)}, f32[1,32,64]{2,1,0:T(8,128)S(1)}, u32[]{:S(2)}, u32[]{:S(2)}) collective-permute-start(f32[1,32,64]{2,1,0:T(8,128)S(1)} %copy-done), channel_id=1, source_target_pairs={{0,0},{8,16},{16,8},{24,32},{32,24},{40,48},{48,40},{56,64},{64,56... | collective-permute-start | bytes 24584 | tf_op jit(solution)/shard_map/ppermute | solution.py:487
  13.6 0.0 copy-start.1
  13.6 0.0 copy-start.2
  13.6 0.0 copy-start.4
  13.6 1.4 %tree_upper.1 = (bf16[8,4,64,128]{3,2,1,0:T(8,128)(2,1)S(1)}, bf16[4,4,64,128]{3,2,1,0:T(8,128)(2,1)S(1)}, bf16[2,4,64,128]{3,2,1,0:T(8,128)(2,1)S(1)}, bf16[1,64,128]{2,1,0:T(8,128)(2,1)S(1)}, f32[128,128]{1,0:T(8,128)S(1)}) custom-call(bf16[16,3,64,128]{3,2,1,0:T(8,128)(2,1)S(1)} %get-tuple-element.39.n1_ref, ...), custom_call_target="tpu_custom_call" | custom-call | flops 2147483648 | bytes 65536 | tf_op jit(solution)/shard_map/tree_upper/pallas_call | solution.py:442
  15.0 0.3 collective-permute-done.4.odd_ref
  15.3 2.2 %upsweep.1 = (f32[128,128]{1,0:T(8,128)S(1)}, f32[4,64,128]{2,1,0:T(8,128)S(1)}, f32[7,64,128]{2,1,0:T(8,128)S(1)}, f32[7,64,128]{2,1,0:T(8,128)S(1)}) custom-call(s32[1,4]{1,0:T(1,128)S(1)} %copy-done.4, f32[32,64]{1,0:T(8,128)S(1)} %get-tuple-element.33.after_ref.part_ref, f32[1,32,64]{2,1,0:T(8,128)S(1)} %collective-permute-done.a_ref, ...), custom_call_target="tpu_custom_call" | custom-call | flops 33554432 | bytes 65536 | tf_op jit(solution)/shard_map/upsweep/pallas_call | solution.py:442
  17.5 0.1 collective-permute-start.5
  17.6 4.1 %collective-permute-start.6 = (f32[128,128]{1,0:T(8,128)S(1)}, f32[128,128]{1,0:T(8,128)S(1)}, u32[]{:S(2)}, u32[]{:S(2)}) collective-permute-start(f32[128,128]{1,0:T(8,128)S(1)} %get-tuple-element.46.refs_0_), channel_id=1, source_target_pairs={{0,16},{8,24},{16,0},{24,8},{32,48},{40,56},{48,32},{56,40},{64,80... | collective-permute-start | bytes 196616 | tf_op jit(solution)/shard_map/ppermute | solution.py:472
  21.7 0.5 collective-permute-start.7
  22.1 2.5 %collective-permute-done.6.refs_2_ = f32[128,128]{1,0:T(8,128)S(1)} collective-permute-done((f32[128,128]{1,0:T(8,128)S(1)}, f32[128,128]{1,0:T(8,128)S(1)}, u32[]{:S(2)}, u32[]{:S(2)}) %collective-permute-start.6) | collective-permute-done | bytes 65568 | tf_op jit(solution)/shard_map/ppermute | solution.py:472
  24.6 1.9 %collective-permute-done.7.refs_3_ = f32[128,128]{1,0:T(8,128)S(1)} collective-permute-done((f32[128,128]{1,0:T(8,128)S(1)}, f32[128,128]{1,0:T(8,128)S(1)}, u32[]{:S(2)}, u32[]{:S(2)}) %collective-permute-start.7) | collective-permute-done | bytes 65568 | tf_op jit(solution)/shard_map/ppermute | solution.py:472
  26.5 1.0 %combine_low.1 = (f32[128,128]{1,0:T(8,128)S(1)}, f32[128,128]{1,0:T(8,128)S(1)}) custom-call(f32[128,128]{1,0:T(8,128)S(1)} %get-tuple-element.46.refs_0_, f32[128,128]{1,0:T(8,128)S(1)} %collective-permute-done.5.refs_1_, f32[128,128]{1,0:T(8,128)S(1)} %collective-permute-done.6.refs_2_, f32[128,128]{1,0:T(8,128)S(1)} %collective-permute-done.7.refs_3_), custom_call_target="tpu_custom_call" | custom-call | flops 16777216 | bytes 65536 | tf_op jit(solution)/shard_map/combine_low/pallas_call | solution.py:442
  27.4 6.0 %collective-permute-start.10 = (f32[128,128]{1,0:T(8,128)S(1)}, f32[128,128]{1,0:T(8,128)S(1)}, u32[]{:S(2)}, u32[]{:S(2)}) collective-permute-start(f32[128,128]{1,0:T(8,128)S(1)} %get-tuple-element.47.refs_0_), channel_id=1, source_target_pairs={{0,120},{8,112},{16,104},{24,96},{32,88},{40,80},{48,72},{56,64},{... | collective-permute-start | bytes 196616 | tf_op jit(solution)/shard_map/ppermute | solution.py:472
  33.5 0.5 collective-permute-start.8
  33.9 0.2 collective-permute-start.9
  34.1 0.7 %prepare.1 = (bf16[15,64,128]{2,1,0:T(8,128)(2,1)S(1)}, f32[4,64,128]{2,1,0:T(8,128)S(1)}, f32[4,64,128]{2,1,0:T(8,128)S(1)}, f32[64,128]{1,0:T(8,128)S(1)}) custom-call(f32[4,64,128]{2,1,0:T(8,128)S(1)} %get-tuple-element.54.pair_ref, f32[7,64,128]{2,1,0:T(8,128)S(1)} %get-tuple-element.55.v_ref, f32[7,64,128]{2,1,0:T(8,128)S(1)} %get-tuple-element.56.w_ref, ...), custom_call_target="tpu_custom_call" | custom-call | flops 1073741824 | bytes 65536 | tf_op jit(solution)/shard_map/prepare/pallas_call | solution.py:442
  34.8 1.0 %collective-permute-done.10.refs_3_ = f32[128,128]{1,0:T(8,128)S(1)} collective-permute-done((f32[128,128]{1,0:T(8,128)S(1)}, f32[128,128]{1,0:T(8,128)S(1)}, u32[]{:S(2)}, u32[]{:S(2)}) %collective-permute-start.10) | collective-permute-done | bytes 65568 | tf_op jit(solution)/shard_map/ppermute | solution.py:472
  35.9 4.9 %collective-permute-done.8.refs_1_ = f32[128,128]{1,0:T(8,128)S(1)} collective-permute-done((f32[128,128]{1,0:T(8,128)S(1)}, f32[128,128]{1,0:T(8,128)S(1)}, u32[]{:S(2)}, u32[]{:S(2)}) %collective-permute-start.8) | collective-permute-done | bytes 65568 | tf_op jit(solution)/shard_map/ppermute | solution.py:472
  40.8 0.9 %combine_high.1 = (f32[64,128]{1,0:T(8,128)S(1)}, f32[128,128]{1,0:T(8,128)S(1)}) custom-call(f32[128,128]{1,0:T(8,128)S(1)} %get-tuple-element.47.refs_0_, f32[128,128]{1,0:T(8,128)S(1)} %collective-permute-done.8.refs_1_, f32[128,128]{1,0:T(8,128)S(1)} %collective-permute-done.9.refs_2_, f32[128,128]{1,0:T(8,128)S(1)} %collective-permute-done.10.refs_3_, ...), custom_call_target="tpu_custom_call" | custom-call | flops 16777216 | bytes 65536 | tf_op jit(solution)/shard_map/combine_high/pallas_call | solution.py:442
  41.7 2.3 %collective-permute-start.11 = (f32[64,128]{1,0:T(8,128)S(1)}, f32[64,128]{1,0:T(8,128)S(1)}, u32[]{:S(2)}, u32[]{:S(2)}) collective-permute-start(f32[64,128]{1,0:T(8,128)S(1)} %get-tuple-element.49.own_ref), channel_id=1, source_target_pairs={{0,192},{8,200},{16,208},{24,216},{32,224},{40,232},{48,240},{56,2... | collective-permute-start | bytes 98312 | tf_op jit(solution)/shard_map/ppermute | solution.py:472
  44.0 0.1 prepare_last.1
  44.1 2.8 %collective-permute-done.11.other_ref = f32[64,128]{1,0:T(8,128)S(1)} collective-permute-done((f32[64,128]{1,0:T(8,128)S(1)}, f32[64,128]{1,0:T(8,128)S(1)}, u32[]{:S(2)}, u32[]{:S(2)}) %collective-permute-start.11) | collective-permute-done | bytes 32800 | tf_op jit(solution)/shard_map/ppermute | solution.py:472
  46.9 2.4 %downsweep.1 = f32[32,64]{1,0:T(8,128)} custom-call(f32[64,128]{1,0:T(8,128)S(1)} %collective-permute-done.11.other_ref, bf16[2,64,128]{2,1,0:T(8,128)(2,1)S(1)} %get-tuple-element.51.maps_ref, f32[2,64,128]{2,1,0:T(8,128)S(1)} %get-tuple-element.52.vecs_ref, bf16[2,256,128]{2,1,0:T(8,128)(2,1)S(1)} %get-tuple-element.53.own_rhs, ...), custom_call_target="tpu_custom_call" | custom-call | flops 33554432 | bytes 65536 | tf_op jit(solution)/shard_map/downsweep/pallas_call | solution.py:442
  (15 shorter events, 0.0 us)
Async XLA Ops:
  0.0 2.3 %copy-start = (f32[1,32,64]{2,1,0:T(8,128)S(1)}, f32[1,32,64]{2,1,0:T(8,128)}, u32[]{:S(2)}) copy-start(f32[1,32,64]{2,1,0:T(8,128)} %param.9) | copy-start | bytes 24580
  0.0 3.9 %copy-start.3 = (f32[1,32,64]{2,1,0:T(8,128)S(1)}, f32[1,32,64]{2,1,0:T(8,128)}, u32[]{:S(2)}) copy-start(f32[1,32,64]{2,1,0:T(8,128)} %param.17) | copy-start | bytes 24580
  0.0 3.9 %copy-start.5 = (f32[1,32,4096]{2,1,0:T(8,128)S(1)}, f32[1,32,4096]{2,1,0:T(8,128)}, u32[]{:S(2)}) copy-start(f32[1,32,4096]{2,1,0:T(8,128)} %param.16) | copy-start | bytes 1572868
  0.0 2.3 %collective-permute-start = (f32[1,32,64]{2,1,0:T(8,128)}, f32[1,32,64]{2,1,0:T(8,128)S(1)}, u32[]{:S(2)}, u32[]{:S(2)}) collective-permute-start(f32[1,32,64]{2,1,0:T(8,128)} %param.9), channel_id=1, source_target_pairs={{0,1},{1,0},{2,3},{3,2},{4,5},{5,4},{6,7},{7,6},{8,9},{9,8},{10,11... | collective-permute-start | bytes 24584 | tf_op jit(solution)/shard_map/ppermute | solution.py:469
  2.3 4.0 %collective-permute-start.1 = (f32[2,32,64]{2,1,0:T(8,128)S(1)}, f32[2,32,64]{2,1,0:T(8,128)S(1)}, u32[]{:S(2)}, u32[]{:S(2)}) collective-permute-start(f32[2,32,64]{2,1,0:T(8,128)S(1)} %pad_maximum_fusion.1), channel_id=1, source_target_pairs={{0,2},{1,3},{2,0},{3,1},{4,6},{5,7},{6,4},{7,5},{8,10},{9,11},{10,... | collective-permute-start | bytes 49160 | tf_op jit(solution)/shard_map/ppermute | solution.py:469
  5.6 9.4 %collective-permute-start.3 = (f32[1,32,64]{2,1,0:T(8,128)S(1)}, f32[1,32,64]{2,1,0:T(8,128)S(1)}, u32[]{:S(2)}, u32[]{:S(2)}) collective-permute-start(f32[1,32,64]{2,1,0:T(8,128)S(1)} %copy-done), channel_id=1, source_target_pairs={{0,8},{8,0},{16,24},{24,16},{32,40},{40,32},{48,56},{56,48},{64,72... | collective-permute-start | bytes 24584 | tf_op jit(solution)/shard_map/ppermute | solution.py:472
  6.3 8.9 %collective-permute-start.2 = (f32[4,32,64]{2,1,0:T(8,128)S(1)}, f32[4,32,64]{2,1,0:T(8,128)S(1)}, u32[]{:S(2)}, u32[]{:S(2)}) collective-permute-start(f32[4,32,64]{2,1,0:T(8,128)S(1)} %pad_maximum_fusion), channel_id=1, source_target_pairs={{0,6},{1,7},{2,4},{3,5},{4,2},{5,3},{6,0},{7,1},{8,14},{9,15},{10,... | collective-permute-start | bytes 98312 | tf_op jit(solution)/shard_map/ppermute | solution.py:469
  9.2 6.1 %collective-permute-start.4 = (f32[1,32,64]{2,1,0:T(8,128)S(1)}, f32[1,32,64]{2,1,0:T(8,128)S(1)}, u32[]{:S(2)}, u32[]{:S(2)}) collective-permute-start(f32[1,32,64]{2,1,0:T(8,128)S(1)} %copy-done), channel_id=1, source_target_pairs={{0,0},{8,16},{16,8},{24,32},{32,24},{40,48},{48,40},{56,64},{64,56... | collective-permute-start | bytes 24584 | tf_op jit(solution)/shard_map/ppermute | solution.py:487
  13.6 1.7 %copy-start.1 = (f32[1,32,64]{2,1,0:T(8,128)S(1)}, f32[1,32,64]{2,1,0:T(8,128)}, u32[]{:S(2)}) copy-start(f32[1,32,64]{2,1,0:T(8,128)} %param.13) | copy-start | bytes 24580
  13.6 1.7 %copy-start.2 = (f32[1,32,64]{2,1,0:T(8,128)S(1)}, f32[1,32,64]{2,1,0:T(8,128)}, u32[]{:S(2)}) copy-start(f32[1,32,64]{2,1,0:T(8,128)} %param.14) | copy-start | bytes 24580
  13.6 1.7 %copy-start.4 = (s32[1,4]{1,0:T(1,128)S(1)}, s32[1,4]{1,0:T(1,128)}, u32[]{:S(2)}) copy-start(s32[1,4]{1,0:T(1,128)} %neigh_ref.1) | copy-start | bytes 52
  17.5 4.7 %collective-permute-start.5 = (f32[128,128]{1,0:T(8,128)S(1)}, f32[128,128]{1,0:T(8,128)S(1)}, u32[]{:S(2)}, u32[]{:S(2)}) collective-permute-start(f32[128,128]{1,0:T(8,128)S(1)} %get-tuple-element.46.refs_0_), channel_id=1, source_target_pairs={{0,8},{8,0},{16,24},{24,16},{32,40},{40,32},{48,56},{56,48},{64,72... | collective-permute-start | bytes 196616 | tf_op jit(solution)/shard_map/ppermute | solution.py:472
  17.6 7.0 %collective-permute-start.6 = (f32[128,128]{1,0:T(8,128)S(1)}, f32[128,128]{1,0:T(8,128)S(1)}, u32[]{:S(2)}, u32[]{:S(2)}) collective-permute-start(f32[128,128]{1,0:T(8,128)S(1)} %get-tuple-element.46.refs_0_), channel_id=1, source_target_pairs={{0,16},{8,24},{16,0},{24,8},{32,48},{40,56},{48,32},{56,40},{64,80... | collective-permute-start | bytes 196616 | tf_op jit(solution)/shard_map/ppermute | solution.py:472
  21.7 4.8 %collective-permute-start.7 = (f32[128,128]{1,0:T(8,128)S(1)}, f32[128,128]{1,0:T(8,128)S(1)}, u32[]{:S(2)}, u32[]{:S(2)}) collective-permute-start(f32[128,128]{1,0:T(8,128)S(1)} %get-tuple-element.46.refs_0_), channel_id=1, source_target_pairs={{0,24},{8,16},{16,8},{24,0},{32,56},{40,48},{48,40},{56,32},{64,88... | collective-permute-start | bytes 196616 | tf_op jit(solution)/shard_map/ppermute | solution.py:472
  27.4 8.4 %collective-permute-start.10 = (f32[128,128]{1,0:T(8,128)S(1)}, f32[128,128]{1,0:T(8,128)S(1)}, u32[]{:S(2)}, u32[]{:S(2)}) collective-permute-start(f32[128,128]{1,0:T(8,128)S(1)} %get-tuple-element.47.refs_0_), channel_id=1, source_target_pairs={{0,120},{8,112},{16,104},{24,96},{32,88},{40,80},{48,72},{56,64},{... | collective-permute-start | bytes 196616 | tf_op jit(solution)/shard_map/ppermute | solution.py:472
  33.5 7.3 %collective-permute-start.8 = (f32[128,128]{1,0:T(8,128)S(1)}, f32[128,128]{1,0:T(8,128)S(1)}, u32[]{:S(2)}, u32[]{:S(2)}) collective-permute-start(f32[128,128]{1,0:T(8,128)S(1)} %get-tuple-element.47.refs_0_), channel_id=1, source_target_pairs={{0,56},{8,48},{16,40},{24,32},{32,24},{40,16},{48,8},{56,0},{64,12... | collective-permute-start | bytes 196616 | tf_op jit(solution)/shard_map/ppermute | solution.py:472
  33.9 6.8 %collective-permute-start.9 = (f32[128,128]{1,0:T(8,128)S(1)}, f32[128,128]{1,0:T(8,128)S(1)}, u32[]{:S(2)}, u32[]{:S(2)}) collective-permute-start(f32[128,128]{1,0:T(8,128)S(1)} %get-tuple-element.47.refs_0_), channel_id=1, source_target_pairs={{0,64},{8,72},{16,80},{24,88},{32,96},{40,104},{48,112},{56,120},{... | collective-permute-start | bytes 196616 | tf_op jit(solution)/shard_map/ppermute | solution.py:472
  41.7 5.2 %collective-permute-start.11 = (f32[64,128]{1,0:T(8,128)S(1)}, f32[64,128]{1,0:T(8,128)S(1)}, u32[]{:S(2)}, u32[]{:S(2)}) collective-permute-start(f32[64,128]{1,0:T(8,128)S(1)} %get-tuple-element.49.own_ref), channel_id=1, source_target_pairs={{0,192},{8,200},{16,208},{24,216},{32,224},{40,232},{48,240},{56,2... | collective-permute-start | bytes 98312 | tf_op jit(solution)/shard_map/ppermute | solution.py:472

commit v9 on v8

--- a/solution.py
+++ b/solution.py
@@ -485,8 +485,9 @@
     )
     top_even = xor_depth(lax.optimization_barrier((densities, cols))[0], 1)
     top_odd = lax.ppermute(
-        lax.optimization_barrier((densities, line_b))[0], "depth",
-        [(i, i if i in (0, 31) else i + 1 if i % 2 else i - 1) for i in range(32)],
+        lax.optimization_barrier((densities, line_b))[0], ("depth", "lat"),
+        [(8 * i + l, 8 * (i + 1 if i % 2 else i - 1) + l if 0 < i < 31 else 8 * i + (l ^ 1))
+         for i in range(32) for l in range(8)],
     )
     line_c = xor_lat(jnp.concatenate([densities, line_a, line_b], axis=0), 6)
     n2, n3, n4, n5, root = call(

time: 49.4 us -> 47.5 us (0.962)
  starting transfers between devices: 22.8 us -> 20.9 us
    ppermute x1, starting transfers between devices: 4.38 us -> 2.48 us  [on_device(): lax.ppermute(lax.optimization_barrier((densities, line_b))[0], ('depth',...]
  transfers between devices with their start and end apart: 12 -> 12, of which waited for: 7 -> 7; matrix products, arithmetic and copies ran while one was open for 0% -> 0% of each run, Pallas kernels for 12% -> 13%
where the time goes in v9:
time: 47.5 us; the launch traced here: 47.4 us
  starting transfers between devices  20.9 us (44%)
  waiting for transfers between devices  13.9 us (29%)
  Pallas kernels  12.4 us (26%)
    ppermute x8, starting transfers between devices, xor_depth(): return lax.ppermute(value, 'depth', [(i, i ^ bits) for i in range(32)])  14 us
    ppermute x8, waiting for transfers between devices, xor_depth(): return lax.ppermute(value, 'depth', [(i, i ^ bits) for i in range(32)])  13.1 us
    pallas_call x9, Pallas kernels, call(): pl.pallas_call(body, out_shape=outs, in_specs=[pl.BlockSpec(memory_space=...  12.4 us
    ppermute x3, starting transfers between devices, xor_lat(): return lax.ppermute(value, 'lat', [(i, i ^ bits) for i in range(8)])  4.52 us
    ppermute x1, starting transfers between devices, on_device(): lax.ppermute(lax.optimization_barrier((densities, line_b))[0], ('depth',...  2.48 us
  transfers between devices with their start and end apart: 12, of which 7 were waited for; matrix products, arithmetic and copies ran while one was open for 0% of the time, Pallas kernels for 13%

profile of v9, /device:TPU:32, one launch (start us, length us, event | category | flops | bytes accessed | tf_op | source)
XLA Modules:
  0.0 47.4 jit_solution(7147706853631521708)
XLA Ops:
  0.0 0.1 collective-permute-start
  0.1 2.2 %react.1 = (f32[32,64]{1,0:T(8,128)S(1)}, f32[64,128]{1,0:T(8,128)S(1)}) custom-call(f32[32,4096]{1,0:T(8,128)} %bitcast.21, f32[32,64]{1,0:T(8,128)} %bitcast.12, f32[32,64]{1,0:T(8,128)} %bitcast.22, f32[32,64]{1,0:T(8,128)} %bitcast.14, s32[8,8]{1,0:T(8,128)} %pat_hbm.1), custom_call_target="tpu_custom_call" | custom-call | flops 1073741824 | bytes 65536 | tf_op jit(solution)/shard_map/react/pallas_call | solution.py:442
  2.3 0.0 collective-permute-done.a_ref
  2.3 1.6 %collective-permute-start.1 = (f32[2,32,64]{2,1,0:T(8,128)S(1)}, f32[2,32,64]{2,1,0:T(8,128)S(1)}, u32[]{:S(2)}, u32[]{:S(2)}) collective-permute-start(f32[2,32,64]{2,1,0:T(8,128)S(1)} %pad_maximum_fusion.1), channel_id=1, source_target_pairs={{0,2},{1,3},{2,0},{3,1},{4,6},{5,7},{6,4},{7,5},{8,10},{9,11},{10,... | collective-permute-start | bytes 49160 | tf_op jit(solution)/shard_map/ppermute | solution.py:469
  3.9 1.6 %tree_leaves.1 = (bf16[16,4,64,256]{3,2,1,0:T(8,128)(2,1)S(1)}, bf16[16,3,64,128]{3,2,1,0:T(8,128)(2,1)S(1)}, f32[16,3,64,128]{3,2,1,0:T(8,128)S(1)}, f32[2,64,128]{2,1,0:T(8,128)S(1)}) custom-call(f32[1024,128]{1,0:T(8,128)S(1)} %bitcast.20, f32[32,64]{1,0:T(8,128)S(1)} %bitcast.17, f32[32,64]{1,0:T(8,128)S(1)} %get-tuple-element.33.after_ref.part_ref), custom_call_target="tpu_custom_call" | custom-call | flops 2147483648 | bytes 65536 | tf_op jit(solution)/shard_map/tree_leaves/pallas_call | solution.py:442
  5.5 0.3 collective-permute-start.3
  5.9 0.5 collective-permute-done.1.b_ref
  6.3 2.8 %collective-permute-start.2 = (f32[4,32,64]{2,1,0:T(8,128)S(1)}, f32[4,32,64]{2,1,0:T(8,128)S(1)}, u32[]{:S(2)}, u32[]{:S(2)}) collective-permute-start(f32[4,32,64]{2,1,0:T(8,128)S(1)} %pad_maximum_fusion), channel_id=1, source_target_pairs={{0,6},{1,7},{2,4},{3,5},{4,2},{5,3},{6,0},{7,1},{8,14},{9,15},{10,... | collective-permute-start | bytes 98312 | tf_op jit(solution)/shard_map/ppermute | solution.py:469
  9.2 2.5 %collective-permute-start.4 = (f32[1,32,64]{2,1,0:T(8,128)S(1)}, f32[1,32,64]{2,1,0:T(8,128)S(1)}, u32[]{:S(2)}, u32[]{:S(2)}) collective-permute-start(f32[1,32,64]{2,1,0:T(8,128)S(1)} %copy-done), channel_id=1, source_target_pairs={{0,1},{1,0},{2,3},{3,2},{4,5},{5,4},{6,7},{7,6},{8,16},{9,17},{10,... | collective-permute-start | bytes 24584 | tf_op jit(solution)/shard_map/ppermute | solution.py:487
  11.7 1.4 %tree_upper.1 = (bf16[8,4,64,128]{3,2,1,0:T(8,128)(2,1)S(1)}, bf16[4,4,64,128]{3,2,1,0:T(8,128)(2,1)S(1)}, bf16[2,4,64,128]{3,2,1,0:T(8,128)(2,1)S(1)}, bf16[1,64,128]{2,1,0:T(8,128)(2,1)S(1)}, f32[128,128]{1,0:T(8,128)S(1)}) custom-call(bf16[16,3,64,128]{3,2,1,0:T(8,128)(2,1)S(1)} %get-tuple-element.39.n1_ref, ...), custom_call_target="tpu_custom_call" | custom-call | flops 2147483648 | bytes 65536 | tf_op jit(solution)/shard_map/tree_upper/pallas_call | solution.py:442
  13.1 0.0 collective-permute-done.3.even_ref
  13.1 0.3 collective-permute-done.4.odd_ref
  13.4 0.0 collective-permute-done.2.c_ref
  13.4 2.2 %upsweep.1 = (f32[128,128]{1,0:T(8,128)S(1)}, f32[4,64,128]{2,1,0:T(8,128)S(1)}, f32[7,64,128]{2,1,0:T(8,128)S(1)}, f32[7,64,128]{2,1,0:T(8,128)S(1)}) custom-call(s32[1,4]{1,0:T(1,128)S(1)} %copy-done.4, f32[32,64]{1,0:T(8,128)S(1)} %get-tuple-element.33.after_ref.part_ref, f32[1,32,64]{2,1,0:T(8,128)S(1)} %collective-permute-done.a_ref, ...), custom_call_target="tpu_custom_call" | custom-call | flops 33554432 | bytes 65536 | tf_op jit(solution)/shard_map/upsweep/pallas_call | solution.py:442
  15.6 0.3 collective-permute-start.5
  15.9 3.9 %collective-permute-start.6 = (f32[128,128]{1,0:T(8,128)S(1)}, f32[128,128]{1,0:T(8,128)S(1)}, u32[]{:S(2)}, u32[]{:S(2)}) collective-permute-start(f32[128,128]{1,0:T(8,128)S(1)} %get-tuple-element.46.refs_0_), channel_id=1, source_target_pairs={{0,16},{8,24},{16,0},{24,8},{32,48},{40,56},{48,32},{56,40},{64,80... | collective-permute-start | bytes 196616 | tf_op jit(solution)/shard_map/ppermute | solution.py:472
  19.8 0.5 collective-permute-start.7
  20.3 0.0 collective-permute-done.5.refs_1_
  20.3 2.5 %collective-permute-done.6.refs_2_ = f32[128,128]{1,0:T(8,128)S(1)} collective-permute-done((f32[128,128]{1,0:T(8,128)S(1)}, f32[128,128]{1,0:T(8,128)S(1)}, u32[]{:S(2)}, u32[]{:S(2)}) %collective-permute-start.6) | collective-permute-done | bytes 65568 | tf_op jit(solution)/shard_map/ppermute | solution.py:472
  22.7 1.9 %collective-permute-done.7.refs_3_ = f32[128,128]{1,0:T(8,128)S(1)} collective-permute-done((f32[128,128]{1,0:T(8,128)S(1)}, f32[128,128]{1,0:T(8,128)S(1)}, u32[]{:S(2)}, u32[]{:S(2)}) %collective-permute-start.7) | collective-permute-done | bytes 65568 | tf_op jit(solution)/shard_map/ppermute | solution.py:472
  24.6 1.0 %combine_low.1 = (f32[128,128]{1,0:T(8,128)S(1)}, f32[128,128]{1,0:T(8,128)S(1)}) custom-call(f32[128,128]{1,0:T(8,128)S(1)} %get-tuple-element.46.refs_0_, f32[128,128]{1,0:T(8,128)S(1)} %collective-permute-done.5.refs_1_, f32[128,128]{1,0:T(8,128)S(1)} %collective-permute-done.6.refs_2_, f32[128,128]{1,0:T(8,128)S(1)} %collective-permute-done.7.refs_3_), custom_call_target="tpu_custom_call" | custom-call | flops 16777216 | bytes 65536 | tf_op jit(solution)/shard_map/combine_low/pallas_call | solution.py:442
  25.6 6.0 %collective-permute-start.10 = (f32[128,128]{1,0:T(8,128)S(1)}, f32[128,128]{1,0:T(8,128)S(1)}, u32[]{:S(2)}, u32[]{:S(2)}) collective-permute-start(f32[128,128]{1,0:T(8,128)S(1)} %get-tuple-element.47.refs_0_), channel_id=1, source_target_pairs={{0,120},{8,112},{16,104},{24,96},{32,88},{40,80},{48,72},{56,64},{... | collective-permute-start | bytes 196616 | tf_op jit(solution)/shard_map/ppermute | solution.py:472
  31.6 0.5 collective-permute-start.8
  32.1 0.2 collective-permute-start.9
  32.3 0.7 %prepare.1 = (bf16[15,64,128]{2,1,0:T(8,128)(2,1)S(1)}, f32[4,64,128]{2,1,0:T(8,128)S(1)}, f32[4,64,128]{2,1,0:T(8,128)S(1)}, f32[64,128]{1,0:T(8,128)S(1)}) custom-call(f32[4,64,128]{2,1,0:T(8,128)S(1)} %get-tuple-element.54.pair_ref, f32[7,64,128]{2,1,0:T(8,128)S(1)} %get-tuple-element.55.v_ref, f32[7,64,128]{2,1,0:T(8,128)S(1)} %get-tuple-element.56.w_ref, ...), custom_call_target="tpu_custom_call" | custom-call | flops 1073741824 | bytes 65536 | tf_op jit(solution)/shard_map/prepare/pallas_call | solution.py:442
  33.0 1.1 %collective-permute-done.10.refs_3_ = f32[128,128]{1,0:T(8,128)S(1)} collective-permute-done((f32[128,128]{1,0:T(8,128)S(1)}, f32[128,128]{1,0:T(8,128)S(1)}, u32[]{:S(2)}, u32[]{:S(2)}) %collective-permute-start.10) | collective-permute-done | bytes 65568 | tf_op jit(solution)/shard_map/ppermute | solution.py:472
  34.0 4.9 %collective-permute-done.8.refs_1_ = f32[128,128]{1,0:T(8,128)S(1)} collective-permute-done((f32[128,128]{1,0:T(8,128)S(1)}, f32[128,128]{1,0:T(8,128)S(1)}, u32[]{:S(2)}, u32[]{:S(2)}) %collective-permute-start.8) | collective-permute-done | bytes 65568 | tf_op jit(solution)/shard_map/ppermute | solution.py:472
  38.9 0.9 %combine_high.1 = (f32[64,128]{1,0:T(8,128)S(1)}, f32[128,128]{1,0:T(8,128)S(1)}) custom-call(f32[128,128]{1,0:T(8,128)S(1)} %get-tuple-element.47.refs_0_, f32[128,128]{1,0:T(8,128)S(1)} %collective-permute-done.8.refs_1_, f32[128,128]{1,0:T(8,128)S(1)} %collective-permute-done.9.refs_2_, f32[128,128]{1,0:T(8,128)S(1)} %collective-permute-done.10.refs_3_, ...), custom_call_target="tpu_custom_call" | custom-call | flops 16777216 | bytes 65536 | tf_op jit(solution)/shard_map/combine_high/pallas_call | solution.py:442
  39.8 2.3 %collective-permute-start.11 = (f32[64,128]{1,0:T(8,128)S(1)}, f32[64,128]{1,0:T(8,128)S(1)}, u32[]{:S(2)}, u32[]{:S(2)}) collective-permute-start(f32[64,128]{1,0:T(8,128)S(1)} %get-tuple-element.49.own_ref), channel_id=1, source_target_pairs={{0,192},{8,200},{16,208},{24,216},{32,224},{40,232},{48,240},{56,2... | collective-permute-start | bytes 98312 | tf_op jit(solution)/shard_map/ppermute | solution.py:472
  42.1 0.1 prepare_last.1
  42.2 2.8 %collective-permute-done.11.other_ref = f32[64,128]{1,0:T(8,128)S(1)} collective-permute-done((f32[64,128]{1,0:T(8,128)S(1)}, f32[64,128]{1,0:T(8,128)S(1)}, u32[]{:S(2)}, u32[]{:S(2)}) %collective-permute-start.11) | collective-permute-done | bytes 32800 | tf_op jit(solution)/shard_map/ppermute | solution.py:472
  45.0 2.4 %downsweep.1 = f32[32,64]{1,0:T(8,128)} custom-call(f32[64,128]{1,0:T(8,128)S(1)} %collective-permute-done.11.other_ref, bf16[2,64,128]{2,1,0:T(8,128)(2,1)S(1)} %get-tuple-element.51.maps_ref, f32[2,64,128]{2,1,0:T(8,128)S(1)} %get-tuple-element.52.vecs_ref, bf16[2,256,128]{2,1,0:T(8,128)(2,1)S(1)} %get-tuple-element.53.own_rhs, ...), custom_call_target="tpu_custom_call" | custom-call | flops 33554432 | bytes 65536 | tf_op jit(solution)/shard_map/downsweep/pallas_call | solution.py:442
  (15 shorter events, 0.0 us)
Async XLA Ops:
  0.0 2.3 %copy-start = (f32[1,32,64]{2,1,0:T(8,128)S(1)}, f32[1,32,64]{2,1,0:T(8,128)}, u32[]{:S(2)}) copy-start(f32[1,32,64]{2,1,0:T(8,128)} %param.9) | copy-start | bytes 24580
  0.0 3.9 %copy-start.3 = (f32[1,32,64]{2,1,0:T(8,128)S(1)}, f32[1,32,64]{2,1,0:T(8,128)}, u32[]{:S(2)}) copy-start(f32[1,32,64]{2,1,0:T(8,128)} %param.17) | copy-start | bytes 24580
  0.0 3.9 %copy-start.5 = (f32[1,32,4096]{2,1,0:T(8,128)S(1)}, f32[1,32,4096]{2,1,0:T(8,128)}, u32[]{:S(2)}) copy-start(f32[1,32,4096]{2,1,0:T(8,128)} %param.16) | copy-start | bytes 1572868
  0.0 2.3 %collective-permute-start = (f32[1,32,64]{2,1,0:T(8,128)}, f32[1,32,64]{2,1,0:T(8,128)S(1)}, u32[]{:S(2)}, u32[]{:S(2)}) collective-permute-start(f32[1,32,64]{2,1,0:T(8,128)} %param.9), channel_id=1, source_target_pairs={{0,1},{1,0},{2,3},{3,2},{4,5},{5,4},{6,7},{7,6},{8,9},{9,8},{10,11... | collective-permute-start | bytes 24584 | tf_op jit(solution)/shard_map/ppermute | solution.py:469
  2.3 4.0 %collective-permute-start.1 = (f32[2,32,64]{2,1,0:T(8,128)S(1)}, f32[2,32,64]{2,1,0:T(8,128)S(1)}, u32[]{:S(2)}, u32[]{:S(2)}) collective-permute-start(f32[2,32,64]{2,1,0:T(8,128)S(1)} %pad_maximum_fusion.1), channel_id=1, source_target_pairs={{0,2},{1,3},{2,0},{3,1},{4,6},{5,7},{6,4},{7,5},{8,10},{9,11},{10,... | collective-permute-start | bytes 49160 | tf_op jit(solution)/shard_map/ppermute | solution.py:469
  5.5 7.5 %collective-permute-start.3 = (f32[1,32,64]{2,1,0:T(8,128)S(1)}, f32[1,32,64]{2,1,0:T(8,128)S(1)}, u32[]{:S(2)}, u32[]{:S(2)}) collective-permute-start(f32[1,32,64]{2,1,0:T(8,128)S(1)} %copy-done), channel_id=1, source_target_pairs={{0,8},{8,0},{16,24},{24,16},{32,40},{40,32},{48,56},{56,48},{64,72... | collective-permute-start | bytes 24584 | tf_op jit(solution)/shard_map/ppermute | solution.py:472
  6.3 7.0 %collective-permute-start.2 = (f32[4,32,64]{2,1,0:T(8,128)S(1)}, f32[4,32,64]{2,1,0:T(8,128)S(1)}, u32[]{:S(2)}, u32[]{:S(2)}) collective-permute-start(f32[4,32,64]{2,1,0:T(8,128)S(1)} %pad_maximum_fusion), channel_id=1, source_target_pairs={{0,6},{1,7},{2,4},{3,5},{4,2},{5,3},{6,0},{7,1},{8,14},{9,15},{10,... | collective-permute-start | bytes 98312 | tf_op jit(solution)/shard_map/ppermute | solution.py:469
  9.2 4.2 %collective-permute-start.4 = (f32[1,32,64]{2,1,0:T(8,128)S(1)}, f32[1,32,64]{2,1,0:T(8,128)S(1)}, u32[]{:S(2)}, u32[]{:S(2)}) collective-permute-start(f32[1,32,64]{2,1,0:T(8,128)S(1)} %copy-done), channel_id=1, source_target_pairs={{0,1},{1,0},{2,3},{3,2},{4,5},{5,4},{6,7},{7,6},{8,16},{9,17},{10,... | collective-permute-start | bytes 24584 | tf_op jit(solution)/shard_map/ppermute | solution.py:487
  11.7 1.7 %copy-start.1 = (f32[1,32,64]{2,1,0:T(8,128)S(1)}, f32[1,32,64]{2,1,0:T(8,128)}, u32[]{:S(2)}) copy-start(f32[1,32,64]{2,1,0:T(8,128)} %param.13) | copy-start | bytes 24580
  11.7 1.7 %copy-start.2 = (f32[1,32,64]{2,1,0:T(8,128)S(1)}, f32[1,32,64]{2,1,0:T(8,128)}, u32[]{:S(2)}) copy-start(f32[1,32,64]{2,1,0:T(8,128)} %param.14) | copy-start | bytes 24580
  11.7 1.7 %copy-start.4 = (s32[1,4]{1,0:T(1,128)S(1)}, s32[1,4]{1,0:T(1,128)}, u32[]{:S(2)}) copy-start(s32[1,4]{1,0:T(1,128)} %neigh_ref.1) | copy-start | bytes 52
  15.6 4.7 %collective-permute-start.5 = (f32[128,128]{1,0:T(8,128)S(1)}, f32[128,128]{1,0:T(8,128)S(1)}, u32[]{:S(2)}, u32[]{:S(2)}) collective-permute-start(f32[128,128]{1,0:T(8,128)S(1)} %get-tuple-element.46.refs_0_), channel_id=1, source_target_pairs={{0,8},{8,0},{16,24},{24,16},{32,40},{40,32},{48,56},{56,48},{64,72... | collective-permute-start | bytes 196616 | tf_op jit(solution)/shard_map/ppermute | solution.py:472
  15.9 6.8 %collective-permute-start.6 = (f32[128,128]{1,0:T(8,128)S(1)}, f32[128,128]{1,0:T(8,128)S(1)}, u32[]{:S(2)}, u32[]{:S(2)}) collective-permute-start(f32[128,128]{1,0:T(8,128)S(1)} %get-tuple-element.46.refs_0_), channel_id=1, source_target_pairs={{0,16},{8,24},{16,0},{24,8},{32,48},{40,56},{48,32},{56,40},{64,80... | collective-permute-start | bytes 196616 | tf_op jit(solution)/shard_map/ppermute | solution.py:472
  19.8 4.8 %collective-permute-start.7 = (f32[128,128]{1,0:T(8,128)S(1)}, f32[128,128]{1,0:T(8,128)S(1)}, u32[]{:S(2)}, u32[]{:S(2)}) collective-permute-start(f32[128,128]{1,0:T(8,128)S(1)} %get-tuple-element.46.refs_0_), channel_id=1, source_target_pairs={{0,24},{8,16},{16,8},{24,0},{32,56},{40,48},{48,40},{56,32},{64,88... | collective-permute-start | bytes 196616 | tf_op jit(solution)/shard_map/ppermute | solution.py:472
  25.6 8.4 %collective-permute-start.10 = (f32[128,128]{1,0:T(8,128)S(1)}, f32[128,128]{1,0:T(8,128)S(1)}, u32[]{:S(2)}, u32[]{:S(2)}) collective-permute-start(f32[128,128]{1,0:T(8,128)S(1)} %get-tuple-element.47.refs_0_), channel_id=1, source_target_pairs={{0,120},{8,112},{16,104},{24,96},{32,88},{40,80},{48,72},{56,64},{... | collective-permute-start | bytes 196616 | tf_op jit(solution)/shard_map/ppermute | solution.py:472
  31.6 7.3 %collective-permute-start.8 = (f32[128,128]{1,0:T(8,128)S(1)}, f32[128,128]{1,0:T(8,128)S(1)}, u32[]{:S(2)}, u32[]{:S(2)}) collective-permute-start(f32[128,128]{1,0:T(8,128)S(1)} %get-tuple-element.47.refs_0_), channel_id=1, source_target_pairs={{0,56},{8,48},{16,40},{24,32},{32,24},{40,16},{48,8},{56,0},{64,12... | collective-permute-start | bytes 196616 | tf_op jit(solution)/shard_map/ppermute | solution.py:472
  32.1 6.8 %collective-permute-start.9 = (f32[128,128]{1,0:T(8,128)S(1)}, f32[128,128]{1,0:T(8,128)S(1)}, u32[]{:S(2)}, u32[]{:S(2)}) collective-permute-start(f32[128,128]{1,0:T(8,128)S(1)} %get-tuple-element.47.refs_0_), channel_id=1, source_target_pairs={{0,64},{8,72},{16,80},{24,88},{32,96},{40,104},{48,112},{56,120},{... | collective-permute-start | bytes 196616 | tf_op jit(solution)/shard_map/ppermute | solution.py:472
  39.8 5.2 %collective-permute-start.11 = (f32[64,128]{1,0:T(8,128)S(1)}, f32[64,128]{1,0:T(8,128)S(1)}, u32[]{:S(2)}, u32[]{:S(2)}) collective-permute-start(f32[64,128]{1,0:T(8,128)S(1)} %get-tuple-element.49.own_ref), channel_id=1, source_target_pairs={{0,192},{8,200},{16,208},{24,216},{32,224},{40,232},{48,240},{56,2... | collective-permute-start | bytes 98312 | tf_op jit(solution)/shard_map/ppermute | solution.py:472

commit v10 on v6

--- a/solution.py
+++ b/solution.py
@@ -75,8 +75,13 @@
         node[j, 3] = pack(u)
 
 
-def tree_leaves(fac_ref, coup_ref, after_ref, quad_ref, n1_ref, full_ref, cols_ref, rows):
-    del after_ref
+def tree_leaves(fac_hbm, coup_hbm, quad_ref, n1_ref, full_ref, cols_ref, fac_ref, coup_ref, rows, sems):
+    parts = [pl.ds(i * 256, 256) for i in range(4)]
+    pairs = [(coup_hbm, coup_ref)] + [(fac_hbm.at[part], fac_ref.at[part]) for part in parts]
+    copies = [pltpu.make_async_copy(a, b, sems.at[i]) for i, (a, b) in enumerate(pairs)]
+    for copy in copies:
+        copy.start()
+    copies[0].wait()
     c = coup_ref[...]
     cols_ref[0] = column(c[CELLS - 1 : CELLS])
     cols_ref[1] = column(1.0 / c[0:1])
@@ -95,6 +100,8 @@
         return a * c2[before : before + 1] - eye, a * c2[k : k + 1] - eye
 
     for j in range(CELLS // 2):
+        if j % 4 == 0:
+            copies[1 + j // 4].wait()
         p1, q1 = leaf(2 * j)
         p2, q2 = leaf(2 * j + 1)
         kq1 = pack(q1)
@@ -133,18 +140,10 @@
         node, full = node_to, full_to
 
 
-def react(jac_hbm, dens_hbm, src_hbm, tran_hbm, pat_hbm, out_ref, flux_ref, jac_ref, dens_ref, src_ref, tran_ref,
-          pat_ref, sems):
-    parts = [(slice(None), pl.ds(i * 1024, 1024)) for i in range(4)]
-    pairs = [(dens_hbm, dens_ref), (pat_hbm, pat_ref)] + [(jac_hbm.at[part], jac_ref.at[part]) for part in parts]
-    pairs += [(src_hbm, src_ref), (tran_hbm, tran_ref)]
-    copies = [pltpu.make_async_copy(a, b, sems.at[i]) for i, (a, b) in enumerate(pairs)]
-    for copy in copies:
-        copy.start()
+def react(jac_ref, dens_ref, src_ref, tran_ref, pat_ref, after_ref, out_ref, flux_ref):
+    del after_ref
     half = lanes((128, N)) % 2 == lax.broadcasted_iota(jnp.int32, (128, N), 0) // N
     half = jnp.where(half, 1.0, 0.0).astype(bf16)
-    copies[0].wait()
-    copies[1].wait()
     u = dens_ref[...]
     u2 = jnp.concatenate([u, u], axis=1)
     lane8 = lanes((8, 128))
@@ -155,15 +154,11 @@
     lane = lanes((CELLS, N))
     acc = jnp.zeros((CELLS, N), f32)
     for m in range(32):
-        if m % 8 == 0:
-            copies[2 + m // 8].wait()
         y = jac_ref[:, m * 128 : (m + 1) * 128] * (u2 * mask_rows[m // 4 : m // 4 + 1])
         hi = y.astype(bf16)
         lo = (y - hi.astype(f32)).astype(bf16)
         z = jnp.dot(hi, half, preferred_element_type=f32) + jnp.dot(lo, half, preferred_element_type=f32)
         acc = jnp.where(lane // 2 == m, z, acc)
-    copies[6].wait()
-    copies[7].wait()
     tran = tran_ref[...]
     flux = tran * u
     flux_ref[...] = column(flux[CELLS - 1 : CELLS])
@@ -286,19 +281,6 @@
     add_x[...] = repeat(w0 + roll(w1, 2) + roll(v0, 1) + roll(v1, 3))
 
 
-def prepare_last(own_ref, fun_ref, maps_ref, vecs_ref, own_rhs):
-    is_low = lax.axis_index("depth") < 2 * ZS
-    f, hh, k, g, e = unpack(fun_ref[...])
-    maps_ref[0], maps_ref[1] = pack(f), pack(jnp.where(is_low, hh, k))
-    vecs_ref[0], vecs_ref[1] = g, e
-    v = jnp.broadcast_to(own_ref[:, N : N + 1], (N, 128))
-    hi = v.astype(bf16)
-    lo = (v - hi.astype(f32)).astype(bf16)
-    zero = jnp.zeros((N, 128), bf16)
-    own_rhs[0] = jnp.concatenate([hi, zero, hi, zero], axis=0)
-    own_rhs[1] = jnp.concatenate([lo, zero, lo, zero], axis=0)
-
-
 def unpack(b):
     low = lanes((N, 128)) < N
     b1, b2 = b[:N], b[N:]
@@ -368,51 +350,49 @@
         ref[N:] = tail
 
 
-def combine_two(level, own_ref, other_ref, fun_ref, out_ref, fun_out):
-    is_low = ((lax.axis_index("depth") // (1, 2, 4, 8)[level]) % 2) == 0
-    own, other = own_ref[...], other_ref[...]
-    one = unpack(jnp.where(is_low, own, other))
-    two = unpack(jnp.where(is_low, other, own))
-    total, extra = join(one, two, last=level == 3)
-    put_map(out_ref, *total, last=level == 3)
-    put_map(fun_out, *track(is_low, unpack(fun_ref[...]), extra))
+def fill(slots, at, refs):
+    for bits, ref in enumerate(refs):
+        slots[at ^ bits] = ref[...]
+    return [unpack(slots[i]) for i in range(4)]
 
 
 def combine_four(own_ref, x1_ref, x2_ref, x3_ref, out_ref, fun_out, slots):
     at = lax.axis_index("depth") % 4
-    slots[at] = own_ref[...]
-    slots[at ^ 1] = x1_ref[...]
-    slots[at ^ 2] = x2_ref[...]
-    slots[at ^ 3] = x3_ref[...]
-    maps = [unpack(slots[i]) for i in range(4)]
+    maps = fill(slots, at, (own_ref, x1_ref, x2_ref, x3_ref))
     lower, extra_lower = join(maps[0], maps[1])
     upper, extra_upper = join(maps[2], maps[3])
     in_lower = at < 2
-    mine = lambda a, b: jnp.where(in_lower, a, b)
+    mine = lambda x, y: [jnp.where(in_lower, a, b) for a, b in zip(x, y)]
     fun = track_first(
-        at % 2 == 0,
-        [mine(a, b) for a, b in zip(maps[0], maps[2])],
-        [mine(a, b) for a, b in zip(maps[1], maps[3])],
-        [mine(a, b) for a, b in zip(extra_lower[:2], extra_upper[:2])],
+        at % 2 == 0, mine(maps[0], maps[2]), mine(maps[1], maps[3]), mine(extra_lower[:2], extra_upper[:2])
     )
     total, extra = join(lower, upper)
     put_map(out_ref, *total)
     put_map(fun_out, *track(in_lower, fun, extra))
 
 
-def downsweep(other_ref, maps_ref, vecs_ref, own_rhs, cols_ref, add_v, add_a, add_x, quad_ref, n1_ref, n2_ref, n3_ref,
-              n4_ref, t_ref, out_ref):
-    is_low = lax.axis_index("depth") < 2 * ZS
-    g, e = vecs_ref[0], vecs_ref[1]
-    other = other_ref[...]
-    hi = other.astype(bf16)
-    wide = jnp.concatenate([hi, (other - hi.astype(f32)).astype(bf16)], axis=1)
-    v_other = jnp.broadcast_to(other[:, N : N + 1], (N, 128))
-    w_other = jnp.broadcast_to(other[:, N + 1 : N + 2], (N, 128))
-    t = w_other + jnp.dot(wide, own_rhs[0], preferred_element_type=f32)
-    t = t + jnp.dot(wide, own_rhs[1], preferred_element_type=f32)
-    up = g + dot(maps_ref[0], rhs(v_other))
-    aa = e + dot(maps_ref[1], rhs(jnp.where(is_low, t, v_other)))
+def combine_two(own_ref, other_ref, fun_ref, out_ref, fun_out):
+    is_low = lax.axis_index("depth") % ZS < 4
+    own, other = own_ref[...], other_ref[...]
+    total, extra = join(unpack(jnp.where(is_low, own, other)), unpack(jnp.where(is_low, other, own)))
+    put_map(out_ref, *total)
+    for i, value in enumerate(track(is_low, unpack(fun_ref[...]), extra)):
+        fun_out[i] = value
+
+
+def downsweep(own_ref, y1_ref, y2_ref, y3_ref, fun_ref, cols_ref, add_v, add_a, add_x, quad_ref, n1_ref, n2_ref, n3_ref,
+              n4_ref, t_ref, out_ref, slots):
+    at = lax.axis_index("depth") // ZS
+    maps = fill(slots, at, (own_ref, y1_ref, y2_ref, y3_ref))
+    lower, extra_lower = join(maps[0], maps[1], last=True)
+    upper, extra_upper = join(maps[2], maps[3], last=True)
+    is_low = at < 2
+    extra = [jnp.where(is_low, a, b) for a, b in zip(extra_lower, extra_upper)]
+    f, hh, k, g, e = track(at % 2 == 0, [fun_ref[i] for i in range(5)], extra)
+    yv = rhs(lower[3])
+    t = upper[4] + dot(pack(upper[2]), yv)
+    up = g + dot(pack(f), yv)
+    aa = e + dot(pack(jnp.where(is_low, hh, k)), jnp.where(is_low, rhs(t), yv))
     ss = jnp.where(is_low, g, up) * cols_ref[1]
     lane = lanes((N, 128)) % CELLS
     for level, size, ref, base in ((3, 32, n4_ref, 6), (2, 16, n3_ref, 4), (1, 8, n2_ref, 0), (0, 4, n1_ref, 7)):
@@ -477,21 +457,22 @@
         return lax.ppermute(value, "depth", [(i, i ^ bits) for i in range(32)])
 
     line_a = xor_lat(densities, 1)
-    part, flux = call(
-        react, (sds(CELLS, N), sds(N, 128)), jac, u, src, tran, pattern, hbm=5, flops=1 << 30, name="react",
-        scratch=[pltpu.VMEM((CELLS, N * N), f32)] + [pltpu.VMEM((CELLS, N), f32)] * 3
-        + [pltpu.VMEM((8, 8), jnp.int32), pltpu.SemaphoreType.DMA((8,))],
-    )
-    line_b = xor_lat(jnp.concatenate([densities, line_a], axis=0), 2)
     quad, n1, full, cols = call(
         tree_leaves,
         (sds(16, 4, N, 256, dtype=bf16), sds(16, 3, N, 128, dtype=bf16), sds(16, 3, N, 128), sds(2, N, 128)),
-        fac, coup, part, scratch=[pltpu.VMEM((2, N, 128), f32)], flops=2 << 30, name="tree_leaves",
-    )
-    top_even = xor_depth(lax.optimization_barrier((densities, cols))[0], 1)
+        fac, coup, hbm=2, flops=1 << 30, name="tree_leaves",
+        scratch=[pltpu.VMEM((1024, 128), f32), pltpu.VMEM((CELLS, N), f32), pltpu.VMEM((2, N, 128), f32),
+                 pltpu.SemaphoreType.DMA((5,))],
+    )
+    line_b = xor_lat(jnp.concatenate([densities, line_a], axis=0), 2)
+    part, flux = call(
+        react, (sds(CELLS, N), sds(N, 128)), jac, u, src, tran, pattern, cols, flops=1 << 30, name="react",
+    )
+    top_even = xor_depth(lax.optimization_barrier((densities, part))[0], 1)
     top_odd = lax.ppermute(
-        lax.optimization_barrier((densities, line_b))[0], "depth",
-        [(i, (i + 1) % 32 if i % 2 else (i - 1) % 32) for i in range(32)],
+        lax.optimization_barrier((densities, line_b))[0], ("depth", "lat"),
+        [(8 * i + l, 8 * (i + 1 if i % 2 else i - 1) + l if 0 < i < 31 else 8 * i + (l ^ 1))
+         for i in range(32) for l in range(8)],
     )
     line_c = xor_lat(jnp.concatenate([densities, line_a, line_b], axis=0), 6)
     n2, n3, n4, n5, root = call(
@@ -506,30 +487,22 @@
         smem=1, flops=1 << 25, name="upsweep",
     )
     others = [xor_depth(pay, bits) for bits in (1, 2, 3)]
+    slots = [pltpu.VMEM((4, 128, 128), f32)]
+    pay, fun = call(
+        combine_four, (sds(128, 128), sds(128, 128)), pay, *others, scratch=slots, flops=1 << 24, name="combine_four",
+    )
+    other = xor_depth(pay, 7)
+    pay, fun = call(
+        combine_two, (sds(128, 128), sds(5, N, 128)), pay, other, fun, flops=1 << 24, name="combine_two",
+    )
+    others = [xor_depth(pay, bits) for bits in (8, 16, 24)]
     tees, add_v, add_a, add_x = call(
         prepare, (sds(15, N, 128, dtype=bf16), sds(4, N, 128), sds(4, N, 128), sds(N, 128)),
         pair, vs, ws, n1, n2, n3, n4, flops=1 << 30, name="prepare",
     )
-    pay, fun = call(
-        combine_four, (sds(128, 128), sds(128, 128)), pay, *others, scratch=[pltpu.VMEM((4, 128, 128), f32)],
-        flops=1 << 24, name="combine_four",
-    )
-    for level, bits in ((2, 7), (3, 8)):
-        other = xor_depth(pay, bits)
-        pay, fun = call(
-            lambda *refs, level=level: combine_two(level, *refs),
-            (sds(N if level == 3 else 128, 128), sds(128, 128)), pay, other, fun, flops=1 << 24,
-            name=f"combine{level}",
-        )
-    other = xor_depth(pay, 24)
-    maps, vecs, own_rhs = call(
-        prepare_last,
-        (sds(2, N, 128, dtype=bf16), sds(2, N, 128), sds(2, 256, 128, dtype=bf16)),
-        pay, fun, flops=1 << 30, name="prepare_last",
-    )
     out = call(
-        downsweep, sds(CELLS, N), other, maps, vecs, own_rhs, cols, add_v, add_a, add_x, quad, n1, n2, n3, n4, tees,
-        flops=1 << 25, name="downsweep",
+        downsweep, sds(CELLS, N), pay, *others, fun, cols, add_v, add_a, add_x, quad, n1, n2, n3, n4, tees,
+        scratch=slots, flops=1 << 25, name="downsweep",
     )
     return out.reshape(line_count, cell_count, species)
 

time: 49.3 us -> 46.4 us (0.941)
  waiting for transfers between devices: 19.4 us -> 12.1 us
  starting transfers between devices: 17.2 us -> 21.7 us
    ppermute x7 -> x8, waiting for transfers between devices: 18.6 us -> 10.5 us  [xor_depth(): return lax.ppermute(value, 'depth', [(i, i ^ bits) for i in range(32)])]
    ppermute x7 -> x8, starting transfers between devices: 10.2 us -> 15.2 us  [xor_depth(): return lax.ppermute(value, 'depth', [(i, i ^ bits) for i in range(32)])]
    ppermute x3, waiting for transfers between devices: 0.46 us -> 1.25 us  [xor_lat(): return lax.ppermute(value, 'lat', [(i, i ^ bits) for i in range(8)])]
    ppermute x1, starting transfers between devices: 2.48 us -> 1.92 us  [on_device(): lax.ppermute(lax.optimization_barrier((densities, line_b))[0], ('depth',...]
    pallas_call x10 -> x8, Pallas kernels: 12.4 us -> 12.2 us  [call(): pl.pallas_call(body, out_shape=outs, in_specs=[pl.BlockSpec(memory_space=...]
  transfers between devices with their start and end apart: 11 -> 12, of which waited for: 8 -> 7; matrix products, arithmetic and copies ran while one was open for 0% -> 0% of each run, Pallas kernels for 12% -> 13%
where the time goes in v10:
time: 46.4 us; the launch traced here: 46.2 us
  starting transfers between devices  21.7 us (47%)
  Pallas kernels  12.2 us (26%)
  waiting for transfers between devices  12.1 us (26%)
    ppermute x8, starting transfers between devices, xor_depth(): return lax.ppermute(value, 'depth', [(i, i ^ bits) for i in range(32)])  15.2 us
    pallas_call x8, Pallas kernels, call(): pl.pallas_call(body, out_shape=outs, in_specs=[pl.BlockSpec(memory_space=...  12.2 us
    ppermute x8, waiting for transfers between devices, xor_depth(): return lax.ppermute(value, 'depth', [(i, i ^ bits) for i in range(32)])  10.5 us
    ppermute x3, starting transfers between devices, xor_lat(): return lax.ppermute(value, 'lat', [(i, i ^ bits) for i in range(8)])  4.52 us
    ppermute x1, starting transfers between devices, on_device(): lax.ppermute(lax.optimization_barrier((densities, line_b))[0], ('depth',...  1.92 us
    ppermute x3, waiting for transfers between devices, xor_lat(): return lax.ppermute(value, 'lat', [(i, i ^ bits) for i in range(8)])  1.25 us
  transfers between devices with their start and end apart: 12, of which 7 were waited for; matrix products, arithmetic and copies ran while one was open for 0% of the time, Pallas kernels for 13%

profile of v10, /device:TPU:32, one launch (start us, length us, event | category | flops | bytes accessed | tf_op | source)
XLA Modules:
  0.0 46.2 jit_solution(6486774292504039546)
XLA Ops:
  0.0 0.1 collective-permute-start
  0.1 3.1 %tree_leaves.1 = (bf16[16,4,64,256]{3,2,1,0:T(8,128)(2,1)S(1)}, bf16[16,3,64,128]{3,2,1,0:T(8,128)(2,1)S(1)}, f32[16,3,64,128]{3,2,1,0:T(8,128)S(1)}, f32[2,64,128]{2,1,0:T(8,128)S(1)}) custom-call(f32[1024,128]{1,0:T(8,128)} %bitcast.22, f32[32,64]{1,0:T(8,128)} %bitcast.16), custom_call_target="tpu_custom_call" | custom-call | flops 1073741824 | bytes 65536 | tf_op jit(solution)/shard_map/tree_leaves/pallas_call | solution.py:427
  3.2 0.0 copy-start.2
  3.2 0.0 collective-permute-done.a_ref
  3.3 1.6 %collective-permute-start.1 = (f32[2,32,64]{2,1,0:T(8,128)S(1)}, f32[2,32,64]{2,1,0:T(8,128)S(1)}, u32[]{:S(2)}, u32[]{:S(2)}) collective-permute-start(f32[2,32,64]{2,1,0:T(8,128)S(1)} %pad_maximum_fusion.1), channel_id=1, source_target_pairs={{0,2},{1,3},{2,0},{3,1},{4,6},{5,7},{6,4},{7,5},{8,10},{9,11},{10,... | collective-permute-start | bytes 49160 | tf_op jit(solution)/shard_map/ppermute | solution.py:454
  4.9 0.7 %react.1 = (f32[32,64]{1,0:T(8,128)S(1)}, f32[64,128]{1,0:T(8,128)S(1)}) custom-call(f32[32,4096]{1,0:T(8,128)S(1)} %bitcast.20, f32[32,64]{1,0:T(8,128)S(1)} %bitcast.12, f32[32,64]{1,0:T(8,128)S(1)} %bitcast.21, f32[32,64]{1,0:T(8,128)S(1)} %bitcast.14, s32[8,8]{1,0:T(8,128)S(1)} %copy-done.7, f32[2,64,128]{2,1,0:T(8,128)S(1)} %get-tuple-element.30.after_ref.cols_ref), custom_call_target="tpu_custom_call" | custom-call | flops 1073741824 | bytes 65536 | tf_op jit(solution)/shard_map/react/pallas_call | solution.py:427
  5.6 0.4 collective-permute-start.3
  6.0 1.2 %collective-permute-done.1.b_ref = f32[2,32,64]{2,1,0:T(8,128)S(1)} collective-permute-done((f32[2,32,64]{2,1,0:T(8,128)S(1)}, f32[2,32,64]{2,1,0:T(8,128)S(1)}, u32[]{:S(2)}, u32[]{:S(2)}) %collective-permute-start.1) | collective-permute-done | bytes 16416 | tf_op jit(solution)/shard_map/ppermute | solution.py:454
  7.3 2.8 %collective-permute-start.2 = (f32[4,32,64]{2,1,0:T(8,128)S(1)}, f32[4,32,64]{2,1,0:T(8,128)S(1)}, u32[]{:S(2)}, u32[]{:S(2)}) collective-permute-start(f32[4,32,64]{2,1,0:T(8,128)S(1)} %pad_maximum_fusion), channel_id=1, source_target_pairs={{0,6},{1,7},{2,4},{3,5},{4,2},{5,3},{6,0},{7,1},{8,14},{9,15},{10,... | collective-permute-start | bytes 98312 | tf_op jit(solution)/shard_map/ppermute | solution.py:454
  10.1 1.9 %collective-permute-start.4 = (f32[1,32,64]{2,1,0:T(8,128)S(1)}, f32[1,32,64]{2,1,0:T(8,128)S(1)}, u32[]{:S(2)}, u32[]{:S(2)}) collective-permute-start(f32[1,32,64]{2,1,0:T(8,128)S(1)} %copy-done), channel_id=1, source_target_pairs={{0,1},{1,0},{2,3},{3,2},{4,5},{5,4},{6,7},{7,6},{8,16},{9,17},{10,... | collective-permute-start | bytes 24584 | tf_op jit(solution)/shard_map/ppermute | solution.py:472
  12.1 1.4 %tree_upper.1 = (bf16[8,4,64,128]{3,2,1,0:T(8,128)(2,1)S(1)}, bf16[4,4,64,128]{3,2,1,0:T(8,128)(2,1)S(1)}, bf16[2,4,64,128]{3,2,1,0:T(8,128)(2,1)S(1)}, bf16[1,64,128]{2,1,0:T(8,128)(2,1)S(1)}, f32[128,128]{1,0:T(8,128)S(1)}) custom-call(bf16[16,3,64,128]{3,2,1,0:T(8,128)(2,1)S(1)} %get-tuple-element.36.n1_ref, ...), custom_call_target="tpu_custom_call" | custom-call | flops 2147483648 | bytes 65536 | tf_op jit(solution)/shard_map/tree_upper/pallas_call | solution.py:427
  13.4 0.0 collective-permute-done.3.even_ref
  13.5 0.4 collective-permute-done.4.odd_ref
  13.9 0.0 collective-permute-done.2.c_ref
  13.9 2.2 %upsweep.1 = (f32[128,128]{1,0:T(8,128)S(1)}, f32[4,64,128]{2,1,0:T(8,128)S(1)}, f32[7,64,128]{2,1,0:T(8,128)S(1)}, f32[7,64,128]{2,1,0:T(8,128)S(1)}) custom-call(s32[1,4]{1,0:T(1,128)S(1)} %copy-done.4, f32[32,64]{1,0:T(8,128)S(1)} %get-tuple-element.31.after_ref.part_ref, f32[1,32,64]{2,1,0:T(8,128)S(1)} %collective-permute-done.a_ref, ...), custom_call_target="tpu_custom_call" | custom-call | flops 33554432 | bytes 65536 | tf_op jit(solution)/shard_map/upsweep/pallas_call | solution.py:427
  16.1 0.9 %collective-permute-start.5 = (f32[128,128]{1,0:T(8,128)S(1)}, f32[128,128]{1,0:T(8,128)S(1)}, u32[]{:S(2)}, u32[]{:S(2)}) collective-permute-start(f32[128,128]{1,0:T(8,128)S(1)} %get-tuple-element.43.own_ref), channel_id=1, source_target_pairs={{0,8},{8,0},{16,24},{24,16},{32,40},{40,32},{48,56},{56,48},{64,72... | collective-permute-start | bytes 196616 | tf_op jit(solution)/shard_map/ppermute | solution.py:457
  16.9 3.8 %collective-permute-start.6 = (f32[128,128]{1,0:T(8,128)S(1)}, f32[128,128]{1,0:T(8,128)S(1)}, u32[]{:S(2)}, u32[]{:S(2)}) collective-permute-start(f32[128,128]{1,0:T(8,128)S(1)} %get-tuple-element.43.own_ref), channel_id=1, source_target_pairs={{0,16},{8,24},{16,0},{24,8},{32,48},{40,56},{48,32},{56,40},{64,80... | collective-permute-start | bytes 196616 | tf_op jit(solution)/shard_map/ppermute | solution.py:457
  20.7 0.5 %collective-permute-start.7 = (f32[128,128]{1,0:T(8,128)S(1)}, f32[128,128]{1,0:T(8,128)S(1)}, u32[]{:S(2)}, u32[]{:S(2)}) collective-permute-start(f32[128,128]{1,0:T(8,128)S(1)} %get-tuple-element.43.own_ref), channel_id=1, source_target_pairs={{0,24},{8,16},{16,8},{24,0},{32,56},{40,48},{48,40},{56,32},{64,88... | collective-permute-start | bytes 196616 | tf_op jit(solution)/shard_map/ppermute | solution.py:457
  21.2 0.0 collective-permute-done.5.x1_ref
  21.2 2.7 %collective-permute-done.6.x2_ref = f32[128,128]{1,0:T(8,128)S(1)} collective-permute-done((f32[128,128]{1,0:T(8,128)S(1)}, f32[128,128]{1,0:T(8,128)S(1)}, u32[]{:S(2)}, u32[]{:S(2)}) %collective-permute-start.6) | collective-permute-done | bytes 65568 | tf_op jit(solution)/shard_map/ppermute | solution.py:457
  23.9 1.6 %collective-permute-done.7.x3_ref = f32[128,128]{1,0:T(8,128)S(1)} collective-permute-done((f32[128,128]{1,0:T(8,128)S(1)}, f32[128,128]{1,0:T(8,128)S(1)}, u32[]{:S(2)}, u32[]{:S(2)}) %collective-permute-start.7) | collective-permute-done | bytes 65568 | tf_op jit(solution)/shard_map/ppermute | solution.py:457
  25.5 1.0 %combine_four.1 = (f32[128,128]{1,0:T(8,128)S(1)}, f32[128,128]{1,0:T(8,128)S(1)}) custom-call(f32[128,128]{1,0:T(8,128)S(1)} %get-tuple-element.43.own_ref, f32[128,128]{1,0:T(8,128)S(1)} %collective-permute-done.5.x1_ref, f32[128,128]{1,0:T(8,128)S(1)} %collective-permute-done.6.x2_ref, f32[128,128]{1,0:T(8,128)S(1)} %collective-permute-done.7.x3_ref), custom_call_target="tpu_custom_call" | custom-call | flops 16777216 | bytes 65536 | tf_op jit(solution)/shard_map/combine_four/pallas_call | solution.py:427
  26.5 5.0 %collective-permute-start.8 = (f32[128,128]{1,0:T(8,128)S(1)}, f32[128,128]{1,0:T(8,128)S(1)}, u32[]{:S(2)}, u32[]{:S(2)}) collective-permute-start(f32[128,128]{1,0:T(8,128)S(1)} %get-tuple-element.44.own_ref), channel_id=1, source_target_pairs={{0,56},{8,48},{16,40},{24,32},{32,24},{40,16},{48,8},{56,0},{64,12... | collective-permute-start | bytes 196616 | tf_op jit(solution)/shard_map/ppermute | solution.py:457
  31.5 2.4 %collective-permute-done.8.other_ref = f32[128,128]{1,0:T(8,128)S(1)} collective-permute-done((f32[128,128]{1,0:T(8,128)S(1)}, f32[128,128]{1,0:T(8,128)S(1)}, u32[]{:S(2)}, u32[]{:S(2)}) %collective-permute-start.8) | collective-permute-done | bytes 65568 | tf_op jit(solution)/shard_map/ppermute | solution.py:457
  33.9 0.5 combine_two.1
  34.3 3.6 %collective-permute-start.10 = (f32[128,128]{1,0:T(8,128)S(1)}, f32[128,128]{1,0:T(8,128)S(1)}, u32[]{:S(2)}, u32[]{:S(2)}) collective-permute-start(f32[128,128]{1,0:T(8,128)S(1)} %get-tuple-element.46.own_ref), channel_id=1, source_target_pairs={{0,128},{8,136},{16,144},{24,152},{32,160},{40,168},{48,176},{56,1... | collective-permute-start | bytes 196616 | tf_op jit(solution)/shard_map/ppermute | solution.py:457
  38.0 1.1 %collective-permute-start.11 = (f32[128,128]{1,0:T(8,128)S(1)}, f32[128,128]{1,0:T(8,128)S(1)}, u32[]{:S(2)}, u32[]{:S(2)}) collective-permute-start(f32[128,128]{1,0:T(8,128)S(1)} %get-tuple-element.46.own_ref), channel_id=1, source_target_pairs={{0,192},{8,200},{16,208},{24,216},{32,224},{40,232},{48,240},{56,2... | collective-permute-start | bytes 196616 | tf_op jit(solution)/shard_map/ppermute | solution.py:457
  39.0 0.0 collective-permute-start.9
  39.0 0.7 %prepare.1 = (bf16[15,64,128]{2,1,0:T(8,128)(2,1)S(1)}, f32[4,64,128]{2,1,0:T(8,128)S(1)}, f32[4,64,128]{2,1,0:T(8,128)S(1)}, f32[64,128]{1,0:T(8,128)S(1)}) custom-call(f32[4,64,128]{2,1,0:T(8,128)S(1)} %get-tuple-element.48.pair_ref, f32[7,64,128]{2,1,0:T(8,128)S(1)} %get-tuple-element.49.v_ref, f32[7,64,128]{2,1,0:T(8,128)S(1)} %get-tuple-element.50.w_ref, ...), custom_call_target="tpu_custom_call" | custom-call | flops 1073741824 | bytes 65536 | tf_op jit(solution)/shard_map/prepare/pallas_call | solution.py:427
  39.7 0.8 %collective-permute-done.10.y2_ref = f32[128,128]{1,0:T(8,128)S(1)} collective-permute-done((f32[128,128]{1,0:T(8,128)S(1)}, f32[128,128]{1,0:T(8,128)S(1)}, u32[]{:S(2)}, u32[]{:S(2)}) %collective-permute-start.10) | collective-permute-done | bytes 65568 | tf_op jit(solution)/shard_map/ppermute | solution.py:457
  40.5 2.9 %collective-permute-done.11.y3_ref = f32[128,128]{1,0:T(8,128)S(1)} collective-permute-done((f32[128,128]{1,0:T(8,128)S(1)}, f32[128,128]{1,0:T(8,128)S(1)}, u32[]{:S(2)}, u32[]{:S(2)}) %collective-permute-start.11) | collective-permute-done | bytes 65568 | tf_op jit(solution)/shard_map/ppermute | solution.py:457
  43.4 2.8 %downsweep.1 = f32[32,64]{1,0:T(8,128)} custom-call(f32[128,128]{1,0:T(8,128)S(1)} %get-tuple-element.46.own_ref, f32[128,128]{1,0:T(8,128)S(1)} %collective-permute-done.9.y1_ref, f32[128,128]{1,0:T(8,128)S(1)} %collective-permute-done.10.y2_ref, f32[128,128]{1,0:T(8,128)S(1)} %collective-permute-done.11.y3_ref, ...), custom_call_target="tpu_custom_call" | custom-call | flops 33554432 | bytes 65536 | tf_op jit(solution)/shard_map/downsweep/pallas_call | solution.py:427
  (18 shorter events, 0.0 us)
Async XLA Ops:
  0.0 3.2 %copy-start = (f32[1,32,64]{2,1,0:T(8,128)S(1)}, f32[1,32,64]{2,1,0:T(8,128)}, u32[]{:S(2)}) copy-start(f32[1,32,64]{2,1,0:T(8,128)} %param.9) | copy-start | bytes 24580
  0.0 4.9 %copy-start.1 = (f32[1,32,64]{2,1,0:T(8,128)S(1)}, f32[1,32,64]{2,1,0:T(8,128)}, u32[]{:S(2)}) copy-start(f32[1,32,64]{2,1,0:T(8,128)} %param.13) | copy-start | bytes 24580
  0.0 4.9 %copy-start.5 = (f32[1,32,4096]{2,1,0:T(8,128)S(1)}, f32[1,32,4096]{2,1,0:T(8,128)}, u32[]{:S(2)}) copy-start(f32[1,32,4096]{2,1,0:T(8,128)} %param.11) | copy-start | bytes 1572868
  0.0 4.8 %copy-start.6 = (f32[1,32,64]{2,1,0:T(8,128)S(1)}, f32[1,32,64]{2,1,0:T(8,128)}, u32[]{:S(2)}) copy-start(f32[1,32,64]{2,1,0:T(8,128)} %param.10) | copy-start | bytes 24580
  0.0 4.8 %copy-start.7 = (s32[8,8]{1,0:T(8,128)S(1)}, s32[8,8]{1,0:T(8,128)}, u32[]{:S(2)}) copy-start(s32[8,8]{1,0:T(8,128)} %pat_ref.1) | copy-start | bytes 772
  0.0 3.2 %collective-permute-start = (f32[1,32,64]{2,1,0:T(8,128)}, f32[1,32,64]{2,1,0:T(8,128)S(1)}, u32[]{:S(2)}, u32[]{:S(2)}) collective-permute-start(f32[1,32,64]{2,1,0:T(8,128)} %param.9), channel_id=1, source_target_pairs={{0,1},{1,0},{2,3},{3,2},{4,5},{5,4},{6,7},{7,6},{8,9},{9,8},{10,11... | collective-permute-start | bytes 24584 | tf_op jit(solution)/shard_map/ppermute | solution.py:454
  3.2 8.8 %copy-start.2 = (f32[1,32,64]{2,1,0:T(8,128)S(1)}, f32[1,32,64]{2,1,0:T(8,128)}, u32[]{:S(2)}) copy-start(f32[1,32,64]{2,1,0:T(8,128)} %param.17) | copy-start | bytes 24580
  3.3 4.0 %collective-permute-start.1 = (f32[2,32,64]{2,1,0:T(8,128)S(1)}, f32[2,32,64]{2,1,0:T(8,128)S(1)}, u32[]{:S(2)}, u32[]{:S(2)}) collective-permute-start(f32[2,32,64]{2,1,0:T(8,128)S(1)} %pad_maximum_fusion.1), channel_id=1, source_target_pairs={{0,2},{1,3},{2,0},{3,1},{4,6},{5,7},{6,4},{7,5},{8,10},{9,11},{10,... | collective-permute-start | bytes 49160 | tf_op jit(solution)/shard_map/ppermute | solution.py:454
  5.6 7.8 %collective-permute-start.3 = (f32[1,32,64]{2,1,0:T(8,128)S(1)}, f32[1,32,64]{2,1,0:T(8,128)S(1)}, u32[]{:S(2)}, u32[]{:S(2)}) collective-permute-start(f32[1,32,64]{2,1,0:T(8,128)S(1)} %copy-done), channel_id=1, source_target_pairs={{0,8},{8,0},{16,24},{24,16},{32,40},{40,32},{48,56},{56,48},{64,72... | collective-permute-start | bytes 24584 | tf_op jit(solution)/shard_map/ppermute | solution.py:457
  7.3 6.6 %collective-permute-start.2 = (f32[4,32,64]{2,1,0:T(8,128)S(1)}, f32[4,32,64]{2,1,0:T(8,128)S(1)}, u32[]{:S(2)}, u32[]{:S(2)}) collective-permute-start(f32[4,32,64]{2,1,0:T(8,128)S(1)} %pad_maximum_fusion), channel_id=1, source_target_pairs={{0,6},{1,7},{2,4},{3,5},{4,2},{5,3},{6,0},{7,1},{8,14},{9,15},{10,... | collective-permute-start | bytes 98312 | tf_op jit(solution)/shard_map/ppermute | solution.py:454
  10.1 3.7 %collective-permute-start.4 = (f32[1,32,64]{2,1,0:T(8,128)S(1)}, f32[1,32,64]{2,1,0:T(8,128)S(1)}, u32[]{:S(2)}, u32[]{:S(2)}) collective-permute-start(f32[1,32,64]{2,1,0:T(8,128)S(1)} %copy-done), channel_id=1, source_target_pairs={{0,1},{1,0},{2,3},{3,2},{4,5},{5,4},{6,7},{7,6},{8,16},{9,17},{10,... | collective-permute-start | bytes 24584 | tf_op jit(solution)/shard_map/ppermute | solution.py:472
  12.1 1.8 %copy-start.3 = (f32[1,32,64]{2,1,0:T(8,128)S(1)}, f32[1,32,64]{2,1,0:T(8,128)}, u32[]{:S(2)}) copy-start(f32[1,32,64]{2,1,0:T(8,128)} %param.14) | copy-start | bytes 24580
  12.1 1.8 %copy-start.4 = (s32[1,4]{1,0:T(1,128)S(1)}, s32[1,4]{1,0:T(1,128)}, u32[]{:S(2)}) copy-start(s32[1,4]{1,0:T(1,128)} %neigh_ref.1) | copy-start | bytes 52
  16.1 5.1 %collective-permute-start.5 = (f32[128,128]{1,0:T(8,128)S(1)}, f32[128,128]{1,0:T(8,128)S(1)}, u32[]{:S(2)}, u32[]{:S(2)}) collective-permute-start(f32[128,128]{1,0:T(8,128)S(1)} %get-tuple-element.43.own_ref), channel_id=1, source_target_pairs={{0,8},{8,0},{16,24},{24,16},{32,40},{40,32},{48,56},{56,48},{64,72... | collective-permute-start | bytes 196616 | tf_op jit(solution)/shard_map/ppermute | solution.py:457
  16.9 7.0 %collective-permute-start.6 = (f32[128,128]{1,0:T(8,128)S(1)}, f32[128,128]{1,0:T(8,128)S(1)}, u32[]{:S(2)}, u32[]{:S(2)}) collective-permute-start(f32[128,128]{1,0:T(8,128)S(1)} %get-tuple-element.43.own_ref), channel_id=1, source_target_pairs={{0,16},{8,24},{16,0},{24,8},{32,48},{40,56},{48,32},{56,40},{64,80... | collective-permute-start | bytes 196616 | tf_op jit(solution)/shard_map/ppermute | solution.py:457
  20.7 4.8 %collective-permute-start.7 = (f32[128,128]{1,0:T(8,128)S(1)}, f32[128,128]{1,0:T(8,128)S(1)}, u32[]{:S(2)}, u32[]{:S(2)}) collective-permute-start(f32[128,128]{1,0:T(8,128)S(1)} %get-tuple-element.43.own_ref), channel_id=1, source_target_pairs={{0,24},{8,16},{16,8},{24,0},{32,56},{40,48},{48,40},{56,32},{64,88... | collective-permute-start | bytes 196616 | tf_op jit(solution)/shard_map/ppermute | solution.py:457
  26.5 7.4 %collective-permute-start.8 = (f32[128,128]{1,0:T(8,128)S(1)}, f32[128,128]{1,0:T(8,128)S(1)}, u32[]{:S(2)}, u32[]{:S(2)}) collective-permute-start(f32[128,128]{1,0:T(8,128)S(1)} %get-tuple-element.44.own_ref), channel_id=1, source_target_pairs={{0,56},{8,48},{16,40},{24,32},{32,24},{40,16},{48,8},{56,0},{64,12... | collective-permute-start | bytes 196616 | tf_op jit(solution)/shard_map/ppermute | solution.py:457
  34.3 6.2 %collective-permute-start.10 = (f32[128,128]{1,0:T(8,128)S(1)}, f32[128,128]{1,0:T(8,128)S(1)}, u32[]{:S(2)}, u32[]{:S(2)}) collective-permute-start(f32[128,128]{1,0:T(8,128)S(1)} %get-tuple-element.46.own_ref), channel_id=1, source_target_pairs={{0,128},{8,136},{16,144},{24,152},{32,160},{40,168},{48,176},{56,1... | collective-permute-start | bytes 196616 | tf_op jit(solution)/shard_map/ppermute | solution.py:457
  38.0 5.5 %collective-permute-start.11 = (f32[128,128]{1,0:T(8,128)S(1)}, f32[128,128]{1,0:T(8,128)S(1)}, u32[]{:S(2)}, u32[]{:S(2)}) collective-permute-start(f32[128,128]{1,0:T(8,128)S(1)} %get-tuple-element.46.own_ref), channel_id=1, source_target_pairs={{0,192},{8,200},{16,208},{24,216},{32,224},{40,232},{48,240},{56,2... | collective-permute-start | bytes 196616 | tf_op jit(solution)/shard_map/ppermute | solution.py:457
  39.0 4.4 %collective-permute-start.9 = (f32[128,128]{1,0:T(8,128)S(1)}, f32[128,128]{1,0:T(8,128)S(1)}, u32[]{:S(2)}, u32[]{:S(2)}) collective-permute-start(f32[128,128]{1,0:T(8,128)S(1)} %get-tuple-element.46.own_ref), channel_id=1, source_target_pairs={{0,64},{8,72},{16,80},{24,88},{32,96},{40,104},{48,112},{56,120},{... | collective-permute-start | bytes 196616 | tf_op jit(solution)/shard_map/ppermute | solution.py:457

commit v11 on v10

--- a/solution.py
+++ b/solution.py
@@ -75,13 +75,8 @@
         node[j, 3] = pack(u)
 
 
-def tree_leaves(fac_hbm, coup_hbm, quad_ref, n1_ref, full_ref, cols_ref, fac_ref, coup_ref, rows, sems):
-    parts = [pl.ds(i * 256, 256) for i in range(4)]
-    pairs = [(coup_hbm, coup_ref)] + [(fac_hbm.at[part], fac_ref.at[part]) for part in parts]
-    copies = [pltpu.make_async_copy(a, b, sems.at[i]) for i, (a, b) in enumerate(pairs)]
-    for copy in copies:
-        copy.start()
-    copies[0].wait()
+def tree_leaves(fac_ref, coup_ref, after_ref, quad_ref, n1_ref, full_ref, cols_ref, rows):
+    del after_ref
     c = coup_ref[...]
     cols_ref[0] = column(c[CELLS - 1 : CELLS])
     cols_ref[1] = column(1.0 / c[0:1])
@@ -100,8 +95,6 @@
         return a * c2[before : before + 1] - eye, a * c2[k : k + 1] - eye
 
     for j in range(CELLS // 2):
-        if j % 4 == 0:
-            copies[1 + j // 4].wait()
         p1, q1 = leaf(2 * j)
         p2, q2 = leaf(2 * j + 1)
         kq1 = pack(q1)
@@ -140,10 +133,18 @@
         node, full = node_to, full_to
 
 
-def react(jac_ref, dens_ref, src_ref, tran_ref, pat_ref, after_ref, out_ref, flux_ref):
-    del after_ref
+def react(jac_hbm, dens_hbm, src_hbm, tran_hbm, pat_hbm, out_ref, flux_ref, jac_ref, dens_ref, src_ref, tran_ref,
+          pat_ref, sems):
+    parts = [(slice(None), pl.ds(i * 1024, 1024)) for i in range(4)]
+    pairs = [(dens_hbm, dens_ref), (pat_hbm, pat_ref)] + [(jac_hbm.at[part], jac_ref.at[part]) for part in parts]
+    pairs += [(src_hbm, src_ref), (tran_hbm, tran_ref)]
+    copies = [pltpu.make_async_copy(a, b, sems.at[i]) for i, (a, b) in enumerate(pairs)]
+    for copy in copies:
+        copy.start()
     half = lanes((128, N)) % 2 == lax.broadcasted_iota(jnp.int32, (128, N), 0) // N
     half = jnp.where(half, 1.0, 0.0).astype(bf16)
+    copies[0].wait()
+    copies[1].wait()
     u = dens_ref[...]
     u2 = jnp.concatenate([u, u], axis=1)
     lane8 = lanes((8, 128))
@@ -154,11 +155,15 @@
     lane = lanes((CELLS, N))
     acc = jnp.zeros((CELLS, N), f32)
     for m in range(32):
+        if m % 8 == 0:
+            copies[2 + m // 8].wait()
         y = jac_ref[:, m * 128 : (m + 1) * 128] * (u2 * mask_rows[m // 4 : m // 4 + 1])
         hi = y.astype(bf16)
         lo = (y - hi.astype(f32)).astype(bf16)
         z = jnp.dot(hi, half, preferred_element_type=f32) + jnp.dot(lo, half, preferred_element_type=f32)
         acc = jnp.where(lane // 2 == m, z, acc)
+    copies[6].wait()
+    copies[7].wait()
     tran = tran_ref[...]
     flux = tran * u
     flux_ref[...] = column(flux[CELLS - 1 : CELLS])
@@ -457,18 +462,18 @@
         return lax.ppermute(value, "depth", [(i, i ^ bits) for i in range(32)])
 
     line_a = xor_lat(densities, 1)
+    part, flux = call(
+        react, (sds(CELLS, N), sds(N, 128)), jac, u, src, tran, pattern, hbm=5, flops=1 << 30, name="react",
+        scratch=[pltpu.VMEM((CELLS, N * N), f32)] + [pltpu.VMEM((CELLS, N), f32)] * 3
+        + [pltpu.VMEM((8, 8), jnp.int32), pltpu.SemaphoreType.DMA((8,))],
+    )
+    line_b = xor_lat(jnp.concatenate([densities, line_a], axis=0), 2)
     quad, n1, full, cols = call(
         tree_leaves,
         (sds(16, 4, N, 256, dtype=bf16), sds(16, 3, N, 128, dtype=bf16), sds(16, 3, N, 128), sds(2, N, 128)),
-        fac, coup, hbm=2, flops=1 << 30, name="tree_leaves",
-        scratch=[pltpu.VMEM((1024, 128), f32), pltpu.VMEM((CELLS, N), f32), pltpu.VMEM((2, N, 128), f32),
-                 pltpu.SemaphoreType.DMA((5,))],
-    )
-    line_b = xor_lat(jnp.concatenate([densities, line_a], axis=0), 2)
-    part, flux = call(
-        react, (sds(CELLS, N), sds(N, 128)), jac, u, src, tran, pattern, cols, flops=1 << 30, name="react",
-    )
-    top_even = xor_depth(lax.optimization_barrier((densities, part))[0], 1)
+        fac, coup, part, scratch=[pltpu.VMEM((2, N, 128), f32)], flops=2 << 30, name="tree_leaves",
+    )
+    top_even = xor_depth(lax.optimization_barrier((densities, cols))[0], 1)
     top_odd = lax.ppermute(
         lax.optimization_barrier((densities, line_b))[0], ("depth", "lat"),
         [(8 * i + l, 8 * (i + 1 if i % 2 else i - 1) + l if 0 < i < 31 else 8 * i + (l ^ 1))

time: 46.4 us -> 45.5 us (0.981)
  waiting for transfers between devices: 12.1 us -> 11.2 us
    ppermute x3, waiting for transfers between devices: 1.25 us -> 0.46 us  [xor_lat(): return lax.ppermute(value, 'lat', [(i, i ^ bits) for i in range(8)])]
    ppermute x1, starting transfers between devices: 1.92 us -> 2.48 us  [on_device(): lax.ppermute(lax.optimization_barrier((densities, line_b))[0], ('depth',...]
    ppermute x8, starting transfers between devices: 15.2 us -> 14.7 us  [xor_depth(): return lax.ppermute(value, 'depth', [(i, i ^ bits) for i in range(32)])]
where the time goes in v11:
time: 45.5 us; the launch traced here: 45.3 us
  starting transfers between devices  21.7 us (48%)
  Pallas kernels  12.2 us (27%)
  waiting for transfers between devices  11.2 us (25%)
    ppermute x8, starting transfers between devices, xor_depth(): return lax.ppermute(value, 'depth', [(i, i ^ bits) for i in range(32)])  14.7 us
    pallas_call x8, Pallas kernels, call(): pl.pallas_call(body, out_shape=outs, in_specs=[pl.BlockSpec(memory_space=...  12.2 us
    ppermute x8, waiting for transfers between devices, xor_depth(): return lax.ppermute(value, 'depth', [(i, i ^ bits) for i in range(32)])  10.4 us
    ppermute x3, starting transfers between devices, xor_lat(): return lax.ppermute(value, 'lat', [(i, i ^ bits) for i in range(8)])  4.52 us
    ppermute x1, starting transfers between devices, on_device(): lax.ppermute(lax.optimization_barrier((densities, line_b))[0], ('depth',...  2.48 us
  transfers between devices with their start and end apart: 12, of which 7 were waited for; matrix products, arithmetic and copies ran while one was open for 0% of the time, Pallas kernels for 13%

profile of v11, /device:TPU:32, one launch (start us, length us, event | category | flops | bytes accessed | tf_op | source)
XLA Modules:
  0.0 45.3 jit_solution(3129017433258937137)
XLA Ops:
  0.0 0.1 collective-permute-start
  0.1 2.2 %react.1 = (f32[32,64]{1,0:T(8,128)S(1)}, f32[64,128]{1,0:T(8,128)S(1)}) custom-call(f32[32,4096]{1,0:T(8,128)} %bitcast.21, f32[32,64]{1,0:T(8,128)} %bitcast.12, f32[32,64]{1,0:T(8,128)} %bitcast.22, f32[32,64]{1,0:T(8,128)} %bitcast.14, s32[8,8]{1,0:T(8,128)} %pat_hbm.1), custom_call_target="tpu_custom_call" | custom-call | flops 1073741824 | bytes 65536 | tf_op jit(solution)/shard_map/react/pallas_call | solution.py:432
  2.3 0.0 collective-permute-done.a_ref
  2.3 1.6 %collective-permute-start.1 = (f32[2,32,64]{2,1,0:T(8,128)S(1)}, f32[2,32,64]{2,1,0:T(8,128)S(1)}, u32[]{:S(2)}, u32[]{:S(2)}) collective-permute-start(f32[2,32,64]{2,1,0:T(8,128)S(1)} %pad_maximum_fusion.1), channel_id=1, source_target_pairs={{0,2},{1,3},{2,0},{3,1},{4,6},{5,7},{6,4},{7,5},{8,10},{9,11},{10,... | collective-permute-start | bytes 49160 | tf_op jit(solution)/shard_map/ppermute | solution.py:459
  3.9 1.6 %tree_leaves.1 = (bf16[16,4,64,256]{3,2,1,0:T(8,128)(2,1)S(1)}, bf16[16,3,64,128]{3,2,1,0:T(8,128)(2,1)S(1)}, f32[16,3,64,128]{3,2,1,0:T(8,128)S(1)}, f32[2,64,128]{2,1,0:T(8,128)S(1)}) custom-call(f32[1024,128]{1,0:T(8,128)S(1)} %bitcast.20, f32[32,64]{1,0:T(8,128)S(1)} %bitcast.17, f32[32,64]{1,0:T(8,128)S(1)} %get-tuple-element.30.after_ref.part_ref), custom_call_target="tpu_custom_call" | custom-call | flops 2147483648 | bytes 65536 | tf_op jit(solution)/shard_map/tree_leaves/pallas_call | solution.py:432
  5.6 0.3 collective-permute-start.3
  5.9 0.5 %collective-permute-done.1.b_ref = f32[2,32,64]{2,1,0:T(8,128)S(1)} collective-permute-done((f32[2,32,64]{2,1,0:T(8,128)S(1)}, f32[2,32,64]{2,1,0:T(8,128)S(1)}, u32[]{:S(2)}, u32[]{:S(2)}) %collective-permute-start.1) | collective-permute-done | bytes 16416 | tf_op jit(solution)/shard_map/ppermute | solution.py:459
  6.3 2.8 %collective-permute-start.2 = (f32[4,32,64]{2,1,0:T(8,128)S(1)}, f32[4,32,64]{2,1,0:T(8,128)S(1)}, u32[]{:S(2)}, u32[]{:S(2)}) collective-permute-start(f32[4,32,64]{2,1,0:T(8,128)S(1)} %pad_maximum_fusion), channel_id=1, source_target_pairs={{0,6},{1,7},{2,4},{3,5},{4,2},{5,3},{6,0},{7,1},{8,14},{9,15},{10,... | collective-permute-start | bytes 98312 | tf_op jit(solution)/shard_map/ppermute | solution.py:459
  9.2 2.5 %collective-permute-start.4 = (f32[1,32,64]{2,1,0:T(8,128)S(1)}, f32[1,32,64]{2,1,0:T(8,128)S(1)}, u32[]{:S(2)}, u32[]{:S(2)}) collective-permute-start(f32[1,32,64]{2,1,0:T(8,128)S(1)} %copy-done), channel_id=1, source_target_pairs={{0,1},{1,0},{2,3},{3,2},{4,5},{5,4},{6,7},{7,6},{8,16},{9,17},{10,... | collective-permute-start | bytes 24584 | tf_op jit(solution)/shard_map/ppermute | solution.py:477
  11.7 1.4 %tree_upper.1 = (bf16[8,4,64,128]{3,2,1,0:T(8,128)(2,1)S(1)}, bf16[4,4,64,128]{3,2,1,0:T(8,128)(2,1)S(1)}, bf16[2,4,64,128]{3,2,1,0:T(8,128)(2,1)S(1)}, bf16[1,64,128]{2,1,0:T(8,128)(2,1)S(1)}, f32[128,128]{1,0:T(8,128)S(1)}) custom-call(bf16[16,3,64,128]{3,2,1,0:T(8,128)(2,1)S(1)} %get-tuple-element.36.n1_ref, ...), custom_call_target="tpu_custom_call" | custom-call | flops 2147483648 | bytes 65536 | tf_op jit(solution)/shard_map/tree_upper/pallas_call | solution.py:432
  13.1 0.0 collective-permute-done.3.even_ref
  13.1 0.3 collective-permute-done.4.odd_ref
  13.4 0.0 collective-permute-done.2.c_ref
  13.4 2.2 %upsweep.1 = (f32[128,128]{1,0:T(8,128)S(1)}, f32[4,64,128]{2,1,0:T(8,128)S(1)}, f32[7,64,128]{2,1,0:T(8,128)S(1)}, f32[7,64,128]{2,1,0:T(8,128)S(1)}) custom-call(s32[1,4]{1,0:T(1,128)S(1)} %copy-done.4, f32[32,64]{1,0:T(8,128)S(1)} %get-tuple-element.30.after_ref.part_ref, f32[1,32,64]{2,1,0:T(8,128)S(1)} %collective-permute-done.a_ref, ...), custom_call_target="tpu_custom_call" | custom-call | flops 33554432 | bytes 65536 | tf_op jit(solution)/shard_map/upsweep/pallas_call | solution.py:432
  15.6 0.3 collective-permute-start.5
  15.9 3.9 %collective-permute-start.6 = (f32[128,128]{1,0:T(8,128)S(1)}, f32[128,128]{1,0:T(8,128)S(1)}, u32[]{:S(2)}, u32[]{:S(2)}) collective-permute-start(f32[128,128]{1,0:T(8,128)S(1)} %get-tuple-element.43.own_ref), channel_id=1, source_target_pairs={{0,16},{8,24},{16,0},{24,8},{32,48},{40,56},{48,32},{56,40},{64,80... | collective-permute-start | bytes 196616 | tf_op jit(solution)/shard_map/ppermute | solution.py:462
  19.8 0.5 %collective-permute-start.7 = (f32[128,128]{1,0:T(8,128)S(1)}, f32[128,128]{1,0:T(8,128)S(1)}, u32[]{:S(2)}, u32[]{:S(2)}) collective-permute-start(f32[128,128]{1,0:T(8,128)S(1)} %get-tuple-element.43.own_ref), channel_id=1, source_target_pairs={{0,24},{8,16},{16,8},{24,0},{32,56},{40,48},{48,40},{56,32},{64,88... | collective-permute-start | bytes 196616 | tf_op jit(solution)/shard_map/ppermute | solution.py:462
  20.3 0.0 collective-permute-done.5.x1_ref
  20.3 2.5 %collective-permute-done.6.x2_ref = f32[128,128]{1,0:T(8,128)S(1)} collective-permute-done((f32[128,128]{1,0:T(8,128)S(1)}, f32[128,128]{1,0:T(8,128)S(1)}, u32[]{:S(2)}, u32[]{:S(2)}) %collective-permute-start.6) | collective-permute-done | bytes 65568 | tf_op jit(solution)/shard_map/ppermute | solution.py:462
  22.7 1.9 %collective-permute-done.7.x3_ref = f32[128,128]{1,0:T(8,128)S(1)} collective-permute-done((f32[128,128]{1,0:T(8,128)S(1)}, f32[128,128]{1,0:T(8,128)S(1)}, u32[]{:S(2)}, u32[]{:S(2)}) %collective-permute-start.7) | collective-permute-done | bytes 65568 | tf_op jit(solution)/shard_map/ppermute | solution.py:462
  24.6 1.0 %combine_four.1 = (f32[128,128]{1,0:T(8,128)S(1)}, f32[128,128]{1,0:T(8,128)S(1)}) custom-call(f32[128,128]{1,0:T(8,128)S(1)} %get-tuple-element.43.own_ref, f32[128,128]{1,0:T(8,128)S(1)} %collective-permute-done.5.x1_ref, f32[128,128]{1,0:T(8,128)S(1)} %collective-permute-done.6.x2_ref, f32[128,128]{1,0:T(8,128)S(1)} %collective-permute-done.7.x3_ref), custom_call_target="tpu_custom_call" | custom-call | flops 16777216 | bytes 65536 | tf_op jit(solution)/shard_map/combine_four/pallas_call | solution.py:432
  25.6 5.0 %collective-permute-start.8 = (f32[128,128]{1,0:T(8,128)S(1)}, f32[128,128]{1,0:T(8,128)S(1)}, u32[]{:S(2)}, u32[]{:S(2)}) collective-permute-start(f32[128,128]{1,0:T(8,128)S(1)} %get-tuple-element.44.own_ref), channel_id=1, source_target_pairs={{0,56},{8,48},{16,40},{24,32},{32,24},{40,16},{48,8},{56,0},{64,12... | collective-permute-start | bytes 196616 | tf_op jit(solution)/shard_map/ppermute | solution.py:462
  30.6 2.4 %collective-permute-done.8.other_ref = f32[128,128]{1,0:T(8,128)S(1)} collective-permute-done((f32[128,128]{1,0:T(8,128)S(1)}, f32[128,128]{1,0:T(8,128)S(1)}, u32[]{:S(2)}, u32[]{:S(2)}) %collective-permute-start.8) | collective-permute-done | bytes 65568 | tf_op jit(solution)/shard_map/ppermute | solution.py:462
  32.9 0.5 %combine_two.1 = (f32[128,128]{1,0:T(8,128)S(1)}, f32[5,64,128]{2,1,0:T(8,128)S(1)}) custom-call(f32[128,128]{1,0:T(8,128)S(1)} %get-tuple-element.44.own_ref, f32[128,128]{1,0:T(8,128)S(1)} %collective-permute-done.8.other_ref, f32[128,128]{1,0:T(8,128)S(1)} %get-tuple-element.45.fun_ref), custom_call_target="tpu_custom_call" | custom-call | flops 16777216 | bytes 65536 | tf_op jit(solution)/shard_map/combine_two/pallas_call | solution.py:432
  33.4 3.6 %collective-permute-start.10 = (f32[128,128]{1,0:T(8,128)S(1)}, f32[128,128]{1,0:T(8,128)S(1)}, u32[]{:S(2)}, u32[]{:S(2)}) collective-permute-start(f32[128,128]{1,0:T(8,128)S(1)} %get-tuple-element.46.own_ref), channel_id=1, source_target_pairs={{0,128},{8,136},{16,144},{24,152},{32,160},{40,168},{48,176},{56,1... | collective-permute-start | bytes 196616 | tf_op jit(solution)/shard_map/ppermute | solution.py:462
  37.0 1.1 %collective-permute-start.11 = (f32[128,128]{1,0:T(8,128)S(1)}, f32[128,128]{1,0:T(8,128)S(1)}, u32[]{:S(2)}, u32[]{:S(2)}) collective-permute-start(f32[128,128]{1,0:T(8,128)S(1)} %get-tuple-element.46.own_ref), channel_id=1, source_target_pairs={{0,192},{8,200},{16,208},{24,216},{32,224},{40,232},{48,240},{56,2... | collective-permute-start | bytes 196616 | tf_op jit(solution)/shard_map/ppermute | solution.py:462
  38.1 0.0 collective-permute-start.9
  38.1 0.7 %prepare.1 = (bf16[15,64,128]{2,1,0:T(8,128)(2,1)S(1)}, f32[4,64,128]{2,1,0:T(8,128)S(1)}, f32[4,64,128]{2,1,0:T(8,128)S(1)}, f32[64,128]{1,0:T(8,128)S(1)}) custom-call(f32[4,64,128]{2,1,0:T(8,128)S(1)} %get-tuple-element.48.pair_ref, f32[7,64,128]{2,1,0:T(8,128)S(1)} %get-tuple-element.49.v_ref, f32[7,64,128]{2,1,0:T(8,128)S(1)} %get-tuple-element.50.w_ref, ...), custom_call_target="tpu_custom_call" | custom-call | flops 1073741824 | bytes 65536 | tf_op jit(solution)/shard_map/prepare/pallas_call | solution.py:432
  38.8 1.0 %collective-permute-done.10.y2_ref = f32[128,128]{1,0:T(8,128)S(1)} collective-permute-done((f32[128,128]{1,0:T(8,128)S(1)}, f32[128,128]{1,0:T(8,128)S(1)}, u32[]{:S(2)}, u32[]{:S(2)}) %collective-permute-start.10) | collective-permute-done | bytes 65568 | tf_op jit(solution)/shard_map/ppermute | solution.py:462
  39.8 2.7 %collective-permute-done.11.y3_ref = f32[128,128]{1,0:T(8,128)S(1)} collective-permute-done((f32[128,128]{1,0:T(8,128)S(1)}, f32[128,128]{1,0:T(8,128)S(1)}, u32[]{:S(2)}, u32[]{:S(2)}) %collective-permute-start.11) | collective-permute-done | bytes 65568 | tf_op jit(solution)/shard_map/ppermute | solution.py:462
  42.5 0.0 collective-permute-done.9.y1_ref
  42.5 2.8 %downsweep.1 = f32[32,64]{1,0:T(8,128)} custom-call(f32[128,128]{1,0:T(8,128)S(1)} %get-tuple-element.46.own_ref, f32[128,128]{1,0:T(8,128)S(1)} %collective-permute-done.9.y1_ref, f32[128,128]{1,0:T(8,128)S(1)} %collective-permute-done.10.y2_ref, f32[128,128]{1,0:T(8,128)S(1)} %collective-permute-done.11.y3_ref, ...), custom_call_target="tpu_custom_call" | custom-call | flops 33554432 | bytes 65536 | tf_op jit(solution)/shard_map/downsweep/pallas_call | solution.py:432
  (14 shorter events, 0.0 us)
Async XLA Ops:
  0.0 2.3 %copy-start = (f32[1,32,64]{2,1,0:T(8,128)S(1)}, f32[1,32,64]{2,1,0:T(8,128)}, u32[]{:S(2)}) copy-start(f32[1,32,64]{2,1,0:T(8,128)} %param.9) | copy-start | bytes 24580
  0.0 3.9 %copy-start.3 = (f32[1,32,64]{2,1,0:T(8,128)S(1)}, f32[1,32,64]{2,1,0:T(8,128)}, u32[]{:S(2)}) copy-start(f32[1,32,64]{2,1,0:T(8,128)} %param.17) | copy-start | bytes 24580
  0.0 3.9 %copy-start.5 = (f32[1,32,4096]{2,1,0:T(8,128)S(1)}, f32[1,32,4096]{2,1,0:T(8,128)}, u32[]{:S(2)}) copy-start(f32[1,32,4096]{2,1,0:T(8,128)} %param.16) | copy-start | bytes 1572868
  0.0 2.3 %collective-permute-start = (f32[1,32,64]{2,1,0:T(8,128)}, f32[1,32,64]{2,1,0:T(8,128)S(1)}, u32[]{:S(2)}, u32[]{:S(2)}) collective-permute-start(f32[1,32,64]{2,1,0:T(8,128)} %param.9), channel_id=1, source_target_pairs={{0,1},{1,0},{2,3},{3,2},{4,5},{5,4},{6,7},{7,6},{8,9},{9,8},{10,11... | collective-permute-start | bytes 24584 | tf_op jit(solution)/shard_map/ppermute | solution.py:459
  2.3 4.0 %collective-permute-start.1 = (f32[2,32,64]{2,1,0:T(8,128)S(1)}, f32[2,32,64]{2,1,0:T(8,128)S(1)}, u32[]{:S(2)}, u32[]{:S(2)}) collective-permute-start(f32[2,32,64]{2,1,0:T(8,128)S(1)} %pad_maximum_fusion.1), channel_id=1, source_target_pairs={{0,2},{1,3},{2,0},{3,1},{4,6},{5,7},{6,4},{7,5},{8,10},{9,11},{10,... | collective-permute-start | bytes 49160 | tf_op jit(solution)/shard_map/ppermute | solution.py:459
  5.6 7.5 %collective-permute-start.3 = (f32[1,32,64]{2,1,0:T(8,128)S(1)}, f32[1,32,64]{2,1,0:T(8,128)S(1)}, u32[]{:S(2)}, u32[]{:S(2)}) collective-permute-start(f32[1,32,64]{2,1,0:T(8,128)S(1)} %copy-done), channel_id=1, source_target_pairs={{0,8},{8,0},{16,24},{24,16},{32,40},{40,32},{48,56},{56,48},{64,72... | collective-permute-start | bytes 24584 | tf_op jit(solution)/shard_map/ppermute | solution.py:462
  6.3 7.0 %collective-permute-start.2 = (f32[4,32,64]{2,1,0:T(8,128)S(1)}, f32[4,32,64]{2,1,0:T(8,128)S(1)}, u32[]{:S(2)}, u32[]{:S(2)}) collective-permute-start(f32[4,32,64]{2,1,0:T(8,128)S(1)} %pad_maximum_fusion), channel_id=1, source_target_pairs={{0,6},{1,7},{2,4},{3,5},{4,2},{5,3},{6,0},{7,1},{8,14},{9,15},{10,... | collective-permute-start | bytes 98312 | tf_op jit(solution)/shard_map/ppermute | solution.py:459
  9.2 4.2 %collective-permute-start.4 = (f32[1,32,64]{2,1,0:T(8,128)S(1)}, f32[1,32,64]{2,1,0:T(8,128)S(1)}, u32[]{:S(2)}, u32[]{:S(2)}) collective-permute-start(f32[1,32,64]{2,1,0:T(8,128)S(1)} %copy-done), channel_id=1, source_target_pairs={{0,1},{1,0},{2,3},{3,2},{4,5},{5,4},{6,7},{7,6},{8,16},{9,17},{10,... | collective-permute-start | bytes 24584 | tf_op jit(solution)/shard_map/ppermute | solution.py:477
  11.7 1.7 %copy-start.1 = (f32[1,32,64]{2,1,0:T(8,128)S(1)}, f32[1,32,64]{2,1,0:T(8,128)}, u32[]{:S(2)}) copy-start(f32[1,32,64]{2,1,0:T(8,128)} %param.13) | copy-start | bytes 24580
  11.7 1.7 %copy-start.2 = (f32[1,32,64]{2,1,0:T(8,128)S(1)}, f32[1,32,64]{2,1,0:T(8,128)}, u32[]{:S(2)}) copy-start(f32[1,32,64]{2,1,0:T(8,128)} %param.14) | copy-start | bytes 24580
  11.7 1.7 %copy-start.4 = (s32[1,4]{1,0:T(1,128)S(1)}, s32[1,4]{1,0:T(1,128)}, u32[]{:S(2)}) copy-start(s32[1,4]{1,0:T(1,128)} %neigh_ref.1) | copy-start | bytes 52
  15.6 4.7 %collective-permute-start.5 = (f32[128,128]{1,0:T(8,128)S(1)}, f32[128,128]{1,0:T(8,128)S(1)}, u32[]{:S(2)}, u32[]{:S(2)}) collective-permute-start(f32[128,128]{1,0:T(8,128)S(1)} %get-tuple-element.43.own_ref), channel_id=1, source_target_pairs={{0,8},{8,0},{16,24},{24,16},{32,40},{40,32},{48,56},{56,48},{64,72... | collective-permute-start | bytes 196616 | tf_op jit(solution)/shard_map/ppermute | solution.py:462
  15.9 6.9 %collective-permute-start.6 = (f32[128,128]{1,0:T(8,128)S(1)}, f32[128,128]{1,0:T(8,128)S(1)}, u32[]{:S(2)}, u32[]{:S(2)}) collective-permute-start(f32[128,128]{1,0:T(8,128)S(1)} %get-tuple-element.43.own_ref), channel_id=1, source_target_pairs={{0,16},{8,24},{16,0},{24,8},{32,48},{40,56},{48,32},{56,40},{64,80... | collective-permute-start | bytes 196616 | tf_op jit(solution)/shard_map/ppermute | solution.py:462
  19.8 4.8 %collective-permute-start.7 = (f32[128,128]{1,0:T(8,128)S(1)}, f32[128,128]{1,0:T(8,128)S(1)}, u32[]{:S(2)}, u32[]{:S(2)}) collective-permute-start(f32[128,128]{1,0:T(8,128)S(1)} %get-tuple-element.43.own_ref), channel_id=1, source_target_pairs={{0,24},{8,16},{16,8},{24,0},{32,56},{40,48},{48,40},{56,32},{64,88... | collective-permute-start | bytes 196616 | tf_op jit(solution)/shard_map/ppermute | solution.py:462
  25.6 7.4 %collective-permute-start.8 = (f32[128,128]{1,0:T(8,128)S(1)}, f32[128,128]{1,0:T(8,128)S(1)}, u32[]{:S(2)}, u32[]{:S(2)}) collective-permute-start(f32[128,128]{1,0:T(8,128)S(1)} %get-tuple-element.44.own_ref), channel_id=1, source_target_pairs={{0,56},{8,48},{16,40},{24,32},{32,24},{40,16},{48,8},{56,0},{64,12... | collective-permute-start | bytes 196616 | tf_op jit(solution)/shard_map/ppermute | solution.py:462
  33.4 6.4 %collective-permute-start.10 = (f32[128,128]{1,0:T(8,128)S(1)}, f32[128,128]{1,0:T(8,128)S(1)}, u32[]{:S(2)}, u32[]{:S(2)}) collective-permute-start(f32[128,128]{1,0:T(8,128)S(1)} %get-tuple-element.46.own_ref), channel_id=1, source_target_pairs={{0,128},{8,136},{16,144},{24,152},{32,160},{40,168},{48,176},{56,1... | collective-permute-start | bytes 196616 | tf_op jit(solution)/shard_map/ppermute | solution.py:462
  37.0 5.5 %collective-permute-start.11 = (f32[128,128]{1,0:T(8,128)S(1)}, f32[128,128]{1,0:T(8,128)S(1)}, u32[]{:S(2)}, u32[]{:S(2)}) collective-permute-start(f32[128,128]{1,0:T(8,128)S(1)} %get-tuple-element.46.own_ref), channel_id=1, source_target_pairs={{0,192},{8,200},{16,208},{24,216},{32,224},{40,232},{48,240},{56,2... | collective-permute-start | bytes 196616 | tf_op jit(solution)/shard_map/ppermute | solution.py:462
  38.1 4.4 %collective-permute-start.9 = (f32[128,128]{1,0:T(8,128)S(1)}, f32[128,128]{1,0:T(8,128)S(1)}, u32[]{:S(2)}, u32[]{:S(2)}) collective-permute-start(f32[128,128]{1,0:T(8,128)S(1)} %get-tuple-element.46.own_ref), channel_id=1, source_target_pairs={{0,64},{8,72},{16,80},{24,88},{32,96},{40,104},{48,112},{56,120},{... | collective-permute-start | bytes 196616 | tf_op jit(solution)/shard_map/ppermute | solution.py:462

commit v12 on v11

--- a/solution.py
+++ b/solution.py
@@ -4,6 +4,7 @@
 from jax.experimental import pallas as pl
 from jax.experimental.pallas import tpu as pltpu
 from jax.sharding import PartitionSpec as P
+
 
 f32 = jnp.float32
 bf16 = jnp.bfloat16
@@ -328,7 +329,7 @@
 
 def track(is_low, fun, extra):
     f, hh, k, g, e = fun
-    t, th, yp1, yv1, yq2, yt, yth = extra
+    _, _, yp1, yv1, yq2, yt, yth = extra
     x1 = pack(jnp.where(is_low, hh, f))
     x2 = pack(jnp.where(is_low, hh, k))
     prod1 = dot(x1, jnp.where(is_low, yq2, yp1))
@@ -376,7 +377,8 @@
     put_map(fun_out, *track(in_lower, fun, extra))
 
 
-def combine_two(own_ref, other_ref, fun_ref, out_ref, fun_out):
+def combine_two(own_ref, other_ref, fun_ref, after_ref, out_ref, fun_out):
+    del after_ref
     is_low = lax.axis_index("depth") % ZS < 4
     own, other = own_ref[...], other_ref[...]
     total, extra = join(unpack(jnp.where(is_low, own, other)), unpack(jnp.where(is_low, other, own)))
@@ -426,7 +428,7 @@
     return jax.ShapeDtypeStruct(shape, dtype)
 
 
-def call(body, outs, *args, scratch=(), smem=0, hbm=0, flops=0, name=None):
+def call(body, outs, *args, scratch=(), smem=0, hbm=0, flops=0):
     args = [pltpu.with_memory_space_constraint(x, pltpu.HBM) if smem <= i < smem + hbm else x for i, x in enumerate(args)]
     spaces = [pltpu.SMEM] * smem + [pltpu.HBM] * hbm + [pltpu.VMEM] * (len(args) - smem - hbm)
     return pl.pallas_call(
@@ -436,7 +438,6 @@
         out_specs=jax.tree.map(lambda _: pl.BlockSpec(memory_space=pltpu.VMEM), outs),
         scratch_shapes=scratch,
         cost_estimate=pl.CostEstimate(flops=flops, bytes_accessed=1 << 16, transcendentals=0),
-        name=name,
         compiler_params=pltpu.CompilerParams(vmem_limit_bytes=VLIM),
     )(*args)
 
@@ -463,7 +464,7 @@
 
     line_a = xor_lat(densities, 1)
     part, flux = call(
-        react, (sds(CELLS, N), sds(N, 128)), jac, u, src, tran, pattern, hbm=5, flops=1 << 30, name="react",
+        react, (sds(CELLS, N), sds(N, 128)), jac, u, src, tran, pattern, hbm=5, flops=1 << 30,
         scratch=[pltpu.VMEM((CELLS, N * N), f32)] + [pltpu.VMEM((CELLS, N), f32)] * 3
         + [pltpu.VMEM((8, 8), jnp.int32), pltpu.SemaphoreType.DMA((8,))],
     )
@@ -471,7 +472,7 @@
     quad, n1, full, cols = call(
         tree_leaves,
         (sds(16, 4, N, 256, dtype=bf16), sds(16, 3, N, 128, dtype=bf16), sds(16, 3, N, 128), sds(2, N, 128)),
-        fac, coup, part, scratch=[pltpu.VMEM((2, N, 128), f32)], flops=2 << 30, name="tree_leaves",
+        fac, coup, part, scratch=[pltpu.VMEM((2, N, 128), f32)], flops=2 << 30,
     )
     top_even = xor_depth(lax.optimization_barrier((densities, cols))[0], 1)
     top_odd = lax.ppermute(
@@ -484,30 +485,28 @@
         tree_upper,
         (node(8), node(4), node(2), sds(1, N, 128, dtype=bf16), sds(128, 128)),
         n1, full, coup, cols, part, scratch=[pltpu.VMEM((8, 3, N, 128), f32), pltpu.VMEM((4, 3, N, 128), f32)],
-        flops=2 << 30, name="tree_upper",
+        flops=2 << 30,
     )
     pay, pair, vs, ws = call(
         upsweep, (sds(128, 128), sds(4, N, 128), sds(7, N, 128), sds(7, N, 128)),
         neighbours, part, line_a, line_b, line_c, top_even, top_odd, flux, u, tran, lat, coup, cols, quad, n1, n2, n3, n4, n5, root,
-        smem=1, flops=1 << 25, name="upsweep",
-    )
-    others = [xor_depth(pay, bits) for bits in (1, 2, 3)]
+        smem=1, flops=1 << 25,
+    )
+    others = []
+    for bits in (1, 2, 3):
+        others.append(xor_depth(pay, bits))
     slots = [pltpu.VMEM((4, 128, 128), f32)]
-    pay, fun = call(
-        combine_four, (sds(128, 128), sds(128, 128)), pay, *others, scratch=slots, flops=1 << 24, name="combine_four",
-    )
+    pay, fun = call(combine_four, (sds(128, 128), sds(128, 128)), pay, *others, scratch=slots, flops=1 << 24)
     other = xor_depth(pay, 7)
-    pay, fun = call(
-        combine_two, (sds(128, 128), sds(5, N, 128)), pay, other, fun, flops=1 << 24, name="combine_two",
-    )
-    others = [xor_depth(pay, bits) for bits in (8, 16, 24)]
     tees, add_v, add_a, add_x = call(
         prepare, (sds(15, N, 128, dtype=bf16), sds(4, N, 128), sds(4, N, 128), sds(N, 128)),
-        pair, vs, ws, n1, n2, n3, n4, flops=1 << 30, name="prepare",
-    )
+        pair, vs, ws, n1, n2, n3, n4, flops=1 << 30,
+    )
+    pay, fun = call(combine_two, (sds(128, 128), sds(5, N, 128)), pay, other, fun, add_x, flops=1 << 24)
+    others = [xor_depth(pay, bits) for bits in (8, 16, 24)]
     out = call(
         downsweep, sds(CELLS, N), pay, *others, fun, cols, add_v, add_a, add_x, quad, n1, n2, n3, n4, tees,
-        scratch=slots, flops=1 << 25, name="downsweep",
+        scratch=slots, flops=1 << 25,
     )
     return out.reshape(line_count, cell_count, species)
 

time: 45.5 us -> 45.5 us (level)
  no operation moved by 1% of the time
where the time goes in v12:
time: 45.5 us; the launch traced here: 45.3 us
  starting transfers between devices  21.7 us (48%)
  Pallas kernels  12.2 us (27%)
  waiting for transfers between devices  11.2 us (25%)
    ppermute x8, starting transfers between devices, xor_depth(): return lax.ppermute(value, 'depth', [(i, i ^ bits) for i in range(32)])  14.7 us
    pallas_call x8, Pallas kernels, call(): pl.pallas_call(body, out_shape=outs, in_specs=[pl.BlockSpec(memory_space=...  12.2 us
    ppermute x8, waiting for transfers between devices, xor_depth(): return lax.ppermute(value, 'depth', [(i, i ^ bits) for i in range(32)])  10.4 us
    ppermute x3, starting transfers between devices, xor_lat(): return lax.ppermute(value, 'lat', [(i, i ^ bits) for i in range(8)])  4.52 us
    ppermute x1, starting transfers between devices, on_device(): lax.ppermute(lax.optimization_barrier((densities, line_b))[0], ('depth',...  2.48 us
  transfers between devices with their start and end apart: 12, of which 7 were waited for; matrix products, arithmetic and copies ran while one was open for 0% of the time, Pallas kernels for 13%

profile of v12, /device:TPU:32, one launch (start us, length us, event | category | flops | bytes accessed | tf_op | source)
XLA Modules:
  0.0 45.3 jit_solution(14937268818357681080)
XLA Ops:
  0.0 0.1 collective-permute-start
  0.1 2.2 %shard_map.91 = (f32[32,64]{1,0:T(8,128)S(1)}, f32[64,128]{1,0:T(8,128)S(1)}) custom-call(f32[32,4096]{1,0:T(8,128)} %bitcast.21, f32[32,64]{1,0:T(8,128)} %bitcast.12, f32[32,64]{1,0:T(8,128)} %bitcast.22, f32[32,64]{1,0:T(8,128)} %bitcast.14, s32[8,8]{1,0:T(8,128)} %pat_hbm.1), custom_call_target="tpu_custom_call" | custom-call | flops 1073741824 | bytes 65536 | tf_op jit(solution)/shard_map/pallas_call | solution.py:434
  2.3 0.0 collective-permute-done.a_ref
  2.3 1.6 %collective-permute-start.1 = (f32[2,32,64]{2,1,0:T(8,128)S(1)}, f32[2,32,64]{2,1,0:T(8,128)S(1)}, u32[]{:S(2)}, u32[]{:S(2)}) collective-permute-start(f32[2,32,64]{2,1,0:T(8,128)S(1)} %pad_maximum_fusion.1), channel_id=1, source_target_pairs={{0,2},{1,3},{2,0},{3,1},{4,6},{5,7},{6,4},{7,5},{8,10},{9,11},{10,... | collective-permute-start | bytes 49160 | tf_op jit(solution)/shard_map/ppermute | solution.py:460
  3.9 1.6 %shard_map.92 = (bf16[16,4,64,256]{3,2,1,0:T(8,128)(2,1)S(1)}, bf16[16,3,64,128]{3,2,1,0:T(8,128)(2,1)S(1)}, f32[16,3,64,128]{3,2,1,0:T(8,128)S(1)}, f32[2,64,128]{2,1,0:T(8,128)S(1)}) custom-call(f32[1024,128]{1,0:T(8,128)S(1)} %bitcast.20, f32[32,64]{1,0:T(8,128)S(1)} %bitcast.17, f32[32,64]{1,0:T(8,128)S(1)} %get-tuple-element.30.after_ref.part_ref), custom_call_target="tpu_custom_call" | custom-call | flops 2147483648 | bytes 65536 | tf_op jit(solution)/shard_map/pallas_call | solution.py:434
  5.6 0.3 collective-permute-start.3
  5.9 0.5 %collective-permute-done.1.b_ref = f32[2,32,64]{2,1,0:T(8,128)S(1)} collective-permute-done((f32[2,32,64]{2,1,0:T(8,128)S(1)}, f32[2,32,64]{2,1,0:T(8,128)S(1)}, u32[]{:S(2)}, u32[]{:S(2)}) %collective-permute-start.1) | collective-permute-done | bytes 16416 | tf_op jit(solution)/shard_map/ppermute | solution.py:460
  6.3 2.8 %collective-permute-start.2 = (f32[4,32,64]{2,1,0:T(8,128)S(1)}, f32[4,32,64]{2,1,0:T(8,128)S(1)}, u32[]{:S(2)}, u32[]{:S(2)}) collective-permute-start(f32[4,32,64]{2,1,0:T(8,128)S(1)} %pad_maximum_fusion), channel_id=1, source_target_pairs={{0,6},{1,7},{2,4},{3,5},{4,2},{5,3},{6,0},{7,1},{8,14},{9,15},{10,... | collective-permute-start | bytes 98312 | tf_op jit(solution)/shard_map/ppermute | solution.py:460
  9.2 2.5 %collective-permute-start.4 = (f32[1,32,64]{2,1,0:T(8,128)S(1)}, f32[1,32,64]{2,1,0:T(8,128)S(1)}, u32[]{:S(2)}, u32[]{:S(2)}) collective-permute-start(f32[1,32,64]{2,1,0:T(8,128)S(1)} %copy-done), channel_id=1, source_target_pairs={{0,1},{1,0},{2,3},{3,2},{4,5},{5,4},{6,7},{7,6},{8,16},{9,17},{10,... | collective-permute-start | bytes 24584 | tf_op jit(solution)/shard_map/ppermute | solution.py:478
  11.7 1.4 %shard_map.93 = (bf16[8,4,64,128]{3,2,1,0:T(8,128)(2,1)S(1)}, bf16[4,4,64,128]{3,2,1,0:T(8,128)(2,1)S(1)}, bf16[2,4,64,128]{3,2,1,0:T(8,128)(2,1)S(1)}, bf16[1,64,128]{2,1,0:T(8,128)(2,1)S(1)}, f32[128,128]{1,0:T(8,128)S(1)}) custom-call(bf16[16,3,64,128]{3,2,1,0:T(8,128)(2,1)S(1)} %get-tuple-element.36.n1_ref, ...), custom_call_target="tpu_custom_call" | custom-call | flops 2147483648 | bytes 65536 | tf_op jit(solution)/shard_map/pallas_call | solution.py:434
  13.1 0.0 collective-permute-done.3.even_ref
  13.1 0.3 collective-permute-done.4.odd_ref
  13.4 0.0 collective-permute-done.2.c_ref
  13.4 2.2 %shard_map.94 = (f32[128,128]{1,0:T(8,128)S(1)}, f32[4,64,128]{2,1,0:T(8,128)S(1)}, f32[7,64,128]{2,1,0:T(8,128)S(1)}, f32[7,64,128]{2,1,0:T(8,128)S(1)}) custom-call(s32[1,4]{1,0:T(1,128)S(1)} %copy-done.4, f32[32,64]{1,0:T(8,128)S(1)} %get-tuple-element.30.after_ref.part_ref, f32[1,32,64]{2,1,0:T(8,128)S(1)} %collective-permute-done.a_ref, ...), custom_call_target="tpu_custom_call" | custom-call | flops 33554432 | bytes 65536 | tf_op jit(solution)/shard_map/pallas_call | solution.py:434
  15.6 0.3 collective-permute-start.5
  15.9 3.9 %collective-permute-start.6 = (f32[128,128]{1,0:T(8,128)S(1)}, f32[128,128]{1,0:T(8,128)S(1)}, u32[]{:S(2)}, u32[]{:S(2)}) collective-permute-start(f32[128,128]{1,0:T(8,128)S(1)} %get-tuple-element.43.own_ref), channel_id=1, source_target_pairs={{0,16},{8,24},{16,0},{24,8},{32,48},{40,56},{48,32},{56,40},{64,80... | collective-permute-start | bytes 196616 | tf_op jit(solution)/shard_map/ppermute | solution.py:463
  19.8 0.5 %collective-permute-start.7 = (f32[128,128]{1,0:T(8,128)S(1)}, f32[128,128]{1,0:T(8,128)S(1)}, u32[]{:S(2)}, u32[]{:S(2)}) collective-permute-start(f32[128,128]{1,0:T(8,128)S(1)} %get-tuple-element.43.own_ref), channel_id=1, source_target_pairs={{0,24},{8,16},{16,8},{24,0},{32,56},{40,48},{48,40},{56,32},{64,88... | collective-permute-start | bytes 196616 | tf_op jit(solution)/shard_map/ppermute | solution.py:463
  20.3 0.0 collective-permute-done.5.x1_ref
  20.3 2.5 %collective-permute-done.6.x2_ref = f32[128,128]{1,0:T(8,128)S(1)} collective-permute-done((f32[128,128]{1,0:T(8,128)S(1)}, f32[128,128]{1,0:T(8,128)S(1)}, u32[]{:S(2)}, u32[]{:S(2)}) %collective-permute-start.6) | collective-permute-done | bytes 65568 | tf_op jit(solution)/shard_map/ppermute | solution.py:463
  22.7 1.9 %collective-permute-done.7.x3_ref = f32[128,128]{1,0:T(8,128)S(1)} collective-permute-done((f32[128,128]{1,0:T(8,128)S(1)}, f32[128,128]{1,0:T(8,128)S(1)}, u32[]{:S(2)}, u32[]{:S(2)}) %collective-permute-start.7) | collective-permute-done | bytes 65568 | tf_op jit(solution)/shard_map/ppermute | solution.py:463
  24.6 1.0 %shard_map.95 = (f32[128,128]{1,0:T(8,128)S(1)}, f32[128,128]{1,0:T(8,128)S(1)}) custom-call(f32[128,128]{1,0:T(8,128)S(1)} %get-tuple-element.43.own_ref, f32[128,128]{1,0:T(8,128)S(1)} %collective-permute-done.5.x1_ref, f32[128,128]{1,0:T(8,128)S(1)} %collective-permute-done.6.x2_ref, f32[128,128]{1,0:T(8,128)S(1)} %collective-permute-done.7.x3_ref), custom_call_target="tpu_custom_call" | custom-call | flops 16777216 | bytes 65536 | tf_op jit(solution)/shard_map/pallas_call | solution.py:434
  25.6 5.0 %collective-permute-start.8 = (f32[128,128]{1,0:T(8,128)S(1)}, f32[128,128]{1,0:T(8,128)S(1)}, u32[]{:S(2)}, u32[]{:S(2)}) collective-permute-start(f32[128,128]{1,0:T(8,128)S(1)} %get-tuple-element.44.own_ref), channel_id=1, source_target_pairs={{0,56},{8,48},{16,40},{24,32},{32,24},{40,16},{48,8},{56,0},{64,12... | collective-permute-start | bytes 196616 | tf_op jit(solution)/shard_map/ppermute | solution.py:463
  30.6 0.7 %shard_map.96 = (bf16[15,64,128]{2,1,0:T(8,128)(2,1)S(1)}, f32[4,64,128]{2,1,0:T(8,128)S(1)}, f32[4,64,128]{2,1,0:T(8,128)S(1)}, f32[64,128]{1,0:T(8,128)S(1)}) custom-call(f32[4,64,128]{2,1,0:T(8,128)S(1)} %get-tuple-element.46.pair_ref, f32[7,64,128]{2,1,0:T(8,128)S(1)} %get-tuple-element.47.v_ref, f32[7,64,128]{2,1,0:T(8,128)S(1)} %get-tuple-element.48.w_ref, ...), custom_call_target="tpu_custom_call" | custom-call | flops 1073741824 | bytes 65536 | tf_op jit(solution)/shard_map/pallas_call | solution.py:434
  31.3 1.7 %collective-permute-done.8.other_ref = f32[128,128]{1,0:T(8,128)S(1)} collective-permute-done((f32[128,128]{1,0:T(8,128)S(1)}, f32[128,128]{1,0:T(8,128)S(1)}, u32[]{:S(2)}, u32[]{:S(2)}) %collective-permute-start.8) | collective-permute-done | bytes 65568 | tf_op jit(solution)/shard_map/ppermute | solution.py:463
  32.9 0.5 %shard_map.97 = (f32[128,128]{1,0:T(8,128)S(1)}, f32[5,64,128]{2,1,0:T(8,128)S(1)}) custom-call(f32[128,128]{1,0:T(8,128)S(1)} %get-tuple-element.44.own_ref, f32[128,128]{1,0:T(8,128)S(1)} %collective-permute-done.8.other_ref, f32[128,128]{1,0:T(8,128)S(1)} %get-tuple-element.45.fun_ref, f32[64,128]{1,0:T(8,128)S(1)} %get-tuple-element.49.after_ref.add_x), custom_call_target="tpu_custom_call" | custom-call | flops 16777216 | bytes 65536 | tf_op jit(solution)/shard_map/pallas_call | solution.py:434
  33.4 3.6 %collective-permute-start.10 = (f32[128,128]{1,0:T(8,128)S(1)}, f32[128,128]{1,0:T(8,128)S(1)}, u32[]{:S(2)}, u32[]{:S(2)}) collective-permute-start(f32[128,128]{1,0:T(8,128)S(1)} %get-tuple-element.50.own_ref), channel_id=1, source_target_pairs={{0,128},{8,136},{16,144},{24,152},{32,160},{40,168},{48,176},{56,1... | collective-permute-start | bytes 196616 | tf_op jit(solution)/shard_map/ppermute | solution.py:463
  37.0 1.1 %collective-permute-start.11 = (f32[128,128]{1,0:T(8,128)S(1)}, f32[128,128]{1,0:T(8,128)S(1)}, u32[]{:S(2)}, u32[]{:S(2)}) collective-permute-start(f32[128,128]{1,0:T(8,128)S(1)} %get-tuple-element.50.own_ref), channel_id=1, source_target_pairs={{0,192},{8,200},{16,208},{24,216},{32,224},{40,232},{48,240},{56,2... | collective-permute-start | bytes 196616 | tf_op jit(solution)/shard_map/ppermute | solution.py:463
  38.1 0.0 collective-permute-start.9
  38.1 1.7 %collective-permute-done.10.y2_ref = f32[128,128]{1,0:T(8,128)S(1)} collective-permute-done((f32[128,128]{1,0:T(8,128)S(1)}, f32[128,128]{1,0:T(8,128)S(1)}, u32[]{:S(2)}, u32[]{:S(2)}) %collective-permute-start.10) | collective-permute-done | bytes 65568 | tf_op jit(solution)/shard_map/ppermute | solution.py:463
  39.8 2.7 %collective-permute-done.11.y3_ref = f32[128,128]{1,0:T(8,128)S(1)} collective-permute-done((f32[128,128]{1,0:T(8,128)S(1)}, f32[128,128]{1,0:T(8,128)S(1)}, u32[]{:S(2)}, u32[]{:S(2)}) %collective-permute-start.11) | collective-permute-done | bytes 65568 | tf_op jit(solution)/shard_map/ppermute | solution.py:463
  42.5 0.0 collective-permute-done.9.y1_ref
  42.5 2.8 %shard_map.98 = f32[32,64]{1,0:T(8,128)} custom-call(f32[128,128]{1,0:T(8,128)S(1)} %get-tuple-element.50.own_ref, f32[128,128]{1,0:T(8,128)S(1)} %collective-permute-done.9.y1_ref, f32[128,128]{1,0:T(8,128)S(1)} %collective-permute-done.10.y2_ref, f32[128,128]{1,0:T(8,128)S(1)} %collective-permute-done.11.y3_ref, ...), custom_call_target="tpu_custom_call" | custom-call | flops 33554432 | bytes 65536 | tf_op jit(solution)/shard_map/pallas_call | solution.py:434
  (14 shorter events, 0.0 us)
Async XLA Ops:
  0.0 2.3 %copy-start = (f32[1,32,64]{2,1,0:T(8,128)S(1)}, f32[1,32,64]{2,1,0:T(8,128)}, u32[]{:S(2)}) copy-start(f32[1,32,64]{2,1,0:T(8,128)} %param.9) | copy-start | bytes 24580
  0.0 3.9 %copy-start.3 = (f32[1,32,64]{2,1,0:T(8,128)S(1)}, f32[1,32,64]{2,1,0:T(8,128)}, u32[]{:S(2)}) copy-start(f32[1,32,64]{2,1,0:T(8,128)} %param.17) | copy-start | bytes 24580
  0.0 3.9 %copy-start.5 = (f32[1,32,4096]{2,1,0:T(8,128)S(1)}, f32[1,32,4096]{2,1,0:T(8,128)}, u32[]{:S(2)}) copy-start(f32[1,32,4096]{2,1,0:T(8,128)} %param.16) | copy-start | bytes 1572868
  0.0 2.3 %collective-permute-start = (f32[1,32,64]{2,1,0:T(8,128)}, f32[1,32,64]{2,1,0:T(8,128)S(1)}, u32[]{:S(2)}, u32[]{:S(2)}) collective-permute-start(f32[1,32,64]{2,1,0:T(8,128)} %param.9), channel_id=1, source_target_pairs={{0,1},{1,0},{2,3},{3,2},{4,5},{5,4},{6,7},{7,6},{8,9},{9,8},{10,11... | collective-permute-start | bytes 24584 | tf_op jit(solution)/shard_map/ppermute | solution.py:460
  2.3 4.0 %collective-permute-start.1 = (f32[2,32,64]{2,1,0:T(8,128)S(1)}, f32[2,32,64]{2,1,0:T(8,128)S(1)}, u32[]{:S(2)}, u32[]{:S(2)}) collective-permute-start(f32[2,32,64]{2,1,0:T(8,128)S(1)} %pad_maximum_fusion.1), channel_id=1, source_target_pairs={{0,2},{1,3},{2,0},{3,1},{4,6},{5,7},{6,4},{7,5},{8,10},{9,11},{10,... | collective-permute-start | bytes 49160 | tf_op jit(solution)/shard_map/ppermute | solution.py:460
  5.6 7.5 %collective-permute-start.3 = (f32[1,32,64]{2,1,0:T(8,128)S(1)}, f32[1,32,64]{2,1,0:T(8,128)S(1)}, u32[]{:S(2)}, u32[]{:S(2)}) collective-permute-start(f32[1,32,64]{2,1,0:T(8,128)S(1)} %copy-done), channel_id=1, source_target_pairs={{0,8},{8,0},{16,24},{24,16},{32,40},{40,32},{48,56},{56,48},{64,72... | collective-permute-start | bytes 24584 | tf_op jit(solution)/shard_map/ppermute | solution.py:463
  6.3 7.0 %collective-permute-start.2 = (f32[4,32,64]{2,1,0:T(8,128)S(1)}, f32[4,32,64]{2,1,0:T(8,128)S(1)}, u32[]{:S(2)}, u32[]{:S(2)}) collective-permute-start(f32[4,32,64]{2,1,0:T(8,128)S(1)} %pad_maximum_fusion), channel_id=1, source_target_pairs={{0,6},{1,7},{2,4},{3,5},{4,2},{5,3},{6,0},{7,1},{8,14},{9,15},{10,... | collective-permute-start | bytes 98312 | tf_op jit(solution)/shard_map/ppermute | solution.py:460
  9.2 4.2 %collective-permute-start.4 = (f32[1,32,64]{2,1,0:T(8,128)S(1)}, f32[1,32,64]{2,1,0:T(8,128)S(1)}, u32[]{:S(2)}, u32[]{:S(2)}) collective-permute-start(f32[1,32,64]{2,1,0:T(8,128)S(1)} %copy-done), channel_id=1, source_target_pairs={{0,1},{1,0},{2,3},{3,2},{4,5},{5,4},{6,7},{7,6},{8,16},{9,17},{10,... | collective-permute-start | bytes 24584 | tf_op jit(solution)/shard_map/ppermute | solution.py:478
  11.7 1.7 %copy-start.1 = (f32[1,32,64]{2,1,0:T(8,128)S(1)}, f32[1,32,64]{2,1,0:T(8,128)}, u32[]{:S(2)}) copy-start(f32[1,32,64]{2,1,0:T(8,128)} %param.13) | copy-start | bytes 24580
  11.7 1.7 %copy-start.2 = (f32[1,32,64]{2,1,0:T(8,128)S(1)}, f32[1,32,64]{2,1,0:T(8,128)}, u32[]{:S(2)}) copy-start(f32[1,32,64]{2,1,0:T(8,128)} %param.14) | copy-start | bytes 24580
  11.7 1.7 %copy-start.4 = (s32[1,4]{1,0:T(1,128)S(1)}, s32[1,4]{1,0:T(1,128)}, u32[]{:S(2)}) copy-start(s32[1,4]{1,0:T(1,128)} %neigh_ref.1) | copy-start | bytes 52
  15.6 4.7 %collective-permute-start.5 = (f32[128,128]{1,0:T(8,128)S(1)}, f32[128,128]{1,0:T(8,128)S(1)}, u32[]{:S(2)}, u32[]{:S(2)}) collective-permute-start(f32[128,128]{1,0:T(8,128)S(1)} %get-tuple-element.43.own_ref), channel_id=1, source_target_pairs={{0,8},{8,0},{16,24},{24,16},{32,40},{40,32},{48,56},{56,48},{64,72... | collective-permute-start | bytes 196616 | tf_op jit(solution)/shard_map/ppermute | solution.py:463
  15.9 6.9 %collective-permute-start.6 = (f32[128,128]{1,0:T(8,128)S(1)}, f32[128,128]{1,0:T(8,128)S(1)}, u32[]{:S(2)}, u32[]{:S(2)}) collective-permute-start(f32[128,128]{1,0:T(8,128)S(1)} %get-tuple-element.43.own_ref), channel_id=1, source_target_pairs={{0,16},{8,24},{16,0},{24,8},{32,48},{40,56},{48,32},{56,40},{64,80... | collective-permute-start | bytes 196616 | tf_op jit(solution)/shard_map/ppermute | solution.py:463
  19.8 4.8 %collective-permute-start.7 = (f32[128,128]{1,0:T(8,128)S(1)}, f32[128,128]{1,0:T(8,128)S(1)}, u32[]{:S(2)}, u32[]{:S(2)}) collective-permute-start(f32[128,128]{1,0:T(8,128)S(1)} %get-tuple-element.43.own_ref), channel_id=1, source_target_pairs={{0,24},{8,16},{16,8},{24,0},{32,56},{40,48},{48,40},{56,32},{64,88... | collective-permute-start | bytes 196616 | tf_op jit(solution)/shard_map/ppermute | solution.py:463
  25.6 7.4 %collective-permute-start.8 = (f32[128,128]{1,0:T(8,128)S(1)}, f32[128,128]{1,0:T(8,128)S(1)}, u32[]{:S(2)}, u32[]{:S(2)}) collective-permute-start(f32[128,128]{1,0:T(8,128)S(1)} %get-tuple-element.44.own_ref), channel_id=1, source_target_pairs={{0,56},{8,48},{16,40},{24,32},{32,24},{40,16},{48,8},{56,0},{64,12... | collective-permute-start | bytes 196616 | tf_op jit(solution)/shard_map/ppermute | solution.py:463
  33.4 6.5 %collective-permute-start.10 = (f32[128,128]{1,0:T(8,128)S(1)}, f32[128,128]{1,0:T(8,128)S(1)}, u32[]{:S(2)}, u32[]{:S(2)}) collective-permute-start(f32[128,128]{1,0:T(8,128)S(1)} %get-tuple-element.50.own_ref), channel_id=1, source_target_pairs={{0,128},{8,136},{16,144},{24,152},{32,160},{40,168},{48,176},{56,1... | collective-permute-start | bytes 196616 | tf_op jit(solution)/shard_map/ppermute | solution.py:463
  37.0 5.5 %collective-permute-start.11 = (f32[128,128]{1,0:T(8,128)S(1)}, f32[128,128]{1,0:T(8,128)S(1)}, u32[]{:S(2)}, u32[]{:S(2)}) collective-permute-start(f32[128,128]{1,0:T(8,128)S(1)} %get-tuple-element.50.own_ref), channel_id=1, source_target_pairs={{0,192},{8,200},{16,208},{24,216},{32,224},{40,232},{48,240},{56,2... | collective-permute-start | bytes 196616 | tf_op jit(solution)/shard_map/ppermute | solution.py:463
  38.1 4.4 %collective-permute-start.9 = (f32[128,128]{1,0:T(8,128)S(1)}, f32[128,128]{1,0:T(8,128)S(1)}, u32[]{:S(2)}, u32[]{:S(2)}) collective-permute-start(f32[128,128]{1,0:T(8,128)S(1)} %get-tuple-element.50.own_ref), channel_id=1, source_target_pairs={{0,64},{8,72},{16,80},{24,88},{32,96},{40,104},{48,112},{56,120},{... | collective-permute-start | bytes 196616 | tf_op jit(solution)/shard_map/ppermute | solution.py:463

commit v13 on v11

--- a/solution.py
+++ b/solution.py
@@ -246,23 +246,51 @@
     pay_ref[N:] = jnp.where(lane < N, root_ref[N:], tail)
 
 
-def prepare(pair_ref, v_ref, w_ref, n1_ref, n2_ref, n3_ref, n4_ref, t_ref, add_v, add_a, add_x):
+def wide(packed):
+    x = packed.astype(f32)
+    return x + roll(x, N)
+
+
+def prepare(pair_ref, v_ref, w_ref, n1_ref, n2_ref, n3_ref, n4_ref, t_ref, add_ref, resp_ref):
     lane = lanes((N, 128))
     part = lane % CELLS
-    at, vec = 0, 0
-    for level, size, ref in ((1, 8, n2_ref), (2, 16, n3_ref), (3, 32, n4_ref)):
-        acc_v = jnp.zeros((N, 128), f32)
-        acc_a = jnp.zeros((N, 128), f32)
+    eye = eye2()
+    nodes = [(None, None, None)]
+    ss = jnp.zeros((N, 128), f32)
+    aa = jnp.zeros((N, 128), f32)
+    vec = {32: 6, 16: 4, 8: 0}
+    for size, ref in ((32, n4_ref), (16, n3_ref), (8, n2_ref)):
+        ys, ya = rhs(ss), rhs(aa)
+        new_s = jnp.zeros((N, 128), f32)
+        new_a = jnp.zeros((N, 128), f32)
+        children = []
         for j in range(CELLS // size):
-            kw = ref[2 * j + 1, 2]
-            wide = kw.astype(f32)
-            t_ref[at] = pack(wide + roll(wide, N) + mm(kw, ref[2 * j, 0]))
-            at += 1
+            into_s, cross, into_a = nodes[j]
+            ep, eq, kw = ref[2 * j, 0], ref[2 * j + 1, 1], ref[2 * j + 1, 2]
+            t = wide(kw) + mm(kw, ep)
+            kt = pack(t)
+            v1, w2 = v_ref[vec[size] + j], w_ref[vec[size] + j]
+            t0 = w2 + dot(kw, rhs(v1))
             here = part // size == j
-            acc_v = jnp.where(here, v_ref[vec], acc_v)
-            acc_a = jnp.where(here, w_ref[vec] + dot(kw, rhs(v_ref[vec])), acc_a)
-            vec += 1
-        add_v[level], add_a[level] = acc_v, acc_a
+            if size == 32:
+                new_s, new_a = v1, t0
+            else:
+                new_s = jnp.where(here, v1 + dot(ep, ys), new_s)
+                new_a = jnp.where(here, t0 + dot(eq, ya) + dot(kt, ys), new_a)
+            through = t if into_s is None else dot(kt, rhs(into_s))
+            if cross is not None:
+                through = through + cross + dot(eq, rhs(cross))
+            first_a = eye + wide(eq) if into_a is None else into_a + dot(eq, rhs(into_a))
+            second_s = eye + wide(ep) if into_s is None else into_s + dot(ep, rhs(into_s))
+            children += [(into_s, through, first_a), (second_s, cross, into_a)]
+        nodes = children
+        upper = part % size >= size // 2
+        ss, aa = jnp.where(upper, ss + new_s, ss), jnp.where(upper, aa, aa + new_a)
+    add_ref[2], add_ref[3] = ss, aa
+    for j, maps in enumerate(nodes):
+        for i, value in enumerate(maps):
+            if value is not None:
+                resp_ref[j, i] = pack(value)
 
     def repeat(x):
         x = x + roll(x, CELLS)
@@ -274,16 +302,14 @@
     acc_a = jnp.zeros((N, 128), f32)
     for j in range(8):
         kw = n1_ref[2 * j + 1, 2]
-        wide = kw.astype(f32)
-        t_ref[at] = pack(wide + roll(wide, N) + mm(kw, n1_ref[2 * j, 0]))
-        at += 1
+        t_ref[j] = pack(wide(kw) + mm(kw, n1_ref[2 * j, 0]))
         acc_a = jnp.where(lane == 4 * j, dot(kw, y), acc_a)
     acc_a = acc_a + w1
     spread_v = v0 + roll(v0, 1)
     spread_a = acc_a + roll(acc_a, 1)
-    add_v[0] = repeat(spread_v + roll(spread_v, 2))
-    add_a[0] = repeat(spread_a + roll(spread_a, 2))
-    add_x[...] = repeat(w0 + roll(w1, 2) + roll(v0, 1) + roll(v1, 3))
+    add_ref[0] = repeat(spread_v + roll(spread_v, 2))
+    add_ref[1] = repeat(spread_a + roll(spread_a, 2))
+    add_ref[4] = repeat(w0 + roll(w1, 2) + roll(v0, 1) + roll(v1, 3))
 
 
 def unpack(b):
@@ -361,7 +387,8 @@
     return [unpack(slots[i]) for i in range(4)]
 
 
-def combine_four(own_ref, x1_ref, x2_ref, x3_ref, out_ref, fun_out, slots):
+def combine_four(own_ref, x1_ref, x2_ref, x3_ref, after_ref, out_ref, fun_out, slots):
+    del after_ref
     at = lax.axis_index("depth") % 4
     maps = fill(slots, at, (own_ref, x1_ref, x2_ref, x3_ref))
     lower, extra_lower = join(maps[0], maps[1])
@@ -385,8 +412,8 @@
         fun_out[i] = value
 
 
-def downsweep(own_ref, y1_ref, y2_ref, y3_ref, fun_ref, cols_ref, add_v, add_a, add_x, quad_ref, n1_ref, n2_ref, n3_ref,
-              n4_ref, t_ref, out_ref, slots):
+def downsweep(own_ref, y1_ref, y2_ref, y3_ref, fun_ref, cols_ref, add_ref, resp_ref, quad_ref, n1_ref, t_ref, out_ref,
+              slots):
     at = lax.axis_index("depth") // ZS
     maps = fill(slots, at, (own_ref, y1_ref, y2_ref, y3_ref))
     lower, extra_lower = join(maps[0], maps[1], last=True)
@@ -400,25 +427,33 @@
     aa = e + dot(pack(jnp.where(is_low, hh, k)), jnp.where(is_low, rhs(t), yv))
     ss = jnp.where(is_low, g, up) * cols_ref[1]
     lane = lanes((N, 128)) % CELLS
-    for level, size, ref, base in ((3, 32, n4_ref, 6), (2, 16, n3_ref, 4), (1, 8, n2_ref, 0), (0, 4, n1_ref, 7)):
-        ys, ya = rhs(ss), rhs(aa)
-        ds = jnp.zeros((N, 128), f32)
-        da = jnp.zeros((N, 128), f32)
-        for j in range(CELLS // size):
-            here = lane // size == j
-            ds = jnp.where(here, dot(ref[2 * j, 0], ys), ds)
-            da = jnp.where(here, dot(ref[2 * j + 1, 1], ya) + dot(t_ref[base + j], ys), da)
-        upper = lane % size >= size // 2
-        new_s = ss + add_v[level] + ds
-        new_a = aa + add_a[level] + da
-        ss = jnp.where(upper, new_s, ss)
-        aa = jnp.where(upper, aa, new_a)
+    ys, ya = rhs(ss), rhs(aa)
+    part_s, part_a = ss, aa
+    for j in range(8):
+        here = lane // 4 == j
+        if j > 0:
+            part_s = jnp.where(here, dot(resp_ref[j, 0], ys), part_s)
+        if j < 7:
+            part_a = jnp.where(here, dot(resp_ref[j, 1], ys) + dot(resp_ref[j, 2], ya), part_a)
+    ss, aa = part_s + add_ref[2], part_a + add_ref[3]
+    ys, ya = rhs(ss), rhs(aa)
+    ds = jnp.zeros((N, 128), f32)
+    da = jnp.zeros((N, 128), f32)
+    for j in range(8):
+        here = lane // 4 == j
+        ds = jnp.where(here, dot(n1_ref[2 * j, 0], ys), ds)
+        da = jnp.where(here, dot(n1_ref[2 * j + 1, 1], ya) + dot(t_ref[j], ys), da)
+    upper = lane % 4 >= 2
+    ss, aa = (
+        jnp.where(upper, ss + add_ref[0] + ds, ss),
+        jnp.where(upper, aa, aa + add_ref[1] + da),
+    )
     y = pair_rhs(ss, aa)
     x = jnp.zeros((N, 128), f32)
     for j in range(CELLS // 2):
         x = jnp.where(lane == 2 * j, jnp.dot(quad_ref[j, 2], y, preferred_element_type=f32), x)
         x = jnp.where(lane == 2 * j + 1, jnp.dot(quad_ref[j, 3], y, preferred_element_type=f32), x)
-    x = x + roll(x, CELLS) + (aa + add_x[...] + jnp.where(lane % 2 == 1, ss, 0.0))
+    x = x + roll(x, CELLS) + (aa + add_ref[4] + jnp.where(lane % 2 == 1, ss, 0.0))
     out_ref[...] = x.T[:CELLS]
 
 
@@ -492,22 +527,23 @@
         smem=1, flops=1 << 25, name="upsweep",
     )
     others = [xor_depth(pay, bits) for bits in (1, 2, 3)]
+    tees, adds, resp = call(
+        prepare,
+        (sds(8, N, 128, dtype=bf16), sds(5, N, 128), sds(8, 3, N, 128, dtype=bf16)),
+        pair, vs, ws, n1, n2, n3, n4, flops=1 << 30, name="prepare",
+    )
     slots = [pltpu.VMEM((4, 128, 128), f32)]
     pay, fun = call(
-        combine_four, (sds(128, 128), sds(128, 128)), pay, *others, scratch=slots, flops=1 << 24, name="combine_four",
+        combine_four, (sds(128, 128), sds(128, 128)), pay, *others, adds, scratch=slots, flops=1 << 24, name="combine_four",
     )
     other = xor_depth(pay, 7)
     pay, fun = call(
         combine_two, (sds(128, 128), sds(5, N, 128)), pay, other, fun, flops=1 << 24, name="combine_two",
     )
     others = [xor_depth(pay, bits) for bits in (8, 16, 24)]
-    tees, add_v, add_a, add_x = call(
-        prepare, (sds(15, N, 128, dtype=bf16), sds(4, N, 128), sds(4, N, 128), sds(N, 128)),
-        pair, vs, ws, n1, n2, n3, n4, flops=1 << 30, name="prepare",
-    )
     out = call(
-        downsweep, sds(CELLS, N), pay, *others, fun, cols, add_v, add_a, add_x, quad, n1, n2, n3, n4, tees,
-        scratch=slots, flops=1 << 25, name="downsweep",
+        downsweep, sds(CELLS, N), pay, *others, fun, cols, adds, resp, quad, n1, tees, scratch=slots, flops=1 << 25,
+        name="downsweep",
     )
     return out.reshape(line_count, cell_count, species)
 

time: 45.5 us -> 45.5 us (level)
  waiting for transfers between devices: 11.2 us -> 9.95 us
  Pallas kernels: 12.2 us -> 13.2 us
    ppermute x8, waiting for transfers between devices: 10.4 us -> 9.17 us  [xor_depth(): return lax.ppermute(value, 'depth', [(i, i ^ bits) for i in range(32)])]
    pallas_call x8, Pallas kernels: 12.2 us -> 13.2 us  [call(): pl.pallas_call(body, out_shape=outs, in_specs=[pl.BlockSpec(memory_space=...]
  transfers between devices with their start and end apart: 12 -> 12, of which waited for: 7 -> 7; matrix products, arithmetic and copies ran while one was open for 0% -> 0% of each run, Pallas kernels for 13% -> 16%
where the time goes in v13:
time: 45.5 us; the launch traced here: 45.3 us
  starting transfers between devices  21.9 us (48%)
  Pallas kernels  13.2 us (29%)
  waiting for transfers between devices  9.95 us (22%)
    ppermute x8, starting transfers between devices, xor_depth(): return lax.ppermute(value, 'depth', [(i, i ^ bits) for i in range(32)])  14.9 us
    pallas_call x8, Pallas kernels, call(): pl.pallas_call(body, out_shape=outs, in_specs=[pl.BlockSpec(memory_space=...  13.2 us
    ppermute x8, waiting for transfers between devices, xor_depth(): return lax.ppermute(value, 'depth', [(i, i ^ bits) for i in range(32)])  9.17 us
    ppermute x3, starting transfers between devices, xor_lat(): return lax.ppermute(value, 'lat', [(i, i ^ bits) for i in range(8)])  4.52 us
    ppermute x1, starting transfers between devices, on_device(): lax.ppermute(lax.optimization_barrier((densities, line_b))[0], ('depth',...  2.48 us
  transfers between devices with their start and end apart: 12, of which 7 were waited for; matrix products, arithmetic and copies ran while one was open for 0% of the time, Pallas kernels for 16%

profile of v13, /device:TPU:32, one launch (start us, length us, event | category | flops | bytes accessed | tf_op | source)
XLA Modules:
  0.0 45.3 jit_solution(17850278860463667190)
XLA Ops:
  0.0 0.1 collective-permute-start
  0.1 2.2 %react.1 = (f32[32,64]{1,0:T(8,128)S(1)}, f32[64,128]{1,0:T(8,128)S(1)}) custom-call(f32[32,4096]{1,0:T(8,128)} %bitcast.21, f32[32,64]{1,0:T(8,128)} %bitcast.12, f32[32,64]{1,0:T(8,128)} %bitcast.22, f32[32,64]{1,0:T(8,128)} %bitcast.14, s32[8,8]{1,0:T(8,128)} %pat_hbm.1), custom_call_target="tpu_custom_call" | custom-call | flops 1073741824 | bytes 65536 | tf_op jit(solution)/shard_map/react/pallas_call | solution.py:467
  2.3 0.0 collective-permute-done.a_ref
  2.3 1.6 %collective-permute-start.1 = (f32[2,32,64]{2,1,0:T(8,128)S(1)}, f32[2,32,64]{2,1,0:T(8,128)S(1)}, u32[]{:S(2)}, u32[]{:S(2)}) collective-permute-start(f32[2,32,64]{2,1,0:T(8,128)S(1)} %pad_maximum_fusion.1), channel_id=1, source_target_pairs={{0,2},{1,3},{2,0},{3,1},{4,6},{5,7},{6,4},{7,5},{8,10},{9,11},{10,... | collective-permute-start | bytes 49160 | tf_op jit(solution)/shard_map/ppermute | solution.py:494
  3.9 1.6 %tree_leaves.1 = (bf16[16,4,64,256]{3,2,1,0:T(8,128)(2,1)S(1)}, bf16[16,3,64,128]{3,2,1,0:T(8,128)(2,1)S(1)}, f32[16,3,64,128]{3,2,1,0:T(8,128)S(1)}, f32[2,64,128]{2,1,0:T(8,128)S(1)}) custom-call(f32[1024,128]{1,0:T(8,128)S(1)} %bitcast.20, f32[32,64]{1,0:T(8,128)S(1)} %bitcast.17, f32[32,64]{1,0:T(8,128)S(1)} %get-tuple-element.29.after_ref.part_ref), custom_call_target="tpu_custom_call" | custom-call | flops 2147483648 | bytes 65536 | tf_op jit(solution)/shard_map/tree_leaves/pallas_call | solution.py:467
  5.5 0.3 collective-permute-start.3
  5.9 0.5 %collective-permute-done.1.b_ref = f32[2,32,64]{2,1,0:T(8,128)S(1)} collective-permute-done((f32[2,32,64]{2,1,0:T(8,128)S(1)}, f32[2,32,64]{2,1,0:T(8,128)S(1)}, u32[]{:S(2)}, u32[]{:S(2)}) %collective-permute-start.1) | collective-permute-done | bytes 16416 | tf_op jit(solution)/shard_map/ppermute | solution.py:494
  6.3 2.8 %collective-permute-start.2 = (f32[4,32,64]{2,1,0:T(8,128)S(1)}, f32[4,32,64]{2,1,0:T(8,128)S(1)}, u32[]{:S(2)}, u32[]{:S(2)}) collective-permute-start(f32[4,32,64]{2,1,0:T(8,128)S(1)} %pad_maximum_fusion), channel_id=1, source_target_pairs={{0,6},{1,7},{2,4},{3,5},{4,2},{5,3},{6,0},{7,1},{8,14},{9,15},{10,... | collective-permute-start | bytes 98312 | tf_op jit(solution)/shard_map/ppermute | solution.py:494
  9.2 2.5 %collective-permute-start.4 = (f32[1,32,64]{2,1,0:T(8,128)S(1)}, f32[1,32,64]{2,1,0:T(8,128)S(1)}, u32[]{:S(2)}, u32[]{:S(2)}) collective-permute-start(f32[1,32,64]{2,1,0:T(8,128)S(1)} %copy-done), channel_id=1, source_target_pairs={{0,1},{1,0},{2,3},{3,2},{4,5},{5,4},{6,7},{7,6},{8,16},{9,17},{10,... | collective-permute-start | bytes 24584 | tf_op jit(solution)/shard_map/ppermute | solution.py:512
  11.7 1.4 %tree_upper.1 = (bf16[8,4,64,128]{3,2,1,0:T(8,128)(2,1)S(1)}, bf16[4,4,64,128]{3,2,1,0:T(8,128)(2,1)S(1)}, bf16[2,4,64,128]{3,2,1,0:T(8,128)(2,1)S(1)}, bf16[1,64,128]{2,1,0:T(8,128)(2,1)S(1)}, f32[128,128]{1,0:T(8,128)S(1)}) custom-call(bf16[16,3,64,128]{3,2,1,0:T(8,128)(2,1)S(1)} %get-tuple-element.35.n1_ref, ...), custom_call_target="tpu_custom_call" | custom-call | flops 2147483648 | bytes 65536 | tf_op jit(solution)/shard_map/tree_upper/pallas_call | solution.py:467
  13.1 0.0 collective-permute-done.3.even_ref
  13.1 0.3 collective-permute-done.4.odd_ref
  13.4 0.0 collective-permute-done.2.c_ref
  13.4 2.2 %upsweep.1 = (f32[128,128]{1,0:T(8,128)S(1)}, f32[4,64,128]{2,1,0:T(8,128)S(1)}, f32[7,64,128]{2,1,0:T(8,128)S(1)}, f32[7,64,128]{2,1,0:T(8,128)S(1)}) custom-call(s32[1,4]{1,0:T(1,128)S(1)} %copy-done.4, f32[32,64]{1,0:T(8,128)S(1)} %get-tuple-element.29.after_ref.part_ref, f32[1,32,64]{2,1,0:T(8,128)S(1)} %collective-permute-done.a_ref, ...), custom_call_target="tpu_custom_call" | custom-call | flops 33554432 | bytes 65536 | tf_op jit(solution)/shard_map/upsweep/pallas_call | solution.py:467
  15.6 0.3 collective-permute-start.5
  15.9 3.9 %collective-permute-start.6 = (f32[128,128]{1,0:T(8,128)S(1)}, f32[128,128]{1,0:T(8,128)S(1)}, u32[]{:S(2)}, u32[]{:S(2)}) collective-permute-start(f32[128,128]{1,0:T(8,128)S(1)} %get-tuple-element.42.own_ref), channel_id=1, source_target_pairs={{0,16},{8,24},{16,0},{24,8},{32,48},{40,56},{48,32},{56,40},{64,80... | collective-permute-start | bytes 196616 | tf_op jit(solution)/shard_map/ppermute | solution.py:497
  19.8 0.5 %collective-permute-start.7 = (f32[128,128]{1,0:T(8,128)S(1)}, f32[128,128]{1,0:T(8,128)S(1)}, u32[]{:S(2)}, u32[]{:S(2)}) collective-permute-start(f32[128,128]{1,0:T(8,128)S(1)} %get-tuple-element.42.own_ref), channel_id=1, source_target_pairs={{0,24},{8,16},{16,8},{24,0},{32,56},{40,48},{48,40},{56,32},{64,88... | collective-permute-start | bytes 196616 | tf_op jit(solution)/shard_map/ppermute | solution.py:497
  20.3 1.9 %prepare.1 = (bf16[8,64,128]{2,1,0:T(8,128)(2,1)S(1)}, f32[5,64,128]{2,1,0:T(8,128)S(1)}, bf16[8,3,64,128]{3,2,1,0:T(8,128)(2,1)S(1)}) custom-call(f32[4,64,128]{2,1,0:T(8,128)S(1)} %get-tuple-element.43.pair_ref, f32[7,64,128]{2,1,0:T(8,128)S(1)} %get-tuple-element.44.v_ref, f32[7,64,128]{2,1,0:T(8,128)S(1)} %get-tuple-element.45.w_ref, ...), custom_call_target="tpu_custom_call" | custom-call | flops 1073741824 | bytes 65536 | tf_op jit(solution)/shard_map/prepare/pallas_call | solution.py:467
  22.2 0.0 collective-permute-done.5.x1_ref
  22.2 0.5 %collective-permute-done.6.x2_ref = f32[128,128]{1,0:T(8,128)S(1)} collective-permute-done((f32[128,128]{1,0:T(8,128)S(1)}, f32[128,128]{1,0:T(8,128)S(1)}, u32[]{:S(2)}, u32[]{:S(2)}) %collective-permute-start.6) | collective-permute-done | bytes 65568 | tf_op jit(solution)/shard_map/ppermute | solution.py:497
  22.7 1.9 %collective-permute-done.7.x3_ref = f32[128,128]{1,0:T(8,128)S(1)} collective-permute-done((f32[128,128]{1,0:T(8,128)S(1)}, f32[128,128]{1,0:T(8,128)S(1)}, u32[]{:S(2)}, u32[]{:S(2)}) %collective-permute-start.7) | collective-permute-done | bytes 65568 | tf_op jit(solution)/shard_map/ppermute | solution.py:497
  24.6 1.0 %combine_four.1 = (f32[128,128]{1,0:T(8,128)S(1)}, f32[128,128]{1,0:T(8,128)S(1)}) custom-call(f32[128,128]{1,0:T(8,128)S(1)} %get-tuple-element.42.own_ref, f32[128,128]{1,0:T(8,128)S(1)} %collective-permute-done.5.x1_ref, f32[128,128]{1,0:T(8,128)S(1)} %collective-permute-done.6.x2_ref, f32[128,128]{1,0:T(8,128)S(1)} %collective-permute-done.7.x3_ref, ...), custom_call_target="tpu_custom_call" | custom-call | flops 16777216 | bytes 65536 | tf_op jit(solution)/shard_map/combine_four/pallas_call | solution.py:467
  25.6 5.0 %collective-permute-start.8 = (f32[128,128]{1,0:T(8,128)S(1)}, f32[128,128]{1,0:T(8,128)S(1)}, u32[]{:S(2)}, u32[]{:S(2)}) collective-permute-start(f32[128,128]{1,0:T(8,128)S(1)} %get-tuple-element.47.own_ref), channel_id=1, source_target_pairs={{0,56},{8,48},{16,40},{24,32},{32,24},{40,16},{48,8},{56,0},{64,12... | collective-permute-start | bytes 196616 | tf_op jit(solution)/shard_map/ppermute | solution.py:497
  30.6 2.3 %collective-permute-done.8.other_ref = f32[128,128]{1,0:T(8,128)S(1)} collective-permute-done((f32[128,128]{1,0:T(8,128)S(1)}, f32[128,128]{1,0:T(8,128)S(1)}, u32[]{:S(2)}, u32[]{:S(2)}) %collective-permute-start.8) | collective-permute-done | bytes 65568 | tf_op jit(solution)/shard_map/ppermute | solution.py:497
  32.9 0.5 %combine_two.1 = (f32[128,128]{1,0:T(8,128)S(1)}, f32[5,64,128]{2,1,0:T(8,128)S(1)}) custom-call(f32[128,128]{1,0:T(8,128)S(1)} %get-tuple-element.47.own_ref, f32[128,128]{1,0:T(8,128)S(1)} %collective-permute-done.8.other_ref, f32[128,128]{1,0:T(8,128)S(1)} %get-tuple-element.48.fun_ref), custom_call_target="tpu_custom_call" | custom-call | flops 16777216 | bytes 65536 | tf_op jit(solution)/shard_map/combine_two/pallas_call | solution.py:467
  33.4 3.8 %collective-permute-start.10 = (f32[128,128]{1,0:T(8,128)S(1)}, f32[128,128]{1,0:T(8,128)S(1)}, u32[]{:S(2)}, u32[]{:S(2)}) collective-permute-start(f32[128,128]{1,0:T(8,128)S(1)} %get-tuple-element.49.own_ref), channel_id=1, source_target_pairs={{0,128},{8,136},{16,144},{24,152},{32,160},{40,168},{48,176},{56,1... | collective-permute-start | bytes 196616 | tf_op jit(solution)/shard_map/ppermute | solution.py:497
  37.2 1.0 %collective-permute-start.11 = (f32[128,128]{1,0:T(8,128)S(1)}, f32[128,128]{1,0:T(8,128)S(1)}, u32[]{:S(2)}, u32[]{:S(2)}) collective-permute-start(f32[128,128]{1,0:T(8,128)S(1)} %get-tuple-element.49.own_ref), channel_id=1, source_target_pairs={{0,192},{8,200},{16,208},{24,216},{32,224},{40,232},{48,240},{56,2... | collective-permute-start | bytes 196616 | tf_op jit(solution)/shard_map/ppermute | solution.py:497
  38.3 0.0 collective-permute-start.9
  38.3 1.7 %collective-permute-done.10.y2_ref = f32[128,128]{1,0:T(8,128)S(1)} collective-permute-done((f32[128,128]{1,0:T(8,128)S(1)}, f32[128,128]{1,0:T(8,128)S(1)}, u32[]{:S(2)}, u32[]{:S(2)}) %collective-permute-start.10) | collective-permute-done | bytes 65568 | tf_op jit(solution)/shard_map/ppermute | solution.py:497
  40.0 2.7 %collective-permute-done.11.y3_ref = f32[128,128]{1,0:T(8,128)S(1)} collective-permute-done((f32[128,128]{1,0:T(8,128)S(1)}, f32[128,128]{1,0:T(8,128)S(1)}, u32[]{:S(2)}, u32[]{:S(2)}) %collective-permute-start.11) | collective-permute-done | bytes 65568 | tf_op jit(solution)/shard_map/ppermute | solution.py:497
  42.7 0.0 collective-permute-done.9.y1_ref
  42.7 2.6 %downsweep.1 = f32[32,64]{1,0:T(8,128)} custom-call(f32[128,128]{1,0:T(8,128)S(1)} %get-tuple-element.49.own_ref, f32[128,128]{1,0:T(8,128)S(1)} %collective-permute-done.9.y1_ref, f32[128,128]{1,0:T(8,128)S(1)} %collective-permute-done.10.y2_ref, f32[128,128]{1,0:T(8,128)S(1)} %collective-permute-done.11.y3_ref, ...), custom_call_target="tpu_custom_call" | custom-call | flops 33554432 | bytes 65536 | tf_op jit(solution)/shard_map/downsweep/pallas_call | solution.py:467
  (14 shorter events, 0.0 us)
Async XLA Ops:
  0.0 2.3 %copy-start = (f32[1,32,64]{2,1,0:T(8,128)S(1)}, f32[1,32,64]{2,1,0:T(8,128)}, u32[]{:S(2)}) copy-start(f32[1,32,64]{2,1,0:T(8,128)} %param.9) | copy-start | bytes 24580
  0.0 3.9 %copy-start.3 = (f32[1,32,64]{2,1,0:T(8,128)S(1)}, f32[1,32,64]{2,1,0:T(8,128)}, u32[]{:S(2)}) copy-start(f32[1,32,64]{2,1,0:T(8,128)} %param.17) | copy-start | bytes 24580
  0.0 3.9 %copy-start.5 = (f32[1,32,4096]{2,1,0:T(8,128)S(1)}, f32[1,32,4096]{2,1,0:T(8,128)}, u32[]{:S(2)}) copy-start(f32[1,32,4096]{2,1,0:T(8,128)} %param.16) | copy-start | bytes 1572868
  0.0 2.3 %collective-permute-start = (f32[1,32,64]{2,1,0:T(8,128)}, f32[1,32,64]{2,1,0:T(8,128)S(1)}, u32[]{:S(2)}, u32[]{:S(2)}) collective-permute-start(f32[1,32,64]{2,1,0:T(8,128)} %param.9), channel_id=1, source_target_pairs={{0,1},{1,0},{2,3},{3,2},{4,5},{5,4},{6,7},{7,6},{8,9},{9,8},{10,11... | collective-permute-start | bytes 24584 | tf_op jit(solution)/shard_map/ppermute | solution.py:494
  2.3 4.0 %collective-permute-start.1 = (f32[2,32,64]{2,1,0:T(8,128)S(1)}, f32[2,32,64]{2,1,0:T(8,128)S(1)}, u32[]{:S(2)}, u32[]{:S(2)}) collective-permute-start(f32[2,32,64]{2,1,0:T(8,128)S(1)} %pad_maximum_fusion.1), channel_id=1, source_target_pairs={{0,2},{1,3},{2,0},{3,1},{4,6},{5,7},{6,4},{7,5},{8,10},{9,11},{10,... | collective-permute-start | bytes 49160 | tf_op jit(solution)/shard_map/ppermute | solution.py:494
  5.5 7.5 %collective-permute-start.3 = (f32[1,32,64]{2,1,0:T(8,128)S(1)}, f32[1,32,64]{2,1,0:T(8,128)S(1)}, u32[]{:S(2)}, u32[]{:S(2)}) collective-permute-start(f32[1,32,64]{2,1,0:T(8,128)S(1)} %copy-done), channel_id=1, source_target_pairs={{0,8},{8,0},{16,24},{24,16},{32,40},{40,32},{48,56},{56,48},{64,72... | collective-permute-start | bytes 24584 | tf_op jit(solution)/shard_map/ppermute | solution.py:497
  6.3 7.0 %collective-permute-start.2 = (f32[4,32,64]{2,1,0:T(8,128)S(1)}, f32[4,32,64]{2,1,0:T(8,128)S(1)}, u32[]{:S(2)}, u32[]{:S(2)}) collective-permute-start(f32[4,32,64]{2,1,0:T(8,128)S(1)} %pad_maximum_fusion), channel_id=1, source_target_pairs={{0,6},{1,7},{2,4},{3,5},{4,2},{5,3},{6,0},{7,1},{8,14},{9,15},{10,... | collective-permute-start | bytes 98312 | tf_op jit(solution)/shard_map/ppermute | solution.py:494
  9.2 4.2 %collective-permute-start.4 = (f32[1,32,64]{2,1,0:T(8,128)S(1)}, f32[1,32,64]{2,1,0:T(8,128)S(1)}, u32[]{:S(2)}, u32[]{:S(2)}) collective-permute-start(f32[1,32,64]{2,1,0:T(8,128)S(1)} %copy-done), channel_id=1, source_target_pairs={{0,1},{1,0},{2,3},{3,2},{4,5},{5,4},{6,7},{7,6},{8,16},{9,17},{10,... | collective-permute-start | bytes 24584 | tf_op jit(solution)/shard_map/ppermute | solution.py:512
  11.7 1.7 %copy-start.1 = (f32[1,32,64]{2,1,0:T(8,128)S(1)}, f32[1,32,64]{2,1,0:T(8,128)}, u32[]{:S(2)}) copy-start(f32[1,32,64]{2,1,0:T(8,128)} %param.13) | copy-start | bytes 24580
  11.7 1.7 %copy-start.2 = (f32[1,32,64]{2,1,0:T(8,128)S(1)}, f32[1,32,64]{2,1,0:T(8,128)}, u32[]{:S(2)}) copy-start(f32[1,32,64]{2,1,0:T(8,128)} %param.14) | copy-start | bytes 24580
  11.7 1.7 %copy-start.4 = (s32[1,4]{1,0:T(1,128)S(1)}, s32[1,4]{1,0:T(1,128)}, u32[]{:S(2)}) copy-start(s32[1,4]{1,0:T(1,128)} %neigh_ref.1) | copy-start | bytes 52
  15.6 6.6 %collective-permute-start.5 = (f32[128,128]{1,0:T(8,128)S(1)}, f32[128,128]{1,0:T(8,128)S(1)}, u32[]{:S(2)}, u32[]{:S(2)}) collective-permute-start(f32[128,128]{1,0:T(8,128)S(1)} %get-tuple-element.42.own_ref), channel_id=1, source_target_pairs={{0,8},{8,0},{16,24},{24,16},{32,40},{40,32},{48,56},{56,48},{64,72... | collective-permute-start | bytes 196616 | tf_op jit(solution)/shard_map/ppermute | solution.py:497
  15.9 6.8 %collective-permute-start.6 = (f32[128,128]{1,0:T(8,128)S(1)}, f32[128,128]{1,0:T(8,128)S(1)}, u32[]{:S(2)}, u32[]{:S(2)}) collective-permute-start(f32[128,128]{1,0:T(8,128)S(1)} %get-tuple-element.42.own_ref), channel_id=1, source_target_pairs={{0,16},{8,24},{16,0},{24,8},{32,48},{40,56},{48,32},{56,40},{64,80... | collective-permute-start | bytes 196616 | tf_op jit(solution)/shard_map/ppermute | solution.py:497
  19.8 4.8 %collective-permute-start.7 = (f32[128,128]{1,0:T(8,128)S(1)}, f32[128,128]{1,0:T(8,128)S(1)}, u32[]{:S(2)}, u32[]{:S(2)}) collective-permute-start(f32[128,128]{1,0:T(8,128)S(1)} %get-tuple-element.42.own_ref), channel_id=1, source_target_pairs={{0,24},{8,16},{16,8},{24,0},{32,56},{40,48},{48,40},{56,32},{64,88... | collective-permute-start | bytes 196616 | tf_op jit(solution)/shard_map/ppermute | solution.py:497
  25.6 7.4 %collective-permute-start.8 = (f32[128,128]{1,0:T(8,128)S(1)}, f32[128,128]{1,0:T(8,128)S(1)}, u32[]{:S(2)}, u32[]{:S(2)}) collective-permute-start(f32[128,128]{1,0:T(8,128)S(1)} %get-tuple-element.47.own_ref), channel_id=1, source_target_pairs={{0,56},{8,48},{16,40},{24,32},{32,24},{40,16},{48,8},{56,0},{64,12... | collective-permute-start | bytes 196616 | tf_op jit(solution)/shard_map/ppermute | solution.py:497
  33.4 6.6 %collective-permute-start.10 = (f32[128,128]{1,0:T(8,128)S(1)}, f32[128,128]{1,0:T(8,128)S(1)}, u32[]{:S(2)}, u32[]{:S(2)}) collective-permute-start(f32[128,128]{1,0:T(8,128)S(1)} %get-tuple-element.49.own_ref), channel_id=1, source_target_pairs={{0,128},{8,136},{16,144},{24,152},{32,160},{40,168},{48,176},{56,1... | collective-permute-start | bytes 196616 | tf_op jit(solution)/shard_map/ppermute | solution.py:497
  37.2 5.5 %collective-permute-start.11 = (f32[128,128]{1,0:T(8,128)S(1)}, f32[128,128]{1,0:T(8,128)S(1)}, u32[]{:S(2)}, u32[]{:S(2)}) collective-permute-start(f32[128,128]{1,0:T(8,128)S(1)} %get-tuple-element.49.own_ref), channel_id=1, source_target_pairs={{0,192},{8,200},{16,208},{24,216},{32,224},{40,232},{48,240},{56,2... | collective-permute-start | bytes 196616 | tf_op jit(solution)/shard_map/ppermute | solution.py:497
  38.3 4.4 %collective-permute-start.9 = (f32[128,128]{1,0:T(8,128)S(1)}, f32[128,128]{1,0:T(8,128)S(1)}, u32[]{:S(2)}, u32[]{:S(2)}) collective-permute-start(f32[128,128]{1,0:T(8,128)S(1)} %get-tuple-element.49.own_ref), channel_id=1, source_target_pairs={{0,64},{8,72},{16,80},{24,88},{32,96},{40,104},{48,112},{56,120},{... | collective-permute-start | bytes 196616 | tf_op jit(solution)/shard_map/ppermute | solution.py:497

commit v14 on v13

--- a/solution.py
+++ b/solution.py
@@ -173,7 +173,7 @@
     out_ref[...] = src_ref[...] - acc + lower + tran * upper
 
 
-def upsweep(neigh_ref, part_ref, a_ref, b_ref, c_ref, even_ref, odd_ref, flux_ref, dens_ref, tran_ref, lat_ref, coup_ref, cols_ref,
+def upsweep(neigh_ref, part_ref, a_ref, b_ref, c_ref, top_ref, flux_ref, dens_ref, tran_ref, lat_ref, coup_ref, cols_ref,
             quad_ref, n1_ref, n2_ref, n3_ref, n4_ref, n5_ref, root_ref, pay_ref, pair_ref, v_ref, w_ref):
     me = lax.axis_index("lat")
     u = dens_ref[...]
@@ -188,9 +188,7 @@
         total = total + count.astype(f32) * value
     row = lax.broadcasted_iota(jnp.int32, (CELLS, N), 0)
     r = part_ref[...] - lat_ref[...] * (4.0 * u - total)
-    depth = lax.axis_index("depth")
-    above = jnp.where(depth % 2 == 0, even_ref[0, 0:1], odd_ref[0, 0:1])
-    above = jnp.where(depth == lax.axis_size("depth") - 1, 0.0, above)
+    above = jnp.where(lax.axis_index("depth") == lax.axis_size("depth") - 1, 0.0, top_ref[0, 0:1])
     r = r + jnp.where(row == CELLS - 1, tran_ref[...] * above, 0.0)
     c = coup_ref[...]
     g = r / jnp.where(row == 0, c, pltpu.roll(c, 1, 0))
@@ -508,12 +506,7 @@
         (sds(16, 4, N, 256, dtype=bf16), sds(16, 3, N, 128, dtype=bf16), sds(16, 3, N, 128), sds(2, N, 128)),
         fac, coup, part, scratch=[pltpu.VMEM((2, N, 128), f32)], flops=2 << 30, name="tree_leaves",
     )
-    top_even = xor_depth(lax.optimization_barrier((densities, cols))[0], 1)
-    top_odd = lax.ppermute(
-        lax.optimization_barrier((densities, line_b))[0], ("depth", "lat"),
-        [(8 * i + l, 8 * (i + 1 if i % 2 else i - 1) + l if 0 < i < 31 else 8 * i + (l ^ 1))
-         for i in range(32) for l in range(8)],
-    )
+    top = lax.ppermute(lax.optimization_barrier((densities, cols))[0], "depth", [((i + 1) % 32, i) for i in range(32)])
     line_c = xor_lat(jnp.concatenate([densities, line_a, line_b], axis=0), 6)
     n2, n3, n4, n5, root = call(
         tree_upper,
@@ -523,7 +516,7 @@
     )
     pay, pair, vs, ws = call(
         upsweep, (sds(128, 128), sds(4, N, 128), sds(7, N, 128), sds(7, N, 128)),
-        neighbours, part, line_a, line_b, line_c, top_even, top_odd, flux, u, tran, lat, coup, cols, quad, n1, n2, n3, n4, n5, root,
+        neighbours, part, line_a, line_b, line_c, top, flux, u, tran, lat, coup, cols, quad, n1, n2, n3, n4, n5, root,
         smem=1, flops=1 << 25, name="upsweep",
     )
     others = [xor_depth(pay, bits) for bits in (1, 2, 3)]

time: 45.5 us -> 47.5 us (1.044)
  waiting for transfers between devices: 9.95 us -> 14.8 us
  starting transfers between devices: 21.9 us -> 19.2 us
    ppermute x8 -> x7, waiting for transfers between devices: 9.17 us -> 13 us  [xor_depth(): return lax.ppermute(value, 'depth', [(i, i ^ bits) for i in range(32)])]
    ppermute x1, starting transfers between devices: 2.48 us -> 0.31 us  [on_device(): lax.ppermute(lax.optimization_barrier((densities, cols))[0], 'depth', [((...]
    ppermute x3, waiting for transfers between devices: 0.46 us -> 1.79 us  [xor_lat(): return lax.ppermute(value, 'lat', [(i, i ^ bits) for i in range(8)])]
    ppermute x8 -> x7, starting transfers between devices: 14.9 us -> 14.4 us  [xor_depth(): return lax.ppermute(value, 'depth', [(i, i ^ bits) for i in range(32)])]
  transfers between devices with their start and end apart: 12 -> 11, of which waited for: 7 -> 7; matrix products, arithmetic and copies ran while one was open for 0% -> 0% of each run, Pallas kernels for 16% -> 15%
where the time goes in v14:
time: 47.5 us; the launch traced here: 47.4 us
  starting transfers between devices  19.2 us (40%)
  waiting for transfers between devices  14.8 us (31%)
  Pallas kernels  13.2 us (28%)
    ppermute x7, starting transfers between devices, xor_depth(): return lax.ppermute(value, 'depth', [(i, i ^ bits) for i in range(32)])  14.4 us
    pallas_call x8, Pallas kernels, call(): pl.pallas_call(body, out_shape=outs, in_specs=[pl.BlockSpec(memory_space=...  13.2 us
    ppermute x7, waiting for transfers between devices, xor_depth(): return lax.ppermute(value, 'depth', [(i, i ^ bits) for i in range(32)])  13 us
    ppermute x3, starting transfers between devices, xor_lat(): return lax.ppermute(value, 'lat', [(i, i ^ bits) for i in range(8)])  4.52 us
    ppermute x3, waiting for transfers between devices, xor_lat(): return lax.ppermute(value, 'lat', [(i, i ^ bits) for i in range(8)])  1.79 us
  transfers between devices with their start and end apart: 11, of which 7 were waited for; matrix products, arithmetic and copies ran while one was open for 0% of the time, Pallas kernels for 15%

profile of v14, /device:TPU:32, one launch (start us, length us, event | category | flops | bytes accessed | tf_op | source)
XLA Modules:
  0.0 47.4 jit_solution(6576957079404164133)
XLA Ops:
  0.0 0.1 collective-permute-start
  0.1 2.2 %react.1 = (f32[32,64]{1,0:T(8,128)S(1)}, f32[64,128]{1,0:T(8,128)S(1)}) custom-call(f32[32,4096]{1,0:T(8,128)} %bitcast.21, f32[32,64]{1,0:T(8,128)} %bitcast.12, f32[32,64]{1,0:T(8,128)} %bitcast.22, f32[32,64]{1,0:T(8,128)} %bitcast.14, s32[8,8]{1,0:T(8,128)} %pat_hbm.1), custom_call_target="tpu_custom_call" | custom-call | flops 1073741824 | bytes 65536 | tf_op jit(solution)/shard_map/react/pallas_call | solution.py:465
  2.3 0.0 collective-permute-done.a_ref
  2.3 0.0 copy-done
  2.3 1.6 %collective-permute-start.1 = (f32[2,32,64]{2,1,0:T(8,128)S(1)}, f32[2,32,64]{2,1,0:T(8,128)S(1)}, u32[]{:S(2)}, u32[]{:S(2)}) collective-permute-start(f32[2,32,64]{2,1,0:T(8,128)S(1)} %pad_maximum_fusion.1), channel_id=1, source_target_pairs={{0,2},{1,3},{2,0},{3,1},{4,6},{5,7},{6,4},{7,5},{8,10},{9,11},{10,... | collective-permute-start | bytes 49160 | tf_op jit(solution)/shard_map/ppermute | solution.py:492
  3.9 1.6 %tree_leaves.1 = (bf16[16,4,64,256]{3,2,1,0:T(8,128)(2,1)S(1)}, bf16[16,3,64,128]{3,2,1,0:T(8,128)(2,1)S(1)}, f32[16,3,64,128]{3,2,1,0:T(8,128)S(1)}, f32[2,64,128]{2,1,0:T(8,128)S(1)}) custom-call(f32[1024,128]{1,0:T(8,128)S(1)} %bitcast.20, f32[32,64]{1,0:T(8,128)S(1)} %bitcast.17, f32[32,64]{1,0:T(8,128)S(1)} %get-tuple-element.28.after_ref.part_ref), custom_call_target="tpu_custom_call" | custom-call | flops 2147483648 | bytes 65536 | tf_op jit(solution)/shard_map/tree_leaves/pallas_call | solution.py:465
  5.6 0.3 collective-permute-start.3
  5.9 0.5 collective-permute-done.1.b_ref
  6.3 2.8 %collective-permute-start.2 = (f32[4,32,64]{2,1,0:T(8,128)S(1)}, f32[4,32,64]{2,1,0:T(8,128)S(1)}, u32[]{:S(2)}, u32[]{:S(2)}) collective-permute-start(f32[4,32,64]{2,1,0:T(8,128)S(1)} %pad_maximum_fusion), channel_id=1, source_target_pairs={{0,6},{1,7},{2,4},{3,5},{4,2},{5,3},{6,0},{7,1},{8,14},{9,15},{10,... | collective-permute-start | bytes 98312 | tf_op jit(solution)/shard_map/ppermute | solution.py:492
  9.2 1.4 %tree_upper.1 = (bf16[8,4,64,128]{3,2,1,0:T(8,128)(2,1)S(1)}, bf16[4,4,64,128]{3,2,1,0:T(8,128)(2,1)S(1)}, bf16[2,4,64,128]{3,2,1,0:T(8,128)(2,1)S(1)}, bf16[1,64,128]{2,1,0:T(8,128)(2,1)S(1)}, f32[128,128]{1,0:T(8,128)S(1)}) custom-call(bf16[16,3,64,128]{3,2,1,0:T(8,128)(2,1)S(1)} %get-tuple-element.33.n1_ref, ...), custom_call_target="tpu_custom_call" | custom-call | flops 2147483648 | bytes 65536 | tf_op jit(solution)/shard_map/tree_upper/pallas_call | solution.py:465
  10.6 0.0 collective-permute-done.3.top_ref
  10.6 1.3 %collective-permute-done.2.c_ref = f32[4,32,64]{2,1,0:T(8,128)S(1)} collective-permute-done((f32[4,32,64]{2,1,0:T(8,128)S(1)}, f32[4,32,64]{2,1,0:T(8,128)S(1)}, u32[]{:S(2)}, u32[]{:S(2)}) %collective-permute-start.2) | collective-permute-done | bytes 32800 | tf_op jit(solution)/shard_map/ppermute | solution.py:492
  11.9 0.0 copy-done.4
  11.9 2.2 %upsweep.1 = (f32[128,128]{1,0:T(8,128)S(1)}, f32[4,64,128]{2,1,0:T(8,128)S(1)}, f32[7,64,128]{2,1,0:T(8,128)S(1)}, f32[7,64,128]{2,1,0:T(8,128)S(1)}) custom-call(s32[1,4]{1,0:T(1,128)S(1)} %copy-done.4, f32[32,64]{1,0:T(8,128)S(1)} %get-tuple-element.28.after_ref.part_ref, f32[1,32,64]{2,1,0:T(8,128)S(1)} %collective-permute-done.a_ref, ...), custom_call_target="tpu_custom_call" | custom-call | flops 33554432 | bytes 65536 | tf_op jit(solution)/shard_map/upsweep/pallas_call | solution.py:465
  14.1 7.8 %collective-permute-start.4 = (f32[128,128]{1,0:T(8,128)S(1)}, f32[128,128]{1,0:T(8,128)S(1)}, u32[]{:S(2)}, u32[]{:S(2)}) collective-permute-start(f32[128,128]{1,0:T(8,128)S(1)} %get-tuple-element.40.own_ref), channel_id=1, source_target_pairs={{0,8},{8,0},{16,24},{24,16},{32,40},{40,32},{48,56},{56,48},{64,72... | collective-permute-start | bytes 196616 | tf_op jit(solution)/shard_map/ppermute | solution.py:495
  21.9 0.0 collective-permute-start.5
  21.9 1.6 %collective-permute-start.6 = (f32[128,128]{1,0:T(8,128)S(1)}, f32[128,128]{1,0:T(8,128)S(1)}, u32[]{:S(2)}, u32[]{:S(2)}) collective-permute-start(f32[128,128]{1,0:T(8,128)S(1)} %get-tuple-element.40.own_ref), channel_id=1, source_target_pairs={{0,24},{8,16},{16,8},{24,0},{32,56},{40,48},{48,40},{56,32},{64,88... | collective-permute-start | bytes 196616 | tf_op jit(solution)/shard_map/ppermute | solution.py:495
  23.5 1.9 %prepare.1 = (bf16[8,64,128]{2,1,0:T(8,128)(2,1)S(1)}, f32[5,64,128]{2,1,0:T(8,128)S(1)}, bf16[8,3,64,128]{3,2,1,0:T(8,128)(2,1)S(1)}) custom-call(f32[4,64,128]{2,1,0:T(8,128)S(1)} %get-tuple-element.41.pair_ref, f32[7,64,128]{2,1,0:T(8,128)S(1)} %get-tuple-element.42.v_ref, f32[7,64,128]{2,1,0:T(8,128)S(1)} %get-tuple-element.43.w_ref, ...), custom_call_target="tpu_custom_call" | custom-call | flops 1073741824 | bytes 65536 | tf_op jit(solution)/shard_map/prepare/pallas_call | solution.py:465
  25.4 0.0 collective-permute-done.4.x1_ref
  25.4 1.8 %collective-permute-done.5.x2_ref = f32[128,128]{1,0:T(8,128)S(1)} collective-permute-done((f32[128,128]{1,0:T(8,128)S(1)}, f32[128,128]{1,0:T(8,128)S(1)}, u32[]{:S(2)}, u32[]{:S(2)}) %collective-permute-start.5) | collective-permute-done | bytes 65568 | tf_op jit(solution)/shard_map/ppermute | solution.py:495
  27.2 1.2 %collective-permute-done.6.x3_ref = f32[128,128]{1,0:T(8,128)S(1)} collective-permute-done((f32[128,128]{1,0:T(8,128)S(1)}, f32[128,128]{1,0:T(8,128)S(1)}, u32[]{:S(2)}, u32[]{:S(2)}) %collective-permute-start.6) | collective-permute-done | bytes 65568 | tf_op jit(solution)/shard_map/ppermute | solution.py:495
  28.3 1.0 %combine_four.1 = (f32[128,128]{1,0:T(8,128)S(1)}, f32[128,128]{1,0:T(8,128)S(1)}) custom-call(f32[128,128]{1,0:T(8,128)S(1)} %get-tuple-element.40.own_ref, f32[128,128]{1,0:T(8,128)S(1)} %collective-permute-done.4.x1_ref, f32[128,128]{1,0:T(8,128)S(1)} %collective-permute-done.5.x2_ref, f32[128,128]{1,0:T(8,128)S(1)} %collective-permute-done.6.x3_ref, ...), custom_call_target="tpu_custom_call" | custom-call | flops 16777216 | bytes 65536 | tf_op jit(solution)/shard_map/combine_four/pallas_call | solution.py:465
  29.3 0.2 collective-permute-start.7
  29.5 7.2 %collective-permute-done.7.other_ref = f32[128,128]{1,0:T(8,128)S(1)} collective-permute-done((f32[128,128]{1,0:T(8,128)S(1)}, f32[128,128]{1,0:T(8,128)S(1)}, u32[]{:S(2)}, u32[]{:S(2)}) %collective-permute-start.7) | collective-permute-done | bytes 65568 | tf_op jit(solution)/shard_map/ppermute | solution.py:495
  36.7 0.5 combine_two.1
  37.1 0.8 %collective-permute-start.10 = (f32[128,128]{1,0:T(8,128)S(1)}, f32[128,128]{1,0:T(8,128)S(1)}, u32[]{:S(2)}, u32[]{:S(2)}) collective-permute-start(f32[128,128]{1,0:T(8,128)S(1)} %get-tuple-element.47.own_ref), channel_id=1, source_target_pairs={{0,192},{8,200},{16,208},{24,216},{32,224},{40,232},{48,240},{56,2... | collective-permute-start | bytes 196616 | tf_op jit(solution)/shard_map/ppermute | solution.py:495
  38.0 0.0 collective-permute-start.8
  38.0 4.0 %collective-permute-start.9 = (f32[128,128]{1,0:T(8,128)S(1)}, f32[128,128]{1,0:T(8,128)S(1)}, u32[]{:S(2)}, u32[]{:S(2)}) collective-permute-start(f32[128,128]{1,0:T(8,128)S(1)} %get-tuple-element.47.own_ref), channel_id=1, source_target_pairs={{0,128},{8,136},{16,144},{24,152},{32,160},{40,168},{48,176},{56,1... | collective-permute-start | bytes 196616 | tf_op jit(solution)/shard_map/ppermute | solution.py:495
  41.9 0.8 %collective-permute-done.10.y3_ref = f32[128,128]{1,0:T(8,128)S(1)} collective-permute-done((f32[128,128]{1,0:T(8,128)S(1)}, f32[128,128]{1,0:T(8,128)S(1)}, u32[]{:S(2)}, u32[]{:S(2)}) %collective-permute-start.10) | collective-permute-done | bytes 65568 | tf_op jit(solution)/shard_map/ppermute | solution.py:495
  42.7 0.0 collective-permute-done.8.y1_ref
  42.7 2.2 %collective-permute-done.9.y2_ref = f32[128,128]{1,0:T(8,128)S(1)} collective-permute-done((f32[128,128]{1,0:T(8,128)S(1)}, f32[128,128]{1,0:T(8,128)S(1)}, u32[]{:S(2)}, u32[]{:S(2)}) %collective-permute-start.9) | collective-permute-done | bytes 65568 | tf_op jit(solution)/shard_map/ppermute | solution.py:495
  44.9 2.6 %downsweep.1 = f32[32,64]{1,0:T(8,128)} custom-call(f32[128,128]{1,0:T(8,128)S(1)} %get-tuple-element.47.own_ref, f32[128,128]{1,0:T(8,128)S(1)} %collective-permute-done.8.y1_ref, f32[128,128]{1,0:T(8,128)S(1)} %collective-permute-done.9.y2_ref, f32[128,128]{1,0:T(8,128)S(1)} %collective-permute-done.10.y3_ref, ...), custom_call_target="tpu_custom_call" | custom-call | flops 33554432 | bytes 65536 | tf_op jit(solution)/shard_map/downsweep/pallas_call | solution.py:465
  (12 shorter events, 0.0 us)
Async XLA Ops:
  0.0 2.3 %copy-start = (f32[1,32,64]{2,1,0:T(8,128)S(1)}, f32[1,32,64]{2,1,0:T(8,128)}, u32[]{:S(2)}) copy-start(f32[1,32,64]{2,1,0:T(8,128)} %param.9) | copy-start | bytes 24580
  0.0 3.9 %copy-start.3 = (f32[1,32,64]{2,1,0:T(8,128)S(1)}, f32[1,32,64]{2,1,0:T(8,128)}, u32[]{:S(2)}) copy-start(f32[1,32,64]{2,1,0:T(8,128)} %param.17) | copy-start | bytes 24580
  0.0 3.9 %copy-start.5 = (f32[1,32,4096]{2,1,0:T(8,128)S(1)}, f32[1,32,4096]{2,1,0:T(8,128)}, u32[]{:S(2)}) copy-start(f32[1,32,4096]{2,1,0:T(8,128)} %param.16) | copy-start | bytes 1572868
  0.0 2.3 %collective-permute-start = (f32[1,32,64]{2,1,0:T(8,128)}, f32[1,32,64]{2,1,0:T(8,128)S(1)}, u32[]{:S(2)}, u32[]{:S(2)}) collective-permute-start(f32[1,32,64]{2,1,0:T(8,128)} %param.9), channel_id=1, source_target_pairs={{0,1},{1,0},{2,3},{3,2},{4,5},{5,4},{6,7},{7,6},{8,9},{9,8},{10,11... | collective-permute-start | bytes 24584 | tf_op jit(solution)/shard_map/ppermute | solution.py:492
  2.3 4.0 %collective-permute-start.1 = (f32[2,32,64]{2,1,0:T(8,128)S(1)}, f32[2,32,64]{2,1,0:T(8,128)S(1)}, u32[]{:S(2)}, u32[]{:S(2)}) collective-permute-start(f32[2,32,64]{2,1,0:T(8,128)S(1)} %pad_maximum_fusion.1), channel_id=1, source_target_pairs={{0,2},{1,3},{2,0},{3,1},{4,6},{5,7},{6,4},{7,5},{8,10},{9,11},{10,... | collective-permute-start | bytes 49160 | tf_op jit(solution)/shard_map/ppermute | solution.py:492
  5.6 5.0 %collective-permute-start.3 = (f32[1,32,64]{2,1,0:T(8,128)S(1)}, f32[1,32,64]{2,1,0:T(8,128)S(1)}, u32[]{:S(2)}, u32[]{:S(2)}) collective-permute-start(f32[1,32,64]{2,1,0:T(8,128)S(1)} %copy-done), channel_id=1, source_target_pairs={{8,0},{16,8},{24,16},{32,24},{40,32},{48,40},{56,48},{64,56},{72,6... | collective-permute-start | bytes 24584 | tf_op jit(solution)/shard_map/ppermute | solution.py:509
  6.3 5.6 %collective-permute-start.2 = (f32[4,32,64]{2,1,0:T(8,128)S(1)}, f32[4,32,64]{2,1,0:T(8,128)S(1)}, u32[]{:S(2)}, u32[]{:S(2)}) collective-permute-start(f32[4,32,64]{2,1,0:T(8,128)S(1)} %pad_maximum_fusion), channel_id=1, source_target_pairs={{0,6},{1,7},{2,4},{3,5},{4,2},{5,3},{6,0},{7,1},{8,14},{9,15},{10,... | collective-permute-start | bytes 98312 | tf_op jit(solution)/shard_map/ppermute | solution.py:492
  9.2 2.7 %copy-start.1 = (f32[1,32,64]{2,1,0:T(8,128)S(1)}, f32[1,32,64]{2,1,0:T(8,128)}, u32[]{:S(2)}) copy-start(f32[1,32,64]{2,1,0:T(8,128)} %param.13) | copy-start | bytes 24580
  9.2 2.7 %copy-start.2 = (f32[1,32,64]{2,1,0:T(8,128)S(1)}, f32[1,32,64]{2,1,0:T(8,128)}, u32[]{:S(2)}) copy-start(f32[1,32,64]{2,1,0:T(8,128)} %param.14) | copy-start | bytes 24580
  9.2 2.7 %copy-start.4 = (s32[1,4]{1,0:T(1,128)S(1)}, s32[1,4]{1,0:T(1,128)}, u32[]{:S(2)}) copy-start(s32[1,4]{1,0:T(1,128)} %neigh_ref.1) | copy-start | bytes 52
  14.1 11.3 %collective-permute-start.4 = (f32[128,128]{1,0:T(8,128)S(1)}, f32[128,128]{1,0:T(8,128)S(1)}, u32[]{:S(2)}, u32[]{:S(2)}) collective-permute-start(f32[128,128]{1,0:T(8,128)S(1)} %get-tuple-element.40.own_ref), channel_id=1, source_target_pairs={{0,8},{8,0},{16,24},{24,16},{32,40},{40,32},{48,56},{56,48},{64,72... | collective-permute-start | bytes 196616 | tf_op jit(solution)/shard_map/ppermute | solution.py:495
  21.9 5.3 %collective-permute-start.5 = (f32[128,128]{1,0:T(8,128)S(1)}, f32[128,128]{1,0:T(8,128)S(1)}, u32[]{:S(2)}, u32[]{:S(2)}) collective-permute-start(f32[128,128]{1,0:T(8,128)S(1)} %get-tuple-element.40.own_ref), channel_id=1, source_target_pairs={{0,16},{8,24},{16,0},{24,8},{32,48},{40,56},{48,32},{56,40},{64,80... | collective-permute-start | bytes 196616 | tf_op jit(solution)/shard_map/ppermute | solution.py:495
  21.9 6.4 %collective-permute-start.6 = (f32[128,128]{1,0:T(8,128)S(1)}, f32[128,128]{1,0:T(8,128)S(1)}, u32[]{:S(2)}, u32[]{:S(2)}) collective-permute-start(f32[128,128]{1,0:T(8,128)S(1)} %get-tuple-element.40.own_ref), channel_id=1, source_target_pairs={{0,24},{8,16},{16,8},{24,0},{32,56},{40,48},{48,40},{56,32},{64,88... | collective-permute-start | bytes 196616 | tf_op jit(solution)/shard_map/ppermute | solution.py:495
  29.3 7.4 %collective-permute-start.7 = (f32[128,128]{1,0:T(8,128)S(1)}, f32[128,128]{1,0:T(8,128)S(1)}, u32[]{:S(2)}, u32[]{:S(2)}) collective-permute-start(f32[128,128]{1,0:T(8,128)S(1)} %get-tuple-element.45.own_ref), channel_id=1, source_target_pairs={{0,56},{8,48},{16,40},{24,32},{32,24},{40,16},{48,8},{56,0},{64,12... | collective-permute-start | bytes 196616 | tf_op jit(solution)/shard_map/ppermute | solution.py:495
  37.1 5.6 %collective-permute-start.10 = (f32[128,128]{1,0:T(8,128)S(1)}, f32[128,128]{1,0:T(8,128)S(1)}, u32[]{:S(2)}, u32[]{:S(2)}) collective-permute-start(f32[128,128]{1,0:T(8,128)S(1)} %get-tuple-element.47.own_ref), channel_id=1, source_target_pairs={{0,192},{8,200},{16,208},{24,216},{32,224},{40,232},{48,240},{56,2... | collective-permute-start | bytes 196616 | tf_op jit(solution)/shard_map/ppermute | solution.py:495
  38.0 4.7 %collective-permute-start.8 = (f32[128,128]{1,0:T(8,128)S(1)}, f32[128,128]{1,0:T(8,128)S(1)}, u32[]{:S(2)}, u32[]{:S(2)}) collective-permute-start(f32[128,128]{1,0:T(8,128)S(1)} %get-tuple-element.47.own_ref), channel_id=1, source_target_pairs={{0,64},{8,72},{16,80},{24,88},{32,96},{40,104},{48,112},{56,120},{... | collective-permute-start | bytes 196616 | tf_op jit(solution)/shard_map/ppermute | solution.py:495
  38.0 6.9 %collective-permute-start.9 = (f32[128,128]{1,0:T(8,128)S(1)}, f32[128,128]{1,0:T(8,128)S(1)}, u32[]{:S(2)}, u32[]{:S(2)}) collective-permute-start(f32[128,128]{1,0:T(8,128)S(1)} %get-tuple-element.47.own_ref), channel_id=1, source_target_pairs={{0,128},{8,136},{16,144},{24,152},{32,160},{40,168},{48,176},{56,1... | collective-permute-start | bytes 196616 | tf_op jit(solution)/shard_map/ppermute | solution.py:495
